TPU v7x, 32 devices: a whole 2x2x4 slice. The times are simulated.
32 devices in a mesh: ctx: 8 (over y, x, core), wa: 4 (over z).
Axes of the slice: x: 2, y: 2, z: 4, core: 2. Of those that a mesh axis runs over, the one named last changes fastest.
Arguments:
- tokens: bfloat16 [4, 1024, 2048], P('wa', 'ctx'), may hold values from -6 to 6
- lengths: int32 [4, 2], P('wa'), may hold values from 384 to 640, as said below
- dealing: int32 [4, 8], P('wa'), may hold values from 0 to 7, each once within a row
- norm1_gain: float32 [2048], replicated, may hold values from 0.1 to 1.9
- w_qkv: bfloat16 [2048, 6144], P('wa'), may hold values from -0.125 to 0.125
- w_out: bfloat16 [2048, 2048], P('wa'), may hold values from -2 to 2
- norm2_gain: float32 [2048], replicated, may hold values from 0.1 to 1.9
- w_gate_up: bfloat16 [2048, 11008], P('wa'), may hold values from -0.125 to 0.125
- w_down: bfloat16 [5504, 2048], P('wa'), may hold values from -0.078125 to 0.078125
- grad_out: bfloat16 [4, 1024, 2048], P('wa', 'ctx'), may hold values from -6 to 6
Outputs:
- out: bfloat16 [4, 1024, 2048], P('wa', 'ctx')
- d_tokens: bfloat16 [4, 1024, 2048], P('wa', 'ctx')
- d_norm1_gain: float32 [2048], replicated
- d_w_qkv: float32 [2048, 6144], P('wa')
- d_w_out: float32 [2048, 2048], P('wa')
- d_norm2_gain: float32 [2048], replicated
- d_w_gate_up: float32 [2048, 11008], P('wa')
- d_w_down: float32 [5504, 2048], P('wa')
Inputs may be any that keep to these rules, and one draw needn't show every extreme that they name: Each row holds the lengths of the two sequences of that group, first sequence first; they sum to 1024; some row holds a sequence of exactly 384 tokens. `dealing`: each row is a permutation of the block numbers of the group.
All inputs are finite; a program needn't handle non-finite values.
Results may differ from a plain program's by a relative error of at most 0.019.
Values may be sent and summed in bfloat16 or wider, within the bound.
A program may use at most 576 MiB of HBM per device.

v0:
```python
import math

import jax
import jax.numpy as jnp
from jax import lax
from jax.sharding import PartitionSpec as P

HEADS = 16
HEAD = 128
FF = 5504
WINDOW = 2048
BLOCK = 128


EPSILON = 1e-06


def dot_plain(left, right):
    return jnp.dot(left, right, preferred_element_type=jnp.float32)


def dot_right_t(left, right):
    return lax.dot_general(
        left, right, (((1,), (1,)), ((), ())), preferred_element_type=jnp.float32
    )


def dot_left_t(left, right):
    return lax.dot_general(
        left, right, (((0,), (0,)), ((), ())), preferred_element_type=jnp.float32
    )


def rms_scale(values):
    return lax.rsqrt(jnp.mean(values * values, axis=-1, keepdims=True) + EPSILON)


def rotary_tables(seq_pos):
    half_width = HEAD // 2
    inverse_freq = jnp.power(10000.0, -2.0 * jnp.arange(half_width, dtype=jnp.float32) / HEAD)
    angles = seq_pos.astype(jnp.float32)[:, None] * inverse_freq[None, :]
    return (jnp.cos(angles)[:, None, :], jnp.sin(angles)[:, None, :])


def rotate(values, cosine, sine):
    half_width = HEAD // 2
    first_half = values[..., :half_width]
    second_half = values[..., half_width:]
    return jnp.concatenate(
        [first_half * cosine - second_half * sine, first_half * sine + second_half * cosine],
        axis=-1,
    )


def unrotate(values, cosine, sine):
    half_width = HEAD // 2
    first_half = values[..., :half_width]
    second_half = values[..., half_width:]
    return jnp.concatenate(
        [first_half * cosine + second_half * sine, second_half * cosine - first_half * sine],
        axis=-1,
    )


def row_picker(targets, carried, segment):
    inside = (targets >= 0) & (targets < segment.shape[0])
    taken_rows = jnp.take(segment, jnp.clip(targets, 0, segment.shape[0] - 1), axis=0)
    return jnp.where(inside[:, None], taken_rows, carried)


def per_device(
    tokens, lengths, dealing, norm1_gain, w_qkv, w_out, norm2_gain, w_gate_up, w_down, grad_out
):
    tok_rows = tokens.shape[1]
    width = tokens.shape[2]
    ctx_index = lax.axis_index("ctx")
    block_order = dealing[0]
    block_total = block_order.shape[0]
    group_rows = block_total * BLOCK
    own_blocks = tok_rows // BLOCK
    first_length = lengths[0, 0]
    in_block = jnp.arange(BLOCK, dtype=jnp.int32)
    key_pos = jnp.repeat(block_order, BLOCK) * BLOCK + jnp.tile(in_block, block_total)
    key_seg = (key_pos >= first_length).astype(jnp.int32)
    query_pos = lax.dynamic_slice_in_dim(key_pos, ctx_index * tok_rows, tok_rows)
    query_seg = lax.dynamic_slice_in_dim(key_seg, ctx_index * tok_rows, tok_rows)
    cosine, sine = rotary_tables(query_pos - query_seg * first_length)
    distance = query_pos[:, None] - key_pos[None, :]
    allowed = (query_seg[:, None] == key_seg[None, :]) & (distance >= 0) & (distance < WINDOW)
    block_ids = jnp.arange(block_total, dtype=jnp.int32)
    inverse = jnp.sum(
        jnp.where(block_order[None, :] == block_ids[:, None], block_ids[None, :], 0), axis=1
    )
    own_sources = lax.dynamic_slice_in_dim(inverse, ctx_index * own_blocks, own_blocks)
    source_rows = jnp.repeat(own_sources, BLOCK) * BLOCK + jnp.tile(in_block, own_blocks)
    empty_rows = jnp.zeros((tok_rows, width), jnp.bfloat16)
    cotangent = row_picker(
        query_pos, empty_rows, lax.all_gather(grad_out[0], "ctx", axis=0, tiled=True)
    )
    inputs = tokens[0].astype(jnp.float32)
    scale_one = rms_scale(inputs)
    normed_one = inputs * scale_one
    act_one = (normed_one * norm1_gain).astype(jnp.bfloat16)
    full_qkv, full_out = (
        lax.all_gather(w_qkv, "wa", axis=0, tiled=True),
        lax.all_gather(w_out, "wa", axis=0, tiled=True),
    )
    projected = dot_plain(act_one, full_qkv)
    query_b = rotate(projected[:, :width].reshape(tok_rows, HEADS, HEAD), cosine, sine).astype(
        jnp.bfloat16
    )
    key_b = rotate(
        projected[:, width : 2 * width].reshape(tok_rows, HEADS, HEAD), cosine, sine
    ).astype(jnp.bfloat16)
    value_b = projected[:, 2 * width :].astype(jnp.bfloat16)
    kv_local = jnp.concatenate([key_b.reshape(tok_rows, width), value_b], axis=1)
    kv_all = lax.all_gather(kv_local, "ctx", axis=0, tiled=True)
    keys_all = kv_all[:, :width].reshape(group_rows, HEADS, HEAD)
    values_all = kv_all[:, width:].reshape(group_rows, HEADS, HEAD)
    score_scale = math.sqrt(HEAD)
    per_group = min(4, HEADS)
    mixed_parts = []
    total_parts = []
    for head_first in range(0, HEADS, per_group):
        query_part = query_b[:, head_first : head_first + per_group]
        key_part = keys_all[:, head_first : head_first + per_group]
        value_part = values_all[:, head_first : head_first + per_group]
        scores = (
            jnp.einsum("qhe,khe->hqk", query_part, key_part, preferred_element_type=jnp.float32)
            / score_scale
        )
        scores = jnp.where(allowed[None], scores, -jnp.inf)
        largest = jnp.max(scores, axis=2, keepdims=True)
        log_total = largest + jnp.log(jnp.sum(jnp.exp(scores - largest), axis=2, keepdims=True))
        probs_b = jnp.exp(scores - log_total).astype(jnp.bfloat16)
        mixed_parts.append(
            jnp.einsum("hqk,khe->qhe", probs_b, value_part, preferred_element_type=jnp.float32)
        )
        total_parts.append(log_total[:, :, 0])
    log_totals = jnp.concatenate(total_parts, axis=0)
    attended_b = jnp.concatenate(mixed_parts, axis=1).reshape(tok_rows, width).astype(jnp.bfloat16)
    hidden = inputs + dot_plain(attended_b, full_out)
    scale_two = rms_scale(hidden)
    normed_two = hidden * scale_two
    act_two = (normed_two * norm2_gain).astype(jnp.bfloat16)
    full_gate_up, full_down = (
        lax.all_gather(w_gate_up, "wa", axis=0, tiled=True),
        lax.all_gather(w_down, "wa", axis=0, tiled=True),
    )
    gate_up = dot_plain(act_two, full_gate_up)
    gate_part = gate_up[:, :FF]
    up_part = gate_up[:, FF:]
    sigmoid_gate = jax.nn.sigmoid(gate_part)
    silu_gate = gate_part * sigmoid_gate
    inner_b = (silu_gate * up_part).astype(jnp.bfloat16)
    result_b = (hidden + dot_plain(inner_b, full_down)).astype(jnp.bfloat16)
    out_given = row_picker(
        source_rows, empty_rows, lax.all_gather(result_b, "ctx", axis=0, tiled=True)
    )
    back_gate_up, back_down = (
        lax.all_gather(w_gate_up, "wa", axis=0, tiled=True),
        lax.all_gather(w_down, "wa", axis=0, tiled=True),
    )
    down_share = lax.psum_scatter(
        dot_left_t(inner_b, cotangent).astype(jnp.bfloat16), "wa", scatter_dimension=0, tiled=True
    )
    d_inner = dot_right_t(cotangent, back_down)
    d_gate = d_inner * up_part * sigmoid_gate * (1.0 + gate_part * (1.0 - sigmoid_gate))
    d_gate_up_b = jnp.concatenate([d_gate, d_inner * silu_gate], axis=1).astype(jnp.bfloat16)
    gate_up_share = lax.psum_scatter(
        dot_left_t(act_two, d_gate_up_b).astype(jnp.bfloat16), "wa", scatter_dimension=0, tiled=True
    )
    d_normed_two = dot_right_t(d_gate_up_b, back_gate_up)
    gain_two_part = jnp.sum(d_normed_two * normed_two, axis=0)
    scaled_two = d_normed_two * norm2_gain
    d_hidden = cotangent.astype(jnp.float32) + scale_two * (
        scaled_two - normed_two * jnp.mean(scaled_two * normed_two, axis=1, keepdims=True)
    )
    d_branch_b = d_hidden.astype(jnp.bfloat16)
    back_qkv, back_out = (
        lax.all_gather(w_qkv, "wa", axis=0, tiled=True),
        lax.all_gather(w_out, "wa", axis=0, tiled=True),
    )
    grad_mixed_b = (
        dot_right_t(d_branch_b, back_out).astype(jnp.bfloat16).reshape(tok_rows, HEADS, HEAD)
    )
    head_steps = HEADS // per_group

    def make_backward():

        def backward_heads(head_index, carried):
            d_query, d_keys_values, row_dots = carried
            head_first = head_index * per_group
            query_part = lax.dynamic_slice_in_dim(query_b, head_first, per_group, 1)
            key_part = lax.dynamic_slice_in_dim(keys_all, head_first, per_group, 1)
            value_part = lax.dynamic_slice_in_dim(values_all, head_first, per_group, 1)
            grad_part = lax.dynamic_slice_in_dim(grad_mixed_b, head_first, per_group, 1)
            log_part = lax.dynamic_slice_in_dim(log_totals, head_first, per_group, 0)
            scores = (
                jnp.einsum("qhe,khe->hqk", query_part, key_part, preferred_element_type=jnp.float32)
                / score_scale
            )
            scores = jnp.where(allowed[None], scores, -jnp.inf)
            probs = jnp.exp(scores - log_part[:, :, None])
            d_probs = jnp.einsum(
                "qhe,khe->hqk", grad_part, value_part, preferred_element_type=jnp.float32
            )
            row_dot = jnp.sum(probs * d_probs, axis=2)
            d_scores = (probs * (d_probs - row_dot[:, :, None])).astype(jnp.bfloat16)
            query_grad = (
                jnp.einsum("hqk,khe->qhe", d_scores, key_part, preferred_element_type=jnp.float32)
                / score_scale
            )
            d_query = lax.dynamic_update_slice_in_dim(d_query, query_grad, head_first, 1)
            row_dots = lax.dynamic_update_slice_in_dim(row_dots, row_dot, head_first, 0)
            key_grad = (
                jnp.einsum("hqk,qhe->khe", d_scores, query_part, preferred_element_type=jnp.float32)
                / score_scale
            )
            value_grad = jnp.einsum(
                "hqk,qhe->khe",
                probs.astype(jnp.bfloat16),
                grad_part,
                preferred_element_type=jnp.float32,
            )
            d_keys_values = lax.dynamic_update_slice_in_dim(
                d_keys_values, key_grad.reshape(group_rows, per_group * HEAD), head_first * HEAD, 1
            )
            d_keys_values = lax.dynamic_update_slice_in_dim(
                d_keys_values,
                value_grad.reshape(group_rows, per_group * HEAD),
                width + head_first * HEAD,
                1,
            )
            return (d_query, d_keys_values, row_dots)

        return backward_heads

    start_query = jnp.zeros((tok_rows, HEADS, HEAD), jnp.float32)
    start_dots = jnp.zeros((HEADS, tok_rows), jnp.float32)
    start_keys_values = jnp.zeros((group_rows, 2 * width), jnp.float32)
    d_query, d_keys_values, row_dots = lax.fori_loop(
        0, head_steps, make_backward(), (start_query, start_keys_values, start_dots)
    )
    d_kv_mine = lax.psum_scatter(d_keys_values, "ctx", scatter_dimension=0, tiled=True)
    key_rot_grad = d_kv_mine[:, :width].reshape(tok_rows, HEADS, HEAD)
    d_qkv_b = jnp.concatenate(
        [
            unrotate(d_query, cosine, sine).reshape(tok_rows, width),
            unrotate(key_rot_grad, cosine, sine).reshape(tok_rows, width),
            d_kv_mine[:, width:],
        ],
        axis=1,
    ).astype(jnp.bfloat16)
    qkv_part = dot_left_t(act_one, d_qkv_b)
    out_part = dot_left_t(attended_b, d_branch_b)
    attn_share = lax.psum_scatter(
        jnp.concatenate([qkv_part, out_part], axis=1).astype(jnp.bfloat16),
        "wa",
        scatter_dimension=0,
        tiled=True,
    )
    d_normed_one = dot_right_t(d_qkv_b, back_qkv)
    gain_one_part = jnp.sum(d_normed_one * normed_one, axis=0)
    scaled_one = d_normed_one * norm1_gain
    d_inputs = d_hidden + scale_one * (
        scaled_one - normed_one * jnp.mean(scaled_one * normed_one, axis=1, keepdims=True)
    )
    gain_one_sum, gain_two_sum = lax.psum((gain_one_part, gain_two_part), ("ctx", "wa"))
    attn_total, gate_up_total, down_total = (
        lax.psum(attn_share, "ctx").astype(jnp.float32),
        lax.psum(gate_up_share, "ctx").astype(jnp.float32),
        lax.psum(down_share, "ctx").astype(jnp.float32),
    )
    return (
        out_given[None],
        d_inputs.astype(jnp.bfloat16)[None],
        gain_one_sum,
        attn_total[:, : 3 * width],
        attn_total[:, 3 * width :],
        gain_two_sum,
        gate_up_total,
        down_total,
    )


def solution(mesh):
    in_specs = (
        P("wa", "ctx", None),
        P("wa", None),
        P("wa", None),
        P(),
        P("wa", None),
        P("wa", None),
        P(),
        P("wa", None),
        P("wa", None),
        P("wa", "ctx", None),
    )
    out_specs = (
        P("wa", "ctx", None),
        P("wa", "ctx", None),
        P(),
        P("wa", None),
        P("wa", None),
        P(),
        P("wa", None),
        P("wa", None),
    )
    return jax.shard_map(
        per_device, mesh=mesh, in_specs=in_specs, out_specs=out_specs, check_vma=False
    )
```

profile of v0, /device:TPU:9, one launch (start us, length us, event | category | flops | bytes accessed | tf_op | source)
XLA Modules:
  0.0 4123.5 jit_solution(4794331274431847272)
XLA Ops:
  9.7 423.5 %all-gather.9.cloned.1.call-done = bf16[2048,6144]{1,0:T(8,128)(2,1)} async-done(((bf16[512,6144]{1,0:T(8,128)(2,1)}), bf16[2048,6144]{1,0:T(8,128)(2,1)}) %all-gather.9.cloned.1.call-update) | async-done | bytes 25165840 | tf_op jit(solution)/shard_map/all_gather | solution.py:105
  433.2 10.1 fusion.58
  449.4 23.8 all-gather.21.cloned.1.call-done
  477.7 52.4 %all-gather.11.cloned.1.call-done = bf16[1024,4096]{1,0:T(8,128)(2,1)} async-done(((bf16[128,4096]{1,0:T(8,128)(2,1)}), bf16[1024,4096]{1,0:T(8,128)(2,1)}) %all-gather.11.cloned.1.call-update) | async-done | bytes 8388624 | tf_op jit(solution)/shard_map/all_gather | solution.py:117
  545.5 132.4 %all-gather.13.cloned.1.call-done = bf16[2048,2048]{1,0:T(8,128)(2,1)} async-done(((bf16[512,2048]{1,0:T(8,128)(2,1)}), bf16[2048,2048]{1,0:T(8,128)(2,1)}) %all-gather.13.cloned.1.call-update) | async-done | bytes 8388624 | tf_op jit(solution)/shard_map/all_gather | solution.py:106
  678.0 4.8 multiply_reduce_fusion.3
  682.8 745.7 %all-gather.15.cloned.1.call-done = bf16[2048,11008]{1,0:T(8,128)(2,1)} async-done(((bf16[512,11008]{1,0:T(8,128)(2,1)}), bf16[2048,11008]{1,0:T(8,128)(2,1)}) %all-gather.15.cloned.1.call-update) | async-done | bytes 45088784 | tf_op jit(solution)/shard_map/all_gather | solution.py:147
  1428.4 23.2 fusion.64
  1451.6 359.2 %all-gather.17.cloned.1.call-done = bf16[5504,2048]{1,0:T(8,128)(2,1)} async-done(((bf16[1376,2048]{1,0:T(8,128)(2,1)}), bf16[5504,2048]{1,0:T(8,128)(2,1)}) %all-gather.17.cloned.1.call-update) | async-done | bytes 22544400 | tf_op jit(solution)/shard_map/all_gather | solution.py:148
  1810.8 14.9 multiply_convert_fusion.2
  1825.7 21.4 multiply_reduce_fusion.1
  1847.6 6.7 fusion.25
  1855.5 7.9 broadcast_in_dim.154
  1863.4 75.1 %while.18 = (s32[]{:T(128)}, f32[128,16,128]{2,0,1:T(8,128)}, f32[1024,4096]{0,1:T(8,128)}, bf16[1024,16,128]{2,0,1:T(8,128)(2,1)}, bf16[128,16,128]{2,0,1:T(8,1...) while((s32[]{:T(128)}, f32[128,16,128]{2,0,1:T(8,128)}, ...), condition=%wide.region_14.16_spmd.clone, body=%wide.region_12.15_spmd.clone.sunk | while | flops 677182976 | bytes 61174424 | solution.py:242
  1940.0 13.5 convolution_convert_fusion.1
  1955.6 22.4 convolution_convert_fusion
  1979.3 5.7 convolution_convert_fusion.3
  1985.1 70.6 %reduce-scatter.7.cloned.1.call-done = f32[128,4096]{0,1:T(8,128)} async-done(((f32[1024,4096]{0,1:T(8,128)}), f32[128,4096]{0,1:T(8,128)}) %reduce-scatter.7.cloned.1.call-update) | async-done | bytes 2097168 | tf_op jit(solution)/shard_map/reduce_scatter | solution.py:245
  2074.5 13.1 convolution_convert_fusion.2
  2087.6 22.7 pad_maximum_fusion
  2110.4 11.9 fusion.19
  2122.6 308.0 %reduce-scatter.11.cloned.1.call-done = bf16[1376,2048]{1,0:T(8,128)(2,1)} async-done(((bf16[5504,2048]{1,0:T(8,128)(2,1)}), bf16[1376,2048]{1,0:T(8,128)(2,1)}) %reduce-scatter.11.cloned.1.call-update) | async-done | bytes 5636112 | tf_op jit(solution)/shard_map/reduce_scatter | solution.py:164
  2430.6 738.1 %reduce-scatter.9.cloned.1.call-done = bf16[512,11008]{1,0:T(8,128)(2,1)} async-done(((bf16[2048,11008]{1,0:T(8,128)(2,1)}), bf16[512,11008]{1,0:T(8,128)(2,1)}) %reduce-scatter.9.cloned.1.call-update) | async-done | bytes 11272208 | tf_op jit(solution)/shard_map/reduce_scatter | solution.py:170
  3168.7 556.0 %reduce-scatter.13.cloned.1.call-done = bf16[512,8192]{1,0:T(8,128)(2,1)} async-done(((bf16[2048,8192]{1,0:T(8,128)(2,1)}), bf16[512,8192]{1,0:T(8,128)(2,1)}) %reduce-scatter.13.cloned.1.call-update) | async-done | bytes 8388624
  3726.8 41.5 %all-gather.19.cloned.1.call-done = bf16[1024,2048]{1,0:T(8,128)(2,1)} async-done(((bf16[128,2048]{1,0:T(8,128)(2,1)}), bf16[1024,2048]{1,0:T(8,128)(2,1)}) %all-gather.19.cloned.1.call-update) | async-done | bytes 4194320 | tf_op jit(solution)/shard_map/all_gather | solution.py:158
  3768.3 5.0 gather_fusion
  3775.2 21.6 fusion.36
  3796.9 40.7 all-reduce.1
  3840.0 245.1 %all-reduce.5.cloned.1.call-done = (bf16[512,8192]{1,0:T(8,128)(2,1)}, bf16[512,11008]{1,0:T(8,128)(2,1)}, bf16[1376,2048]{1,0:T(8,128)(2,1)}) async-done(((bf16[512,8192]{1,0:T(8,128)(2,1)}, bf16[512,11008]{1,0:T(8,128)(2,1)}, bf16[1376,2048]{1,0:T(8,128)(2,1)}), (bf16[512,8192]{1,0:T(8,128)(2,1)}, bf16[512,11008]{1,0:T(8,128)(2,1)}, bf16[1376,2048]{1,0:T(8,128)(2,1)})) %all-reduce.5.cloned.1.call-update) | async-done | bytes 25296912 | tf_op jit(solution)/shard_map/psum | solution.py:271
  4085.1 9.4 slice.157
  4097.0 13.3 convert_element_type.121
  4110.3 5.9 convert_element_type.123
  (316 shorter events, 136.2 us)
Async XLA Ops:
  7.2 426.0 %copy-start.28 = (f32[2048]{0:T(1024)S(1)}, f32[2048]{0:T(1024)}, u32[]{:S(2)}) copy-start(f32[2048]{0:T(1024)} %param.17) | copy-start | bytes 24580
  7.2 426.0 %all-gather.9.cloned.1.call-start = ((), (), s32[]{:S(2)}) async-start(), calls=%async_computation.4 | async-start | bytes 31457280 | tf_op jit(solution)/shard_map/all_gather | solution.py:105
  7.9 465.3 %all-gather.21.cloned.1.call-start = ((), (), s32[]{:S(2)}) async-start(), calls=%async_computation.13 | async-start | bytes 4718592 | tf_op jit(solution)/shard_map/all_gather | solution.py:98
  8.7 521.4 %all-gather.11.cloned.1.call-start = ((), (), s32[]{:S(2)}) async-start(), calls=%async_computation.5 | async-start | bytes 9437184 | tf_op jit(solution)/shard_map/all_gather | solution.py:117
  8.9 1838.2 %copy-start.41 = (pred[128]{0:T(512)(128)(4,1)}, pred[128]{0:T(512)(128)(4,1)S(1)}, u32[]{:S(2)}) copy-start(pred[128]{0:T(512)(128)(4,1)S(1)} %get-tuple-element.344) | copy-start | bytes 388
  9.1 434.1 %copy-start.37 = (f32[128]{0:T(128)}, f32[128]{0:T(128)S(1)}, u32[]{:S(2)}) copy-start(f32[128]{0:T(128)S(1)} %add_rsqrt_fusion.1) | copy-start | bytes 1540
  9.7 434.9 %copy-start.24 = (f32[128,64]{1,0:T(8,128)}, f32[128,64]{1,0:T(8,128)S(1)}, u32[]{:S(2)}) copy-start(f32[128,64]{1,0:T(8,128)S(1)} %get-tuple-element.381) | copy-start | bytes 98308
  9.7 434.9 %copy-start.26 = (f32[128,64]{1,0:T(8,128)}, f32[128,64]{1,0:T(8,128)S(1)}, u32[]{:S(2)}) copy-start(f32[128,64]{1,0:T(8,128)S(1)} %get-tuple-element.382) | copy-start | bytes 98308
  447.3 230.7 %all-gather.13.cloned.1.call-start = ((), (), s32[]{:S(2)}) async-start(), calls=%async_computation.6 | async-start | bytes 10485760 | tf_op jit(solution)/shard_map/all_gather | solution.py:106
  447.9 980.5 %all-gather.15.cloned.1.call-start = ((), (), s32[]{:S(2)}) async-start(), calls=%async_computation.7 | async-start | bytes 56360960 | tf_op jit(solution)/shard_map/all_gather | solution.py:147
  448.5 1362.3 %all-gather.17.cloned.1.call-start = ((), (), s32[]{:S(2)}) async-start(), calls=%async_computation.8 | async-start | bytes 28180480 | tf_op jit(solution)/shard_map/all_gather | solution.py:148
  449.1 1606.6 %reduce-scatter.7.cloned.1.call-start = ((), (), s32[]{:S(2)}) async-start(), calls=%async_computation.10 | async-start | bytes 18874368 | tf_op jit(solution)/shard_map/reduce_scatter | solution.py:245
  449.1 1398.0 %copy-start.44 = (pred[128]{0:T(512)(128)(4,1)}, pred[128]{0:T(512)(128)(4,1)S(1)}, u32[]{:S(2)}) copy-start(pred[128]{0:T(512)(128)(4,1)S(1)} %get-tuple-element.346) | copy-start | bytes 388
  477.4 1369.7 %copy-start.17 = (bf16[128,2048]{1,0:T(8,128)(2,1)}, bf16[128,2048]{1,0:T(8,128)(2,1)S(1)}, u32[]{:S(2)}) copy-start(bf16[128,2048]{1,0:T(8,128)(2,1)S(1)} %gather_fusion.1) | copy-start | bytes 1572868
  545.5 137.2 %copy-start.10 = (bf16[128,16,128]{0,2,1:T(8,128)(2,1)}, bf16[128,16,128]{0,2,1:T(8,128)(2,1)S(1)}, u32[]{:S(2)}) copy-start(bf16[128,16,128]{0,2,1:T(8,128)(2,1)S(1)} %pad_maximum_fusion.9) | copy-start | bytes 1572868
  678.0 750.5 %copy-start.23 = (f32[2048]{0:T(1024)S(1)}, f32[2048]{0:T(1024)}, u32[]{:S(2)}) copy-start(f32[2048]{0:T(1024)} %param.20) | copy-start | bytes 24580
  682.7 1164.4 %copy-start.3 = (f32[128,2048]{1,0:T(8,128)}, f32[128,2048]{1,0:T(8,128)S(1)}, u32[]{:S(2)}) copy-start(f32[128,2048]{1,0:T(8,128)S(1)} %get-tuple-element.392) | copy-start | bytes 3145732
  682.8 1164.4 %copy-start.30 = (f32[128]{0:T(128)}, f32[128]{0:T(128)S(1)}, u32[]{:S(2)}) copy-start(f32[128]{0:T(128)S(1)} %add_rsqrt_fusion) | copy-start | bytes 1540
  1938.6 492.0 %reduce-scatter.11.cloned.1.call-start = ((), (), s32[]{:S(2)}) async-start(), calls=%async_computation.12 | async-start | bytes 28180480 | tf_op jit(solution)/shard_map/reduce_scatter | solution.py:164
  1953.5 1215.2 %reduce-scatter.9.cloned.1.call-start = ((), (), s32[]{:S(2)}) async-start(), calls=%async_computation.11 | async-start | bytes 56360960 | tf_op jit(solution)/shard_map/reduce_scatter | solution.py:170
  1978.0 1746.7 %reduce-scatter.13.cloned.1.call-start = ((), (), s32[]{:S(2)}) async-start(), calls=%async_computation.14 | async-start | bytes 41943040
  2065.7 8.8 copy-start.9
  2065.7 8.8 copy-start.29
  2065.7 8.8 copy-start.38
  2110.4 1657.9 %all-gather.19.cloned.1.call-start = ((), (), s32[]{:S(2)}) async-start(), calls=%async_computation.9 | async-start | bytes 4718592 | tf_op jit(solution)/shard_map/all_gather | solution.py:158
  2122.3 1962.8 %all-reduce.5.cloned.1.call-start = ((), (), s32[]{:S(2)}) async-start(), calls=%async_computation.15 | async-start | bytes 50593792 | tf_op jit(solution)/shard_map/psum | solution.py:271
  3726.7 48.5 %copy-start.21 = (bf16[128,16,128]{0,2,1:T(8,128)(2,1)S(1)}, bf16[128,16,128]{0,2,1:T(8,128)(2,1)}, u32[]{:S(2)}) copy-start(bf16[128,16,128]{0,2,1:T(8,128)(2,1)} %copy.113) | copy-start | bytes 1572868
  3726.8 48.5 %copy-start.22 = (bf16[128,2048]{0,1:T(8,128)(2,1)S(1)}, bf16[128,2048]{0,1:T(8,128)(2,1)}, u32[]{:S(2)}) copy-start(bf16[128,2048]{0,1:T(8,128)(2,1)} %slice.185) | copy-start | bytes 1572868
  3775.2 21.6 copy-start.36
  4085.1 9.4 copy-start.5
  4094.4 15.8 slice-start
  4097.0 13.3 slice-start.1
  (64 other events, 201.3 us)
Sparse Core Ops, SparseCore 0:
  9.6 423.4 all-gather.8
  435.1 38.1 all-gather.20
  475.7 54.3 all-gather.10
  531.6 146.3 all-gather.12
  679.4 748.9 all-gather.14
  1429.9 380.8 all-gather.16
  1938.7 116.9 reduce-scatter.6
  2058.7 371.9 reduce-scatter.10
  2433.0 735.6 reduce-scatter.8
  3170.9 553.7 reduce-scatter.12
  3727.3 40.9 all-gather.18
  3772.9 312.0 all-reduce.4
where the time goes:
time: 4130 us; the launch traced here: 4120 us
  waiting for transfers between devices  3700 us (90%)
  matrix products  200 us (5%)
  local copies, waits for them, and re-layouts  104 us (3%)
  other arithmetic  61.5 us (1%)
    all_gather x1, waiting for transfers between devices, per_device(): lax.all_gather(w_gate_up, 'wa', axis=0, tiled=True)  746 us
    reduce_scatter x1, waiting for transfers between devices, per_device(): lax.psum_scatter(dot_left_t(act_two, d_gate_up_b).astype(jnp.bfloat16), '...  738 us
    unnamed x13, waiting for transfers between devices  559 us
    all_gather x1, waiting for transfers between devices, per_device(): lax.all_gather(w_qkv, 'wa', axis=0, tiled=True)  423 us
    all_gather x1, waiting for transfers between devices, per_device(): lax.all_gather(w_down, 'wa', axis=0, tiled=True)  359 us
    reduce_scatter x1, waiting for transfers between devices, per_device(): lax.psum_scatter(dot_left_t(inner_b, cotangent).astype(jnp.bfloat16), 'wa...  308 us
    psum x1, waiting for transfers between devices, per_device(): lax.psum(attn_share, 'ctx').astype(jnp.float32)  245 us
    all_gather x1, waiting for transfers between devices, per_device(): lax.all_gather(w_out, 'wa', axis=0, tiled=True)  132 us
  transfers between devices with their start and end apart: 12, of which 12 were waited for; matrix products, arithmetic and copies ran while one was open for 5% of the time, Pallas kernels for 0%

commit v1 on v0

v1 whole, which is shorter than its diff:
```python
import math

import jax
import jax.numpy as jnp
from jax import lax
from jax.sharding import PartitionSpec as P

HEADS = 16
HEAD = 128
WINDOW = 2048
BLOCK = 128

EPSILON = 1e-06
BF = jnp.bfloat16
F32 = jnp.float32


def dot_plain(left, right):
    return jnp.dot(left, right, preferred_element_type=F32)


def dot_right_t(left, right):
    return lax.dot_general(left, right, (((1,), (1,)), ((), ())), preferred_element_type=F32)


def dot_left_t(left, right):
    return lax.dot_general(left, right, (((0,), (0,)), ((), ())), preferred_element_type=F32)


def rms_scale(values):
    return lax.rsqrt(jnp.mean(values * values, axis=-1, keepdims=True) + EPSILON)


def rotary_tables(seq_pos):
    half_width = HEAD // 2
    inverse_freq = jnp.power(10000.0, -2.0 * jnp.arange(half_width, dtype=F32) / HEAD)
    angles = seq_pos.astype(F32)[:, None] * inverse_freq[None, :]
    return (jnp.cos(angles)[:, None, :], jnp.sin(angles)[:, None, :])


def rotate(values, cosine, sine):
    half_width = HEAD // 2
    first = values[..., :half_width]
    second = values[..., half_width:]
    return jnp.concatenate(
        [first * cosine - second * sine, first * sine + second * cosine], axis=-1
    )


def gather_rows(values, axis):
    return lax.all_gather(values, axis, axis=0, tiled=True)


def scatter_rows(values, axis):
    return lax.psum_scatter(values, axis, scatter_dimension=0, tiled=True)


def per_device(
    tokens, lengths, dealing, norm1_gain, w_qkv, w_out, norm2_gain, w_gate_up, w_down, grad_out
):
    tok_rows, width = tokens.shape[1], tokens.shape[2]
    ctx_size = lax.axis_size("ctx")
    wa_size = lax.axis_size("wa")
    ctx_index = lax.axis_index("ctx")
    block_order = dealing[0]
    block_total = block_order.shape[0]
    group_rows = block_total * BLOCK
    own_blocks = tok_rows // BLOCK
    first_length = lengths[0, 0]
    heads_own = HEADS // ctx_size
    head_cols = heads_own * HEAD
    wa_rows = width // wa_size
    ff_total = w_gate_up.shape[1] // 2
    ff_own = w_down.shape[0]
    piece_rows = wa_rows // ctx_size

    block_ids = jnp.arange(block_total, dtype=jnp.int32)
    inverse = jnp.sum(
        jnp.where(block_order[None, :] == block_ids[:, None], block_ids[None, :], 0), axis=1
    )

    def pick_blocks(values, order):
        parts = [
            lax.dynamic_slice_in_dim(values, order[i] * BLOCK, BLOCK) for i in range(block_total)
        ]
        return jnp.concatenate(parts, axis=0)

    qkv_slice = jnp.concatenate(
        [
            lax.dynamic_slice_in_dim(w_qkv, part * width + ctx_index * head_cols, head_cols, 1)
            for part in range(3)
        ],
        axis=1,
    )
    qkv_cols = gather_rows(qkv_slice, "wa")
    out_cols = gather_rows(
        lax.dynamic_slice_in_dim(w_out, ctx_index * head_cols, head_cols, 1), "wa"
    )
    out_rows = lax.all_to_all(out_cols, "ctx", 0, 1, tiled=True)
    gu_piece = lax.dynamic_slice_in_dim(w_gate_up, ctx_index * piece_rows, piece_rows, 0)
    gu_send = jnp.stack(
        [
            jnp.concatenate(
                [
                    gu_piece[:, to * ff_own : (to + 1) * ff_own],
                    gu_piece[:, ff_total + to * ff_own : ff_total + (to + 1) * ff_own],
                ],
                axis=1,
            )
            for to in range(wa_size)
        ]
    )
    gu_mine = lax.all_to_all(gu_send, "wa", 0, 0, tiled=True)
    gu_all = lax.all_gather(gu_mine, "ctx", axis=0)
    gu_weight = jnp.transpose(gu_all, (1, 0, 2, 3)).reshape(width, 2 * ff_own)

    dealt = gather_rows(tokens[0], "ctx")
    given_b = pick_blocks(dealt, inverse)
    given = given_b.astype(F32)
    positions = jnp.arange(group_rows, dtype=jnp.int32)
    segments = (positions >= first_length).astype(jnp.int32)
    cosine, sine = rotary_tables(positions - segments * first_length)
    normed_one = given * rms_scale(given)
    act_one = (normed_one * norm1_gain).astype(BF)

    projected = dot_plain(act_one, qkv_cols)
    parts = [
        projected[:, i * head_cols : (i + 1) * head_cols].reshape(group_rows, heads_own, HEAD)
        for i in range(3)
    ]
    query_b = rotate(parts[0], cosine, sine).astype(BF)
    key_b = rotate(parts[1], cosine, sine).astype(BF)
    value_b = parts[2].astype(BF)
    score_scale = math.sqrt(HEAD)
    distance = positions[:, None] - positions[None, :]
    allowed = (segments[:, None] == segments[None, :]) & (distance >= 0) & (distance < WINDOW)
    scores = jnp.einsum("qhe,khe->hqk", query_b, key_b, preferred_element_type=F32) / score_scale
    scores = jnp.where(allowed[None], scores, -jnp.inf)
    largest = jnp.max(scores, axis=2, keepdims=True)
    weights = jnp.exp(scores - largest)
    probs = weights / jnp.sum(weights, axis=2, keepdims=True)
    probs_b = probs.astype(BF)
    mixed = jnp.einsum("hqk,khe->qhe", probs_b, value_b, preferred_element_type=F32)
    mixed_b = mixed.reshape(group_rows, head_cols).astype(BF)

    branch = scatter_rows(dot_plain(mixed_b, out_rows).astype(BF), "ctx")
    own_given = lax.dynamic_slice_in_dim(given_b, ctx_index * tok_rows, tok_rows)
    hidden = own_given.astype(F32) + branch.astype(F32)
    scale_two = rms_scale(hidden)
    normed_two = hidden * scale_two
    act_two = gather_rows((normed_two * norm2_gain).astype(BF), "wa")
    cotangent = gather_rows(grad_out[0], "wa")

    gate_up = dot_plain(act_two, gu_weight)
    gate_part = gate_up[:, :ff_own]
    up_part = gate_up[:, ff_own:]
    sigmoid_gate = jax.nn.sigmoid(gate_part)
    silu_gate = gate_part * sigmoid_gate
    inner_b = (silu_gate * up_part).astype(BF)
    result = scatter_rows(dot_plain(inner_b, w_down).astype(BF), "wa")
    out_given = (hidden + result.astype(F32)).astype(BF)

    d_inner = dot_right_t(cotangent, w_down)
    d_gate = d_inner * up_part * sigmoid_gate * (1.0 + gate_part * (1.0 - sigmoid_gate))
    d_gu_b = jnp.concatenate([d_gate, d_inner * silu_gate], axis=1).astype(BF)
    d_normed_two = scatter_rows(dot_right_t(d_gu_b, gu_weight).astype(BF), "wa").astype(F32)
    d_down = lax.psum(dot_left_t(inner_b, cotangent).astype(BF), "ctx").astype(F32)

    d_gu_share = dot_left_t(act_two, d_gu_b).astype(BF)
    d_gu_share = jnp.transpose(
        d_gu_share.reshape(wa_size, ctx_size, piece_rows, 2 * ff_own), (1, 0, 2, 3)
    ).reshape(ctx_size * wa_size, piece_rows, 2 * ff_own)
    d_gu_piece = scatter_rows(d_gu_share, "ctx")
    d_gu_back = lax.all_to_all(d_gu_piece, "wa", 0, 0, tiled=True)
    d_gu_rows = jnp.concatenate(
        [d_gu_back[i, :, :ff_own] for i in range(wa_size)]
        + [d_gu_back[i, :, ff_own:] for i in range(wa_size)],
        axis=1,
    )
    d_gate_up = gather_rows(d_gu_rows, "ctx").astype(F32)

    gain_two_part = jnp.sum(d_normed_two * normed_two, axis=0)
    scaled_two = d_normed_two * norm2_gain
    d_hidden = grad_out[0].astype(F32) + scale_two * (
        scaled_two - normed_two * jnp.mean(scaled_two * normed_two, axis=1, keepdims=True)
    )
    d_branch_b = gather_rows(d_hidden.astype(BF), "ctx")
    grad_mixed_b = dot_right_t(d_branch_b, out_rows).astype(BF)
    d_out_part = dot_left_t(mixed_b, d_branch_b).astype(BF)
    d_out_cols = lax.all_to_all(d_out_part, "ctx", 1, 0, tiled=True)
    d_out = lax.all_gather(scatter_rows(d_out_cols, "wa"), "ctx", axis=1, tiled=True).astype(F32)

    grad_heads = grad_mixed_b.reshape(group_rows, heads_own, HEAD)
    d_probs = jnp.einsum("qhe,khe->hqk", grad_heads, value_b, preferred_element_type=F32)
    row_dot = jnp.sum(probs * d_probs, axis=2, keepdims=True)
    d_scores = (probs * (d_probs - row_dot)).astype(BF)
    d_query = jnp.einsum("hqk,khe->qhe", d_scores, key_b, preferred_element_type=F32) / score_scale
    d_key = jnp.einsum("hqk,qhe->khe", d_scores, query_b, preferred_element_type=F32) / score_scale
    d_value = jnp.einsum("hqk,qhe->khe", probs_b, grad_heads, preferred_element_type=F32)
    d_qkv_b = jnp.concatenate(
        [
            rotate(d_query, cosine, -sine).reshape(group_rows, head_cols),
            rotate(d_key, cosine, -sine).reshape(group_rows, head_cols),
            d_value.reshape(group_rows, head_cols),
        ],
        axis=1,
    ).astype(BF)
    d_qkv_share = scatter_rows(dot_left_t(act_one, d_qkv_b).astype(BF), "wa")
    d_qkv_all = lax.all_gather(d_qkv_share, "ctx", axis=0)
    d_qkv = jnp.transpose(
        d_qkv_all.reshape(ctx_size, wa_rows, 3, head_cols), (1, 2, 0, 3)
    ).reshape(wa_rows, 3 * width).astype(F32)

    d_one_part = dot_right_t(d_qkv_b, qkv_cols)
    gain_one_part = jnp.sum(d_one_part * normed_one, axis=0)
    d_normed_one = scatter_rows(pick_blocks(d_one_part.astype(BF), block_order), "ctx").astype(F32)
    own = tokens[0].astype(F32)
    own_scale = rms_scale(own)
    own_normed = own * own_scale
    scaled_one = d_normed_one * norm1_gain
    own_order = lax.dynamic_slice_in_dim(block_order, ctx_index * own_blocks, own_blocks)
    d_hidden_dealt = jnp.concatenate(
        [
            lax.dynamic_slice_in_dim(d_branch_b, own_order[i] * BLOCK, BLOCK)
            for i in range(own_blocks)
        ],
        axis=0,
    ).astype(F32)
    d_tokens = d_hidden_dealt + own_scale * (
        scaled_one - own_normed * jnp.mean(scaled_one * own_normed, axis=1, keepdims=True)
    )
    gain_parts = jnp.stack([gain_one_part, gain_two_part])
    gain_sums = jnp.sum(lax.all_gather(gain_parts, ("ctx", "wa"), axis=0), axis=0)
    return (
        out_given[None],
        d_tokens.astype(BF)[None],
        gain_sums[0],
        d_qkv,
        d_out,
        gain_sums[1],
        d_gate_up,
        d_down,
    )


def solution(mesh):
    in_specs = (
        P("wa", "ctx", None),
        P("wa", None),
        P("wa", None),
        P(),
        P("wa", None),
        P("wa", None),
        P(),
        P("wa", None),
        P("wa", None),
        P("wa", "ctx", None),
    )
    out_specs = (
        P("wa", "ctx", None),
        P("wa", "ctx", None),
        P(),
        P("wa", None),
        P("wa", None),
        P(),
        P("wa", None),
        P("wa", None),
    )
    return jax.shard_map(
        per_device, mesh=mesh, in_specs=in_specs, out_specs=out_specs, check_vma=False
    )
```

time: 4130 us -> 1090 us (0.26)
  waiting for transfers between devices: 3700 us -> 593 us
  blocking collectives: 40.7 us -> 137 us
  matrix products: 200 us -> 118 us
    all_gather x7 -> x10, waiting for transfers between devices: 1780 us -> 332 us  [the longest x7 213 us: gather_rows(): return lax.all_gather(values, axis, axis=0, tiled=True)]
    reduce_scatter x3 -> x7, waiting for transfers between devices: 1120 us -> 191 us  [scatter_rows(): return lax.psum_scatter(values, axis, scatter_dimension=0, tiled=True)]
    unnamed x13 -> x18, waiting for transfers between devices: 559 us -> 2.14 us
    psum x1, waiting for transfers between devices: 245 us -> 61.2 us  [per_device(): lax.psum(dot_left_t(inner_b, cotangent).astype(BF), 'ctx').astype(F32)]
    all_to_all x0 -> x2, blocking collectives: none -> 73.6 us  [the longest x1 37.6 us: per_device(): gu_mine = lax.all_to_all(gu_send, 'wa', 0, 0, tiled=True)]
    all_gather x0 -> x1, blocking collectives: none -> 63.5 us  [per_device(): lax.all_gather(gain_parts, ('ctx', 'wa'), axis=0)]
    convert_element_type x0 -> x3, local copies, waits for them, and re-layouts: none -> 44 us  [the longest x2 28 us: per_device(): d_qkv = jnp.transpose(d_qkv_all.reshape(ctx_size, wa_rows, 3, head_cols),...]
    unnamed x86 -> x76, local copies, waits for them, and re-layouts: 16 us -> 57.7 us
  transfers between devices with their start and end apart: 12 -> 20, of which waited for: 12 -> 17; matrix products, arithmetic and copies ran while one was open for 5% -> 21% of each run, Pallas kernels for 0% -> 0%
where the time goes in v1:
time: 1090 us; the launch traced here: 1080 us
  waiting for transfers between devices  593 us (54%)
  local copies, waits for them, and re-layouts  138 us (13%)
  blocking collectives  137 us (13%)
  matrix products  118 us (11%)
  other arithmetic  61.6 us (6%)
  between operations  25.9 us (2%)
    all_gather x7, waiting for transfers between devices, gather_rows(): return lax.all_gather(values, axis, axis=0, tiled=True)  213 us
    reduce_scatter x7, waiting for transfers between devices, scatter_rows(): return lax.psum_scatter(values, axis, scatter_dimension=0, tiled=True)  191 us
    all_gather x1, waiting for transfers between devices, per_device(): gu_all = lax.all_gather(gu_mine, 'ctx', axis=0)  65.6 us
    all_gather x1, blocking collectives, per_device(): lax.all_gather(gain_parts, ('ctx', 'wa'), axis=0)  63.5 us
    psum x1, waiting for transfers between devices, per_device(): lax.psum(dot_left_t(inner_b, cotangent).astype(BF), 'ctx').astype(F32)  61.2 us
    unnamed x76, local copies, waits for them, and re-layouts  57.7 us
    all_gather x1, waiting for transfers between devices, per_device(): d_qkv_all = lax.all_gather(d_qkv_share, 'ctx', axis=0)  43.3 us
    all_to_all x1, blocking collectives, per_device(): gu_mine = lax.all_to_all(gu_send, 'wa', 0, 0, tiled=True)  37.6 us
  transfers between devices with their start and end apart: 20, of which 17 were waited for; matrix products, arithmetic and copies ran while one was open for 21% of the time, Pallas kernels for 0%

profile of v1, /device:TPU:9, one launch (start us, length us, event | category | flops | bytes accessed | tf_op | source)
XLA Modules:
  0.0 1083.3 jit_solution(8135283047513101627)
XLA Ops:
  13.2 25.8 %all-gather.19.cloned.1.call-done = bf16[2048,256]{1,0:T(8,128)(2,1)} async-done(((bf16[512,256]{1,0:T(8,128)(2,1)}), bf16[2048,256]{1,0:T(8,128)(2,1)}) %all-gather.19.cloned.1.call-update) | async-done | bytes 1048592 | tf_op jit(solution)/shard_map/all_gather | solution.py:51
  61.7 21.1 %all-gather.29.cloned.1.call-done = bf16[1,1024,2048]{2,1,0:T(8,128)(2,1)} async-done(((bf16[1,128,2048]{2,1,0:T(8,128)(2,1)}), bf16[1,1024,2048]{2,1,0:T(8,128)(2,1)}) %all-gather.29.cloned.1.call-update) | async-done | bytes 4194320 | tf_op jit(solution)/shard_map/all_gather | solution.py:51
  90.5 55.0 %all-gather.17.cloned.1.call-done = bf16[2048,768]{1,0:T(8,128)(2,1)} async-done(((bf16[512,768]{1,0:T(8,128)(2,1)}), bf16[2048,768]{1,0:T(8,128)(2,1)}) %all-gather.17.cloned.1.call-update) | async-done | bytes 3145744 | tf_op jit(solution)/shard_map/all_gather | solution.py:51
  167.4 8.7 fusion.67
  186.4 37.6 %all_to_all.48 = bf16[4,64,2752]{2,1,0:T(8,128)(2,1)} all-to-all(bf16[4,64,2752]{2,1,0:T(8,128)(2,1)S(1)} %pad_maximum_fusion.4), channel_id=1, replica_groups=mesh['ctx'=8,'wa'=4] {'wa'}, dimensions={0} | all-to-all | bytes 2818048 | tf_op jit(solution)/shard_map/all_to_all | solution.py:113
  224.1 12.1 %reduce-scatter.8.cloned.1.call-done = bf16[128,2048]{1,0:T(8,128)(2,1)} async-done(((bf16[1024,2048]{1,0:T(8,128)(2,1)}), bf16[128,2048]{1,0:T(8,128)(2,1)}) %reduce-scatter.8.cloned.1.call-update) | async-done | bytes 524304 | tf_op jit(solution)/shard_map/reduce_scatter | solution.py:55
  240.7 65.6 %all-gather.31.cloned.1.call-done = bf16[32,64,2752]{2,1,0:T(8,128)(2,1)} async-done(((bf16[4,64,2752]{2,1,0:T(8,128)(2,1)}), bf16[32,64,2752]{2,1,0:T(8,128)(2,1)}) %all-gather.31.cloned.1.call-update) | async-done | bytes 11272208 | tf_op jit(solution)/shard_map/all_gather | solution.py:114
  306.2 10.2 copy.109
  316.4 35.6 %all-gather.21.cloned.1.call-done = bf16[512,2048]{1,0:T(8,128)(2,1)} async-done(((bf16[128,2048]{1,0:T(8,128)(2,1)}), bf16[512,2048]{1,0:T(8,128)(2,1)}) %all-gather.21.cloned.1.call-update) | async-done | bytes 2097168 | tf_op jit(solution)/shard_map/all_gather | solution.py:51
  352.0 15.3 %fusion.68 = f32[512,2752]{0,1:T(8,128)} fusion(bf16[512,2048]{1,0:T(8,128)(2,1)} %all-gather.21.cloned.1.call-done, bf16[2048,2752]{1,0:T(8,128)(2,1)} %bitcast.155), kind=kOutput, calls=%fused_computation.157 | convolution fusion | flops 5771362304 | bytes 19005440 | tf_op jit(solution)/shard_map/dot_general | solution.py:19
  367.3 31.0 %all-gather.33.cloned.1.call-done = bf16[1,512,2048]{2,1,0:T(8,128)(2,1)} async-done(((bf16[1,128,2048]{2,1,0:T(8,128)(2,1)}), bf16[1,512,2048]{2,1,0:T(8,128)(2,1)}) %all-gather.33.cloned.1.call-update) | async-done | bytes 2097168 | tf_op jit(solution)/shard_map/all_gather | solution.py:51
  398.3 10.5 multiply_convert_fusion.2
  425.8 34.2 %reduce-scatter.12.cloned.1.call-done = bf16[128,2048]{1,0:T(8,128)(2,1)} async-done(((bf16[512,2048]{1,0:T(8,128)(2,1)}), bf16[128,2048]{1,0:T(8,128)(2,1)}) %reduce-scatter.12.cloned.1.call-update) | async-done | bytes 524304 | tf_op jit(solution)/shard_map/reduce_scatter | solution.py:55
  461.7 44.4 %reduce-scatter.10.cloned.1.call-done = bf16[128,2048]{1,0:T(8,128)(2,1)} async-done(((bf16[512,2048]{1,0:T(8,128)(2,1)}), bf16[128,2048]{1,0:T(8,128)(2,1)}) %reduce-scatter.10.cloned.1.call-update) | async-done | bytes 524304 | tf_op jit(solution)/shard_map/reduce_scatter | solution.py:55
  509.0 39.0 %all-gather.23.cloned.1.call-done = bf16[1024,2048]{1,0:T(8,128)(2,1)} async-done(((bf16[128,2048]{1,0:T(8,128)(2,1)}), bf16[1024,2048]{1,0:T(8,128)(2,1)}) %all-gather.23.cloned.1.call-update) | async-done | bytes 4194320 | tf_op jit(solution)/shard_map/all_gather | solution.py:51
  551.5 8.3 multiply_reduce_fusion
  593.4 11.1 %convolution_convert_fusion = bf16[2048,2752]{0,1:T(8,128)(2,1)} fusion(bf16[512,2048]{1,0:T(8,128)(2,1)} %all-gather.21.cloned.1.call-done, bf16[512,1376]{0,1:T(8,128)(2,1)} %copy-done.27, bf16[512,1376]{0,1:T(8,128)(2,1)} %copy-done.26), kind=kOutput, calls=%fused_computation.1 | convolution fusion | flops 5782634496 | bytes 16187392 | tf_op jit(solution)/shard_map/dot_general | solution.py:27
  604.4 15.9 %copy.124 = bf16[2048,2752]{1,0:T(8,128)(2,1)} copy(bf16[2048,2752]{0,1:T(8,128)(2,1)} %convolution_convert_fusion) | data formatting | bytes 22544384 | tf_op jit(solution)/shard_map/convert_element_type | solution.py:169
  620.3 10.0 copy.125
  659.0 9.5 reduce-scatter.16.cloned.1.call-done
  668.6 91.3 %reduce-scatter.20.cloned.1.call-done = bf16[4,64,2752]{2,1,0:T(8,128)(2,1)} async-done(((bf16[32,64,2752]{2,1,0:T(8,128)(2,1)}), bf16[4,64,2752]{2,1,0:T(8,128)(2,1)}) %reduce-scatter.20.cloned.1.call-update) | async-done | bytes 1409040 | tf_op jit(solution)/shard_map/reduce_scatter | solution.py:55
  759.9 36.0 %all_to_all.49 = bf16[4,64,2752]{2,1,0:T(8,128)(2,1)S(1)} all-to-all(bf16[4,64,2752]{2,1,0:T(8,128)(2,1)} %reduce-scatter.20.cloned.1.call-done), channel_id=1, replica_groups=mesh['ctx'=8,'wa'=4] {'wa'}, dimensions={0} | all-to-all | bytes 2818048 | tf_op jit(solution)/shard_map/all_to_all | solution.py:174
  799.3 61.2 %all-reduce.2.cloned.1.call-done = bf16[1376,2048]{1,0:T(8,128)(2,1)} async-done(((bf16[1376,2048]{1,0:T(8,128)(2,1)}), bf16[1376,2048]{1,0:T(8,128)(2,1)}) %all-reduce.2.cloned.1.call-update) | async-done | bytes 5636112 | tf_op jit(solution)/shard_map/psum | solution.py:167
  860.6 8.5 convert_element_type.174
  869.1 63.5 %all-gather.5 = f32[32,2,2048]{2,1,0:T(2,128)S(1)} all-gather(f32[1,2,2048]{2,1,0:T(2,128)S(1)} %maximum_bitcast_fusion.4), channel_id=5, replica_groups=mesh['ctx'=8,'wa'=4] {'ctx','wa'}, dimensions={0}, use_global_device_ids=true | all-gather | bytes 540672 | tf_op jit(solution)/shard_map/all_gather | solution.py:233
  937.2 10.2 all-gather.25.cloned.1.call-done
  951.5 43.3 %all-gather.35.cloned.1.call-done = bf16[4096,768]{1,0:T(8,128)(2,1)} async-done(((bf16[512,768]{1,0:T(8,128)(2,1)}), bf16[4096,768]{1,0:T(8,128)(2,1)}) %all-gather.35.cloned.1.call-update) | async-done | bytes 6291472 | tf_op jit(solution)/shard_map/all_gather | solution.py:209
  994.8 9.8 copy.121
  1004.6 22.7 %copy.142 = f32[96,8,8,512]{3,2,1,0:T(8,128)} copy(f32[96,8,8,512]{3,1,2,0:T(8,128)} %bitcast.149) | data formatting | bytes 25165824
  1027.3 18.3 %copy.122 = f32[512,3,8,256]{0,3,2,1:T(8,128)} copy(f32[512,3,8,256]{0,2,3,1:T(8,128)} %bitcast.150) | data formatting | bytes 25165824 | tf_op jit(solution)/shard_map/convert_element_type | solution.py:212
  1045.5 12.7 %copy.126 = f32[512,6144]{1,0:T(8,128)} copy(f32[512,6144]{0,1:T(8,128)} %bitcast.151) | data formatting | bytes 25165824
  1063.4 12.9 %convert_element_type.172 = f32[512,11008]{1,0:T(8,128)} convert(bf16[512,11008]{1,0:T(8,128)(2,1)} %all-gather.27.cloned.1.call-done) | non-fusion elementwise | flops 5636096 | bytes 33816576 | tf_op jit(solution)/shard_map/convert_element_type | solution.py:180
  (179 shorter events, 166.2 us)
Async XLA Ops:
  7.2 41.6 %copy-start.24 = (s32[1,2]{1,0:T(1,128)S(1)}, s32[1,2]{1,0:T(1,128)}, u32[]{:S(2)}) copy-start(s32[1,2]{1,0:T(1,128)} %param.11) | copy-start | bytes 28
  7.2 31.8 %all-gather.19.cloned.1.call-start = ((), (), s32[]{:S(2)}) async-start(), calls=%async_computation.12 | async-start | bytes 1310720 | tf_op jit(solution)/shard_map/all_gather | solution.py:51
  9.5 73.2 %all-gather.29.cloned.1.call-start = ((), (), s32[]{:S(2)}) async-start(), calls=%async_computation.25 | async-start | bytes 4718592 | tf_op jit(solution)/shard_map/all_gather | solution.py:51
  10.3 135.3 %all-gather.17.cloned.1.call-start = ((), (), s32[]{:S(2)}) async-start(), calls=%async_computation.11 | async-start | bytes 3932160 | tf_op jit(solution)/shard_map/all_gather | solution.py:51
  39.1 22.1 %all-to-all-start = ((bf16[8,256,256]{2,1,0:T(8,128)(2,1)}), bf16[8,256,256]{2,1,0:T(8,128)(2,1)S(1)}, u32[]{:S(2)}, u32[]{:S(2)}) async-start(bf16[8,256,256]{2,1,0:T(8,128)(2,1)} %bitcast.164), calls=%async_computation | async-start | bytes 2097152 | tf_op jit(solution)/shard_map/all_to_all | solution.py:99
  43.6 192.6 %reduce-scatter.8.cloned.1.call-start = ((), (), s32[]{:S(2)}) async-start(), calls=%async_computation.13 | async-start | bytes 4718592 | tf_op jit(solution)/shard_map/reduce_scatter | solution.py:55
  61.7 118.6 %copy-start.7 = (bf16[256,8,256]{0,2,1:T(8,128)(2,1)}, bf16[256,8,256]{0,2,1:T(8,128)(2,1)S(1)}, u32[]{:S(2)}) copy-start(bf16[256,8,256]{0,2,1:T(8,128)(2,1)S(1)} %copy.108) | copy-start | bytes 3145732
  87.4 58.1 %copy-start.23 = (f32[2048]{0:T(1024)S(1)}, f32[2048]{0:T(1024)}, u32[]{:S(2)}) copy-start(f32[2048]{0:T(1024)} %param.13) | copy-start | bytes 24580
  167.4 8.7 copy-start.17
  183.6 122.6 %all-gather.31.cloned.1.call-start = ((), (), s32[]{:S(2)}) async-start(), calls=%async_computation.26 | async-start | bytes 12976128 | tf_op jit(solution)/shard_map/all_gather | solution.py:114
  186.2 51.5 %copy-start.19 = (f32[2048]{0:T(1024)S(1)}, f32[2048]{0:T(1024)}, u32[]{:S(2)}) copy-start(f32[2048]{0:T(1024)} %param.16) | copy-start | bytes 24580
  224.0 127.9 %all-gather.21.cloned.1.call-start = ((), (), s32[]{:S(2)}) async-start(), calls=%async_computation.14 | async-start | bytes 2621440 | tf_op jit(solution)/shard_map/all_gather | solution.py:51
  239.9 158.4 %all-gather.33.cloned.1.call-start = ((), (), s32[]{:S(2)}) async-start(), calls=%async_computation.27 | async-start | bytes 2621440 | tf_op jit(solution)/shard_map/all_gather | solution.py:51
  240.6 219.4 %reduce-scatter.12.cloned.1.call-start = ((), (), s32[]{:S(2)}) async-start(), calls=%async_computation.16 | async-start | bytes 2621440 | tf_op jit(solution)/shard_map/reduce_scatter | solution.py:55
  398.3 11.7 %copy-start.2 = (bf16[8,4,64,2752]{3,2,0,1:T(8,128)(2,1)S(1)}, bf16[8,4,64,2752]{3,2,0,1:T(8,128)(2,1)}, u32[]{:S(2)}) copy-start(bf16[8,4,64,2752]{3,2,0,1:T(8,128)(2,1)} %copy.109) | copy-start | bytes 33816580
  408.8 8.9 copy-start.26
  417.8 88.3 %reduce-scatter.10.cloned.1.call-start = ((), (), s32[]{:S(2)}) async-start(), calls=%async_computation.15 | async-start | bytes 2621440 | tf_op jit(solution)/shard_map/reduce_scatter | solution.py:55
  417.8 42.2 %copy-start.6 = (bf16[128,2048]{1,0:T(8,128)(2,1)S(1)}, bf16[128,2048]{1,0:T(8,128)(2,1)}, u32[]{:S(2)}) copy-start(bf16[128,2048]{1,0:T(8,128)(2,1)} %reduce-scatter.8.cloned.1.call-done) | copy-start | bytes 1572868
  417.8 88.2 %copy-start.14 = (bf16[1,128,2048]{2,1,0:T(8,128)(2,1)S(1)}, bf16[1,128,2048]{2,1,0:T(8,128)(2,1)}, u32[]{:S(2)}) copy-start(bf16[1,128,2048]{2,1,0:T(8,128)(2,1)} %param.19) | copy-start | bytes 1572868
  425.7 122.3 %copy-start.8 = (bf16[256,8,256]{0,2,1:T(8,128)(2,1)S(1)}, bf16[256,8,256]{0,2,1:T(8,128)(2,1)}, u32[]{:S(2)}) copy-start(bf16[256,8,256]{0,2,1:T(8,128)(2,1)} %copy-done.7) | copy-start | bytes 3145732
  425.8 122.2 %all-gather.23.cloned.1.call-start = ((), (), s32[]{:S(2)}) async-start(), calls=%async_computation.17 | async-start | bytes 4718592 | tf_op jit(solution)/shard_map/all_gather | solution.py:51
  509.0 42.5 %copy-start.18 = (bf16[1024,256]{0,1:T(8,128)(2,1)S(1)}, bf16[1024,256]{0,1:T(8,128)(2,1)}, u32[]{:S(2)}) copy-start(bf16[1024,256]{0,1:T(8,128)(2,1)} %slice.249) | copy-start | bytes 1572868
  562.2 16.9 %all-to-all-start.2 = ((bf16[256,8,256]{2,0,1:T(8,128)(2,1)}), bf16[256,8,256]{2,0,1:T(8,128)(2,1)}, u32[]{:S(2)}, u32[]{:S(2)}) async-start(bf16[256,8,256]{2,0,1:T(8,128)(2,1)} %bitcast.147), calls=%async_computation.7 | async-start | bytes 2097152 | tf_op jit(solution)/shard_map/all_to_all | solution.py:190
  566.6 91.9 %reduce-scatter.18.cloned.1.call-start = ((), (), s32[]{:S(2)}) async-start(), calls=%async_computation.20 | async-start | bytes 1310720 | tf_op jit(solution)/shard_map/reduce_scatter | solution.py:55
  579.2 89.4 %reduce-scatter.16.cloned.1.call-start = ((), (), s32[]{:S(2)}) async-start(), calls=%async_computation.19 | async-start | bytes 3932160 | tf_op jit(solution)/shard_map/reduce_scatter | solution.py:55
  593.3 166.6 %reduce-scatter.20.cloned.1.call-start = ((), (), s32[]{:S(2)}) async-start(), calls=%async_computation.22 | async-start | bytes 12976128 | tf_op jit(solution)/shard_map/reduce_scatter | solution.py:55
  630.4 230.2 %all-reduce.2.cloned.1.call-start = ((), (), s32[]{:S(2)}) async-start(), calls=%async_computation.24 | async-start | bytes 11272192 | tf_op jit(solution)/shard_map/psum | solution.py:167
  641.2 292.2 %reduce-scatter.14.cloned.1.call-start = ((), (), s32[]{:S(2)}) async-start(), calls=%async_computation.18 | async-start | bytes 4718592 | tf_op jit(solution)/shard_map/reduce_scatter | solution.py:55
  658.4 289.0 %all-gather.25.cloned.1.call-start = ((), (), s32[]{:S(2)}) async-start(), calls=%async_computation.21 | async-start | bytes 2359296 | tf_op jit(solution)/shard_map/all_gather | solution.py:191
  659.0 335.9 %all-gather.35.cloned.1.call-start = ((), (), s32[]{:S(2)}) async-start(), calls=%async_computation.28 | async-start | bytes 7077888 | tf_op jit(solution)/shard_map/all_gather | solution.py:209
  668.6 394.8 %all-gather.27.cloned.1.call-start = ((), (), s32[]{:S(2)}) async-start(), calls=%async_computation.23 | async-start | bytes 12681216 | tf_op jit(solution)/shard_map/all_gather | solution.py:51
  1063.4 12.9 %copy-start.1 = (bf16[512,2048]{1,0:T(8,128)(2,1)S(1)}, bf16[512,2048]{1,0:T(8,128)(2,1)}, u32[]{:S(2)}) copy-start(bf16[512,2048]{1,0:T(8,128)(2,1)} %param.15) | copy-start | bytes 6291460
  (16 other events, 70.1 us)
Sparse Core Ops, SparseCore 0:
  10.2 28.8 all-gather.18
  40.9 41.7 all-gather.28
  84.9 60.6 all-gather.16
  183.7 52.4 reduce-scatter.7
  238.1 68.1 all-gather.30
  308.3 43.6 all-gather.20
  353.6 44.6 all-gather.32
  417.9 42.0 reduce-scatter.11
  462.9 43.1 reduce-scatter.9
  509.1 38.8 all-gather.22
  579.3 26.5 reduce-scatter.17
  608.0 60.4 reduce-scatter.15
  672.6 87.2 reduce-scatter.19
  763.7 96.8 all-reduce.1
  864.3 51.9 reduce-scatter.13
  918.2 29.1 all-gather.24
  949.3 45.5 all-gather.34
  996.7 66.5 all-gather.26

commit v2 on v1

--- a/solution.py
+++ b/solution.py
@@ -1,8 +1,11 @@
+import functools
 import math
 
 import jax
 import jax.numpy as jnp
 from jax import lax
+from jax.experimental import pallas as pl
+from jax.experimental.pallas import tpu as pltpu
 from jax.sharding import PartitionSpec as P
 
 HEADS = 16
@@ -13,6 +16,7 @@
 EPSILON = 1e-06
 BF = jnp.bfloat16
 F32 = jnp.float32
+VMEM_LIMIT = 56 * 1024 * 1024
 
 
 def dot_plain(left, right):
@@ -51,8 +55,389 @@
     return lax.all_gather(values, axis, axis=0, tiled=True)
 
 
-def scatter_rows(values, axis):
-    return lax.psum_scatter(values, axis, scatter_dimension=0, tiled=True)
+def shifted(values, axis, step):
+    size = lax.axis_size(axis)
+    return lax.ppermute(values, axis, [(i, (i + step) % size) for i in range(size)])
+
+
+def crossed(values, axis, mask):
+    size = lax.axis_size(axis)
+    return lax.ppermute(values, axis, [(i, i ^ mask) for i in range(size)])
+
+
+def direct_scatter(parts, axis):
+    total = parts[0].astype(F32)
+    for step in range(1, len(parts)):
+        total = total + shifted(parts[step].astype(BF), axis, -step).astype(F32)
+    return total
+
+
+def sum_everywhere(values):
+    for axis in ("ctx", "wa"):
+        mask = 1
+        while mask < lax.axis_size(axis):
+            values = values + crossed(values, axis, mask)
+            mask *= 2
+    return values
+
+
+def take(values, index):
+    return lax.dynamic_index_in_dim(values, index, 0, keepdims=False)
+
+
+def split(values, count):
+    rows = values.shape[0] // count
+    return [values[i * rows : (i + 1) * rows] for i in range(count)]
+
+
+MESH = pl.DeviceIdType.MESH
+
+
+def greet(ctx_peers, wa_peers):
+    barrier = pltpu.get_barrier_semaphore()
+    for peer in ctx_peers:
+        pl.semaphore_signal(barrier, inc=1, device_id={"ctx": peer}, device_id_type=MESH)
+    for peer in wa_peers:
+        pl.semaphore_signal(barrier, inc=1, device_id={"wa": peer}, device_id_type=MESH)
+    pl.semaphore_wait(barrier, len(ctx_peers) + len(wa_peers))
+
+
+def send(source, target, send_sem, recv_sem, **peer):
+    copy = pltpu.make_async_remote_copy(
+        src_ref=source,
+        dst_ref=target,
+        send_sem=send_sem,
+        recv_sem=recv_sem,
+        device_id=peer,
+        device_id_type=MESH,
+    )
+    copy.start()
+    return copy
+
+
+def places(ctx_size, wa_size):
+    chips = ctx_size // 2
+    ctx, wa = lax.axis_index("ctx"), lax.axis_index("wa")
+    core, chip = lax.rem(ctx, 2), lax.div(ctx, 2)
+    beside = chip * 2 + 1 - core
+    ahead = [lax.rem(chip + m, chips) * 2 + core for m in range(chips)]
+    behind = [lax.rem(chip + chips - m, chips) * 2 + core for m in range(chips)]
+    up = [lax.rem(wa + s, wa_size) for s in range(wa_size)]
+    down = [lax.rem(wa + wa_size - s, wa_size) for s in range(wa_size)]
+    return ctx, wa, core, chip, beside, ahead, behind, up, down
+
+
+def plane_gather_start(own, found, ctx, beside, ahead, sems):
+    send_sem, recv_sem, side_send, side_recv = sems
+    copies = [
+        send(own, found.at[ctx], send_sem.at[m], recv_sem.at[m], ctx=ahead[m])
+        for m in range(1, len(ahead))
+    ]
+    side = [send(own, found.at[ctx], side_send.at[0], side_recv.at[0], ctx=beside)]
+    return copies, side
+
+
+def plane_gather_finish(found, beside, behind, copies, side, sems):
+    send_sem, recv_sem, side_send, side_recv = sems
+    for m in range(1, len(behind)):
+        copies[m - 1].wait_recv()
+        block = found.at[behind[m]]
+        side.append(send(block, block, side_send.at[m], side_recv.at[m], ctx=beside))
+    for copy in copies:
+        copy.wait_send()
+    for copy in side:
+        copy.wait()
+
+
+def gather_kernel(ctx_size, wa_size, cuts, x_ref, w_ref, xs_ref, ws_ref, *sems):
+    plane_sems, (ring_send, ring_recv, local) = sems[:4], sems[4:]
+    ctx, wa, _, _, beside, ahead, behind, up, down = places(ctx_size, wa_size)
+    greet([beside] + ahead[1:], [up[1], down[1]])
+    rows = w_ref.shape[0] // cuts
+    ring = []
+    for i in range(cuts):
+        part = pl.ds(i * rows, rows)
+        ring.append(
+            send(
+                w_ref.at[part],
+                ws_ref.at[wa, part],
+                ring_send.at[0, i],
+                ring_recv.at[0, i],
+                wa=up[1],
+            )
+        )
+    copies, side = plane_gather_start(x_ref, xs_ref, ctx, beside, ahead, plane_sems)
+    own_x = pltpu.make_async_copy(x_ref, xs_ref.at[ctx], local.at[0])
+    own_w = pltpu.make_async_copy(w_ref, ws_ref.at[wa], local.at[1])
+    own_x.start()
+    own_w.start()
+    late = []
+    for step in range(1, wa_size):
+        for i in range(cuts):
+            ring[i].wait_recv()
+            late.append(ring[i])
+            if step < wa_size - 1:
+                block = ws_ref.at[down[step], pl.ds(i * rows, rows)]
+                ring[i] = send(
+                    block, block, ring_send.at[step, i], ring_recv.at[step, i], wa=up[1]
+                )
+        if step == 1:
+            plane_gather_finish(xs_ref, beside, behind, copies, side, plane_sems)
+    for copy in late:
+        copy.wait_send()
+    own_x.wait()
+    own_w.wait()
+
+
+def gather_both(x, w, ctx_size, wa_size, cuts=4):
+    chips = ctx_size // 2
+    anywhere = pl.BlockSpec(memory_space=pl.ANY)
+    return pl.pallas_call(
+        functools.partial(gather_kernel, ctx_size, wa_size, cuts),
+        out_shape=(
+            jax.ShapeDtypeStruct((ctx_size,) + x.shape, x.dtype),
+            jax.ShapeDtypeStruct((wa_size,) + w.shape, w.dtype),
+        ),
+        in_specs=[anywhere] * 2,
+        out_specs=[anywhere] * 2,
+        scratch_shapes=[pltpu.SemaphoreType.DMA((chips,))] * 4
+        + [pltpu.SemaphoreType.DMA((wa_size - 1, cuts))] * 2
+        + [pltpu.SemaphoreType.DMA((2,))],
+        compiler_params=pltpu.CompilerParams(collective_id=0, has_side_effects=True),
+        cost_estimate=pl.CostEstimate(flops=0, bytes_accessed=200_000_000, transcendentals=0),
+        name="gather_both",
+    )(x, w)
+
+
+def plane_scatter(part_of, ctx_size, core, chip, beside, ahead, refs):
+    chips = ctx_size // 2
+    side_out, side_in, chip_out, chip_in, side_send, side_recv, chip_send, chip_recv = refs
+    side, out = [], []
+    order = list(range(1, chips)) + [0]
+    for m in order:
+        there = lax.rem(chip + m, chips) * 2
+        side_out[m] = part_of(there + 1 - core).astype(BF)
+        side.append(
+            send(side_out.at[m], side_in.at[m], side_send.at[m], side_recv.at[m], ctx=beside)
+        )
+    total = None
+    for i, m in enumerate(order):
+        there = lax.rem(chip + m, chips) * 2
+        mine = part_of(there + core)
+        side[i].wait_recv()
+        total = mine + side_in[m].astype(F32)
+        if m > 0:
+            chip_out[m - 1] = total.astype(BF)
+            out.append(
+                send(
+                    chip_out.at[m - 1],
+                    chip_in.at[m - 1],
+                    chip_send.at[m - 1],
+                    chip_recv.at[m - 1],
+                    ctx=ahead[m],
+                )
+            )
+    for m in range(1, chips):
+        out[m - 1].wait_recv()
+        total = total + chip_in[m - 1].astype(F32)
+    return total, side + out
+
+
+def scatter_scratch(ctx_size, rows, width):
+    chips = ctx_size // 2
+    return [
+        pltpu.VMEM((chips, rows, width), BF),
+        pltpu.VMEM((chips, rows, width), BF),
+        pltpu.VMEM((chips - 1, rows, width), BF),
+        pltpu.VMEM((chips - 1, rows, width), BF),
+    ] + [pltpu.SemaphoreType.DMA((chips,))] * 4
+
+
+def out_kernel(
+    ctx_size, wa_size, mixed_ref, w_ref, x_ref, gain_ref, hidden_ref, acts_ref, *scratch
+):
+    refs, (act_send, act_recv) = scratch[:8], scratch[8:]
+    ctx, wa, core, chip, beside, ahead, behind, up, down = places(ctx_size, wa_size)
+    greet([beside] + ahead[1:], up[1:])
+    rows = x_ref.shape[0]
+
+    def part_of(device):
+        block = mixed_ref[pl.ds(pl.multiple_of(device * rows, rows), rows), :]
+        return jnp.dot(block, w_ref[...], preferred_element_type=F32)
+
+    total, pending = plane_scatter(part_of, ctx_size, core, chip, beside, ahead, refs)
+    hidden = x_ref[...].astype(F32) + total
+    hidden_ref[...] = hidden
+    scale = lax.rsqrt(jnp.mean(hidden * hidden, axis=-1, keepdims=True) + EPSILON)
+    acts_ref[0] = (hidden * scale * gain_ref[...]).astype(BF)
+    copies = [
+        send(acts_ref.at[0], acts_ref.at[s], act_send.at[s], act_recv.at[s], wa=up[s])
+        for s in range(1, wa_size)
+    ]
+    for copy in pending:
+        copy.wait_send()
+    for copy in copies:
+        copy.wait()
+
+
+def out_project(mixed, w_rows, x_own, gain, ctx_size, wa_size):
+    rows, width = x_own.shape
+    vmem = pl.BlockSpec(memory_space=pltpu.VMEM)
+    return pl.pallas_call(
+        functools.partial(out_kernel, ctx_size, wa_size),
+        out_shape=(
+            jax.ShapeDtypeStruct((rows, width), F32),
+            jax.ShapeDtypeStruct((wa_size, rows, width), BF),
+        ),
+        in_specs=[vmem] * 4,
+        out_specs=[vmem] * 2,
+        scratch_shapes=scatter_scratch(ctx_size, rows, width)
+        + [pltpu.SemaphoreType.DMA((wa_size,))] * 2,
+        compiler_params=pltpu.CompilerParams(
+            collective_id=1, has_side_effects=True, vmem_limit_bytes=VMEM_LIMIT
+        ),
+        cost_estimate=pl.CostEstimate(
+            flops=2 * mixed.size * width, bytes_accessed=200_000_000, transcendentals=0
+        ),
+        name="out_project",
+    )(mixed, w_rows, x_own, gain)
+
+
+def turn_kernel(
+    ctx_size, wa_size, parts_ref, hidden_ref, gain_ref, dz_ref, all_ref, gain_out_ref, *scratch
+):
+    got_ref, wa_send, wa_recv = scratch[:3]
+    plane_sems = scratch[3:]
+    ctx, wa, core, chip, beside, ahead, behind, up, down = places(ctx_size, wa_size)
+    greet([beside] + ahead[1:], down[1:])
+    copies = [
+        send(parts_ref.at[s], got_ref.at[s], wa_send.at[s], wa_recv.at[s], wa=down[s])
+        for s in range(1, wa_size)
+    ]
+    hidden = hidden_ref[...]
+    scale = lax.rsqrt(jnp.mean(hidden * hidden, axis=-1, keepdims=True) + EPSILON)
+    normed = hidden * scale
+    d_normed = parts_ref[0].astype(F32)
+    for s in range(1, wa_size):
+        copies[s - 1].wait_recv()
+        d_normed = d_normed + got_ref[s].astype(F32)
+    gain_out_ref[...] = jnp.sum(d_normed * normed, axis=0, keepdims=True)
+    scaled = d_normed * gain_ref[...]
+    d_hidden = dz_ref[...].astype(F32) + scale * (
+        scaled - normed * jnp.mean(scaled * normed, axis=-1, keepdims=True)
+    )
+    all_ref[ctx] = d_hidden.astype(BF)
+    own = all_ref.at[ctx]
+    plane, side = plane_gather_start(own, all_ref, ctx, beside, ahead, plane_sems)
+    for copy in copies:
+        copy.wait_send()
+    plane_gather_finish(all_ref, beside, behind, plane, side, plane_sems)
+
+
+def turn(parts, hidden, gain, dz, ctx_size, wa_size):
+    rows, width = hidden.shape
+    chips = ctx_size // 2
+    vmem = pl.BlockSpec(memory_space=pltpu.VMEM)
+    return pl.pallas_call(
+        functools.partial(turn_kernel, ctx_size, wa_size),
+        out_shape=(
+            jax.ShapeDtypeStruct((ctx_size, rows, width), BF),
+            jax.ShapeDtypeStruct((1, width), F32),
+        ),
+        in_specs=[vmem] * 4,
+        out_specs=[vmem] * 2,
+        scratch_shapes=[pltpu.VMEM((wa_size, rows, width), BF)]
+        + [pltpu.SemaphoreType.DMA((wa_size,))] * 2
+        + [pltpu.SemaphoreType.DMA((chips,))] * 4,
+        compiler_params=pltpu.CompilerParams(
+            collective_id=2, has_side_effects=True, vmem_limit_bytes=VMEM_LIMIT
+        ),
+        cost_estimate=pl.CostEstimate(flops=0, bytes_accessed=200_000_000, transcendentals=0),
+        name="turn",
+    )(parts, hidden, gain, dz)
+
+
+def last_kernel(
+    ctx_size,
+    wa_size,
+    grads_ref,
+    w_ref,
+    dw_ref,
+    dealt_ref,
+    x_ref,
+    gain_ref,
+    dh_ref,
+    out_ref,
+    dw_out_ref,
+    gain_out_ref,
+    *scratch,
+):
+    refs, (dw_in, dw_send, dw_recv) = scratch[:8], scratch[8:]
+    ctx, wa, core, chip, beside, ahead, behind, up, down = places(ctx_size, wa_size)
+    greet([beside] + ahead[1:], up[1:])
+    copies = [
+        send(dw_ref.at[up[s]], dw_in.at[s], dw_send.at[s], dw_recv.at[s], wa=up[s])
+        for s in range(1, wa_size)
+    ]
+    rows = x_ref.shape[0]
+    gain_out_ref[...] = jnp.zeros_like(gain_out_ref)
+
+    def part_of(device):
+        place = pl.ds(pl.multiple_of(device * rows, rows), rows)
+        part = lax.dot_general(
+            grads_ref[place, :],
+            w_ref[...],
+            (((1,), (1,)), ((), ())),
+            preferred_element_type=F32,
+        )
+        x = dealt_ref[place, :].astype(F32)
+        scale = lax.rsqrt(jnp.mean(x * x, axis=-1, keepdims=True) + EPSILON)
+        gain_out_ref[...] += jnp.sum(part * (x * scale), axis=0, keepdims=True)
+        return part
+
+    d_normed, pending = plane_scatter(part_of, ctx_size, core, chip, beside, ahead, refs)
+    x = x_ref[...].astype(F32)
+    scale = lax.rsqrt(jnp.mean(x * x, axis=-1, keepdims=True) + EPSILON)
+    normed = x * scale
+    scaled = d_normed * gain_ref[...]
+    d_x = dh_ref[...].astype(F32) + scale * (
+        scaled - normed * jnp.mean(scaled * normed, axis=-1, keepdims=True)
+    )
+    out_ref[...] = d_x.astype(BF)
+    for copy in pending:
+        copy.wait_send()
+    total = dw_ref[wa].astype(F32)
+    for s in range(1, wa_size):
+        copies[s - 1].wait_recv()
+        total = total + dw_in[s].astype(F32)
+    dw_out_ref[...] = total.astype(BF)
+    for copy in copies:
+        copy.wait_send()
+
+
+def last_exchange(grads, w, dw, dealt, x_own, gain, dh, ctx_size, wa_size):
+    rows, width = x_own.shape
+    vmem = pl.BlockSpec(memory_space=pltpu.VMEM)
+    return pl.pallas_call(
+        functools.partial(last_kernel, ctx_size, wa_size),
+        out_shape=(
+            jax.ShapeDtypeStruct((rows, width), BF),
+            jax.ShapeDtypeStruct(dw.shape[1:], BF),
+            jax.ShapeDtypeStruct((1, width), F32),
+        ),
+        in_specs=[vmem] * 7,
+        out_specs=[vmem] * 3,
+        scratch_shapes=scatter_scratch(ctx_size, rows, width)
+        + [pltpu.VMEM(dw.shape, BF)]
+        + [pltpu.SemaphoreType.DMA((wa_size,))] * 2,
+        compiler_params=pltpu.CompilerParams(
+            collective_id=3, has_side_effects=True, vmem_limit_bytes=VMEM_LIMIT
+        ),
+        cost_estimate=pl.CostEstimate(
+            flops=2 * grads.size * width, bytes_accessed=250_000_000, transcendentals=0
+        ),
+        name="last_exchange",
+    )(grads, w, dw, dealt, x_own, gain, dh)
 
 
 def per_device(
@@ -62,6 +447,7 @@
     ctx_size = lax.axis_size("ctx")
     wa_size = lax.axis_size("wa")
     ctx_index = lax.axis_index("ctx")
+    wa_index = lax.axis_index("wa")
     block_order = dealing[0]
     block_total = block_order.shape[0]
     group_rows = block_total * BLOCK
@@ -92,12 +478,14 @@
         ],
         axis=1,
     )
-    qkv_cols = gather_rows(qkv_slice, "wa")
-    out_cols = gather_rows(
-        lax.dynamic_slice_in_dim(w_out, ctx_index * head_cols, head_cols, 1), "wa"
-    )
+    dealt, qkv_cols = gather_both(tokens[0], qkv_slice, ctx_size, wa_size)
+    dealt = dealt.reshape(group_rows, width)
+    qkv_cols = qkv_cols.reshape(width, 3 * head_cols)
+    out_slice = lax.dynamic_slice_in_dim(w_out, ctx_index * head_cols, head_cols, 1)
+    out_cols = gather_rows(out_slice, "wa")
     out_rows = lax.all_to_all(out_cols, "ctx", 0, 1, tiled=True)
     gu_piece = lax.dynamic_slice_in_dim(w_gate_up, ctx_index * piece_rows, piece_rows, 0)
+    gu_piece, qkv_cols = lax.optimization_barrier((gu_piece, qkv_cols))
     gu_send = jnp.stack(
         [
             jnp.concatenate(
@@ -110,11 +498,13 @@
             for to in range(wa_size)
         ]
     )
-    gu_mine = lax.all_to_all(gu_send, "wa", 0, 0, tiled=True)
+    gu_parts = [take(gu_send, (wa_index - s) % wa_size) for s in range(wa_size)]
+    gu_got = [gu_parts[0]] + [shifted(gu_parts[s], "wa", -s) for s in range(1, wa_size)]
+    gu_mine = jnp.stack([gu_got[(wa_size - s) % wa_size] for s in range(wa_size)])
+    gu_mine = jnp.stack([take(gu_mine, (wa_index - i) % wa_size) for i in range(wa_size)])
     gu_all = lax.all_gather(gu_mine, "ctx", axis=0)
     gu_weight = jnp.transpose(gu_all, (1, 0, 2, 3)).reshape(width, 2 * ff_own)
 
-    dealt = gather_rows(tokens[0], "ctx")
     given_b = pick_blocks(dealt, inverse)
     given = given_b.astype(F32)
     positions = jnp.arange(group_rows, dtype=jnp.int32)
@@ -143,13 +533,15 @@
     mixed = jnp.einsum("hqk,khe->qhe", probs_b, value_b, preferred_element_type=F32)
     mixed_b = mixed.reshape(group_rows, head_cols).astype(BF)
 
-    branch = scatter_rows(dot_plain(mixed_b, out_rows).astype(BF), "ctx")
     own_given = lax.dynamic_slice_in_dim(given_b, ctx_index * tok_rows, tok_rows)
-    hidden = own_given.astype(F32) + branch.astype(F32)
-    scale_two = rms_scale(hidden)
-    normed_two = hidden * scale_two
-    act_two = gather_rows((normed_two * norm2_gain).astype(BF), "wa")
-    cotangent = gather_rows(grad_out[0], "wa")
+    gain_two = norm2_gain[None, :]
+    hidden, acts = out_project(mixed_b, out_rows, own_given, gain_two, ctx_size, wa_size)
+    act_two = acts.reshape(wa_size * tok_rows, width)
+    early = lax.optimization_barrier((grad_out[0], qkv_cols))[0]
+    grads_all = lax.all_gather(early, "wa", axis=0)
+    cotangent = jnp.concatenate(
+        [take(grads_all, (wa_index - s) % wa_size) for s in range(wa_size)], axis=0
+    )
 
     gate_up = dot_plain(act_two, gu_weight)
     gate_part = gate_up[:, :ff_own]
@@ -157,21 +549,49 @@
     sigmoid_gate = jax.nn.sigmoid(gate_part)
     silu_gate = gate_part * sigmoid_gate
     inner_b = (silu_gate * up_part).astype(BF)
-    result = scatter_rows(dot_plain(inner_b, w_down).astype(BF), "wa")
-    out_given = (hidden + result.astype(F32)).astype(BF)
 
     d_inner = dot_right_t(cotangent, w_down)
     d_gate = d_inner * up_part * sigmoid_gate * (1.0 + gate_part * (1.0 - sigmoid_gate))
     d_gu_b = jnp.concatenate([d_gate, d_inner * silu_gate], axis=1).astype(BF)
-    d_normed_two = scatter_rows(dot_right_t(d_gu_b, gu_weight).astype(BF), "wa").astype(F32)
-    d_down = lax.psum(dot_left_t(inner_b, cotangent).astype(BF), "ctx").astype(F32)
-
-    d_gu_share = dot_left_t(act_two, d_gu_b).astype(BF)
-    d_gu_share = jnp.transpose(
-        d_gu_share.reshape(wa_size, ctx_size, piece_rows, 2 * ff_own), (1, 0, 2, 3)
-    ).reshape(ctx_size * wa_size, piece_rows, 2 * ff_own)
-    d_gu_piece = scatter_rows(d_gu_share, "ctx")
-    d_gu_back = lax.all_to_all(d_gu_piece, "wa", 0, 0, tiled=True)
+    d_act = dot_right_t(d_gu_b, gu_weight).astype(BF).reshape(wa_size, tok_rows, width)
+    d_branches, gain_two_part = turn(d_act, hidden, gain_two, grad_out[0], ctx_size, wa_size)
+    d_branch_b = d_branches.reshape(group_rows, width)
+    mlp_parts, d_branch_b = lax.optimization_barrier((dot_plain(inner_b, w_down).astype(BF), d_branch_b))
+    result = direct_scatter(split(mlp_parts, wa_size), "wa")
+    out_given = (hidden + result).astype(BF)
+
+    core = ctx_index % 2
+    chip = ctx_index // 2
+    chips = ctx_size // 2
+    down_part = dot_left_t(inner_b, cotangent).astype(BF)
+    down_half = width // 2
+    down_send = lax.dynamic_slice_in_dim(down_part, (1 - core) * down_half, down_half, 1)
+    down_keep = lax.dynamic_slice_in_dim(down_part, core * down_half, down_half, 1)
+    down_sum = (down_keep.astype(F32) + crossed(down_send, "ctx", 1).astype(F32)).astype(BF)
+    down_cols = down_half // chips
+    down_mine = lax.dynamic_slice_in_dim(down_sum, chip * down_cols, down_cols, 1).astype(F32)
+    for i in range(1, chips):
+        down_piece = lax.dynamic_slice_in_dim(down_sum, (chip ^ i) * down_cols, down_cols, 1)
+        down_mine = down_mine + crossed(down_piece, "ctx", 2 * i).astype(F32)
+    down_all = lax.all_gather(down_mine.astype(BF), "ctx", axis=0)
+    d_down = jnp.concatenate(
+        [down_all[(i % chips) * 2 + i // chips] for i in range(ctx_size)], axis=1
+    ).astype(F32)
+
+    gu_share = dot_left_t(act_two, d_gu_b).astype(BF)
+    gu_share = gu_share.reshape(wa_size, chips, 2, piece_rows, 2 * ff_own)
+    gu_send_back = lax.dynamic_slice_in_dim(gu_share, 1 - core, 1, 2)[:, :, 0]
+    gu_keep = lax.dynamic_slice_in_dim(gu_share, core, 1, 2)[:, :, 0]
+    gu_sum = (gu_keep.astype(F32) + crossed(gu_send_back, "ctx", 1).astype(F32)).astype(BF)
+    d_gu_piece = lax.dynamic_slice_in_dim(gu_sum, chip, 1, 1)[:, 0].astype(F32)
+    for i in range(1, chips):
+        gu_one = lax.dynamic_slice_in_dim(gu_sum, chip ^ i, 1, 1)[:, 0]
+        d_gu_piece = d_gu_piece + crossed(gu_one, "ctx", 2 * i).astype(F32)
+    d_gu_piece = d_gu_piece.astype(BF)
+    back = [take(d_gu_piece, (wa_index - s) % wa_size) for s in range(wa_size)]
+    back = [back[0]] + [shifted(back[s], "wa", -s) for s in range(1, wa_size)]
+    d_gu_back = jnp.stack([back[(wa_size - s) % wa_size] for s in range(wa_size)])
+    d_gu_back = jnp.stack([take(d_gu_back, (wa_index - i) % wa_size) for i in range(wa_size)])
     d_gu_rows = jnp.concatenate(
         [d_gu_back[i, :, :ff_own] for i in range(wa_size)]
         + [d_gu_back[i, :, ff_own:] for i in range(wa_size)],
@@ -179,16 +599,14 @@
     )
     d_gate_up = gather_rows(d_gu_rows, "ctx").astype(F32)
 
-    gain_two_part = jnp.sum(d_normed_two * normed_two, axis=0)
-    scaled_two = d_normed_two * norm2_gain
-    d_hidden = grad_out[0].astype(F32) + scale_two * (
-        scaled_two - normed_two * jnp.mean(scaled_two * normed_two, axis=1, keepdims=True)
-    )
-    d_branch_b = gather_rows(d_hidden.astype(BF), "ctx")
     grad_mixed_b = dot_right_t(d_branch_b, out_rows).astype(BF)
     d_out_part = dot_left_t(mixed_b, d_branch_b).astype(BF)
     d_out_cols = lax.all_to_all(d_out_part, "ctx", 1, 0, tiled=True)
-    d_out = lax.all_gather(scatter_rows(d_out_cols, "wa"), "ctx", axis=1, tiled=True).astype(F32)
+    out_parts = d_out_cols.reshape(wa_size, wa_rows, head_cols)
+    d_out_mine = direct_scatter(
+        [take(out_parts, (wa_index - s) % wa_size) for s in range(wa_size)], "wa"
+    ).astype(BF)
+    d_out = lax.all_gather(d_out_mine, "ctx", axis=1, tiled=True).astype(F32)
 
     grad_heads = grad_mixed_b.reshape(group_rows, heads_own, HEAD)
     d_probs = jnp.einsum("qhe,khe->hqk", grad_heads, value_b, preferred_element_type=F32)
@@ -205,19 +623,7 @@
         ],
         axis=1,
     ).astype(BF)
-    d_qkv_share = scatter_rows(dot_left_t(act_one, d_qkv_b).astype(BF), "wa")
-    d_qkv_all = lax.all_gather(d_qkv_share, "ctx", axis=0)
-    d_qkv = jnp.transpose(
-        d_qkv_all.reshape(ctx_size, wa_rows, 3, head_cols), (1, 2, 0, 3)
-    ).reshape(wa_rows, 3 * width).astype(F32)
-
-    d_one_part = dot_right_t(d_qkv_b, qkv_cols)
-    gain_one_part = jnp.sum(d_one_part * normed_one, axis=0)
-    d_normed_one = scatter_rows(pick_blocks(d_one_part.astype(BF), block_order), "ctx").astype(F32)
-    own = tokens[0].astype(F32)
-    own_scale = rms_scale(own)
-    own_normed = own * own_scale
-    scaled_one = d_normed_one * norm1_gain
+    qkv_parts = dot_left_t(act_one, d_qkv_b).astype(BF).reshape(wa_size, wa_rows, 3 * head_cols)
     own_order = lax.dynamic_slice_in_dim(block_order, ctx_index * own_blocks, own_blocks)
     d_hidden_dealt = jnp.concatenate(
         [
@@ -225,15 +631,28 @@
             for i in range(own_blocks)
         ],
         axis=0,
-    ).astype(F32)
-    d_tokens = d_hidden_dealt + own_scale * (
-        scaled_one - own_normed * jnp.mean(scaled_one * own_normed, axis=1, keepdims=True)
-    )
-    gain_parts = jnp.stack([gain_one_part, gain_two_part])
-    gain_sums = jnp.sum(lax.all_gather(gain_parts, ("ctx", "wa"), axis=0), axis=0)
+    )
+    d_tokens, d_qkv_share, gain_one_part = last_exchange(
+        pick_blocks(d_qkv_b, block_order),
+        qkv_cols,
+        qkv_parts,
+        dealt,
+        tokens[0],
+        norm1_gain[None, :],
+        d_hidden_dealt,
+        ctx_size,
+        wa_size,
+    )
+    d_qkv_all = lax.all_gather(d_qkv_share, "ctx", axis=0)
+    d_qkv = jnp.transpose(
+        d_qkv_all.reshape(ctx_size, wa_rows, 3, head_cols), (1, 2, 0, 3)
+    ).reshape(wa_rows, 3 * width).astype(F32)
+
+    gain_parts = jnp.concatenate([gain_one_part, gain_two_part], axis=0)
+    gain_sums = sum_everywhere(gain_parts)
     return (
         out_given[None],
-        d_tokens.astype(BF)[None],
+        d_tokens[None],
         gain_sums[0],
         d_qkv,
         d_out,

time: 1090 us -> 984 us (0.903)
  waiting for transfers between devices: 593 us -> 263 us
  Pallas kernels: 0 us -> 299 us
  blocking collectives: 137 us -> 0 us
  starting transfers between devices: 9.56 us -> 51.4 us
  matrix products: 118 us -> 98.5 us
  other arithmetic: 61.6 us -> 79 us
  local copies, waits for them, and re-layouts: 138 us -> 153 us
    pallas_call x0 -> x4, Pallas kernels: none -> 299 us  [the longest x1 82.9 us: out_project(): pl.pallas_call(functools.partial(out_kernel, ctx_size, wa_size), out_shap...]
    ppermute x0 -> x25, waiting for transfers between devices: none -> 255 us  [the longest x13 151 us: crossed(): return lax.ppermute(values, axis, [(i, i ^ mask) for i in range(size)])]
    all_gather x7 -> x2, waiting for transfers between devices: 213 us -> 0.01 us  [gather_rows(): return lax.all_gather(values, axis, axis=0, tiled=True)]
    reduce_scatter x7 -> x0, waiting for transfers between devices: 191 us -> none  [scatter_rows(): return lax.psum_scatter(values, axis, scatter_dimension=0, tiled=True)]
    all_to_all x2 -> x0, blocking collectives: 73.6 us -> none  [the longest x1 37.6 us: per_device(): gu_mine = lax.all_to_all(gu_send, 'wa', 0, 0, tiled=True)]
    all_gather x1, waiting for transfers between devices: 65.6 us -> 0.01 us  [per_device(): gu_all = lax.all_gather(gu_mine, 'ctx', axis=0)]
    all_gather x1 -> x0, blocking collectives: 63.5 us -> none  [per_device(): lax.all_gather(gain_parts, ('ctx', 'wa'), axis=0)]
    psum x1 -> x0, waiting for transfers between devices: 61.2 us -> none  [per_device(): lax.psum(dot_left_t(inner_b, cotangent).astype(BF), 'ctx').astype(F32)]
  transfers between devices with their start and end apart: 20 -> 34, of which waited for: 17 -> 19; matrix products, arithmetic and copies ran while one was open for 21% -> 25% of each run, Pallas kernels for 0% -> 24%
where the time goes in v2:
time: 984 us; the launch traced here: 971 us
  Pallas kernels  299 us (30%)
  waiting for transfers between devices  263 us (27%)
  local copies, waits for them, and re-layouts  153 us (16%)
  matrix products  98.5 us (10%)
  other arithmetic  79 us (8%)
  starting transfers between devices  51.4 us (5%)
  between operations  26.5 us (3%)
    ppermute x13, waiting for transfers between devices, crossed(): return lax.ppermute(values, axis, [(i, i ^ mask) for i in range(size)])  151 us
    ppermute x12, waiting for transfers between devices, shifted(): lax.ppermute(values, axis, [(i, (i + step) % size) for i in range(size)])  105 us
    pallas_call x1, Pallas kernels, out_project(): pl.pallas_call(functools.partial(out_kernel, ctx_size, wa_size), out_shap...  82.9 us
    pallas_call x1, Pallas kernels, last_exchange(): pl.pallas_call(functools.partial(last_kernel, ctx_size, wa_size), out_sha...  76.2 us
    pallas_call x1, Pallas kernels, gather_both(): pl.pallas_call(functools.partial(gather_kernel, ctx_size, wa_size, cuts),...  71.7 us
    pallas_call x1, Pallas kernels, turn(): pl.pallas_call(functools.partial(turn_kernel, ctx_size, wa_size), out_sha...  68.2 us
    unnamed x124, local copies, waits for them, and re-layouts  65.8 us
    dot_general x3, matrix products, dot_plain(): return jnp.dot(left, right, preferred_element_type=F32)  28.1 us
  transfers between devices with their start and end apart: 34, of which 19 were waited for; matrix products, arithmetic and copies ran while one was open for 25% of the time, Pallas kernels for 24%

profile of v2, /device:TPU:9, one launch (start us, length us, event | category | flops | bytes accessed | tf_op | source)
XLA Modules:
  0.0 970.6 jit_solution(16509646771975600630)
XLA Ops:
  11.7 71.7 %gather_both.1 = (bf16[8,128,2048]{2,1,0:T(8,128)(2,1)}, bf16[4,512,768]{2,1,0:T(8,128)(2,1)}) custom-call(bf16[128,2048]{1,0:T(8,128)(2,1)} %bitcast.208, bf16[512,768]{1,0:T(8,128)(2,1)} %pad_maximum_fusion.9.w_ref), custom_call_target="tpu_custom_call" | custom-call | bytes 200000000 | tf_op jit(solution)/shard_map/gather_both/pallas_call | solution.py:195
  95.1 32.2 %collective-permute-done.1 = bf16[64,2752]{1,0:T(8,128)(2,1)S(1)} collective-permute-done((bf16[64,2752]{1,0:T(8,128)(2,1)S(1)}, bf16[64,2752]{1,0:T(8,128)(2,1)S(1)}, u32[]{:S(2)}, u32[]{:S(2)}) %collective-permute-start.1) | collective-permute-done | bytes 352288 | tf_op jit(solution)/shard_map/ppermute | solution.py:60
  127.4 23.9 %collective-permute-done = bf16[64,2752]{1,0:T(8,128)(2,1)S(1)} collective-permute-done((bf16[64,2752]{1,0:T(8,128)(2,1)S(1)}, bf16[64,2752]{1,0:T(8,128)(2,1)S(1)}, u32[]{:S(2)}, u32[]{:S(2)}) %collective-permute-start) | collective-permute-done | bytes 352288 | tf_op jit(solution)/shard_map/ppermute | solution.py:60
  187.6 15.3 %fusion.39 = (f32[1024,64]{1,0:T(8,128)}, f32[1024,64]{1,0:T(8,128)S(1)}, f32[1024,64]{1,0:T(8,128)S(1)}) fusion(f32[64]{0:T(128)S(1)} %multiply_power_fusion, f32[1024]{0:T(1024)S(1)} %subtract_convert_fusion.4), kind=kLoop, calls=%fused_computation.138 | loop fusion | flops 131072 | bytes 790784 | tf_op jit(solution)/shard_map/neg | solution.py:620
  207.6 8.5 fusion.55
  233.6 82.9 %out_project.1 = (f32[128,2048]{1,0:T(8,128)}, bf16[4,128,2048]{2,1,0:T(8,128)(2,1)}) custom-call(bf16[1024,256]{1,0:T(8,128)(2,1)} %copy.149.mixed_ref, bf16[256,2048]{1,0:T(8,128)(2,1)} %bitcast.212, bf16[128,2048]{1,0:T(8,128)(2,1)} %constant_dynamic-slice_fusion.12.x_ref, f32[1,2048]{1,0:T(1,128)} %bitcast.231), custom_call_target="tpu_custom_call" | custom-call | flops 1073741824 | bytes 200000000 | tf_op jit(solution)/shard_map/out_project/pallas_call | solution.py:286
  319.3 10.4 %copy.121 = bf16[8,4,64,2752]{3,2,0,1:T(8,128)(2,1)} copy(bf16[8,4,64,2752]{3,2,1,0:T(8,128)(2,1)} %bitcast.190) | data formatting | bytes 22544384 | tf_op jit(solution)/shard_map/all_gather | solution.py:505
  329.7 15.4 %fusion.56 = f32[512,2752]{0,1:T(8,128)} fusion(bf16[512,2048]{1,0:T(8,128)(2,1)} %bitcast.238, bf16[2048,2752]{1,0:T(8,128)(2,1)} %bitcast.191), kind=kOutput, calls=%fused_computation.180 | convolution fusion | flops 5771362304 | bytes 19005440 | tf_op jit(solution)/shard_map/dot_general | solution.py:23
  345.1 8.8 multiply_convert_fusion.2
  354.0 8.8 convolution_convert_fusion.4
  362.8 7.4 convolution_convert_fusion.3
  370.2 68.2 %turn.1 = (bf16[8,128,2048]{2,1,0:T(8,128)(2,1)}, f32[1,2048]{1,0:T(1,128)}) custom-call(bf16[4,128,2048]{2,1,0:T(8,128)(2,1)} %bitcast.205, f32[128,2048]{1,0:T(8,128)} %get-tuple-element.25.hidden_ref, f32[1,2048]{1,0:T(1,128)} %bitcast.232, bf16[128,2048]{1,0:T(8,128)(2,1)} %bitcast.207), custom_call_target="tpu_custom_call" | custom-call | bytes 200000000 | tf_op jit(solution)/shard_map/turn/pallas_call | solution.py:341
  452.7 8.8 multiply_convert_fusion
  465.6 12.2 %collective-permute-start.13 = (bf16[512,256]{1,0:T(8,128)(2,1)}, bf16[512,256]{1,0:T(8,128)(2,1)S(1)}, u32[]{:S(2)}, u32[]{:S(2)}) collective-permute-start(bf16[512,256]{1,0:T(8,128)(2,1)} %get-tuple-element.118), channel_id=1, source_target_pairs={{0,1},{1,2},{2,3},{3,0},{4,5},{5,6},{6,7},{7,4},{8,9},{9,10},{10,1... | collective-permute-start | bytes 786440 | tf_op jit(solution)/shard_map/ppermute | solution.py:60
  488.0 10.3 %collective-permute-done.12 = bf16[512,256]{1,0:T(8,128)(2,1)} collective-permute-done((bf16[512,256]{1,0:T(8,128)(2,1)}, bf16[512,256]{1,0:T(8,128)(2,1)}, u32[]{:S(2)}, u32[]{:S(2)}) %collective-permute-start.12) | collective-permute-done | bytes 262176 | tf_op jit(solution)/shard_map/ppermute | solution.py:60
  520.9 76.2 %last_exchange.1 = (bf16[128,2048]{1,0:T(8,128)(2,1)}, bf16[512,768]{1,0:T(8,128)(2,1)}, f32[1,2048]{1,0:T(1,128)}) custom-call(bf16[1024,768]{1,0:T(8,128)(2,1)} %copy-done.16, bf16[2048,768]{1,0:T(8,128)(2,1)} %bitcast.202, bf16[4,512,768]{2,1,0:T(8,128)(2,1)} %bitcast.204, bf16[1024,2048]{1,0:T(8,128)(2,1)} %bitcast.185, bf16[128,2048]{1,0:T(8,128)(2,1)} %bitcast.209, ...), custom_call_target="tpu_custom_call" | custom-call | flops 3221225472 | bytes 250000000 | tf_op jit(solution)/shard_map/last_exchange/pallas_call | solution.py:421
  607.4 10.2 %convolution_convert_fusion = bf16[2048,2752]{0,1:T(8,128)(2,1)} fusion(bf16[512,2048]{1,0:T(8,128)(2,1)S(1)} %bitcast.239, bf16[512,1376]{0,1:T(8,128)(2,1)} %copy-done.42, bf16[512,1376]{0,1:T(8,128)(2,1)S(1)} %copy-done.41), kind=kOutput, calls=%fused_computation.3 | convolution fusion | flops 5782634496 | bytes 16187392 | tf_op jit(solution)/shard_map/dot_general | solution.py:31
  617.6 15.6 %copy.137 = bf16[2048,2752]{1,0:T(8,128)(2,1)} copy(bf16[2048,2752]{0,1:T(8,128)(2,1)} %convolution_convert_fusion) | data formatting | bytes 22544384 | tf_op jit(solution)/shard_map/convert_element_type | solution.py:581
  647.5 11.9 %collective-permute-done.24 = bf16[1376,256]{1,0:T(8,128)(2,1)S(1)} collective-permute-done((bf16[1376,256]{1,0:T(8,128)(2,1)S(1)}, bf16[1376,256]{1,0:T(8,128)(2,1)S(1)}, u32[]{:S(2)}, u32[]{:S(2)}) %collective-permute-start.24) | collective-permute-done | bytes 704544 | tf_op jit(solution)/shard_map/ppermute | solution.py:65
  659.4 14.1 %collective-permute-done.23 = bf16[1376,256]{1,0:T(8,128)(2,1)} collective-permute-done((bf16[1376,256]{1,0:T(8,128)(2,1)S(1)}, bf16[1376,256]{1,0:T(8,128)(2,1)}, u32[]{:S(2)}, u32[]{:S(2)}) %collective-permute-start.23) | collective-permute-done | bytes 704544 | tf_op jit(solution)/shard_map/ppermute | solution.py:65
  676.3 6.0 fusion.1
  688.3 38.1 %collective-permute-done.17 = bf16[4,64,2752]{2,1,0:T(8,128)(2,1)} collective-permute-done((bf16[4,64,2752]{2,1,0:T(8,128)(2,1)}, bf16[4,64,2752]{2,1,0:T(8,128)(2,1)}, u32[]{:S(2)}, u32[]{:S(2)}) %collective-permute-start.17) | collective-permute-done | bytes 1409056 | tf_op jit(solution)/shard_map/ppermute | solution.py:65
  726.5 45.8 %collective-permute-done.16 = bf16[4,64,2752]{2,1,0:T(8,128)(2,1)} collective-permute-done((bf16[4,64,2752]{2,1,0:T(8,128)(2,1)S(1)}, bf16[4,64,2752]{2,1,0:T(8,128)(2,1)}, u32[]{:S(2)}, u32[]{:S(2)}) %collective-permute-start.16) | collective-permute-done | bytes 1409056 | tf_op jit(solution)/shard_map/ppermute | solution.py:65
  785.1 16.0 %collective-permute-done.19 = bf16[64,2752]{1,0:T(8,128)(2,1)S(1)} collective-permute-done((bf16[64,2752]{1,0:T(8,128)(2,1)S(1)}, bf16[64,2752]{1,0:T(8,128)(2,1)S(1)}, u32[]{:S(2)}, u32[]{:S(2)}) %collective-permute-start.19) | collective-permute-done | bytes 352288 | tf_op jit(solution)/shard_map/ppermute | solution.py:60
  801.1 7.7 collective-permute-done.18
  827.4 26.9 %collective-permute-done.9 = f32[2,2048]{1,0:T(2,128)S(1)} collective-permute-done((f32[2,2048]{1,0:T(2,128)S(1)}, f32[2,2048]{1,0:T(2,128)S(1)}, u32[]{:S(2)}, u32[]{:S(2)}) %collective-permute-start.9) | collective-permute-done | bytes 16416 | tf_op jit(solution)/shard_map/ppermute | solution.py:65
  855.3 10.4 %collective-permute-done.10 = f32[2,2048]{1,0:T(2,128)S(1)} collective-permute-done((f32[2,2048]{1,0:T(2,128)S(1)}, f32[2,2048]{1,0:T(2,128)S(1)}, u32[]{:S(2)}, u32[]{:S(2)}) %collective-permute-start.10) | collective-permute-done | bytes 16416 | tf_op jit(solution)/shard_map/ppermute | solution.py:65
  873.5 9.9 %copy.134 = f32[4096,768]{0,1:T(8,128)} copy(bf16[4096,768]{1,0:T(8,128)(2,1)} %all-gather.22.cloned.1.call-done) | data formatting | bytes 18874368 | tf_op jit(solution)/shard_map/convert_element_type | solution.py:649
  883.4 21.9 %copy.159 = f32[96,8,8,512]{3,2,1,0:T(8,128)} copy(f32[96,8,8,512]{3,1,2,0:T(8,128)} %bitcast.176) | data formatting | bytes 25165824
  905.3 16.4 %copy.135 = f32[512,3,8,256]{0,3,2,1:T(8,128)} copy(f32[512,3,8,256]{0,2,3,1:T(8,128)} %bitcast.177) | data formatting | bytes 25165824 | tf_op jit(solution)/shard_map/convert_element_type | solution.py:649
  921.7 12.6 %copy.138 = f32[512,6144]{1,0:T(8,128)} copy(f32[512,6144]{0,1:T(8,128)} %bitcast.178) | data formatting | bytes 25165824
  949.9 12.9 %convert_element_type.220 = f32[512,11008]{1,0:T(8,128)} convert(bf16[512,11008]{1,0:T(8,128)(2,1)} %all-gather.16.cloned.1.call-done) | non-fusion elementwise | flops 5636096 | bytes 33816576 | tf_op jit(solution)/shard_map/convert_element_type | solution.py:600
  (261 shorter events, 206.6 us)
Async XLA Ops:
  7.2 208.9 %all-gather.12.cloned.1.call-start = ((), (), s32[]{:S(2)}) async-start(), calls=%async_computation.2 | async-start | bytes 1310720 | tf_op jit(solution)/shard_map/all_gather | solution.py:55
  9.5 307.0 %all-gather.20.cloned.1.call-start = ((), (), s32[]{:S(2)}) async-start(), calls=%async_computation.6 | async-start | bytes 2621440 | tf_op jit(solution)/shard_map/all_gather | solution.py:541
  84.9 234.4 %all-gather.18.cloned.1.call-start = ((), (), s32[]{:S(2)}) async-start(), calls=%async_computation.5 | async-start | bytes 12976128 | tf_op jit(solution)/shard_map/all_gather | solution.py:505
  86.2 9.0 collective-permute-start.2
  88.5 38.9 %collective-permute-start.1 = (bf16[64,2752]{1,0:T(8,128)(2,1)S(1)}, bf16[64,2752]{1,0:T(8,128)(2,1)S(1)}, u32[]{:S(2)}, u32[]{:S(2)}) collective-permute-start(bf16[64,2752]{1,0:T(8,128)(2,1)S(1)} %get-tuple-element.107), channel_id=1, source_target_pairs={{0,2},{1,3},{2,0},{3,1},{4,6},{5,7},{6,4},{7,5},{8,10},{9,11},{10,... | collective-permute-start | bytes 1056776 | tf_op jit(solution)/shard_map/ppermute | solution.py:60
  88.5 62.8 %collective-permute-start = (bf16[64,2752]{1,0:T(8,128)(2,1)S(1)}, bf16[64,2752]{1,0:T(8,128)(2,1)S(1)}, u32[]{:S(2)}, u32[]{:S(2)}) collective-permute-start(bf16[64,2752]{1,0:T(8,128)(2,1)S(1)} %get-tuple-element.108), channel_id=1, source_target_pairs={{0,1},{1,2},{2,3},{3,0},{4,5},{5,6},{6,7},{7,4},{8,9},{9,10},{10,1... | collective-permute-start | bytes 1056776 | tf_op jit(solution)/shard_map/ppermute | solution.py:60
  216.1 16.4 %all-to-all-start = ((bf16[8,256,256]{2,1,0:T(8,128)(2,1)}), bf16[8,256,256]{2,1,0:T(8,128)(2,1)S(1)}, u32[]{:S(2)}, u32[]{:S(2)}) async-start(bf16[8,256,256]{2,1,0:T(8,128)(2,1)} %bitcast.211), calls=%async_computation | async-start | bytes 2097152 | tf_op jit(solution)/shard_map/all_to_all | solution.py:486
  449.1 15.5 %all-to-all-start.1 = ((bf16[256,8,256]{2,0,1:T(8,128)(2,1)}), bf16[256,8,256]{2,0,1:T(8,128)(2,1)S(1)}, u32[]{:S(2)}, u32[]{:S(2)}) async-start(bf16[256,8,256]{2,0,1:T(8,128)(2,1)} %bitcast.174), calls=%async_computation.1 | async-start | bytes 2097152 | tf_op jit(solution)/shard_map/all_to_all | solution.py:604
  452.7 416.6 %all-gather.14.cloned.1.call-start = ((), (), s32[]{:S(2)}) async-start(), calls=%async_computation.3 | async-start | bytes 2359296 | tf_op jit(solution)/shard_map/all_gather | solution.py:609
  465.6 22.5 %collective-permute-start.13 = (bf16[512,256]{1,0:T(8,128)(2,1)}, bf16[512,256]{1,0:T(8,128)(2,1)S(1)}, u32[]{:S(2)}, u32[]{:S(2)}) collective-permute-start(bf16[512,256]{1,0:T(8,128)(2,1)} %get-tuple-element.118), channel_id=1, source_target_pairs={{0,1},{1,2},{2,3},{3,0},{4,5},{5,6},{6,7},{7,4},{8,9},{9,10},{10,1... | collective-permute-start | bytes 786440 | tf_op jit(solution)/shard_map/ppermute | solution.py:60
  477.8 20.5 %collective-permute-start.12 = (bf16[512,256]{1,0:T(8,128)(2,1)}, bf16[512,256]{1,0:T(8,128)(2,1)}, u32[]{:S(2)}, u32[]{:S(2)}) collective-permute-start(bf16[512,256]{1,0:T(8,128)(2,1)} %get-tuple-element.119), channel_id=1, source_target_pairs={{0,2},{1,3},{2,0},{3,1},{4,6},{5,7},{6,4},{7,5},{8,10},{9,11},{10,... | collective-permute-start | bytes 786440 | tf_op jit(solution)/shard_map/ppermute | solution.py:60
  479.7 22.2 %collective-permute-start.11 = (bf16[512,256]{1,0:T(8,128)(2,1)}, bf16[512,256]{1,0:T(8,128)(2,1)}, u32[]{:S(2)}, u32[]{:S(2)}) collective-permute-start(bf16[512,256]{1,0:T(8,128)(2,1)} %get-tuple-element.117), channel_id=1, source_target_pairs={{0,3},{1,0},{2,1},{3,2},{4,7},{5,4},{6,5},{7,6},{8,11},{9,8},{10,9... | collective-permute-start | bytes 786440 | tf_op jit(solution)/shard_map/ppermute | solution.py:60
  503.8 369.7 %all-gather.22.cloned.1.call-start = ((), (), s32[]{:S(2)}) async-start(), calls=%async_computation.7 | async-start | bytes 7077888 | tf_op jit(solution)/shard_map/all_gather | solution.py:646
  597.1 337.2 %all-gather.24.cloned.1.call-start = ((), (), s32[]{:S(2)}) async-start(), calls=%async_computation.8 | async-start | bytes 6340608 | tf_op jit(solution)/shard_map/all_gather | solution.py:576
  605.1 28.1 %collective-permute-start.21 = (bf16[1376,1024]{1,0:T(8,128)(2,1)}, bf16[1376,1024]{1,0:T(8,128)(2,1)}, u32[]{:S(2)}, u32[]{:S(2)}) collective-permute-start(bf16[1376,1024]{1,0:T(8,128)(2,1)} %constant_dynamic-slice_fusion.3), channel_id=1, source_target_pairs={{0,4},{4,0},{8,12},{12,8},{16,20},{20,16},{24,28},{28,24},{1,5},{5... | collective-permute-start | bytes 8454152 | tf_op jit(solution)/shard_map/ppermute | solution.py:65
  639.3 20.1 %collective-permute-start.24 = (bf16[1376,256]{1,0:T(8,128)(2,1)S(1)}, bf16[1376,256]{1,0:T(8,128)(2,1)S(1)}, u32[]{:S(2)}, u32[]{:S(2)}) collective-permute-start(bf16[1376,256]{1,0:T(8,128)(2,1)S(1)} %get-tuple-element.76), channel_id=1, source_target_pairs={{0,24},{4,28},{8,16},{12,20},{16,8},{20,12},{24,0},{28,4},{1,25},{... | collective-permute-start | bytes 2113544 | tf_op jit(solution)/shard_map/ppermute | solution.py:65
  641.3 32.2 %collective-permute-start.23 = (bf16[1376,256]{1,0:T(8,128)(2,1)S(1)}, bf16[1376,256]{1,0:T(8,128)(2,1)}, u32[]{:S(2)}, u32[]{:S(2)}) collective-permute-start(bf16[1376,256]{1,0:T(8,128)(2,1)S(1)} %get-tuple-element.77), channel_id=1, source_target_pairs={{0,16},{4,20},{8,24},{12,28},{16,0},{20,4},{24,8},{28,12},{1,17},{... | collective-permute-start | bytes 2113544 | tf_op jit(solution)/shard_map/ppermute | solution.py:65
  642.8 30.7 %collective-permute-start.22 = (bf16[1376,256]{1,0:T(8,128)(2,1)S(1)}, bf16[1376,256]{1,0:T(8,128)(2,1)}, u32[]{:S(2)}, u32[]{:S(2)}) collective-permute-start(bf16[1376,256]{1,0:T(8,128)(2,1)S(1)} %get-tuple-element.75), channel_id=1, source_target_pairs={{0,8},{4,12},{8,0},{12,4},{16,24},{20,28},{24,16},{28,20},{1,9},{5... | collective-permute-start | bytes 2113544 | tf_op jit(solution)/shard_map/ppermute | solution.py:65
  645.8 30.5 %collective-permute-start.14 = (bf16[4,4,64,2752]{3,2,1,0:T(8,128)(2,1)}, bf16[4,4,64,2752]{3,2,1,0:T(8,128)(2,1)}, u32[]{:S(2)}, u32[]{:S(2)}) collective-permute-start(bf16[4,4,64,2752]{3,2,1,0:T(8,128)(2,1)} %dynamic-slice_bitcast_fusion), channel_id=1, source_target_pairs={{0,4},{4,0},{8,12},{12,8},{16,20},{20,16},{24,28},{28,24},{1,5},{5... | collective-permute-start | bytes 16908296 | tf_op jit(solution)/shard_map/ppermute | solution.py:65
  676.2 273.7 %all-gather.16.cloned.1.call-start = ((), (), s32[]{:S(2)}) async-start(), calls=%async_computation.4 | async-start | bytes 12681216 | tf_op jit(solution)/shard_map/all_gather | solution.py:55
  685.3 41.1 %collective-permute-start.17 = (bf16[4,64,2752]{2,1,0:T(8,128)(2,1)}, bf16[4,64,2752]{2,1,0:T(8,128)(2,1)}, u32[]{:S(2)}, u32[]{:S(2)}) collective-permute-start(bf16[4,64,2752]{2,1,0:T(8,128)(2,1)} %get-tuple-element.66), channel_id=1, source_target_pairs={{0,24},{4,28},{8,16},{12,20},{16,8},{20,12},{24,0},{28,4},{1,25},{... | collective-permute-start | bytes 4227080 | tf_op jit(solution)/shard_map/ppermute | solution.py:65
  687.1 85.2 %collective-permute-start.16 = (bf16[4,64,2752]{2,1,0:T(8,128)(2,1)S(1)}, bf16[4,64,2752]{2,1,0:T(8,128)(2,1)}, u32[]{:S(2)}, u32[]{:S(2)}) collective-permute-start(bf16[4,64,2752]{2,1,0:T(8,128)(2,1)S(1)} %get-tuple-element.67), channel_id=1, source_target_pairs={{0,16},{4,20},{8,24},{12,28},{16,0},{20,4},{24,8},{28,12},{1,17},{... | collective-permute-start | bytes 4227080 | tf_op jit(solution)/shard_map/ppermute | solution.py:65
  688.3 84.0 %collective-permute-start.15 = (bf16[4,64,2752]{2,1,0:T(8,128)(2,1)S(1)}, bf16[4,64,2752]{2,1,0:T(8,128)(2,1)}, u32[]{:S(2)}, u32[]{:S(2)}) collective-permute-start(bf16[4,64,2752]{2,1,0:T(8,128)(2,1)S(1)} %get-tuple-element.65), channel_id=1, source_target_pairs={{0,8},{4,12},{8,0},{12,4},{16,24},{20,28},{24,16},{28,20},{1,9},{5... | collective-permute-start | bytes 4227080 | tf_op jit(solution)/shard_map/ppermute | solution.py:65
  775.8 9.3 collective-permute-start.20
  776.2 24.9 %collective-permute-start.19 = (bf16[64,2752]{1,0:T(8,128)(2,1)S(1)}, bf16[64,2752]{1,0:T(8,128)(2,1)S(1)}, u32[]{:S(2)}, u32[]{:S(2)}) collective-permute-start(bf16[64,2752]{1,0:T(8,128)(2,1)S(1)} %get-tuple-element.99), channel_id=1, source_target_pairs={{0,2},{1,3},{2,0},{3,1},{4,6},{5,7},{6,4},{7,5},{8,10},{9,11},{10,... | collective-permute-start | bytes 1056776 | tf_op jit(solution)/shard_map/ppermute | solution.py:60
  778.2 30.6 %collective-permute-start.18 = (bf16[64,2752]{1,0:T(8,128)(2,1)S(1)}, bf16[64,2752]{1,0:T(8,128)(2,1)S(1)}, u32[]{:S(2)}, u32[]{:S(2)}) collective-permute-start(bf16[64,2752]{1,0:T(8,128)(2,1)S(1)} %get-tuple-element.100), channel_id=1, source_target_pairs={{0,1},{1,2},{2,3},{3,0},{4,5},{5,6},{6,7},{7,4},{8,9},{9,10},{10,1... | collective-permute-start | bytes 1056776 | tf_op jit(solution)/shard_map/ppermute | solution.py:60
  815.7 6.2 collective-permute-start.7
  818.4 47.9 %collective-permute-start.5 = (bf16[128,2048]{1,0:T(8,128)(2,1)S(1)}, bf16[128,2048]{1,0:T(8,128)(2,1)S(1)}, u32[]{:S(2)}, u32[]{:S(2)}) collective-permute-start(bf16[128,2048]{1,0:T(8,128)(2,1)S(1)} %get-tuple-element.83), channel_id=1, source_target_pairs={{0,1},{1,2},{2,3},{3,0},{4,5},{5,6},{6,7},{7,4},{8,9},{9,10},{10,1... | collective-permute-start | bytes 1572872 | tf_op jit(solution)/shard_map/ppermute | solution.py:60
  820.6 45.7 %collective-permute-start.4 = (bf16[128,2048]{1,0:T(8,128)(2,1)S(1)}, bf16[128,2048]{1,0:T(8,128)(2,1)S(1)}, u32[]{:S(2)}, u32[]{:S(2)}) collective-permute-start(bf16[128,2048]{1,0:T(8,128)(2,1)S(1)} %get-tuple-element.84), channel_id=1, source_target_pairs={{0,2},{1,3},{2,0},{3,1},{4,6},{5,7},{6,4},{7,5},{8,10},{9,11},{10,... | collective-permute-start | bytes 1572872 | tf_op jit(solution)/shard_map/ppermute | solution.py:60
  821.6 45.5 %collective-permute-start.3 = (bf16[128,2048]{1,0:T(8,128)(2,1)S(1)}, bf16[128,2048]{1,0:T(8,128)(2,1)S(1)}, u32[]{:S(2)}, u32[]{:S(2)}) collective-permute-start(bf16[128,2048]{1,0:T(8,128)(2,1)S(1)} %get-tuple-element.82), channel_id=1, source_target_pairs={{0,3},{1,0},{2,1},{3,2},{4,7},{5,4},{6,5},{7,6},{8,11},{9,8},{10,9... | collective-permute-start | bytes 1572872 | tf_op jit(solution)/shard_map/ppermute | solution.py:60
  824.9 29.4 %collective-permute-start.9 = (f32[2,2048]{1,0:T(2,128)S(1)}, f32[2,2048]{1,0:T(2,128)S(1)}, u32[]{:S(2)}, u32[]{:S(2)}) collective-permute-start(f32[2,2048]{1,0:T(2,128)S(1)} %add.324), channel_id=1, source_target_pairs={{0,1},{1,0},{2,3},{3,2},{4,5},{5,4},{6,7},{7,6},{8,9},{9,8},{10,11... | collective-permute-start | bytes 49160 | tf_op jit(solution)/shard_map/ppermute | solution.py:65
  854.3 11.4 %collective-permute-start.10 = (f32[2,2048]{1,0:T(2,128)S(1)}, f32[2,2048]{1,0:T(2,128)S(1)}, u32[]{:S(2)}, u32[]{:S(2)}) collective-permute-start(f32[2,2048]{1,0:T(2,128)S(1)} %add.325), channel_id=1, source_target_pairs={{0,2},{1,3},{2,0},{3,1},{4,6},{5,7},{6,4},{7,5},{8,10},{9,11},{10,... | collective-permute-start | bytes 49160 | tf_op jit(solution)/shard_map/ppermute | solution.py:65
  (50 other events, 975.2 us)
Sparse Core Ops, SparseCore 0:
  9.7 45.4 all-gather.11
  85.0 68.4 all-gather.19
  156.0 69.1 all-gather.17
  503.9 31.1 all-gather.13
  597.3 49.9 all-gather.21
  676.4 95.8 all-gather.23
  813.6 67.6 all-gather.15

commit v3 on v1

--- a/solution.py
+++ b/solution.py
@@ -1,8 +1,12 @@
+import functools
 import math
+import types
 
 import jax
 import jax.numpy as jnp
 from jax import lax
+from jax.experimental import pallas as pl
+from jax.experimental.pallas import tpu as pltpu
 from jax.sharding import PartitionSpec as P
 
 HEADS = 16
@@ -13,6 +17,7 @@
 EPSILON = 1e-06
 BF = jnp.bfloat16
 F32 = jnp.float32
+VMEM_LIMIT = 56 * 1024 * 1024
 
 
 def dot_plain(left, right):
@@ -51,8 +56,925 @@
     return lax.all_gather(values, axis, axis=0, tiled=True)
 
 
-def scatter_rows(values, axis):
-    return lax.psum_scatter(values, axis, scatter_dimension=0, tiled=True)
+def take(values, index):
+    return lax.dynamic_index_in_dim(values, index, 0, keepdims=False)
+
+
+def split(values, count):
+    rows = values.shape[0] // count
+    return [values[i * rows : (i + 1) * rows] for i in range(count)]
+
+
+MESH = pl.DeviceIdType.MESH
+
+
+def greet(ctx_peers, wa_peers):
+    barrier = pltpu.get_barrier_semaphore()
+    for peer in ctx_peers:
+        pl.semaphore_signal(barrier, inc=1, device_id={"ctx": peer}, device_id_type=MESH)
+    for peer in wa_peers:
+        pl.semaphore_signal(barrier, inc=1, device_id={"wa": peer}, device_id_type=MESH)
+    pl.semaphore_wait(barrier, len(ctx_peers) + len(wa_peers))
+
+
+def send(source, target, send_sem, recv_sem, **peer):
+    copy = pltpu.make_async_remote_copy(
+        src_ref=source,
+        dst_ref=target,
+        send_sem=send_sem,
+        recv_sem=recv_sem,
+        device_id=peer,
+        device_id_type=MESH,
+    )
+    copy.start()
+    return copy
+
+
+def place_of(ctx_size, wa_size):
+    chips = ctx_size // 2
+    p = types.SimpleNamespace(ctx_size=ctx_size, wa_size=wa_size, chips=chips)
+    p.ctx, p.wa = lax.axis_index("ctx"), lax.axis_index("wa")
+    p.core, p.chip = lax.rem(p.ctx, 2), lax.div(p.ctx, 2)
+    p.beside = p.chip * 2 + 1 - p.core
+    p.ahead = [lax.rem(p.chip + m, chips) * 2 + p.core for m in range(chips)]
+    p.behind = [lax.rem(p.chip + chips - m, chips) * 2 + p.core for m in range(chips)]
+    p.up = [lax.rem(p.wa + s, wa_size) for s in range(wa_size)]
+    p.down = [lax.rem(p.wa + wa_size - s, wa_size) for s in range(wa_size)]
+    p.square = chips == 4
+    if p.square:
+        p.near = [p.chip + 1 - 2 * lax.rem(p.chip, 2), lax.rem(p.chip + 2, 4)]
+        p.far = 3 - p.chip
+    return p
+
+
+def on_core(p, chip):
+    return chip * 2 + p.core
+
+
+def off_core(p, chip):
+    return chip * 2 + 1 - p.core
+
+
+def plane_sems(ctx_size):
+    count = max(ctx_size // 2, 5)
+    return [pltpu.SemaphoreType.DMA((count,))] * 4
+
+
+class Spread:
+    def __init__(self, p, own, slot, half, sems):
+        self.p, self.own, self.slot, self.half = p, own, slot, half
+        self.chip_send, self.chip_recv, self.side_send, self.side_recv = sems
+        self.chip, self.side = [], []
+
+    def across(self, source, target, chip):
+        i = len(self.chip)
+        self.chip.append(
+            send(source, target, self.chip_send.at[i], self.chip_recv.at[i], ctx=on_core(self.p, chip))
+        )
+
+    def aside(self, source, target):
+        i = len(self.side)
+        self.side.append(
+            send(source, target, self.side_send.at[i], self.side_recv.at[i], ctx=self.p.beside)
+        )
+
+    def start(self):
+        p = self.p
+        target = self.slot(p.ctx)
+        if p.square:
+            for chip in p.near:
+                self.across(self.own, target, chip)
+        else:
+            for m in range(1, p.chips):
+                self.across(self.own, target, lax.rem(p.chip + m, p.chips))
+        self.aside(self.own, target)
+
+    def arrivals(self):
+        p = self.p
+        if not p.square:
+            for m in range(1, p.chips):
+                self.chip[m - 1].wait_recv()
+                block = self.slot(p.behind[m])
+                self.aside(block, block)
+                yield p.behind[m]
+            self.side[0].wait_recv()
+            yield p.beside
+            for m in range(1, p.chips):
+                self.side[m].wait_recv()
+                yield off_core(p, lax.rem(p.chip + p.chips - m, p.chips))
+            return
+        for i in range(2):
+            self.chip[i].wait_recv()
+            device = on_core(p, p.near[i])
+            part = self.half(device, i)
+            self.across(part, part, p.near[1 - i])
+            self.aside(self.slot(device), self.slot(device))
+            yield device
+        self.side[0].wait_recv()
+        yield p.beside
+        for i in range(2):
+            self.side[1 + i].wait_recv()
+            yield off_core(p, p.near[i])
+        device = on_core(p, p.far)
+        for i in range(2):
+            self.chip[2 + i].wait_recv()
+            part = self.half(device, i)
+            self.aside(part, part)
+        yield device
+        for i in range(2):
+            self.side[3 + i].wait_recv()
+        yield off_core(p, p.far)
+
+    def finish(self):
+        for copy in self.chip + self.side:
+            copy.wait_send()
+
+
+class Fold:
+    def __init__(self, p, source, kept, got, near, sent, piece, half, add, sems):
+        self.p, self.source, self.kept, self.got, self.near, self.sent = p, source, kept, got, near, sent
+        self.piece, self.half, self.add = piece, half, add
+        self.chip_send, self.chip_recv, self.side_send, self.side_recv = sems
+        self.chip = []
+
+    def across(self, source, target, chip):
+        i = len(self.chip)
+        self.chip.append(
+            send(source, target, self.chip_send.at[i], self.chip_recv.at[i], ctx=on_core(self.p, chip))
+        )
+
+    def start(self):
+        p = self.p
+        self.side = send(
+            self.source(1 - p.core), self.got, self.side_send.at[0], self.side_recv.at[0], ctx=p.beside
+        )
+        self.load = pltpu.make_async_copy(self.source(p.core), self.kept, self.side_send.at[1])
+        self.load.start()
+
+    def between(self):
+        p = self.p
+        self.load.wait()
+        self.side.wait_recv()
+        self.add(self.kept, self.got)
+        if not p.square:
+            for m in range(1, p.chips):
+                chip = lax.rem(p.chip + m, p.chips)
+                self.across(self.piece(self.kept, chip), self.sent.at[m - 1], chip)
+            return
+        for i in range(2):
+            self.across(self.half(self.kept, p.far, i), self.near.at[i], p.near[i])
+        for i in range(2):
+            self.across(
+                self.half(self.kept, p.near[i], i), self.half(self.sent.at[i], None, i), p.near[i]
+            )
+
+    def onward(self):
+        p = self.p
+        if not p.square:
+            return
+        for i in range(2):
+            self.chip[i].wait_recv()
+            part = self.half(self.kept, p.near[1 - i], i)
+            self.add(part, self.near.at[i])
+            self.across(part, self.half(self.sent.at[1 - i], None, i), p.near[1 - i])
+
+    def total(self):
+        p = self.p
+        for copy in self.chip[2:] if p.square else self.chip:
+            copy.wait_recv()
+        mine = self.piece(self.kept, p.chip)
+        for i in range(2 if p.square else p.chips - 1):
+            self.add(mine, self.sent.at[i])
+        return mine
+
+    def finish(self):
+        self.side.wait_send()
+        for copy in self.chip:
+            copy.wait_send()
+
+
+def add_rows(into, other, step):
+    def one(i, carried):
+        place = pl.ds(pl.multiple_of(i * step, step), step)
+        into[place, :] = (into[place, :].astype(F32) + other[place, :].astype(F32)).astype(BF)
+        return carried
+
+    lax.fori_loop(0, into.shape[0] // step, one, 0)
+
+
+def add_blocks(into, other):
+    lead = into.shape[:-2]
+
+    def one(i, carried):
+        at = (i,) if len(lead) == 1 else (i // lead[1], i % lead[1])
+        into[at] = (into[at].astype(F32) + other[at].astype(F32)).astype(BF)
+        return carried
+
+    lax.fori_loop(0, math.prod(lead), one, 0)
+
+
+class Stager:
+    def __init__(self, stage, sems, widen):
+        self.stage, self.sems, self.widen = stage, sems, widen
+        self.flying = [[], []]
+        self.count = 0
+
+    def put(self, block, targets):
+        slot = self.count % 2
+        self.count += 1
+        for copy in self.flying[slot]:
+            copy.wait()
+        stage = self.stage.at[slot]
+        self.widen(stage, block)
+        self.flying[slot] = []
+        for i, (target, columns) in enumerate(targets):
+            part = stage if columns is None else stage.at[:, columns]
+            copy = pltpu.make_async_copy(part, target, self.sems.at[slot, i])
+            copy.start()
+            self.flying[slot].append(copy)
+
+    def finish(self):
+        for copies in self.flying:
+            for copy in copies:
+                copy.wait()
+
+
+def widen_rows(step):
+    def widen(stage, block):
+        def one(i, carried):
+            place = pl.ds(pl.multiple_of(i * step, step), step)
+            stage[place, :] = block[place, :].astype(F32)
+            return carried
+
+        lax.fori_loop(0, stage.shape[0] // step, one, 0)
+
+    return widen
+
+
+class Scatter:
+    def __init__(self, p, part_of, refs):
+        self.p, self.part_of, self.refs = p, part_of, refs
+
+    def start(self):
+        p = self.p
+        side_out, side_in, chip_out, chip_in, side_send, side_recv, chip_send, chip_recv = self.refs
+        self.side, self.out = [], []
+        order = list(range(1, p.chips)) + [0]
+        for m in order:
+            side_out[m] = self.part_of(lax.div(p.ahead[m], 2) * 2 + 1 - p.core).astype(BF)
+            self.side.append(
+                send(side_out.at[m], side_in.at[m], side_send.at[m], side_recv.at[m], ctx=p.beside)
+            )
+        for i, m in enumerate(order):
+            mine = self.part_of(p.ahead[m])
+            self.side[i].wait_recv()
+            self.kept = mine + side_in[m].astype(F32)
+            if m > 0:
+                chip_out[m - 1] = self.kept.astype(BF)
+                self.out.append(
+                    send(
+                        chip_out.at[m - 1],
+                        chip_in.at[m - 1],
+                        chip_send.at[m - 1],
+                        chip_recv.at[m - 1],
+                        ctx=p.ahead[m],
+                    )
+                )
+
+    def total(self):
+        chip_in = self.refs[3]
+        total = self.kept
+        for m in range(1, self.p.chips):
+            self.out[m - 1].wait_recv()
+            total = total + chip_in[m - 1].astype(F32)
+        return total
+
+    def finish(self):
+        for copy in self.side + self.out:
+            copy.wait_send()
+
+
+def scatter_scratch(ctx_size, rows, width):
+    chips = ctx_size // 2
+    return [
+        pltpu.VMEM((chips, rows, width), BF),
+        pltpu.VMEM((chips, rows, width), BF),
+        pltpu.VMEM((chips - 1, rows, width), BF),
+        pltpu.VMEM((chips - 1, rows, width), BF),
+    ] + [pltpu.SemaphoreType.DMA((chips,))] * 4
+
+
+def norm_back(x, scale, gain, d_scaled, d_other):
+    normed = x * scale
+    scaled = d_scaled * gain
+    return d_other + scale * (
+        scaled - normed * jnp.mean(scaled * normed, axis=-1, keepdims=True)
+    )
+
+
+def gather_kernel(ctx_size, wa_size, cuts, x_ref, w_ref, xs_ref, ws_ref, *sems):
+    p = place_of(ctx_size, wa_size)
+    ring_send, ring_recv, local = sems[4:]
+    greet([p.beside] + p.ahead[1:], [p.up[1], p.down[1]])
+    rows = w_ref.shape[0] // cuts
+    half_rows = x_ref.shape[0] // 2
+    ring = []
+    for i in range(cuts):
+        part = pl.ds(i * rows, rows)
+        ring.append(
+            send(
+                w_ref.at[part],
+                ws_ref.at[p.wa, part],
+                ring_send.at[0, i],
+                ring_recv.at[0, i],
+                wa=p.up[1],
+            )
+        )
+    spread = Spread(
+        p,
+        x_ref,
+        lambda d: xs_ref.at[d],
+        lambda d, h: xs_ref.at[d, pl.ds(h * half_rows, half_rows)],
+        sems[:4],
+    )
+    spread.start()
+    own_x = pltpu.make_async_copy(x_ref, xs_ref.at[p.ctx], local.at[0])
+    own_w = pltpu.make_async_copy(w_ref, ws_ref.at[p.wa], local.at[1])
+    own_x.start()
+    own_w.start()
+    late = []
+    for step in range(1, wa_size):
+        for i in range(cuts):
+            ring[i].wait_recv()
+            late.append(ring[i])
+            if step < wa_size - 1:
+                block = ws_ref.at[p.down[step], pl.ds(i * rows, rows)]
+                ring[i] = send(
+                    block, block, ring_send.at[step, i], ring_recv.at[step, i], wa=p.up[1]
+                )
+        if step == 1:
+            for _ in spread.arrivals():
+                pass
+    for copy in late:
+        copy.wait_send()
+    spread.finish()
+    own_x.wait()
+    own_w.wait()
+
+
+def gather_both(x, w, ctx_size, wa_size, cuts=4):
+    anywhere = pl.BlockSpec(memory_space=pl.ANY)
+    return pl.pallas_call(
+        functools.partial(gather_kernel, ctx_size, wa_size, cuts),
+        out_shape=(
+            jax.ShapeDtypeStruct((ctx_size,) + x.shape, x.dtype),
+            jax.ShapeDtypeStruct((wa_size,) + w.shape, w.dtype),
+        ),
+        in_specs=[anywhere] * 2,
+        out_specs=[anywhere] * 2,
+        scratch_shapes=plane_sems(ctx_size)
+        + [pltpu.SemaphoreType.DMA((wa_size - 1, cuts))] * 2
+        + [pltpu.SemaphoreType.DMA((2,))],
+        compiler_params=pltpu.CompilerParams(collective_id=0, has_side_effects=True),
+        cost_estimate=pl.CostEstimate(flops=0, bytes_accessed=200_000_000, transcendentals=0),
+        name="gather_both",
+    )(x, w)
+
+
+def out_kernel(
+    ctx_size,
+    wa_size,
+    mixed_ref,
+    w_ref,
+    x_ref,
+    gain_ref,
+    gu_ref,
+    hidden_ref,
+    acts_ref,
+    gw_ref,
+    *scratch,
+):
+    p = place_of(ctx_size, wa_size)
+    act_send, act_recv, gu_send, gu_recv, local = scratch[12:]
+    greet([p.beside] + p.ahead[1:], p.up[1:])
+    deal = [
+        send(
+            gu_ref.at[p.up[s]], gw_ref.at[p.wa, p.ctx], gu_send.at[s], gu_recv.at[s], wa=p.up[s]
+        )
+        for s in range(1, wa_size)
+    ]
+    own = pltpu.make_async_copy(gu_ref.at[p.wa], gw_ref.at[p.wa, p.ctx], local.at[0])
+    own.start()
+    rows = x_ref.shape[0]
+
+    def part_of(device):
+        block = mixed_ref[pl.ds(pl.multiple_of(device * rows, rows), rows), :]
+        return jnp.dot(block, w_ref[...], preferred_element_type=F32)
+
+    scatter = Scatter(p, part_of, scratch[:8])
+    scatter.start()
+    hidden = x_ref[...].astype(F32) + scatter.total()
+    hidden_ref[...] = hidden
+    scale = lax.rsqrt(jnp.mean(hidden * hidden, axis=-1, keepdims=True) + EPSILON)
+    acts_ref[0] = (hidden * scale * gain_ref[...]).astype(BF)
+    copies = [
+        send(acts_ref.at[0], acts_ref.at[s], act_send.at[s], act_recv.at[s], wa=p.up[s])
+        for s in range(1, wa_size)
+    ]
+    own.wait()
+    for copy in deal:
+        copy.wait_recv()
+    half = wa_size // 2
+    spread = Spread(
+        p,
+        gw_ref.at[:, p.ctx],
+        lambda d: gw_ref.at[:, d],
+        lambda d, h: gw_ref.at[pl.ds(h * half, half), d],
+        scratch[8:12],
+    )
+    spread.start()
+    for _ in spread.arrivals():
+        pass
+    scatter.finish()
+    spread.finish()
+    for copy in deal:
+        copy.wait_send()
+    for copy in copies:
+        copy.wait()
+
+
+def out_project(mixed, w_rows, x_own, gain, gu, ctx_size, wa_size):
+    rows, width = x_own.shape
+    vmem = pl.BlockSpec(memory_space=pltpu.VMEM)
+    anywhere = pl.BlockSpec(memory_space=pl.ANY)
+    return pl.pallas_call(
+        functools.partial(out_kernel, ctx_size, wa_size),
+        out_shape=(
+            jax.ShapeDtypeStruct((rows, width), F32),
+            jax.ShapeDtypeStruct((wa_size, rows, width), BF),
+            jax.ShapeDtypeStruct((wa_size, ctx_size) + gu.shape[1:], BF),
+        ),
+        in_specs=[vmem] * 4 + [anywhere],
+        out_specs=[vmem] * 2 + [anywhere],
+        scratch_shapes=scatter_scratch(ctx_size, rows, width)
+        + plane_sems(ctx_size)
+        + [pltpu.SemaphoreType.DMA((wa_size,))] * 5,
+        compiler_params=pltpu.CompilerParams(
+            collective_id=1, has_side_effects=True, vmem_limit_bytes=VMEM_LIMIT
+        ),
+        cost_estimate=pl.CostEstimate(
+            flops=2 * mixed.size * width, bytes_accessed=200_000_000, transcendentals=0
+        ),
+        name="out_project",
+    )(mixed, w_rows, x_own, gain, gu)
+
+
+def turn_kernel(
+    ctx_size,
+    wa_size,
+    parts_ref,
+    mlp_ref,
+    hidden_ref,
+    gain_ref,
+    dz_ref,
+    gu_ref,
+    down_ref,
+    all_ref,
+    gain_out_ref,
+    out_ref,
+    gu_out_ref,
+    down_out_ref,
+    *scratch,
+):
+    p = place_of(ctx_size, wa_size)
+    got_ref, more_ref, wa_send, wa_recv, more_send, more_recv = scratch[:6]
+    gu_kept, gu_got, gu_near, gu_sent, down_kept, down_got, down_near, down_sent = scratch[6:14]
+    gu_sems, down_sems, spread_sems = scratch[14:18], scratch[18:22], scratch[22:26]
+    greet([p.beside] + p.ahead[1:], p.down[1:])
+    copies = [
+        send(parts_ref.at[s], got_ref.at[s], wa_send.at[s], wa_recv.at[s], wa=p.down[s])
+        for s in range(1, wa_size)
+    ]
+    columns = down_ref.shape[1] // ctx_size
+    core_columns = columns * p.chips
+    down_rows = down_ref.shape[0] // 2
+    half = wa_size // 2
+
+    def down_piece(ref, chip):
+        return ref.at[:, pl.ds(pl.multiple_of(chip * columns, columns), columns)]
+
+    def down_half(ref, chip, h):
+        place = pl.ds(h * down_rows, down_rows)
+        if chip is None:
+            return ref.at[place]
+        return ref.at[place, pl.ds(pl.multiple_of(chip * columns, columns), columns)]
+
+    down = Fold(
+        p,
+        lambda core: down_ref.at[
+            :, pl.ds(pl.multiple_of(core * core_columns, core_columns), core_columns)
+        ],
+        down_kept,
+        down_got,
+        down_near,
+        down_sent,
+        down_piece,
+        down_half,
+        lambda into, other: add_rows(into, other, 16),
+        down_sems,
+    )
+
+    def gu_half(ref, chip, h):
+        place = pl.ds(h * half, half)
+        return ref.at[place] if chip is None else ref.at[place, chip]
+
+    gu = Fold(
+        p,
+        lambda core: gu_ref.at[:, :, core],
+        gu_kept,
+        gu_got,
+        gu_near,
+        gu_sent,
+        lambda ref, chip: ref.at[:, chip],
+        gu_half,
+        add_blocks,
+        gu_sems,
+    )
+    down.start()
+    gu.start()
+    down.between()
+    gu.between()
+    hidden = hidden_ref[...]
+    scale = lax.rsqrt(jnp.mean(hidden * hidden, axis=-1, keepdims=True) + EPSILON)
+    down.onward()
+    d_normed = parts_ref[0].astype(F32)
+    for s in range(1, wa_size):
+        copies[s - 1].wait_recv()
+        d_normed = d_normed + got_ref[s].astype(F32)
+    more = [
+        send(mlp_ref.at[s], more_ref.at[s], more_send.at[s], more_recv.at[s], wa=p.down[s])
+        for s in range(1, wa_size)
+    ]
+    gain_out_ref[...] = jnp.sum(d_normed * (hidden * scale), axis=0, keepdims=True)
+    d_hidden = norm_back(hidden, scale, gain_ref[...], d_normed, dz_ref[...].astype(F32))
+    all_ref[p.ctx] = d_hidden.astype(BF)
+    half_rows = all_ref.shape[1] // 2
+    spread = Spread(
+        p,
+        all_ref.at[p.ctx],
+        lambda d: all_ref.at[d],
+        lambda d, h: all_ref.at[d, pl.ds(h * half_rows, half_rows)],
+        spread_sems,
+    )
+    spread.start()
+    gu.onward()
+    down_out_ref[...] = down.total()[...]
+    for _ in spread.arrivals():
+        pass
+    gu_out_ref[...] = gu.total()[...]
+    result = hidden + mlp_ref[0].astype(F32)
+    for s in range(1, wa_size):
+        more[s - 1].wait_recv()
+        result = result + more_ref[s].astype(F32)
+    out_ref[...] = result.astype(BF)
+    for copy in copies + more:
+        copy.wait_send()
+    down.finish()
+    gu.finish()
+    spread.finish()
+
+
+def turn(parts, mlp, hidden, gain, dz, gu, down, ctx_size, wa_size):
+    rows, width = hidden.shape
+    chips = ctx_size // 2
+    columns = down.shape[1] // ctx_size
+    gu_rows, gu_columns = gu.shape[3:]
+    vmem = pl.BlockSpec(memory_space=pltpu.VMEM)
+    anywhere = pl.BlockSpec(memory_space=pl.ANY)
+    many = 2 if chips == 4 else chips - 1
+    return pl.pallas_call(
+        functools.partial(turn_kernel, ctx_size, wa_size),
+        out_shape=(
+            jax.ShapeDtypeStruct((ctx_size, rows, width), BF),
+            jax.ShapeDtypeStruct((1, width), F32),
+            jax.ShapeDtypeStruct((rows, width), BF),
+            jax.ShapeDtypeStruct((wa_size, gu_rows, gu_columns), BF),
+            jax.ShapeDtypeStruct((down.shape[0], columns), BF),
+        ),
+        in_specs=[vmem] * 5 + [anywhere] * 2,
+        out_specs=[vmem] * 5,
+        scratch_shapes=[pltpu.VMEM((wa_size, rows, width), BF)] * 2
+        + [pltpu.SemaphoreType.DMA((wa_size,))] * 4
+        + [
+            pltpu.VMEM((wa_size, chips, gu_rows, gu_columns), BF),
+            pltpu.VMEM((wa_size, chips, gu_rows, gu_columns), BF),
+            pltpu.VMEM((2, wa_size // 2, gu_rows, gu_columns), BF),
+            pltpu.VMEM((many, wa_size, gu_rows, gu_columns), BF),
+            pltpu.VMEM((down.shape[0], columns * chips), BF),
+            pltpu.VMEM((down.shape[0], columns * chips), BF),
+            pltpu.VMEM((2, down.shape[0] // 2, columns), BF),
+            pltpu.VMEM((many, down.shape[0], columns), BF),
+        ]
+        + [pltpu.SemaphoreType.DMA((max(chips, 6),))] * 8
+        + plane_sems(ctx_size),
+        compiler_params=pltpu.CompilerParams(
+            collective_id=2, has_side_effects=True, vmem_limit_bytes=VMEM_LIMIT
+        ),
+        cost_estimate=pl.CostEstimate(flops=0, bytes_accessed=200_000_000, transcendentals=0),
+        name="turn",
+    )(parts, mlp, hidden, gain, dz, gu, down)
+
+
+def last_kernel(
+    ctx_size,
+    wa_size,
+    grads_ref,
+    w_ref,
+    dealt_ref,
+    x_ref,
+    gain_ref,
+    dh_ref,
+    gu_ref,
+    dw_ref,
+    down_ref,
+    out_ref,
+    gain_out_ref,
+    rows_ref,
+    dw_out_ref,
+    down_out_ref,
+    *scratch,
+):
+    p = place_of(ctx_size, wa_size)
+    gu_in, dw_in, gu_send, gu_recv, dw_send, dw_recv = scratch[8:14]
+    downs, stage, stage_sems = scratch[14:17]
+    greet([p.beside] + p.ahead[1:], p.up[1:])
+    deal = [
+        send(gu_ref.at[p.up[s]], gu_in.at[p.wa], gu_send.at[s], gu_recv.at[s], wa=p.up[s])
+        for s in range(1, wa_size)
+    ]
+    copies = [
+        send(dw_ref.at[p.up[s]], dw_in.at[s], dw_send.at[s], dw_recv.at[s], wa=p.up[s])
+        for s in range(1, wa_size)
+    ]
+    rows = x_ref.shape[0]
+    gain_out_ref[...] = jnp.zeros_like(gain_out_ref)
+
+    def part_of(device):
+        place = pl.ds(pl.multiple_of(device * rows, rows), rows)
+        part = lax.dot_general(
+            grads_ref[place, :],
+            w_ref[...],
+            (((1,), (1,)), ((), ())),
+            preferred_element_type=F32,
+        )
+        x = dealt_ref[place, :].astype(F32)
+        scale = lax.rsqrt(jnp.mean(x * x, axis=-1, keepdims=True) + EPSILON)
+        gain_out_ref[...] += jnp.sum(part * (x * scale), axis=0, keepdims=True)
+        return part
+
+    scatter = Scatter(p, part_of, scratch[:8])
+    scatter.start()
+    columns = down_ref.shape[1]
+    down_rows = down_ref.shape[0] // 2
+    spread = Spread(
+        p,
+        down_ref,
+        lambda d: downs.at[d],
+        lambda d, h: downs.at[d, pl.ds(h * down_rows, down_rows)],
+        scratch[17:21],
+    )
+    spread.start()
+    stager = Stager(stage, stage_sems, widen_rows(16))
+
+    def put(block, device):
+        first = (lax.rem(device, 2) * p.chips + lax.div(device, 2)) * columns
+        place = pl.ds(pl.multiple_of(first, columns), columns)
+        stager.put(block, [(down_out_ref.at[:, place], None)])
+
+    put(down_ref, p.ctx)
+    gu_in[p.wa] = gu_ref[p.wa]
+    x = x_ref[...].astype(F32)
+    scale = lax.rsqrt(jnp.mean(x * x, axis=-1, keepdims=True) + EPSILON)
+    d_normed = scatter.total()
+    out_ref[...] = norm_back(
+        x, scale, gain_ref[...], d_normed, dh_ref[...].astype(F32)
+    ).astype(BF)
+    for copy in deal:
+        copy.wait_recv()
+    own_columns = gu_in.shape[2] // 2
+    total_columns = rows_ref.shape[1] // 2
+    for i in range(wa_size):
+        for part in range(2):
+            first = part * total_columns + i * own_columns
+            rows_ref[:, first : first + own_columns] = gu_in[
+                i, :, part * own_columns : (part + 1) * own_columns
+            ]
+    for device in spread.arrivals():
+        put(downs.at[device], device)
+    total = dw_ref[p.wa].astype(F32)
+    for s in range(1, wa_size):
+        copies[s - 1].wait_recv()
+        total = total + dw_in[s].astype(F32)
+    dw_out_ref[...] = total.astype(BF)
+    stager.finish()
+    scatter.finish()
+    spread.finish()
+    for copy in copies + deal:
+        copy.wait_send()
+
+
+def last_exchange(grads, w, dealt, x_own, gain, dh, gu, dw, down, ctx_size, wa_size):
+    rows, width = x_own.shape
+    vmem = pl.BlockSpec(memory_space=pltpu.VMEM)
+    anywhere = pl.BlockSpec(memory_space=pl.ANY)
+    return pl.pallas_call(
+        functools.partial(last_kernel, ctx_size, wa_size),
+        out_shape=(
+            jax.ShapeDtypeStruct((rows, width), BF),
+            jax.ShapeDtypeStruct((1, width), F32),
+            jax.ShapeDtypeStruct((gu.shape[1], wa_size * gu.shape[2]), BF),
+            jax.ShapeDtypeStruct(dw.shape[1:], BF),
+            jax.ShapeDtypeStruct((down.shape[0], ctx_size * down.shape[1]), F32),
+        ),
+        in_specs=[vmem] * 9,
+        out_specs=[vmem] * 4 + [anywhere],
+        scratch_shapes=scatter_scratch(ctx_size, rows, width)
+        + [pltpu.VMEM(gu.shape, BF), pltpu.VMEM(dw.shape, BF)]
+        + [pltpu.SemaphoreType.DMA((wa_size,))] * 4
+        + [
+            pltpu.VMEM((ctx_size,) + down.shape, BF),
+            pltpu.VMEM((2,) + down.shape, F32),
+            pltpu.SemaphoreType.DMA((2, 1)),
+        ]
+        + plane_sems(ctx_size),
+        compiler_params=pltpu.CompilerParams(
+            collective_id=3, has_side_effects=True, vmem_limit_bytes=VMEM_LIMIT
+        ),
+        cost_estimate=pl.CostEstimate(
+            flops=2 * grads.size * width, bytes_accessed=250_000_000, transcendentals=0
+        ),
+        name="last_exchange",
+    )(grads, w, dealt, x_own, gain, dh, gu, dw, down)
+
+
+def final_kernel(
+    ctx_size,
+    wa_size,
+    dw_ref,
+    rows_ref,
+    out_ref,
+    gains_ref,
+    d_gu_ref,
+    d_qkv_ref,
+    d_out_ref,
+    sums_ref,
+    *scratch,
+):
+    p = place_of(ctx_size, wa_size)
+    dw_in, dw_send, dw_recv, share = scratch[:4]
+    gus, gu_stage, gu_sems = scratch[4:7]
+    qkvs, qkv_stage, qkv_sems = scratch[7:10]
+    outs, out_stage, out_sems = scratch[10:13]
+    wa_gains, ctx_gains, wa_send, wa_recv, ctx_send, ctx_recv = scratch[13:19]
+    gu_plane, qkv_plane, out_plane = scratch[19:23], scratch[23:27], scratch[27:31]
+    peers = [lax.rem(p.ctx + i, ctx_size) for i in range(1, ctx_size)]
+    greet(peers, p.up[1:])
+    small = [
+        send(gains_ref, wa_gains.at[p.wa], wa_send.at[s], wa_recv.at[s], wa=p.up[s])
+        for s in range(1, wa_size)
+    ]
+    copies = [
+        send(dw_ref.at[p.up[s]], dw_in.at[s], dw_send.at[s], dw_recv.at[s], wa=p.up[s])
+        for s in range(1, wa_size)
+    ]
+
+    def spread_of(own, slots, sems):
+        half = slots.shape[1] // 2
+        return Spread(
+            p,
+            own,
+            lambda d: slots.at[d],
+            lambda d, h: slots.at[d, pl.ds(h * half, half)],
+            sems,
+        )
+
+    out_spread = spread_of(out_ref, outs, out_plane)
+    gu_spread = spread_of(rows_ref, gus, gu_plane)
+    out_spread.start()
+    gu_spread.start()
+    gu_stager = Stager(gu_stage, gu_sems, widen_rows(16))
+    qkv_stager = Stager(qkv_stage, qkv_sems, widen_rows(16))
+    out_stager = Stager(out_stage, out_sems, widen_rows(16))
+    gu_rows = rows_ref.shape[0]
+    head_columns = out_ref.shape[1]
+    width = d_out_ref.shape[1]
+
+    def put_gu(block, device):
+        place = pl.ds(pl.multiple_of(device * gu_rows, gu_rows), gu_rows)
+        gu_stager.put(block, [(d_gu_ref.at[place], None)])
+
+    def put_columns(stager, block, target, device, count):
+        places = []
+        for part in range(count):
+            first = pl.multiple_of(part * width + device * head_columns, head_columns)
+            columns = pl.ds(part * head_columns, head_columns)
+            places.append((target.at[:, pl.ds(first, head_columns)], columns))
+        stager.put(block, places)
+
+    put_gu(rows_ref, p.ctx)
+    put_columns(out_stager, out_ref, d_out_ref, p.ctx, 1)
+    for device in out_spread.arrivals():
+        put_columns(out_stager, outs.at[device], d_out_ref, device, 1)
+    wa_gains[p.wa] = gains_ref[...]
+    for copy in small:
+        copy.wait()
+    plane_gain = wa_gains[0]
+    for i in range(1, wa_size):
+        plane_gain = plane_gain + wa_gains[i]
+    ctx_gains[p.ctx] = plane_gain
+    own_gain = ctx_gains.at[p.ctx]
+    small = [
+        send(own_gain, own_gain, ctx_send.at[i], ctx_recv.at[i], ctx=peer)
+        for i, peer in enumerate(peers)
+    ]
+    for device in gu_spread.arrivals():
+        put_gu(gus.at[device], device)
+    share[...] = dw_ref[p.wa]
+    for s in range(1, wa_size):
+        copies[s - 1].wait_recv()
+    step = 16
+
+    def add_up(i, carried):
+        place = pl.ds(pl.multiple_of(i * step, step), step)
+        total = share[place, :].astype(F32)
+        for s in range(1, wa_size):
+            total = total + dw_in[s, place, :].astype(F32)
+        share[place, :] = total.astype(BF)
+        return carried
+
+    lax.fori_loop(0, share.shape[0] // step, add_up, 0)
+    qkv_spread = spread_of(share, qkvs, qkv_plane)
+    qkv_spread.start()
+    put_columns(qkv_stager, share, d_qkv_ref, p.ctx, 3)
+    for device in qkv_spread.arrivals():
+        put_columns(qkv_stager, qkvs.at[device], d_qkv_ref, device, 3)
+    for copy in small:
+        copy.wait()
+    total_gain = ctx_gains[0]
+    for i in range(1, ctx_size):
+        total_gain = total_gain + ctx_gains[i]
+    sums_ref[...] = total_gain
+    for stager in (gu_stager, qkv_stager, out_stager):
+        stager.finish()
+    for spread in (out_spread, gu_spread, qkv_spread):
+        spread.finish()
+    for copy in copies:
+        copy.wait_send()
+
+
+def final_gather(dw, gu_rows, out_share, gains, ctx_size, wa_size):
+    vmem = pl.BlockSpec(memory_space=pltpu.VMEM)
+    anywhere = pl.BlockSpec(memory_space=pl.ANY)
+    qkv_rows, qkv_columns = dw.shape[1:]
+    out_rows, out_columns = out_share.shape
+    rows, columns = gu_rows.shape
+
+    def staged(shape, count):
+        return [
+            pltpu.VMEM((ctx_size,) + shape, BF),
+            pltpu.VMEM((2,) + shape, F32),
+            pltpu.SemaphoreType.DMA((2, count)),
+        ]
+
+    return pl.pallas_call(
+        functools.partial(final_kernel, ctx_size, wa_size),
+        out_shape=(
+            jax.ShapeDtypeStruct((ctx_size * rows, columns), F32),
+            jax.ShapeDtypeStruct((qkv_rows, ctx_size * qkv_columns), F32),
+            jax.ShapeDtypeStruct((out_rows, ctx_size * out_columns), F32),
+            jax.ShapeDtypeStruct(gains.shape, F32),
+        ),
+        in_specs=[vmem] * 4,
+        out_specs=[anywhere] * 3 + [vmem],
+        scratch_shapes=[pltpu.VMEM(dw.shape, BF)]
+        + [pltpu.SemaphoreType.DMA((wa_size,))] * 2
+        + [pltpu.VMEM((qkv_rows, qkv_columns), BF)]
+        + staged((rows, columns), 1)
+        + staged((qkv_rows, qkv_columns), 3)
+        + staged((out_rows, out_columns), 1)
+        + [
+            pltpu.VMEM((wa_size,) + gains.shape, F32),
+            pltpu.VMEM((ctx_size,) + gains.shape, F32),
+        ]
+        + [pltpu.SemaphoreType.DMA((wa_size,))] * 2
+        + [pltpu.SemaphoreType.DMA((ctx_size,))] * 2
+        + plane_sems(ctx_size) * 3,
+        compiler_params=pltpu.CompilerParams(
+            collective_id=4, has_side_effects=True, vmem_limit_bytes=VMEM_LIMIT
+        ),
+        cost_estimate=pl.CostEstimate(flops=0, bytes_accessed=300_000_000, transcendentals=0),
+        name="final_gather",
+    )(dw, gu_rows, out_share, gains)
 
 
 def per_device(
@@ -62,6 +984,7 @@
     ctx_size = lax.axis_size("ctx")
     wa_size = lax.axis_size("wa")
     ctx_index = lax.axis_index("ctx")
+    wa_index = lax.axis_index("wa")
     block_order = dealing[0]
     block_total = block_order.shape[0]
     group_rows = block_total * BLOCK
@@ -92,10 +1015,11 @@
         ],
         axis=1,
     )
-    qkv_cols = gather_rows(qkv_slice, "wa")
-    out_cols = gather_rows(
-        lax.dynamic_slice_in_dim(w_out, ctx_index * head_cols, head_cols, 1), "wa"
-    )
+    dealt, qkv_cols = gather_both(tokens[0], qkv_slice, ctx_size, wa_size)
+    dealt = dealt.reshape(group_rows, width)
+    qkv_cols = qkv_cols.reshape(width, 3 * head_cols)
+    out_slice = lax.dynamic_slice_in_dim(w_out, ctx_index * head_cols, head_cols, 1)
+    out_cols = gather_rows(out_slice, "wa")
     out_rows = lax.all_to_all(out_cols, "ctx", 0, 1, tiled=True)
     gu_piece = lax.dynamic_slice_in_dim(w_gate_up, ctx_index * piece_rows, piece_rows, 0)
     gu_send = jnp.stack(
@@ -110,11 +1034,7 @@
             for to in range(wa_size)
         ]
     )
-    gu_mine = lax.all_to_all(gu_send, "wa", 0, 0, tiled=True)
-    gu_all = lax.all_gather(gu_mine, "ctx", axis=0)
-    gu_weight = jnp.transpose(gu_all, (1, 0, 2, 3)).reshape(width, 2 * ff_own)
-
-    dealt = gather_rows(tokens[0], "ctx")
+
     given_b = pick_blocks(dealt, inverse)
     given = given_b.astype(F32)
     positions = jnp.arange(group_rows, dtype=jnp.int32)
@@ -143,13 +1063,18 @@
     mixed = jnp.einsum("hqk,khe->qhe", probs_b, value_b, preferred_element_type=F32)
     mixed_b = mixed.reshape(group_rows, head_cols).astype(BF)
 
-    branch = scatter_rows(dot_plain(mixed_b, out_rows).astype(BF), "ctx")
     own_given = lax.dynamic_slice_in_dim(given_b, ctx_index * tok_rows, tok_rows)
-    hidden = own_given.astype(F32) + branch.astype(F32)
-    scale_two = rms_scale(hidden)
-    normed_two = hidden * scale_two
-    act_two = gather_rows((normed_two * norm2_gain).astype(BF), "wa")
-    cotangent = gather_rows(grad_out[0], "wa")
+    gain_two = norm2_gain[None, :]
+    hidden, acts, gu_weight = out_project(
+        mixed_b, out_rows, own_given, gain_two, gu_send, ctx_size, wa_size
+    )
+    gu_weight = gu_weight.reshape(width, 2 * ff_own)
+    act_two = acts.reshape(wa_size * tok_rows, width)
+    early = lax.optimization_barrier((grad_out[0], qkv_cols))[0]
+    grads_all = lax.all_gather(early, "wa", axis=0)
+    cotangent = jnp.concatenate(
+        [take(grads_all, (wa_index - s) % wa_size) for s in range(wa_size)], axis=0
+    )
 
     gate_up = dot_plain(act_two, gu_weight)
     gate_part = gate_up[:, :ff_own]
@@ -157,38 +1082,23 @@
     sigmoid_gate = jax.nn.sigmoid(gate_part)
     silu_gate = gate_part * sigmoid_gate
     inner_b = (silu_gate * up_part).astype(BF)
-    result = scatter_rows(dot_plain(inner_b, w_down).astype(BF), "wa")
-    out_given = (hidden + result.astype(F32)).astype(BF)
 
     d_inner = dot_right_t(cotangent, w_down)
     d_gate = d_inner * up_part * sigmoid_gate * (1.0 + gate_part * (1.0 - sigmoid_gate))
     d_gu_b = jnp.concatenate([d_gate, d_inner * silu_gate], axis=1).astype(BF)
-    d_normed_two = scatter_rows(dot_right_t(d_gu_b, gu_weight).astype(BF), "wa").astype(F32)
-    d_down = lax.psum(dot_left_t(inner_b, cotangent).astype(BF), "ctx").astype(F32)
-
-    d_gu_share = dot_left_t(act_two, d_gu_b).astype(BF)
-    d_gu_share = jnp.transpose(
-        d_gu_share.reshape(wa_size, ctx_size, piece_rows, 2 * ff_own), (1, 0, 2, 3)
-    ).reshape(ctx_size * wa_size, piece_rows, 2 * ff_own)
-    d_gu_piece = scatter_rows(d_gu_share, "ctx")
-    d_gu_back = lax.all_to_all(d_gu_piece, "wa", 0, 0, tiled=True)
-    d_gu_rows = jnp.concatenate(
-        [d_gu_back[i, :, :ff_own] for i in range(wa_size)]
-        + [d_gu_back[i, :, ff_own:] for i in range(wa_size)],
-        axis=1,
-    )
-    d_gate_up = gather_rows(d_gu_rows, "ctx").astype(F32)
-
-    gain_two_part = jnp.sum(d_normed_two * normed_two, axis=0)
-    scaled_two = d_normed_two * norm2_gain
-    d_hidden = grad_out[0].astype(F32) + scale_two * (
-        scaled_two - normed_two * jnp.mean(scaled_two * normed_two, axis=1, keepdims=True)
-    )
-    d_branch_b = gather_rows(d_hidden.astype(BF), "ctx")
+    d_act = dot_right_t(d_gu_b, gu_weight).astype(BF).reshape(wa_size, tok_rows, width)
+    mlp_parts = dot_plain(inner_b, w_down).astype(BF).reshape(wa_size, tok_rows, width)
+    down_part = dot_left_t(inner_b, cotangent).astype(BF)
+    gu_part = dot_left_t(act_two, d_gu_b).astype(BF)
+    gu_part = gu_part.reshape(wa_size, ctx_size // 2, 2, piece_rows, 2 * ff_own)
+    d_branches, gain_two_part, out_given, gu_piece_grad, down_piece_grad = turn(
+        d_act, mlp_parts, hidden, gain_two, grad_out[0], gu_part, down_part, ctx_size, wa_size
+    )
+    d_branch_b = d_branches.reshape(group_rows, width)
     grad_mixed_b = dot_right_t(d_branch_b, out_rows).astype(BF)
     d_out_part = dot_left_t(mixed_b, d_branch_b).astype(BF)
     d_out_cols = lax.all_to_all(d_out_part, "ctx", 1, 0, tiled=True)
-    d_out = lax.all_gather(scatter_rows(d_out_cols, "wa"), "ctx", axis=1, tiled=True).astype(F32)
+    out_parts = d_out_cols.reshape(wa_size, wa_rows, head_cols)
 
     grad_heads = grad_mixed_b.reshape(group_rows, heads_own, HEAD)
     d_probs = jnp.einsum("qhe,khe->hqk", grad_heads, value_b, preferred_element_type=F32)
@@ -205,19 +1115,7 @@
         ],
         axis=1,
     ).astype(BF)
-    d_qkv_share = scatter_rows(dot_left_t(act_one, d_qkv_b).astype(BF), "wa")
-    d_qkv_all = lax.all_gather(d_qkv_share, "ctx", axis=0)
-    d_qkv = jnp.transpose(
-        d_qkv_all.reshape(ctx_size, wa_rows, 3, head_cols), (1, 2, 0, 3)
-    ).reshape(wa_rows, 3 * width).astype(F32)
-
-    d_one_part = dot_right_t(d_qkv_b, qkv_cols)
-    gain_one_part = jnp.sum(d_one_part * normed_one, axis=0)
-    d_normed_one = scatter_rows(pick_blocks(d_one_part.astype(BF), block_order), "ctx").astype(F32)
-    own = tokens[0].astype(F32)
-    own_scale = rms_scale(own)
-    own_normed = own * own_scale
-    scaled_one = d_normed_one * norm1_gain
+    qkv_parts = dot_left_t(act_one, d_qkv_b).astype(BF).reshape(wa_size, wa_rows, 3 * head_cols)
     own_order = lax.dynamic_slice_in_dim(block_order, ctx_index * own_blocks, own_blocks)
     d_hidden_dealt = jnp.concatenate(
         [
@@ -225,15 +1123,27 @@
             for i in range(own_blocks)
         ],
         axis=0,
-    ).astype(F32)
-    d_tokens = d_hidden_dealt + own_scale * (
-        scaled_one - own_normed * jnp.mean(scaled_one * own_normed, axis=1, keepdims=True)
-    )
-    gain_parts = jnp.stack([gain_one_part, gain_two_part])
-    gain_sums = jnp.sum(lax.all_gather(gain_parts, ("ctx", "wa"), axis=0), axis=0)
+    )
+    d_tokens, gain_one_part, d_gu_rows, d_out_share, d_down = last_exchange(
+        pick_blocks(d_qkv_b, block_order),
+        qkv_cols,
+        dealt,
+        tokens[0],
+        norm1_gain[None, :],
+        d_hidden_dealt,
+        gu_piece_grad,
+        out_parts,
+        down_piece_grad,
+        ctx_size,
+        wa_size,
+    )
+    gain_parts = jnp.concatenate([gain_one_part, gain_two_part], axis=0)
+    d_gate_up, d_qkv, d_out, gain_sums = final_gather(
+        qkv_parts, d_gu_rows, d_out_share, gain_parts, ctx_size, wa_size
+    )
     return (
         out_given[None],
-        d_tokens.astype(BF)[None],
+        d_tokens[None],
         gain_sums[0],
         d_qkv,
         d_out,

time: 1090 us -> 723 us (0.66)
  waiting for transfers between devices: 593 us -> 7.68 us
  Pallas kernels: 0 us -> 469 us
  blocking collectives: 137 us -> 0 us
  local copies, waits for them, and re-layouts: 138 us -> 94.8 us
  other arithmetic: 61.6 us -> 18.6 us
  matrix products: 118 us -> 90.5 us
    pallas_call x0 -> x5, Pallas kernels: none -> 469 us  [the longest x1 115 us: out_project(): pl.pallas_call(functools.partial(out_kernel, ctx_size, wa_size), out_shap...]
    all_gather x7 -> x1, waiting for transfers between devices: 213 us -> 0.02 us  [gather_rows(): return lax.all_gather(values, axis, axis=0, tiled=True)]
    reduce_scatter x7 -> x0, waiting for transfers between devices: 191 us -> none  [scatter_rows(): return lax.psum_scatter(values, axis, scatter_dimension=0, tiled=True)]
    all_gather x3 -> x1, waiting for transfers between devices: 119 us -> 0.01 us  [per_device(): grads_all = lax.all_gather(early, 'wa', axis=0)]
    all_to_all x2 -> x0, blocking collectives: 73.6 us -> none  [the longest x1 37.6 us: per_device(): gu_mine = lax.all_to_all(gu_send, 'wa', 0, 0, tiled=True)]
    all_gather x1 -> x0, blocking collectives: 63.5 us -> none  [per_device(): lax.all_gather(gain_parts, ('ctx', 'wa'), axis=0)]
    psum x1 -> x0, waiting for transfers between devices: 61.2 us -> none  [per_device(): lax.psum(dot_left_t(inner_b, cotangent).astype(BF), 'ctx').astype(F32)]
    convert_element_type x5 -> x0, other arithmetic: 30.7 us -> none  [the longest x1 12.9 us: per_device(): d_gate_up = gather_rows(d_gu_rows, 'ctx').astype(F32)]
  transfers between devices with their start and end apart: 20 -> 4, of which waited for: 17 -> 1; matrix products, arithmetic and copies ran while one was open for 21% -> 11% of each run, Pallas kernels for 0% -> 26%
where the time goes in v3:
time: 723 us; the launch traced here: 716 us
  Pallas kernels  469 us (65%)
  local copies, waits for them, and re-layouts  94.8 us (13%)
  matrix products  90.5 us (13%)
  between operations  25.6 us (4%)
  other arithmetic  18.6 us (3%)
  starting transfers between devices  10.6 us (1%)
  waiting for transfers between devices  7.68 us (1%)
    pallas_call x1, Pallas kernels, out_project(): pl.pallas_call(functools.partial(out_kernel, ctx_size, wa_size), out_shap...  115 us
    pallas_call x1, Pallas kernels, final_gather(): pl.pallas_call(functools.partial(final_kernel, ctx_size, wa_size), out_sh...  109 us
    pallas_call x1, Pallas kernels, turn(): pl.pallas_call(functools.partial(turn_kernel, ctx_size, wa_size), out_sha...  106 us
    pallas_call x1, Pallas kernels, gather_both(): pl.pallas_call(functools.partial(gather_kernel, ctx_size, wa_size, cuts),...  71.8 us
    pallas_call x1, Pallas kernels, last_exchange(): pl.pallas_call(functools.partial(last_kernel, ctx_size, wa_size), out_sha...  67.9 us
    unnamed x88, local copies, waits for them, and re-layouts  58.8 us
    dot_general x3, matrix products, dot_plain(): return jnp.dot(left, right, preferred_element_type=F32)  24 us
    dot_general x4, matrix products, dot_left_t(): lax.dot_general(left, right, (((0,), (0,)), ((), ())), preferred_element_...  22.4 us
  transfers between devices with their start and end apart: 4, of which 1 were waited for; matrix products, arithmetic and copies ran while one was open for 11% of the time, Pallas kernels for 26%

profile of v3, /device:TPU:9, one launch (start us, length us, event | category | flops | bytes accessed | tf_op | source)
XLA Modules:
  0.0 716.4 jit_solution(3972968075135488629)
XLA Ops:
  11.7 71.8 %gather_both.1 = (bf16[8,128,2048]{2,1,0:T(8,128)(2,1)}, bf16[4,512,768]{2,1,0:T(8,128)(2,1)}) custom-call(bf16[128,2048]{1,0:T(8,128)(2,1)} %bitcast.127, bf16[512,768]{1,0:T(8,128)(2,1)} %pad_maximum_fusion.6.w_ref), custom_call_target="tpu_custom_call" | custom-call | bytes 200000000 | tf_op jit(solution)/shard_map/gather_both/pallas_call | solution.py:427
  101.5 2.3 copy-done.6
  103.8 3.9 fusion.26
  108.8 2.7 fusion.10
  113.2 2.4 copy.94
  116.9 2.9 fusion.31
  119.8 3.1 subtract_convert_fusion.3
  122.9 8.7 %fusion.44 = (f32[2,1024]{1,0:T(2,128)S(1)}, f32[2,1024,1024]{1,2,0:T(8,128)}) fusion(pred[1024,1024]{0,1:T(8,128)(4,1)} %fusion.10, bf16[1024,2,64]{2,0,1:T(8,128)(2,1)S(1)} %get-tuple-element.78, bf16[1024,2,64]{2,0,1:T(8,128)(2,1)} %get-tuple-element.79, bf16[1024,2,64]{2,0,1:T(8,128)(2,1)} %get-tuple-element.63, bf16[1024,2,64]{2,0,1:T(8,128)(2,1)} %get-tuple-element.62), kind=kOutput, calls=%fused_computation.120 | convolution fusion | flops 547357696 | bytes 10493952 | tf_op jit(solution)/shard_map/sub | solution.py:1060
  131.6 4.1 fusion.19
  136.8 2.8 constant_dynamic-slice_fusion
  139.7 5.9 all-to-all-start
  149.9 7.6 %all-to-all-done = bf16[8,256,256]{2,1,0:T(8,128)(2,1)S(1)} async-done(((bf16[8,256,256]{2,1,0:T(8,128)(2,1)}), bf16[8,256,256]{2,1,0:T(8,128)(2,1)S(1)}, u32[]{:S(2)}, u32[]{:S(2)}) %all-to-all-start) | async-done | bytes 1048608 | tf_op jit(solution)/shard_map/all_to_all | solution.py:1023
  158.7 114.5 %out_project.1 = (f32[128,2048]{1,0:T(8,128)}, bf16[4,128,2048]{2,1,0:T(8,128)(2,1)}, bf16[4,8,64,2752]{3,2,1,0:T(8,128)(2,1)}) custom-call(bf16[1024,256]{1,0:T(8,128)(2,1)} %copy.91.mixed_ref, bf16[256,2048]{1,0:T(8,128)(2,1)} %bitcast.135, bf16[128,2048]{1,0:T(8,128)(2,1)} %constant_dynamic-slice_fusion.3.x_ref, f32[1,2048]{1,0:T(1,128)} %bitcast.149, ...), custom_call_target="tpu_custom_call" | custom-call | flops 1073741824 | bytes 200000000 | tf_op jit(solution)/shard_map/out_project/pallas_call | solution.py:510
  273.3 15.3 %fusion.45 = f32[512,2752]{0,1:T(8,128)} fusion(bf16[512,2048]{1,0:T(8,128)(2,1)} %bitcast.162, bf16[2048,2752]{1,0:T(8,128)(2,1)} %bitcast.158), kind=kOutput, calls=%fused_computation.121 | convolution fusion | flops 5771362304 | bytes 19005440 | tf_op jit(solution)/shard_map/dot_general | solution.py:24
  290.5 9.4 %multiply_convert_fusion.3 = (bf16[512,1376]{0,1:T(8,128)(2,1)S(1)}, bf16[512,1376]{0,1:T(8,128)(2,1)S(1)}, bf16[512,1376]{0,1:T(8,128)(2,1)S(1)}) fusion(f32[512,2752]{0,1:T(8,128)} %fusion.45, bf16[1376,2048]{1,0:T(8,128)(2,1)} %param.18, bf16[128,2048]{1,0:T(8,128)(2,1)S(1)} %get-tuple-element.73, bf16[128,2048]{1,0:T(8,128)(2,1)S(1)} %get-tuple-element.74, ...), kind=kOutput, calls=%fused_computation.28 | convolution fusion | flops 2904637440 | bytes 17596416 | tf_op jit(solution)/shard_map/dot_general | solution.py:28
  300.0 4.8 convolution_convert_fusion.4
  304.8 4.9 convolution_convert_fusion.1.down_ref
  309.8 7.4 %convolution_convert_fusion.3 = bf16[512,2048]{1,0:T(8,128)(2,1)} fusion(bf16[2048,2752]{1,0:T(8,128)(2,1)S(1)} %bitcast.161, bf16[512,1376]{0,1:T(8,128)(2,1)S(1)} %get-tuple-element.57, bf16[512,1376]{0,1:T(8,128)(2,1)S(1)} %get-tuple-element.56), kind=kOutput, calls=%fused_computation.23 | convolution fusion | flops 5778046976 | bytes 16187392 | tf_op jit(solution)/shard_map/dot_general | solution.py:28
  317.2 10.8 %convolution_convert_fusion = bf16[2048,2752]{0,1:T(8,128)(2,1)} fusion(bf16[512,2048]{1,0:T(8,128)(2,1)S(1)} %bitcast.163, bf16[512,1376]{0,1:T(8,128)(2,1)S(1)} %get-tuple-element.57, bf16[512,1376]{0,1:T(8,128)(2,1)S(1)} %get-tuple-element.56), kind=kOutput, calls=%fused_computation.1 | convolution fusion | flops 5782634496 | bytes 16187392 | tf_op jit(solution)/shard_map/dot_general | solution.py:32
  328.0 15.9 %copy.67 = bf16[2048,2752]{1,0:T(8,128)(2,1)} copy(bf16[2048,2752]{0,1:T(8,128)(2,1)} %convolution_convert_fusion) | data formatting | bytes 22544384 | tf_op jit(solution)/shard_map/convert_element_type | solution.py:1092
  343.9 105.7 %turn.1 = (bf16[8,128,2048]{2,1,0:T(8,128)(2,1)}, f32[1,2048]{1,0:T(1,128)}, bf16[128,2048]{1,0:T(8,128)(2,1)}, bf16[4,64,2752]{2,1,0:T(8,128)(2,1)}, bf16[1376,256]{1,0:T(8,128)(2,1)}) custom-call(bf16[4,128,2048]{2,1,0:T(8,128)(2,1)} %bitcast.131, bf16[4,128,2048]{2,1,0:T(8,128)(2,1)} %bitcast.130, f32[128,2048]{1,0:T(8,128)} %get-tuple-element.33.hidden_ref, ...), custom_call_target="tpu_custom_call" | custom-call | bytes 200000000 | tf_op jit(solution)/shard_map/turn/pallas_call | solution.py:655
  449.7 3.6 convolution_convert_fusion.6
  454.6 5.8 fusion.22
  462.1 2.5 multiply_convert_fusion
  469.8 4.6 all-to-all-start.1
  474.5 2.0 copy.92
  483.5 5.5 convolution_convert_fusion.2
  489.0 67.9 %last_exchange.1 = (bf16[128,2048]{1,0:T(8,128)(2,1)}, f32[1,2048]{1,0:T(1,128)}, bf16[64,11008]{1,0:T(8,128)(2,1)}, bf16[512,256]{1,0:T(8,128)(2,1)}, f32[1376,2048]{1,0:T(8,128)}) custom-call(bf16[1024,768]{1,0:T(8,128)(2,1)} %dynamic-slice_dynamic-update-slice_fusion.8.grads_ref, bf16[2048,768]{1,0:T(8,128)(2,1)} %bitcast.125, ...), custom_call_target="tpu_custom_call" | custom-call | flops 3221225472 | bytes 250000000 | tf_op jit(solution)/shard_map/last_exchange/pallas_call | solution.py:790
  558.3 108.7 %final_gather.1 = (f32[512,11008]{1,0:T(8,128)}, f32[512,6144]{1,0:T(8,128)}, f32[512,2048]{1,0:T(8,128)}, f32[2,2048]{1,0:T(2,128)}) custom-call(bf16[4,512,768]{2,1,0:T(8,128)(2,1)} %bitcast.124, bf16[64,11008]{1,0:T(8,128)(2,1)} %get-tuple-element.39.rows_ref, bf16[512,256]{1,0:T(8,128)(2,1)} %get-tuple-element.40.out_ref, ...), custom_call_target="tpu_custom_call" | custom-call | bytes 300000000 | tf_op jit(solution)/shard_map/final_gather/pallas_call | solution.py:949
  670.0 11.0 %copy.127 = f32[512,6144]{1,0:T(8,128)} copy(f32[512,6144]{1,0:T(8,128)} %get-tuple-element.125) | data formatting | bytes 25165824
  683.1 15.8 %copy.129 = f32[512,11008]{1,0:T(8,128)} copy(f32[512,11008]{1,0:T(8,128)} %get-tuple-element.128) | data formatting | bytes 45088768
  698.8 10.5 %copy.130 = f32[1376,2048]{1,0:T(8,128)} copy(f32[1376,2048]{1,0:T(8,128)} %get-tuple-element.129) | data formatting | bytes 22544384
  (129 shorter events, 45.9 us)
Async XLA Ops:
  7.2 76.4 %copy-start.20 = (s32[1,8]{1,0:T(1,128)S(1)}, s32[1,8]{1,0:T(1,128)}, u32[]{:S(2)}) copy-start(s32[1,8]{1,0:T(1,128)} %param.12) | copy-start | bytes 100
  7.2 82.3 %copy-start.23 = (s32[1,2]{1,0:T(1,128)S(1)}, s32[1,2]{1,0:T(1,128)}, u32[]{:S(2)}) copy-start(s32[1,2]{1,0:T(1,128)} %param.11) | copy-start | bytes 28
  7.2 132.5 %all-gather.4.cloned.1.call-start = ((), (), s32[]{:S(2)}) async-start(), calls=%async_computation.2 | async-start | bytes 1310720 | tf_op jit(solution)/shard_map/all_gather | solution.py:56
  9.5 279.1 %all-gather.6.cloned.1.call-start = ((), (), s32[]{:S(2)}) async-start(), calls=%async_computation.3 | async-start | bytes 2621440 | tf_op jit(solution)/shard_map/all_gather | solution.py:1074
  95.7 4.7 copy-start.2
  100.4 3.4 copy-start.6
  100.4 3.4 copy-start.22
  100.6 7.1 copy-start.3
  122.9 8.7 %copy-start.13 = (bf16[1024,256]{0,1:T(8,128)(2,1)S(1)}, bf16[1024,256]{0,1:T(8,128)(2,1)}, u32[]{:S(2)}) copy-start(bf16[1024,256]{0,1:T(8,128)(2,1)} %slice.199) | copy-start | bytes 1572868
  139.7 17.8 %all-to-all-start = ((bf16[8,256,256]{2,1,0:T(8,128)(2,1)}), bf16[8,256,256]{2,1,0:T(8,128)(2,1)S(1)}, u32[]{:S(2)}, u32[]{:S(2)}) async-start(bf16[8,256,256]{2,1,0:T(8,128)(2,1)} %bitcast.134), calls=%async_computation | async-start | bytes 2097152 | tf_op jit(solution)/shard_map/all_to_all | solution.py:1023
  288.6 11.3 %slice-start.2 = ((s8[5636096]{0:T(1024)(128)(4,1)}), s8[4194304]{0:T(1024)(128)(4,1)S(1)}, s32[]{:S(2)}) async-start(s8[5636096]{0:T(1024)(128)(4,1)} %bitcast.156), calls=%async_computation.6 | async-start | bytes 8388608
  290.5 9.4 %slice-start.3 = ((s8[5636096]{0:T(1024)(128)(4,1)}), s8[1441792]{0:T(1024)(128)(4,1)S(1)}, s32[]{:S(2)}) async-start(s8[5636096]{0:T(1024)(128)(4,1)} %bitcast.156), calls=%async_computation.7 | async-start | bytes 2883584
  300.0 9.8 %slice-start.4 = ((s8[11534336]{0:T(1024)(128)(4,1)}), s8[4194304]{0:T(1024)(128)(4,1)S(1)}, s32[]{:S(2)}) async-start(s8[11534336]{0:T(1024)(128)(4,1)} %bitcast.159), calls=%async_computation.8 | async-start | bytes 8388608
  300.0 9.8 %slice-start.5 = ((s8[11534336]{0:T(1024)(128)(4,1)}), s8[4194304]{0:T(1024)(128)(4,1)S(1)}, s32[]{:S(2)}) async-start(s8[11534336]{0:T(1024)(128)(4,1)} %bitcast.159), calls=%async_computation.9 | async-start | bytes 8388608
  304.8 4.9 slice-start.6
  309.7 7.5 %copy-start.24 = (bf16[4,128,2048]{2,1,0:T(8,128)(2,1)S(1)}, bf16[4,128,2048]{2,1,0:T(8,128)(2,1)}, u32[]{:S(2)}) copy-start(bf16[4,128,2048]{2,1,0:T(8,128)(2,1)} %get-tuple-element.31) | copy-start | bytes 6291460
  343.9 105.7 %copy-start.12 = (bf16[8,32,8,256]{3,2,0,1:T(8,128)(2,1)S(1)}, bf16[8,32,8,256]{3,2,0,1:T(8,128)(2,1)}, u32[]{:S(2)}) copy-start(bf16[8,32,8,256]{3,2,0,1:T(8,128)(2,1)} %copy.98) | copy-start | bytes 3145732
  449.6 3.7 copy-start.16
  449.6 3.7 copy-start.19
  453.3 7.2 %slice-start = ((s8[8388608]{0:T(1024)(128)(4,1)}), s8[4194304]{0:T(1024)(128)(4,1)S(1)}, s32[]{:S(2)}) async-start(s8[8388608]{0:T(1024)(128)(4,1)} %bitcast.118), calls=%async_computation.4 | async-start | bytes 8388608
  454.6 5.9 slice-start.1
  454.6 5.9 copy-start.14
  462.1 2.5 copy-start.8
  462.1 2.5 copy-start.9
  468.0 8.6 %copy-start.10 = (f32[1024,64]{1,0:T(8,128)S(1)}, f32[1024,64]{1,0:T(8,128)}, u32[]{:S(2)}) copy-start(f32[1024,64]{1,0:T(8,128)} %get-tuple-element.86) | copy-start | bytes 786436
  469.8 19.2 %all-to-all-start.1 = ((bf16[256,8,256]{2,0,1:T(8,128)(2,1)}), bf16[256,8,256]{2,0,1:T(8,128)(2,1)}, u32[]{:S(2)}, u32[]{:S(2)}) async-start(bf16[256,8,256]{2,0,1:T(8,128)(2,1)} %bitcast.120), calls=%async_computation.1 | async-start | bytes 2097152 | tf_op jit(solution)/shard_map/all_to_all | solution.py:1100
  477.6 5.9 copy-start.4
  489.0 67.9 %copy-start.21 = (f32[1,2048]{1,0:T(1,128)S(1)}, f32[1,2048]{1,0:T(1,128)}, u32[]{:S(2)}) copy-start(f32[1,2048]{1,0:T(1,128)} %get-tuple-element.42) | copy-start | bytes 24580
  556.9 111.5 %copy-start.17 = (bf16[128,2048]{1,0:T(8,128)(2,1)S(1)}, bf16[128,2048]{1,0:T(8,128)(2,1)}, u32[]{:S(2)}) copy-start(bf16[128,2048]{1,0:T(8,128)(2,1)} %get-tuple-element.34) | copy-start | bytes 1572868
  556.9 112.3 %copy-start.18 = (bf16[128,2048]{1,0:T(8,128)(2,1)S(1)}, bf16[128,2048]{1,0:T(8,128)(2,1)}, u32[]{:S(2)}) copy-start(bf16[128,2048]{1,0:T(8,128)(2,1)} %get-tuple-element.38) | copy-start | bytes 1572868
  670.0 11.0 %copy-start.5 = (f32[512,2048]{1,0:T(8,128)S(1)}, f32[512,2048]{1,0:T(8,128)}, u32[]{:S(2)}) copy-start(f32[512,2048]{1,0:T(8,128)} %get-tuple-element.126) | copy-start | bytes 12582916
  698.8 10.5 %copy-start.1 = (bf16[512,2048]{1,0:T(8,128)(2,1)S(1)}, bf16[512,2048]{1,0:T(8,128)(2,1)}, u32[]{:S(2)}) copy-start(bf16[512,2048]{1,0:T(8,128)(2,1)} %param.15) | copy-start | bytes 6291460
  (4 other events, 5.3 us)
Sparse Core Ops, SparseCore 0:
  9.7 45.4 all-gather.3
  83.6 44.0 all-gather.5

commit v4 on v3

v4 whole, which is shorter than its diff:
```python
import functools
import math
import types

import jax
import jax.numpy as jnp
from jax import lax
from jax.experimental import pallas as pl
from jax.experimental.pallas import tpu as pltpu
from jax.sharding import PartitionSpec as P

HEADS = 16
HEAD = 128
WINDOW = 2048
BLOCK = 128

EPSILON = 1e-06
BF = jnp.bfloat16
F32 = jnp.float32
VMEM_LIMIT = 60 * 1024 * 1024
ATTEND_ROWS = 256
CHUNK = 256


def dot_left_t(left, right):
    return lax.dot_general(left, right, (((0,), (0,)), ((), ())), preferred_element_type=F32)


def rotary_tables(seq_pos):
    half_width = HEAD // 2
    inverse_freq = jnp.power(10000.0, -2.0 * jnp.arange(half_width, dtype=F32) / HEAD)
    angles = seq_pos.astype(F32)[:, None] * inverse_freq[None, :]
    cosine, sine = jnp.cos(angles), jnp.sin(angles)
    return (
        jnp.concatenate([cosine, cosine], axis=-1),
        jnp.concatenate([-sine, sine], axis=-1),
    )


def gather_rows(values, axis):
    return lax.all_gather(values, axis, axis=0, tiled=True)


def take(values, index):
    return lax.dynamic_index_in_dim(values, index, 0, keepdims=False)


MESH = pl.DeviceIdType.MESH


def greet(ctx_peers, wa_peers):
    barrier = pltpu.get_barrier_semaphore()
    for peer in ctx_peers:
        pl.semaphore_signal(barrier, inc=1, device_id={"ctx": peer}, device_id_type=MESH)
    for peer in wa_peers:
        pl.semaphore_signal(barrier, inc=1, device_id={"wa": peer}, device_id_type=MESH)
    pl.semaphore_wait(barrier, len(ctx_peers) + len(wa_peers))


def send(source, target, send_sem, recv_sem, **peer):
    copy = pltpu.make_async_remote_copy(
        src_ref=source,
        dst_ref=target,
        send_sem=send_sem,
        recv_sem=recv_sem,
        device_id=peer,
        device_id_type=MESH,
    )
    copy.start()
    return copy


def place_of(ctx_size, wa_size):
    chips = ctx_size // 2
    p = types.SimpleNamespace(ctx_size=ctx_size, wa_size=wa_size, chips=chips)
    p.ctx, p.wa = lax.axis_index("ctx"), lax.axis_index("wa")
    p.core, p.chip = lax.rem(p.ctx, 2), lax.div(p.ctx, 2)
    p.beside = p.chip * 2 + 1 - p.core
    p.ahead = [lax.rem(p.chip + m, chips) * 2 + p.core for m in range(chips)]
    p.behind = [lax.rem(p.chip + chips - m, chips) * 2 + p.core for m in range(chips)]
    p.up = [lax.rem(p.wa + s, wa_size) for s in range(wa_size)]
    p.down = [lax.rem(p.wa + wa_size - s, wa_size) for s in range(wa_size)]
    p.square = chips == 4
    if p.square:
        p.near = [p.chip + 1 - 2 * lax.rem(p.chip, 2), lax.rem(p.chip + 2, 4)]
        p.far = 3 - p.chip
    return p


def on_core(p, chip):
    return chip * 2 + p.core


def off_core(p, chip):
    return chip * 2 + 1 - p.core


def plane_sems(ctx_size):
    count = max(ctx_size // 2, 5)
    return [pltpu.SemaphoreType.DMA((count,))] * 4


class Spread:
    def __init__(self, p, own, slot, half, sems):
        self.p, self.own, self.slot, self.half = p, own, slot, half
        self.chip_send, self.chip_recv, self.side_send, self.side_recv = sems
        self.chip, self.side = [], []

    def across(self, source, target, chip):
        i = len(self.chip)
        self.chip.append(
            send(source, target, self.chip_send.at[i], self.chip_recv.at[i], ctx=on_core(self.p, chip))
        )

    def aside(self, source, target):
        i = len(self.side)
        self.side.append(
            send(source, target, self.side_send.at[i], self.side_recv.at[i], ctx=self.p.beside)
        )

    def start(self):
        p = self.p
        target = self.slot(p.ctx)
        if p.square:
            for chip in p.near:
                self.across(self.own, target, chip)
        else:
            for m in range(1, p.chips):
                self.across(self.own, target, lax.rem(p.chip + m, p.chips))
        self.aside(self.own, target)

    def arrivals(self):
        p = self.p
        if not p.square:
            for m in range(1, p.chips):
                self.chip[m - 1].wait_recv()
                block = self.slot(p.behind[m])
                self.aside(block, block)
                yield p.behind[m]
            self.side[0].wait_recv()
            yield p.beside
            for m in range(1, p.chips):
                self.side[m].wait_recv()
                yield off_core(p, lax.rem(p.chip + p.chips - m, p.chips))
            return
        for i in range(2):
            self.chip[i].wait_recv()
            device = on_core(p, p.near[i])
            part = self.half(device, i)
            self.across(part, part, p.near[1 - i])
            self.aside(self.slot(device), self.slot(device))
            yield device
        self.side[0].wait_recv()
        yield p.beside
        for i in range(2):
            self.side[1 + i].wait_recv()
            yield off_core(p, p.near[i])
        device = on_core(p, p.far)
        for i in range(2):
            self.chip[2 + i].wait_recv()
            part = self.half(device, i)
            self.aside(part, part)
        yield device
        for i in range(2):
            self.side[3 + i].wait_recv()
        yield off_core(p, p.far)

    def finish(self):
        for copy in self.chip + self.side:
            copy.wait_send()


class Fold:
    def __init__(self, p, both, got, near, sent, piece, half, add, sems):
        self.p, self.both, self.got, self.near, self.sent = p, both, got, near, sent
        self.kept = both.at[p.core]
        self.piece, self.half, self.add = piece, half, add
        self.chip_send, self.chip_recv, self.side_send, self.side_recv = sems
        self.chip, self.side = [], []
        if p.square:
            self.order = [p.far] + p.near + [p.chip]
        else:
            self.order = [lax.rem(p.chip + m, p.chips) for m in range(1, p.chips)] + [p.chip]

    def across(self, source, target, chip):
        i = len(self.chip)
        self.chip.append(
            send(source, target, self.chip_send.at[i], self.chip_recv.at[i], ctx=on_core(self.p, chip))
        )

    def start(self, i):
        p = self.p
        chip = self.order[i]
        self.side.append(
            send(
                self.piece(self.both.at[1 - p.core], chip),
                self.piece(self.got, chip),
                self.side_send.at[i],
                self.side_recv.at[i],
                ctx=p.beside,
            )
        )

    def between(self, i):
        p = self.p
        chip = self.order[i]
        self.side[i].wait_recv()
        self.add(self.piece(self.kept, chip), self.piece(self.got, chip))
        if i == p.chips - 1:
            return
        if not p.square:
            self.across(self.piece(self.kept, chip), self.sent.at[i], chip)
        elif i == 0:
            for j in range(2):
                self.across(self.half(self.kept, chip, j), self.near.at[j], p.near[j])
        else:
            j = i - 1
            self.across(self.half(self.kept, chip, j), self.half(self.sent.at[j], None, j), chip)

    def onward(self):
        p = self.p
        if not p.square:
            return
        for i in range(2):
            self.chip[i].wait_recv()
            part = self.half(self.kept, p.near[1 - i], i)
            self.add(part, self.near.at[i])
            self.across(part, self.half(self.sent.at[1 - i], None, i), p.near[1 - i])

    def total(self):
        p = self.p
        for copy in self.chip[2:] if p.square else self.chip:
            copy.wait_recv()
        mine = self.piece(self.kept, p.chip)
        for i in range(2 if p.square else p.chips - 1):
            self.add(mine, self.sent.at[i])
        return mine

    def finish(self):
        for copy in self.side + self.chip:
            copy.wait_send()


def add_rows(into, other, step):
    def one(i, carried):
        place = pl.ds(pl.multiple_of(i * step, step), step)
        into[place, :] = (into[place, :].astype(F32) + other[place, :].astype(F32)).astype(BF)
        return carried

    lax.fori_loop(0, into.shape[0] // step, one, 0)


def add_blocks(into, other):
    lead = into.shape[:-2]

    def one(i, carried):
        at = (i,) if len(lead) == 1 else (i // lead[1], i % lead[1])
        into[at] = (into[at].astype(F32) + other[at].astype(F32)).astype(BF)
        return carried

    lax.fori_loop(0, math.prod(lead), one, 0)


class Scatter:
    def __init__(self, p, part_of, refs):
        self.p, self.part_of, self.refs = p, part_of, refs

    def start(self):
        p = self.p
        side_out, side_in, chip_out, chip_in, side_send, side_recv, chip_send, chip_recv = self.refs
        self.side, self.out = [], []
        order = list(range(1, p.chips)) + [0]
        for m in order:
            side_out[m] = self.part_of(lax.div(p.ahead[m], 2) * 2 + 1 - p.core).astype(BF)
            self.side.append(
                send(side_out.at[m], side_in.at[m], side_send.at[m], side_recv.at[m], ctx=p.beside)
            )
        for i, m in enumerate(order):
            mine = self.part_of(p.ahead[m])
            self.side[i].wait_recv()
            self.kept = mine + side_in[m].astype(F32)
            if m > 0:
                chip_out[m - 1] = self.kept.astype(BF)
                self.out.append(
                    send(
                        chip_out.at[m - 1],
                        chip_in.at[m - 1],
                        chip_send.at[m - 1],
                        chip_recv.at[m - 1],
                        ctx=p.ahead[m],
                    )
                )

    def total(self):
        chip_in = self.refs[3]
        total = self.kept
        for m in range(1, self.p.chips):
            self.out[m - 1].wait_recv()
            total = total + chip_in[m - 1].astype(F32)
        return total

    def finish(self):
        for copy in self.side + self.out:
            copy.wait_send()


def scatter_scratch(ctx_size, rows, width):
    chips = ctx_size // 2
    return [
        pltpu.VMEM((chips, rows, width), BF),
        pltpu.VMEM((chips, rows, width), BF),
        pltpu.VMEM((chips - 1, rows, width), BF),
        pltpu.VMEM((chips - 1, rows, width), BF),
    ] + [pltpu.SemaphoreType.DMA((chips,))] * 4


def norm_back(x, scale, gain, d_scaled, d_other):
    normed = x * scale
    scaled = d_scaled * gain
    return d_other + scale * (
        scaled - normed * jnp.mean(scaled * normed, axis=-1, keepdims=True)
    )


def gather_kernel(ctx_size, wa_size, cuts, x_ref, w_ref, xs_ref, ws_ref, *sems):
    p = place_of(ctx_size, wa_size)
    ring_send, ring_recv, local = sems[4:]
    greet([p.beside] + p.ahead[1:], [p.up[1], p.down[1]])
    rows = w_ref.shape[0] // cuts
    half_rows = x_ref.shape[0] // 2
    ring = []
    for i in range(cuts):
        part = pl.ds(i * rows, rows)
        ring.append(
            send(
                w_ref.at[part],
                ws_ref.at[p.wa, part],
                ring_send.at[0, i],
                ring_recv.at[0, i],
                wa=p.up[1],
            )
        )
    spread = Spread(
        p,
        x_ref,
        lambda d: xs_ref.at[d],
        lambda d, h: xs_ref.at[d, pl.ds(h * half_rows, half_rows)],
        sems[:4],
    )
    spread.start()
    own_x = pltpu.make_async_copy(x_ref, xs_ref.at[p.ctx], local.at[0])
    own_w = pltpu.make_async_copy(w_ref, ws_ref.at[p.wa], local.at[1])
    own_x.start()
    own_w.start()
    late = []
    for step in range(1, wa_size):
        for i in range(cuts):
            ring[i].wait_recv()
            late.append(ring[i])
            if step < wa_size - 1:
                block = ws_ref.at[p.down[step], pl.ds(i * rows, rows)]
                ring[i] = send(
                    block, block, ring_send.at[step, i], ring_recv.at[step, i], wa=p.up[1]
                )
        if step == 1:
            for _ in spread.arrivals():
                pass
    for copy in late:
        copy.wait_send()
    spread.finish()
    own_x.wait()
    own_w.wait()


def gather_both(x, w, ctx_size, wa_size, cuts=4):
    anywhere = pl.BlockSpec(memory_space=pl.ANY)
    return pl.pallas_call(
        functools.partial(gather_kernel, ctx_size, wa_size, cuts),
        out_shape=(
            jax.ShapeDtypeStruct((ctx_size,) + x.shape, x.dtype),
            jax.ShapeDtypeStruct((wa_size,) + w.shape, w.dtype),
        ),
        in_specs=[anywhere] * 2,
        out_specs=[anywhere] * 2,
        scratch_shapes=plane_sems(ctx_size)
        + [pltpu.SemaphoreType.DMA((wa_size - 1, cuts))] * 2
        + [pltpu.SemaphoreType.DMA((2,))],
        compiler_params=pltpu.CompilerParams(collective_id=0, has_side_effects=True),
        cost_estimate=pl.CostEstimate(flops=0, bytes_accessed=200_000_000, transcendentals=0),
        name="gather_both",
    )(x, w)


def exchange_plane(peers, source, target, send_sem, recv_sem):
    here = target(peers[0])
    return [
        send(source(peer), here, send_sem.at[i], recv_sem.at[i], ctx=peer)
        for i, peer in enumerate(peers)
        if i > 0
    ]


def arrange_kernel(own_blocks, order_ref, first_ref, x_ref, gain_ref, act_ref, own_ref):
    x = x_ref[...]
    wide = x.astype(F32)
    scale = lax.rsqrt(jnp.mean(wide * wide, axis=-1, keepdims=True) + EPSILON)
    act_ref[...] = (wide * scale * gain_ref[...]).astype(BF)
    at = pl.program_id(0) - first_ref[0]

    @pl.when((at >= 0) & (at < own_blocks))
    def _():
        own_ref[...] = x


def arrange(order, first, dealt, gain, own_blocks):
    rows, width = dealt.shape
    block = (BLOCK, width)

    def own_place(i, order_ref, first_ref):
        return (jnp.clip(i - first_ref[0], 0, own_blocks - 1), 0)

    return pl.pallas_call(
        functools.partial(arrange_kernel, own_blocks),
        out_shape=(
            jax.ShapeDtypeStruct((rows, width), BF),
            jax.ShapeDtypeStruct((own_blocks * BLOCK, width), BF),
        ),
        grid_spec=pltpu.PrefetchScalarGridSpec(
            num_scalar_prefetch=2,
            grid=(rows // BLOCK,),
            in_specs=[
                pl.BlockSpec(block, lambda i, order_ref, first_ref: (order_ref[i], 0)),
                pl.BlockSpec((1, width), lambda i, order_ref, first_ref: (0, 0)),
            ],
            out_specs=[
                pl.BlockSpec(block, lambda i, order_ref, first_ref: (i, 0)),
                pl.BlockSpec(block, own_place),
            ],
        ),
        name="arrange",
    )(order, first, dealt, gain)


def attend_kernel(
    ctx_size,
    wa_size,
    heads,
    row_seg_ref,
    column_seg_ref,
    act_ref,
    w_ref,
    cos_ref,
    sin_ref,
    gu_ref,
    cols_ref,
    q_ref,
    k_ref,
    v_ref,
    o_ref,
    prob_ref,
    gw_ref,
    rows_ref,
    gu_send,
    gu_recv,
    local,
    out_send,
    out_recv,
):
    wa, ctx = lax.axis_index("wa"), lax.axis_index("ctx")
    up = [lax.rem(wa + s, wa_size) for s in range(wa_size)]
    peers = [lax.rem(ctx + i, ctx_size) for i in range(ctx_size)]
    greet(peers[1:], up[1:])
    deal_out = exchange_plane(
        peers,
        lambda d: cols_ref.at[d],
        lambda d: rows_ref.at[:, pl.ds(pl.multiple_of(d * cols_ref.shape[2], 128), cols_ref.shape[2])],
        out_send,
        out_recv,
    )
    own_out = pltpu.make_async_copy(
        cols_ref.at[ctx],
        rows_ref.at[:, pl.ds(pl.multiple_of(ctx * cols_ref.shape[2], 128), cols_ref.shape[2])],
        local.at[1],
    )
    own_out.start()
    deal = [
        send(gu_ref.at[up[s]], gw_ref.at[:, wa], gu_send.at[s], gu_recv.at[s], wa=up[s])
        for s in range(1, wa_size)
    ]
    own = pltpu.make_async_copy(gu_ref.at[wa], gw_ref.at[:, wa], local.at[0])
    own.start()
    rows = act_ref.shape[0]
    step = ATTEND_ROWS
    head_cols = heads * HEAD

    def project(i, carried):
        place = pl.ds(pl.multiple_of(i * step, step), step)
        made = jnp.dot(act_ref[place, :], w_ref[...], preferred_element_type=F32)
        cosine, sine = cos_ref[place, :], sin_ref[place, :]
        for head in range(heads):
            columns = slice(head * HEAD, (head + 1) * HEAD)
            for part, target in ((0, q_ref), (1, k_ref)):
                first = part * head_cols + head * HEAD
                u = made[:, first : first + HEAD]
                turned = u * cosine + pltpu.roll(u, HEAD // 2, 1) * sine
                target[place, columns] = turned.astype(BF)
        v_ref[place, :] = made[:, 2 * head_cols :].astype(BF)
        return carried

    lax.fori_loop(0, rows // step, project, 0)
    for i in range(rows // step):
        here = slice(i * step, (i + 1) * step)
        keys = (i + 1) * step
        row = lax.broadcasted_iota(jnp.int32, (step, keys), 0) + i * step
        column = lax.broadcasted_iota(jnp.int32, (step, keys), 1)
        allowed = (column <= row) & (row_seg_ref[here, :] == column_seg_ref[:, :keys])
        if rows > WINDOW:
            allowed = allowed & (row - column < WINDOW)
        for head in range(heads):
            columns = slice(head * HEAD, (head + 1) * HEAD)
            scores = lax.dot_general(
                q_ref[here, columns],
                k_ref[:keys, columns],
                (((1,), (1,)), ((), ())),
                preferred_element_type=F32,
            )
            scores = jnp.where(allowed, scores * (1.0 / math.sqrt(HEAD)), -1e30)
            largest = jnp.max(scores, axis=-1, keepdims=True)
            weights = jnp.exp(scores - largest)
            total = jnp.sum(weights, axis=-1, keepdims=True)
            probs = (weights * (1.0 / total)).astype(BF)
            prob_ref[head, here, :keys] = probs
            o_ref[here, columns] = jnp.dot(
                probs, v_ref[:keys, columns], preferred_element_type=F32
            ).astype(BF)
    own.wait()
    own_out.wait()
    for copy in deal + deal_out:
        copy.wait()


def attend(segments, act, w, cosine, sine, gu, out_cols, ctx_size, wa_size):
    rows, width = act.shape
    head_cols = w.shape[1] // 3
    heads = head_cols // HEAD
    vmem = pl.BlockSpec(memory_space=pltpu.VMEM)
    anywhere = pl.BlockSpec(memory_space=pl.ANY)
    heads_shape = jax.ShapeDtypeStruct((rows, head_cols), BF)
    return pl.pallas_call(
        functools.partial(attend_kernel, ctx_size, wa_size, heads),
        out_shape=(
            heads_shape,
            heads_shape,
            heads_shape,
            heads_shape,
            jax.ShapeDtypeStruct((heads, rows, rows), BF),
            jax.ShapeDtypeStruct((2, wa_size) + gu.shape[2:], BF),
            jax.ShapeDtypeStruct((out_cols.shape[1], width), BF),
        ),
        in_specs=[vmem] * 6 + [anywhere] * 2,
        out_specs=[vmem] * 5 + [anywhere] * 2,
        scratch_shapes=[pltpu.SemaphoreType.DMA((wa_size,))] * 3
        + [pltpu.SemaphoreType.DMA((ctx_size,))] * 2,
        compiler_params=pltpu.CompilerParams(
            collective_id=4, has_side_effects=True, vmem_limit_bytes=VMEM_LIMIT
        ),
        cost_estimate=pl.CostEstimate(
            flops=2 * rows * width * 3 * head_cols, bytes_accessed=100_000_000, transcendentals=0
        ),
        name="attend",
    )(segments[:, None], segments[None, :], act, w, cosine, sine, gu, out_cols)


def attend_back_kernel(
    heads,
    place_ref,
    own_ref,
    dy_ref,
    w_ref,
    o_ref,
    q_ref,
    k_ref,
    v_ref,
    prob_ref,
    cos_ref,
    sin_ref,
    grads_ref,
    dealt_ref,
    d_out_ref,
    dh_ref,
    do_ref,
    dk_ref,
    dv_ref,
):
    rows = dy_ref.shape[0]
    step = ATTEND_ROWS
    head_cols = heads * HEAD
    back_scale = 1.0 / math.sqrt(HEAD)

    def project(i, carried):
        place = pl.ds(pl.multiple_of(i * step, step), step)
        do_ref[place, :] = lax.dot_general(
            dy_ref[place, :],
            w_ref[...],
            (((1,), (1,)), ((), ())),
            preferred_element_type=F32,
        ).astype(BF)
        return carried

    lax.fori_loop(0, rows // step, project, 0)
    dk_ref[...] = jnp.zeros_like(dk_ref)
    dv_ref[...] = jnp.zeros_like(dv_ref)

    def unrotate(u, place):
        return u * cos_ref[place, :] - pltpu.roll(u, HEAD // 2, 1) * sin_ref[place, :]

    for i in range(rows // step):
        here = slice(i * step, (i + 1) * step)
        keys = (i + 1) * step
        for head in range(heads):
            columns = slice(head * HEAD, (head + 1) * HEAD)
            d_o = do_ref[here, columns]
            q = q_ref[here, columns]
            probs = prob_ref[head, here, :keys]
            d_probs = lax.dot_general(
                d_o,
                v_ref[:keys, columns],
                (((1,), (1,)), ((), ())),
                preferred_element_type=F32,
            )
            wide = probs.astype(F32)
            row_dot = jnp.sum(wide * d_probs, axis=-1, keepdims=True)
            d_scores = (wide * (d_probs - row_dot)).astype(BF)
            d_query = jnp.dot(d_scores, k_ref[:keys, columns], preferred_element_type=F32)
            grads_ref[here, columns] = unrotate(d_query * back_scale, here).astype(BF)
            dk_ref[:keys, columns] += lax.dot_general(
                d_scores, q, (((0,), (0,)), ((), ())), preferred_element_type=F32
            )
            dv_ref[:keys, columns] += lax.dot_general(
                probs, d_o, (((0,), (0,)), ((), ())), preferred_element_type=F32
            )
    for i in range(rows // BLOCK):
        here = slice(i * BLOCK, (i + 1) * BLOCK)
        for head in range(heads):
            columns = slice(head * HEAD, (head + 1) * HEAD)
            d_key = unrotate(dk_ref[here, columns] * back_scale, here)
            grads_ref[here, head_cols + head * HEAD : head_cols + (head + 1) * HEAD] = d_key.astype(BF)
        grads_ref[here, 2 * head_cols :] = dv_ref[here, :].astype(BF)
        there = pl.ds(pl.multiple_of(place_ref[i] * BLOCK, BLOCK), BLOCK)
        dealt_ref[there, :] = grads_ref[here, :]
    for j in range(dh_ref.shape[0] // BLOCK):
        at = pl.ds(pl.multiple_of(own_ref[j] * BLOCK, BLOCK), BLOCK)
        dh_ref[j * BLOCK : (j + 1) * BLOCK, :] = dy_ref[at, :]
    d_out_ref[...] = lax.dot_general(
        o_ref[...], dy_ref[...], (((0,), (0,)), ((), ())), preferred_element_type=F32
    ).astype(BF)


def attend_back(place, own, dy, w_rows, o, q, k, v, probs, cosine, sine):
    rows, width = dy.shape
    head_cols = o.shape[1]
    heads = head_cols // HEAD
    vmem = pl.BlockSpec(memory_space=pltpu.VMEM)
    grads_shape = jax.ShapeDtypeStruct((rows, 3 * head_cols), BF)
    return pl.pallas_call(
        functools.partial(attend_back_kernel, heads),
        out_shape=(
            grads_shape,
            grads_shape,
            jax.ShapeDtypeStruct((head_cols, width), BF),
            jax.ShapeDtypeStruct((own.shape[0] * BLOCK, width), BF),
        ),
        in_specs=[pl.BlockSpec(memory_space=pltpu.SMEM)] * 2 + [vmem] * 9,
        out_specs=[vmem] * 4,
        scratch_shapes=[
            pltpu.VMEM((rows, head_cols), BF),
            pltpu.VMEM((rows, head_cols), F32),
            pltpu.VMEM((rows, head_cols), F32),
        ],
        compiler_params=pltpu.CompilerParams(vmem_limit_bytes=VMEM_LIMIT),
        cost_estimate=pl.CostEstimate(
            flops=4 * rows * width * head_cols, bytes_accessed=20_000_000, transcendentals=0
        ),
        name="attend_back",
    )(place, own, dy, w_rows, o, q, k, v, probs, cosine, sine)


def out_kernel(
    ctx_size,
    wa_size,
    mixed_ref,
    w_ref,
    x_ref,
    gain_ref,
    gu_ref,
    hidden_ref,
    acts_ref,
    gw_ref,
    *scratch,
):
    p = place_of(ctx_size, wa_size)
    act_send, act_recv, local = scratch[12:]
    greet([p.beside] + p.ahead[1:], [p.up[1], p.down[1]])
    own = pltpu.make_async_copy(gu_ref, gw_ref.at[:, :, p.ctx], local.at[0])
    own.start()
    spread = Spread(
        p,
        gu_ref,
        lambda d: gw_ref.at[:, :, d],
        lambda d, h: gw_ref.at[h, :, d],
        scratch[8:12],
    )
    rows = x_ref.shape[0]

    def part_of(device):
        block = mixed_ref[pl.ds(pl.multiple_of(device * rows, rows), rows), :]
        return jnp.dot(block, w_ref[...], preferred_element_type=F32)

    scatter = Scatter(p, part_of, scratch[:8])
    scatter.start()
    hidden = x_ref[...].astype(F32) + scatter.total()
    hidden_ref[...] = hidden
    scale = lax.rsqrt(jnp.mean(hidden * hidden, axis=-1, keepdims=True) + EPSILON)
    acts_ref[0] = (hidden * scale * gain_ref[...]).astype(BF)
    half_rows = rows // 2

    def pass_on(s, i):
        place = pl.ds(i * half_rows, half_rows)
        return send(
            acts_ref.at[s, place],
            acts_ref.at[s + 1, place],
            act_send.at[s, i],
            act_recv.at[s, i],
            wa=p.up[1],
        )

    ring = [pass_on(0, 0), pass_on(0, 1)]
    spread.start()
    arrivals = spread.arrivals()
    for s in range(1, wa_size):
        for i in range(2):
            ring[2 * (s - 1) + i].wait_recv()
            if s < wa_size - 1:
                ring.append(pass_on(s, i))
        if s == 2:
            next(arrivals)
            next(arrivals)
    for _ in arrivals:
        pass
    scatter.finish()
    spread.finish()
    own.wait()
    for copy in ring:
        copy.wait_send()


def out_project(mixed, w_rows, x_own, gain, gu, ctx_size, wa_size):
    rows, width = x_own.shape
    vmem = pl.BlockSpec(memory_space=pltpu.VMEM)
    anywhere = pl.BlockSpec(memory_space=pl.ANY)
    return pl.pallas_call(
        functools.partial(out_kernel, ctx_size, wa_size),
        out_shape=(
            jax.ShapeDtypeStruct((rows, width), F32),
            jax.ShapeDtypeStruct((wa_size, rows, width), BF),
            jax.ShapeDtypeStruct((2, wa_size, ctx_size) + gu.shape[2:], BF),
        ),
        in_specs=[vmem] * 4 + [anywhere],
        out_specs=[vmem] * 2 + [anywhere],
        scratch_shapes=scatter_scratch(ctx_size, rows, width)
        + plane_sems(ctx_size)
        + [pltpu.SemaphoreType.DMA((wa_size, 2))] * 2
        + [pltpu.SemaphoreType.DMA((1,))],
        compiler_params=pltpu.CompilerParams(
            collective_id=1, has_side_effects=True, vmem_limit_bytes=VMEM_LIMIT
        ),
        cost_estimate=pl.CostEstimate(
            flops=2 * mixed.size * width, bytes_accessed=200_000_000, transcendentals=0
        ),
        name="out_project",
    )(mixed, w_rows, x_own, gain, gu)


def mlp_kernel(
    act_ref,
    dz_ref,
    gw_any,
    wd_any,
    d_act_ref,
    mlp_ref,
    act_t_ref,
    d_gu_ref,
    inner_t_ref,
    gw_ref,
    wd_ref,
    inner_ref,
    sems,
):
    hidden_rows = wd_any.shape[0]
    hidden = inner_ref.shape[1]
    width = act_ref.shape[1]
    loads = [
        pltpu.make_async_copy(gw_any.at[0], gw_ref.at[0], sems.at[0]),
        pltpu.make_async_copy(gw_any.at[1], gw_ref.at[1], sems.at[1]),
        pltpu.make_async_copy(wd_any, wd_ref.at[pl.ds(0, hidden_rows)], sems.at[2]),
    ]
    for copy in loads:
        copy.start()
    if hidden > hidden_rows:
        wd_ref[hidden_rows:, :] = jnp.zeros((hidden - hidden_rows, width), BF)
    act_t_ref[...] = act_ref[...].T
    for copy in loads:
        copy.wait()
    act = act_ref[...]
    dz = dz_ref[...]

    def part(first, size):
        columns = pl.ds(first, size)
        gate = jnp.dot(act, gw_ref[0, :, columns], preferred_element_type=F32)
        up = jnp.dot(act, gw_ref[1, :, columns], preferred_element_type=F32)
        d_inner = lax.dot_general(
            dz, wd_ref[columns, :], (((1,), (1,)), ((), ())), preferred_element_type=F32
        )
        sigmoid = 1.0 / (1.0 + jnp.exp(-gate))
        silu = gate * sigmoid
        inner = (silu * up).astype(BF)
        inner_ref[:, columns] = inner
        d_gate = (d_inner * up * sigmoid * (1.0 + gate * (1.0 - sigmoid))).astype(BF)
        d_up = (d_inner * silu).astype(BF)
        d_gu_ref[0, :, columns] = d_gate
        d_gu_ref[1, :, columns] = d_up
        inner_t_ref[columns, :] = inner.T

    whole = hidden // CHUNK

    def one(i, carried):
        part(pl.multiple_of(i * CHUNK, CHUNK), CHUNK)
        return carried

    lax.fori_loop(0, whole, one, 0)
    if hidden > whole * CHUNK:
        part(whole * CHUNK, hidden - whole * CHUNK)

    def two(i, carried):
        place = pl.ds(pl.multiple_of(i * CHUNK, CHUNK), CHUNK)
        back = lax.dot_general(
            d_gu_ref[0], gw_ref[0, place, :], (((1,), (1,)), ((), ())), preferred_element_type=F32
        )
        back = back + lax.dot_general(
            d_gu_ref[1], gw_ref[1, place, :], (((1,), (1,)), ((), ())), preferred_element_type=F32
        )
        d_act_ref[:, place] = back.astype(BF)
        mlp_ref[:, place] = jnp.dot(
            inner_ref[...], wd_ref[:, place], preferred_element_type=F32
        ).astype(BF)
        return carried

    lax.fori_loop(0, width // CHUNK, two, 0)


def mlp(act, dz, gw, wd):
    tokens, width = act.shape
    hidden = gw.shape[2]
    vmem = pl.BlockSpec(memory_space=pltpu.VMEM)
    anywhere = pl.BlockSpec(memory_space=pl.ANY)
    return pl.pallas_call(
        mlp_kernel,
        out_shape=(
            jax.ShapeDtypeStruct((tokens, width), BF),
            jax.ShapeDtypeStruct((tokens, width), BF),
            jax.ShapeDtypeStruct((width, tokens), BF),
            jax.ShapeDtypeStruct((2, tokens, hidden), BF),
            jax.ShapeDtypeStruct((hidden, tokens), BF),
        ),
        in_specs=[vmem, vmem, anywhere, anywhere],
        out_specs=[vmem] * 5,
        scratch_shapes=[
            pltpu.VMEM(gw.shape, BF),
            pltpu.VMEM((hidden, width), BF),
            pltpu.VMEM((tokens, hidden), BF),
            pltpu.SemaphoreType.DMA((3,)),
        ],
        compiler_params=pltpu.CompilerParams(vmem_limit_bytes=60 * 1024 * 1024),
        cost_estimate=pl.CostEstimate(
            flops=12 * tokens * width * hidden, bytes_accessed=50_000_000, transcendentals=0
        ),
        name="mlp",
    )(act, dz, gw, wd)


def turn_kernel(
    ctx_size,
    wa_size,
    parts_ref,
    mlp_ref,
    hidden_ref,
    gain_ref,
    dz_ref,
    act_t_ref,
    d_gu_ref,
    inner_t_ref,
    dz_all_ref,
    all_ref,
    gain_out_ref,
    out_ref,
    gu_out_ref,
    down_out_ref,
    *scratch,
):
    p = place_of(ctx_size, wa_size)
    got_ref, more_ref, wa_send, wa_recv, more_send, more_recv = scratch[:6]
    gu_both, gu_got, gu_near, gu_sent, down_both, down_got, down_near, down_sent = scratch[6:14]
    gu_sems, down_sems, spread_sems = scratch[14:18], scratch[18:22], scratch[22:26]
    own_parts, own_mlp, local = scratch[26:29]
    greet([p.beside] + p.ahead[1:], p.down[1:])
    copies = [
        send(parts_ref.at[s], got_ref.at[s], wa_send.at[s], wa_recv.at[s], wa=p.down[s])
        for s in range(1, wa_size)
    ]
    loads = [
        pltpu.make_async_copy(parts_ref.at[0], own_parts, local.at[0]),
        pltpu.make_async_copy(mlp_ref.at[0], own_mlp, local.at[1]),
    ]
    for copy in loads:
        copy.start()
    down_total = down_both.shape[1]
    down_rows = down_total // 2
    columns = dz_all_ref.shape[1] // ctx_size
    half = gu_both.shape[1] // 2
    piece_rows = gu_both.shape[3]
    wa_rows = act_t_ref.shape[0] // wa_size

    def down_piece(ref, chip):
        return ref.at[:, pl.ds(pl.multiple_of(chip * columns, columns), columns)]

    def down_half(ref, chip, h):
        place = pl.ds(h * down_rows, down_rows)
        if chip is None:
            return ref.at[place]
        return ref.at[place, pl.ds(pl.multiple_of(chip * columns, columns), columns)]

    down = Fold(
        p,
        down_both,
        down_got,
        down_near,
        down_sent,
        down_piece,
        down_half,
        lambda into, other: add_rows(into, other, 16),
        down_sems,
    )

    def gu_half(ref, chip, h):
        place = pl.ds(h * half, half)
        return ref.at[place] if chip is None else ref.at[place, chip]

    gu = Fold(
        p,
        gu_both,
        gu_got,
        gu_near,
        gu_sent,
        lambda ref, chip: ref.at[:, chip],
        gu_half,
        add_blocks,
        gu_sems,
    )

    def make(chip):
        first = chip * (2 * piece_rows)
        left = jnp.concatenate(
            [
                act_t_ref[pl.ds(pl.multiple_of(i * wa_rows + first, 2 * piece_rows), 2 * piece_rows), :]
                for i in range(wa_size)
            ],
            axis=0,
        )

        def gu_part(part, carried):
            made = jnp.dot(left, d_gu_ref[part], preferred_element_type=F32).astype(BF)
            for i in range(wa_size):
                for core in range(2):
                    at = (2 * i + core) * piece_rows
                    gu_both[core, part * wa_size + i, chip] = made[at : at + piece_rows]
            return carried

        lax.fori_loop(0, 2, gu_part, 0)

        def down_part(core, carried):
            place = pl.multiple_of((core * p.chips + chip) * columns, columns)
            made = jnp.dot(
                inner_t_ref[...], dz_all_ref[:, pl.ds(place, columns)], preferred_element_type=F32
            ).astype(BF)
            target = pl.ds(pl.multiple_of(chip * columns, columns), columns)
            down_both[core, :, target] = made[:down_total]
            return carried

        lax.fori_loop(0, 2, down_part, 0)

    for i in range(p.chips):
        make(gu.order[i])
        gu.start(i)
        down.start(i)
        if i > 0:
            gu.between(i - 1)
            down.between(i - 1)
    gu.between(p.chips - 1)
    down.between(p.chips - 1)
    hidden = hidden_ref[...]
    scale = lax.rsqrt(jnp.mean(hidden * hidden, axis=-1, keepdims=True) + EPSILON)
    down.onward()
    for copy in loads:
        copy.wait()
    d_normed = own_parts[...].astype(F32)
    for s in range(1, wa_size):
        copies[s - 1].wait_recv()
        d_normed = d_normed + got_ref[s].astype(F32)
    more = [
        send(mlp_ref.at[s], more_ref.at[s], more_send.at[s], more_recv.at[s], wa=p.down[s])
        for s in range(1, wa_size)
    ]
    gain_out_ref[...] = jnp.sum(d_normed * (hidden * scale), axis=0, keepdims=True)
    d_hidden = norm_back(hidden, scale, gain_ref[...], d_normed, dz_ref[...].astype(F32))
    all_ref[p.ctx] = d_hidden.astype(BF)
    half_rows = all_ref.shape[1] // 2
    spread = Spread(
        p,
        all_ref.at[p.ctx],
        lambda d: all_ref.at[d],
        lambda d, h: all_ref.at[d, pl.ds(h * half_rows, half_rows)],
        spread_sems,
    )
    spread.start()
    gu.onward()
    down_out_ref[...] = down.total()[...]
    for _ in spread.arrivals():
        pass
    gu_out_ref[...] = gu.total()[...]
    result = hidden + own_mlp[...].astype(F32)
    for s in range(1, wa_size):
        more[s - 1].wait_recv()
        result = result + more_ref[s].astype(F32)
    out_ref[...] = result.astype(BF)
    for copy in copies + more:
        copy.wait_send()
    down.finish()
    gu.finish()
    spread.finish()


def turn(
    parts, mlp, hidden, gain, dz, act_t, d_gu, inner_t, dz_all, hidden_rows, ctx_size, wa_size
):
    rows, width = hidden.shape
    chips = ctx_size // 2
    columns = width // ctx_size
    lead = 2 * wa_size
    gu_rows, gu_columns = width // (ctx_size * wa_size), d_gu.shape[2]
    vmem = pl.BlockSpec(memory_space=pltpu.VMEM)
    anywhere = pl.BlockSpec(memory_space=pl.ANY)
    many = 2 if chips == 4 else chips - 1
    return pl.pallas_call(
        functools.partial(turn_kernel, ctx_size, wa_size),
        out_shape=(
            jax.ShapeDtypeStruct((ctx_size, rows, width), BF),
            jax.ShapeDtypeStruct((1, width), F32),
            jax.ShapeDtypeStruct((rows, width), BF),
            jax.ShapeDtypeStruct((lead, gu_rows, gu_columns), BF),
            jax.ShapeDtypeStruct((hidden_rows, columns), BF),
        ),
        in_specs=[anywhere] * 2 + [vmem] * 7,
        out_specs=[vmem] * 5,
        scratch_shapes=[pltpu.VMEM((wa_size, rows, width), BF)] * 2
        + [pltpu.SemaphoreType.DMA((wa_size,))] * 4
        + [
            pltpu.VMEM((2, lead, chips, gu_rows, gu_columns), BF),
            pltpu.VMEM((lead, chips, gu_rows, gu_columns), BF),
            pltpu.VMEM((2, lead // 2, gu_rows, gu_columns), BF),
            pltpu.VMEM((many, lead, gu_rows, gu_columns), BF),
            pltpu.VMEM((2, hidden_rows, columns * chips), BF),
            pltpu.VMEM((hidden_rows, columns * chips), BF),
            pltpu.VMEM((2, hidden_rows // 2, columns), BF),
            pltpu.VMEM((many, hidden_rows, columns), BF),
        ]
        + [pltpu.SemaphoreType.DMA((max(chips, 6),))] * 8
        + plane_sems(ctx_size)
        + [pltpu.VMEM((rows, width), BF)] * 2
        + [pltpu.SemaphoreType.DMA((2,))],
        compiler_params=pltpu.CompilerParams(
            collective_id=2, has_side_effects=True, vmem_limit_bytes=VMEM_LIMIT
        ),
        cost_estimate=pl.CostEstimate(flops=0, bytes_accessed=200_000_000, transcendentals=0),
        name="turn",
    )(parts, mlp, hidden, gain, dz, act_t, d_gu, inner_t, dz_all)


def close_kernel(
    ctx_size,
    wa_size,
    grads_ref,
    w_ref,
    x_ref,
    gain_ref,
    dh_ref,
    gu_ref,
    dw_ref,
    do_ref,
    down_ref,
    gains_ref,
    out_ref,
    gus_ref,
    downs_ref,
    qkvs_ref,
    outs_ref,
    sums_ref,
    *scratch,
):
    p = place_of(ctx_size, wa_size)
    gu_in, rows_ref, dw_in, share_ref, do_in, out_share_ref = scratch[8:14]
    do_parts, part_send, part_recv = scratch[43:46]
    wa_gains, ctx_gains, local = scratch[14:17]
    gu_sems, dw_sems, do_sems = scratch[17:19], scratch[19:21], scratch[21:23]
    wa_sems, ctx_sems = scratch[23:25], scratch[25:27]
    down_plane, gu_plane, qkv_plane, out_plane = (scratch[i : i + 4] for i in (27, 31, 35, 39))
    peers = [lax.rem(p.ctx + i, ctx_size) for i in range(1, ctx_size)]
    greet(peers, p.up[1:])
    locals_ = []

    def keep(source, target):
        copy = pltpu.make_async_copy(source, target, local.at[len(locals_)])
        copy.start()
        locals_.append(copy)

    def spread_of(own, slots, sems):
        half = slots.shape[1] // 2
        keep(own, slots.at[p.ctx])
        spread = Spread(
            p,
            own,
            lambda d: slots.at[d],
            lambda d, h: slots.at[d, pl.ds(h * half, half)],
            sems,
        )
        spread.start()
        return spread

    def over_wa(source, target, sems):
        return [
            send(
                source(p.up[s]),
                target.at[s],
                sems[0].at[s],
                sems[1].at[s],
                wa=p.up[s],
            )
            for s in range(1, wa_size)
        ]

    def add_up(source, found, into, step):
        def one(i, carried):
            place = pl.ds(pl.multiple_of(i * step, step), step)
            total = source(p.wa)[place, :].astype(F32)
            for s in range(1, wa_size):
                total = total + found[s, place, :].astype(F32)
            into[place, :] = total.astype(BF)
            return carried

        lax.fori_loop(0, into.shape[0] // step, one, 0)

    deal = [
        send(
            gu_ref.at[:, p.up[s]], gu_in.at[p.wa], gu_sems[0].at[s], gu_sems[1].at[s], wa=p.up[s]
        )
        for s in range(1, wa_size)
    ]
    rows = x_ref.shape[0]

    def part_of(device):
        place = pl.ds(pl.multiple_of(device * rows, rows), rows)
        return lax.dot_general(
            grads_ref[place, :],
            w_ref[...],
            (((1,), (1,)), ((), ())),
            preferred_element_type=F32,
        )

    scatter = Scatter(p, part_of, scratch[:8])
    scatter.start()
    head_cols = do_ref.shape[0]

    def do_part(device):
        columns = pl.ds(pl.multiple_of(device * head_cols, head_cols), head_cols)
        return do_ref.at[:, columns]

    part_copies = exchange_plane(
        [p.ctx] + peers, do_part, lambda d: do_parts.at[d], part_send, part_recv
    )
    keep(do_part(p.ctx), do_parts.at[p.ctx])
    down_spread = spread_of(down_ref, downs_ref, down_plane)
    wa_gains[p.wa] = gains_ref[...]
    small = [
        send(gains_ref, wa_gains.at[p.wa], wa_sems[0].at[s], wa_sems[1].at[s], wa=p.up[s])
        for s in range(1, wa_size)
    ]
    gu_in[p.wa] = gu_ref[:, p.wa]
    for copy in deal:
        copy.wait_recv()
    dw_copies = over_wa(lambda d: dw_ref.at[d], dw_in, dw_sems)
    total_columns = rows_ref.shape[1] // 2
    own_columns = total_columns // wa_size
    for i in range(wa_size):
        for part in range(2):
            first = part * total_columns + i * own_columns
            rows_ref[:, first : first + own_columns] = gu_in[i, part, :, :own_columns]
    gu_spread = spread_of(rows_ref, gus_ref, gu_plane)
    for copy in small:
        copy.wait()
    plane_gain = wa_gains[0]
    for i in range(1, wa_size):
        plane_gain = plane_gain + wa_gains[i]
    ctx_gains[p.ctx] = plane_gain
    own_gain = ctx_gains.at[p.ctx]
    small = [
        send(own_gain, own_gain, ctx_sems[0].at[i], ctx_sems[1].at[i], ctx=peer)
        for i, peer in enumerate(peers)
    ]
    x = x_ref[...].astype(F32)
    scale = lax.rsqrt(jnp.mean(x * x, axis=-1, keepdims=True) + EPSILON)
    d_normed = scatter.total()
    out_ref[...] = norm_back(
        x, scale, gain_ref[...], d_normed, dh_ref[...].astype(F32)
    ).astype(BF)
    for _ in down_spread.arrivals():
        pass
    for _ in gu_spread.arrivals():
        pass
    for copy in small:
        copy.wait()
    total_gain = ctx_gains[0]
    for i in range(1, ctx_size):
        total_gain = total_gain + ctx_gains[i]
    sums_ref[...] = total_gain
    for copy in dw_copies:
        copy.wait_recv()
    for copy in part_copies:
        copy.wait_recv()
    locals_[0].wait()
    per_wa = ctx_size // wa_size

    def do_block(device):
        return do_parts.at[pl.ds(device * per_wa, per_wa)]

    do_copies = over_wa(do_block, do_in, do_sems)
    add_up(lambda d: dw_ref.at[d], dw_in, share_ref, 16)
    qkv_spread = spread_of(share_ref, qkvs_ref, qkv_plane)
    for copy in do_copies:
        copy.wait_recv()
    for i in range(per_wa):
        place = pl.ds(i * head_cols, head_cols)
        total = do_parts[p.wa * per_wa + i].astype(F32)
        for s in range(1, wa_size):
            total = total + do_in[s, i].astype(F32)
        out_share_ref[place, :] = total.astype(BF)
    out_spread = spread_of(out_share_ref, outs_ref, out_plane)
    for _ in qkv_spread.arrivals():
        pass
    for _ in out_spread.arrivals():
        pass
    scatter.finish()
    for spread in (down_spread, gu_spread, qkv_spread, out_spread):
        spread.finish()
    for copy in deal + dw_copies + do_copies + part_copies:
        copy.wait_send()
    for copy in locals_[1:]:
        copy.wait()


def close(grads, w, x_own, gain, dh, gu, dw, do, down, gains_own, columns, ctx_size, wa_size):
    rows, width = x_own.shape
    vmem = pl.BlockSpec(memory_space=pltpu.VMEM)
    anywhere = pl.BlockSpec(memory_space=pl.ANY)
    gu_shape = (gu.shape[2], columns)
    out_shape = (width // wa_size, do.shape[0])
    shapes = [gu_shape, down.shape, dw.shape[1:], out_shape]
    gains = (2, width)
    return pl.pallas_call(
        functools.partial(close_kernel, ctx_size, wa_size),
        out_shape=(jax.ShapeDtypeStruct((rows, width), BF),)
        + tuple(jax.ShapeDtypeStruct((ctx_size,) + shape, BF) for shape in shapes)
        + (jax.ShapeDtypeStruct(gains, F32),),
        in_specs=[vmem] * 10,
        out_specs=[vmem] + [anywhere] * 4 + [vmem],
        scratch_shapes=scatter_scratch(ctx_size, rows, width)
        + [
            pltpu.VMEM((wa_size, 2) + gu.shape[2:], BF),
            pltpu.VMEM(gu_shape, BF),
            pltpu.VMEM(dw.shape, BF),
            pltpu.VMEM(dw.shape[1:], BF),
            pltpu.VMEM((wa_size, ctx_size // wa_size, do.shape[0], do.shape[0]), BF),
            pltpu.VMEM(out_shape, BF),
            pltpu.VMEM((wa_size,) + gains, F32),
            pltpu.VMEM((ctx_size,) + gains, F32),
            pltpu.SemaphoreType.DMA((5,)),
        ]
        + [pltpu.SemaphoreType.DMA((wa_size,))] * 8
        + [pltpu.SemaphoreType.DMA((ctx_size,))] * 2
        + plane_sems(ctx_size) * 4
        + [pltpu.VMEM((ctx_size, do.shape[0], do.shape[0]), BF)]
        + [pltpu.SemaphoreType.DMA((ctx_size,))] * 2,
        compiler_params=pltpu.CompilerParams(
            collective_id=3, has_side_effects=True, vmem_limit_bytes=VMEM_LIMIT
        ),
        cost_estimate=pl.CostEstimate(
            flops=2 * grads.size * width, bytes_accessed=400_000_000, transcendentals=0
        ),
        name="close",
    )(grads, w, x_own, gain, dh, gu, dw, do, down, gains_own)


def widen(blocks, columns, order, step):
    count, rows, own = blocks.shape
    parts = own // columns

    def body(block_ref, out_ref):
        for i in range(parts):
            for at, device in enumerate(order):
                first = (i * count + at) * columns
                out_ref[:, first : first + columns] = block_ref[
                    device, :, i * columns : (i + 1) * columns
                ].astype(F32)

    return pl.pallas_call(
        body,
        out_shape=jax.ShapeDtypeStruct((rows, count * own), F32),
        grid=(rows // step,),
        in_specs=[pl.BlockSpec((count, step, own), lambda r: (0, r, 0))],
        out_specs=pl.BlockSpec((step, count * own), lambda r: (r, 0)),
        compiler_params=pltpu.CompilerParams(vmem_limit_bytes=VMEM_LIMIT),
        name="widen",
    )(blocks)


def per_device(
    tokens, lengths, dealing, norm1_gain, w_qkv, w_out, norm2_gain, w_gate_up, w_down, grad_out
):
    tok_rows, width = tokens.shape[1], tokens.shape[2]
    ctx_size = lax.axis_size("ctx")
    wa_size = lax.axis_size("wa")
    ctx_index = lax.axis_index("ctx")
    wa_index = lax.axis_index("wa")
    block_order = dealing[0]
    block_total = block_order.shape[0]
    group_rows = block_total * BLOCK
    own_blocks = tok_rows // BLOCK
    first_length = lengths[0, 0]
    heads_own = HEADS // ctx_size
    head_cols = heads_own * HEAD
    wa_rows = width // wa_size
    ff_total = w_gate_up.shape[1] // 2
    ff_own = w_down.shape[0]
    piece_rows = wa_rows // ctx_size

    block_ids = jnp.arange(block_total, dtype=jnp.int32)
    inverse = jnp.sum(
        jnp.where(block_order[None, :] == block_ids[:, None], block_ids[None, :], 0), axis=1
    )

    qkv_slice = jnp.concatenate(
        [
            lax.dynamic_slice_in_dim(w_qkv, part * width + ctx_index * head_cols, head_cols, 1)
            for part in range(3)
        ],
        axis=1,
    )
    dealt, qkv_cols = gather_both(tokens[0], qkv_slice, ctx_size, wa_size)
    dealt = dealt.reshape(group_rows, width)
    qkv_cols = qkv_cols.reshape(width, 3 * head_cols)
    out_slice = lax.dynamic_slice_in_dim(w_out, ctx_index * head_cols, head_cols, 1)
    out_cols = gather_rows(out_slice, "wa")
    out_cols = out_cols.reshape(ctx_size, head_cols, head_cols)
    gu_piece = lax.dynamic_slice_in_dim(w_gate_up, ctx_index * piece_rows, piece_rows, 0)
    hidden_own = -(-ff_own // 128) * 128
    gu_send = jnp.pad(
        jnp.stack(
            [
                jnp.stack(
                    [
                        gu_piece[:, first + to * ff_own : first + (to + 1) * ff_own]
                        for first in (0, ff_total)
                    ]
                )
                for to in range(wa_size)
            ]
        ),
        ((0, 0), (0, 0), (0, 0), (0, hidden_own - ff_own)),
    )

    positions = jnp.arange(group_rows, dtype=jnp.int32)
    segments = (positions >= first_length).astype(jnp.int32)
    cosine, sine = rotary_tables(positions - segments * first_length)
    first_block = (ctx_index * own_blocks)[None].astype(jnp.int32)
    act_one, own_given = arrange(inverse, first_block, dealt, norm1_gain[None, :], own_blocks)
    query_b, key_b, value_b, mixed_b, probs_b, gu_mine, out_rows = attend(
        segments,
        act_one,
        qkv_cols,
        cosine,
        sine,
        gu_send,
        out_cols,
        ctx_size,
        wa_size,
    )
    gain_two = norm2_gain[None, :]
    hidden, acts, gu_weight = out_project(
        mixed_b, out_rows, own_given, gain_two, gu_mine, ctx_size, wa_size
    )
    gu_weight = gu_weight.reshape(2, width, hidden_own)
    act_two = acts.reshape(wa_size * tok_rows, width)
    early = lax.optimization_barrier((grad_out[0], mixed_b))[0]
    grads_all = lax.all_gather(early, "wa", axis=0)
    cotangent = jnp.concatenate(
        [take(grads_all, (wa_index - s) % wa_size) for s in range(wa_size)], axis=0
    )

    d_act, mlp_parts, act_t, d_gu, inner_t = mlp(act_two, cotangent, gu_weight, w_down)
    d_branches, gain_two_part, out_given, gu_piece_grad, down_piece_grad = turn(
        d_act.reshape(wa_size, tok_rows, width),
        mlp_parts.reshape(wa_size, tok_rows, width),
        hidden,
        gain_two,
        grad_out[0],
        act_t,
        d_gu,
        inner_t,
        cotangent,
        ff_own,
        ctx_size,
        wa_size,
    )
    d_branch_b = d_branches.reshape(group_rows, width)
    own_order = lax.dynamic_slice_in_dim(block_order, ctx_index * own_blocks, own_blocks)
    d_qkv_b, dealt_qkv, d_out_part, d_hidden_dealt = attend_back(
        inverse,
        own_order,
        d_branch_b,
        out_rows,
        mixed_b,
        query_b,
        key_b,
        value_b,
        probs_b,
        cosine,
        sine,
    )
    qkv_grad = dot_left_t(act_one, d_qkv_b)
    gain_one_part = jnp.sum(qkv_grad * qkv_cols.astype(F32), axis=1) / norm1_gain
    qkv_parts = qkv_grad.astype(BF).reshape(wa_size, wa_rows, 3 * head_cols)
    d_tokens, gus, downs, qkvs, outs, gain_sums = close(
        dealt_qkv,
        qkv_cols,
        tokens[0],
        norm1_gain[None, :],
        d_hidden_dealt,
        gu_piece_grad.reshape(2, wa_size, piece_rows, hidden_own),
        qkv_parts,
        d_out_part,
        down_piece_grad,
        jnp.concatenate([gain_one_part[None, :], gain_two_part], axis=0),
        2 * ff_total,
        ctx_size,
        wa_size,
    )
    d_gate_up = gus.reshape(wa_rows, 2 * ff_total).astype(F32)
    in_order = list(range(ctx_size))
    by_core = in_order[0::2] + in_order[1::2]
    d_down = widen(downs, downs.shape[2], by_core, ff_own // 2 if ff_own % 32 == 0 else ff_own)
    d_qkv = widen(qkvs, head_cols, in_order, 64)
    d_out = widen(outs, head_cols, in_order, 128)
    return (
        out_given[None],
        d_tokens[None],
        gain_sums[0],
        d_qkv,
        d_out,
        gain_sums[1],
        d_gate_up,
        d_down,
    )


def solution(mesh):
    in_specs = (
        P("wa", "ctx", None),
        P("wa", None),
        P("wa", None),
        P(),
        P("wa", None),
        P("wa", None),
        P(),
        P("wa", None),
        P("wa", None),
        P("wa", "ctx", None),
    )
    out_specs = (
        P("wa", "ctx", None),
        P("wa", "ctx", None),
        P(),
        P("wa", None),
        P("wa", None),
        P(),
        P("wa", None),
        P("wa", None),
    )
    return jax.shard_map(
        per_device, mesh=mesh, in_specs=in_specs, out_specs=out_specs, check_vma=False
    )
```

time: 723 us -> 630 us (0.87)
  Pallas kernels: 469 us -> 567 us
  local copies, waits for them, and re-layouts: 94.8 us -> 10.1 us
  matrix products: 90.5 us -> 7.98 us
  between operations: 25.6 us -> 14.5 us
  starting transfers between devices: 10.6 us -> 0.08 us
  waiting for transfers between devices: 7.68 us -> 0.06 us
    pallas_call x2 -> x8, Pallas kernels: 177 us -> 298 us  [the longest x1 178 us: close(): pl.pallas_call(functools.partial(close_kernel, ctx_size, wa_size), out_sh...]
    dot_general x11 -> x0, matrix products: 59.4 us -> none  [the longest x3 24 us: dot_plain(): return jnp.dot(left, right, preferred_element_type=F32)]
    unnamed x88 -> x20, local copies, waits for them, and re-layouts: 58.8 us -> 3.16 us
    pallas_call x1, Pallas kernels: 115 us -> 88.3 us  [out_project(): pl.pallas_call(functools.partial(out_kernel, ctx_size, wa_size), out_shap...]
    convert_element_type x2 -> x0, local copies, waits for them, and re-layouts: 17 us -> none  [the longest x1 15.9 us: per_device(): gu_part = dot_left_t(act_two, d_gu_b).astype(BF)]
    dot_general x4 -> x1, matrix products: 22.4 us -> 7.98 us  [dot_left_t(): lax.dot_general(left, right, (((0,), (0,)), ((), ())), preferred_element_...]
    all_to_all x2 -> x0, starting transfers between devices: 10.5 us -> none  [the longest x1 5.85 us: per_device(): out_rows = lax.all_to_all(out_cols, 'ctx', 0, 1, tiled=True)]
    convert_element_type x1, other arithmetic: 2.46 us -> 12.7 us  [per_device(): d_gate_up = gus.reshape(wa_rows, 2 * ff_total).astype(F32)]
  transfers between devices with their start and end apart: 4 -> 2, of which waited for: 1 -> 0; matrix products, arithmetic and copies ran while one was open for 11% -> 2% of each run, Pallas kernels for 26% -> 27%
where the time goes in v4:
time: 630 us; the launch traced here: 625 us
  Pallas kernels  567 us (90%)
  other arithmetic  25.2 us (4%)
  between operations  14.5 us (2%)
  local copies, waits for them, and re-layouts  10.1 us (2%)
  matrix products  7.98 us (1%)
    pallas_call x1, Pallas kernels, close(): pl.pallas_call(functools.partial(close_kernel, ctx_size, wa_size), out_sh...  178 us
    pallas_call x1, Pallas kernels, turn(): pl.pallas_call(functools.partial(turn_kernel, ctx_size, wa_size), out_sha...  109 us
    pallas_call x1, Pallas kernels, out_project(): pl.pallas_call(functools.partial(out_kernel, ctx_size, wa_size), out_shap...  88.3 us
    pallas_call x1, Pallas kernels, gather_both(): pl.pallas_call(functools.partial(gather_kernel, ctx_size, wa_size, cuts),...  71.8 us
    pallas_call x1, Pallas kernels, attend(): pl.pallas_call(functools.partial(attend_kernel, ctx_size, wa_size, heads)...  42 us
    pallas_call x1, Pallas kernels, mlp(): pl.pallas_call(mlp_kernel, out_shape=(jax.ShapeDtypeStruct((tokens, width...  34.4 us
    pallas_call x3, Pallas kernels, widen(): pl.pallas_call(body, out_shape=jax.ShapeDtypeStruct((rows, count * own),...  19.7 us
    pallas_call x1, Pallas kernels, attend_back(): pl.pallas_call(functools.partial(attend_back_kernel, heads), out_shape=(g...  15.3 us
  transfers between devices with their start and end apart: 2, of which 0 were waited for; matrix products, arithmetic and copies ran while one was open for 2% of the time, Pallas kernels for 27%

profile of v4, /device:TPU:9, one launch (start us, length us, event | category | flops | bytes accessed | tf_op | source)
XLA Modules:
  0.0 624.7 jit_solution(13524332145353288416)
XLA Ops:
  7.2 1.5 copy-done
  8.8 0.7 constant_dynamic-slice_fusion.1
  9.6 0.7 subtract_convert_fusion
  10.3 1.5 fusion.7.row_seg_ref
  11.7 1.2 compare_convert_fusion.column_seg_ref
  13.0 1.3 select_reduce_fusion.order_ref.place_ref
  14.3 1.2 constant_dynamic-slice_fusion.4
  15.4 0.9 pad_maximum_fusion.1.w_ref
  16.4 71.8 %gather_both.1 = (bf16[8,128,2048]{2,1,0:T(8,128)(2,1)}, bf16[4,512,768]{2,1,0:T(8,128)(2,1)}) custom-call(bf16[128,2048]{1,0:T(8,128)(2,1)} %bitcast.73, bf16[512,768]{1,0:T(8,128)(2,1)} %pad_maximum_fusion.1.w_ref), custom_call_target="tpu_custom_call" | custom-call | bytes 200000000 | tf_op jit(solution)/shard_map/gather_both/pallas_call | solution.py:377
  88.1 8.2 %arrange.1 = (bf16[1024,2048]{1,0:T(8,128)(2,1)}, bf16[128,2048]{1,0:T(8,128)(2,1)}) custom-call(s32[8]{0:T(128)} %select_reduce_fusion.order_ref.place_ref, s32[1]{0:T(128)} %bitcast.2.first_ref, bf16[1024,2048]{1,0:T(8,128)(2,1)} %bitcast.64, f32[1,2048]{1,0:T(1,128)} %bitcast.78), custom_call_target="tpu_custom_call" | custom-call | tf_op jit(solution)/shard_map/arrange/pallas_call | solution.py:422
  96.3 1.9 fusion.8
  98.2 1.3 pad_maximum_fusion.2
  99.5 2.1 dynamic-slice_bitcast_fusion.11
  101.8 1.2 fusion.6.gu_ref
  103.1 42.0 %attend.1 = (bf16[1024,256]{1,0:T(8,128)(2,1)}, bf16[1024,256]{1,0:T(8,128)(2,1)}, bf16[1024,256]{1,0:T(8,128)(2,1)}, bf16[1024,256]{1,0:T(8,128)(2,1)}, bf16[2,...) custom-call(s32[1024,1]{1,0:T(8,128)} %fusion.7.row_seg_ref, ...), custom_call_target="tpu_custom_call" | custom-call | flops 3221225472 | bytes 100000000 | tf_op jit(solution)/shard_map/attend/pallas_call | solution.py:549
  145.2 0.6 constant_dynamic-slice_fusion
  145.8 88.3 %out_project.1 = (f32[128,2048]{1,0:T(8,128)}, bf16[4,128,2048]{2,1,0:T(8,128)(2,1)}, bf16[2,4,8,64,1408]{4,3,2,1,0:T(8,128)(2,1)}) custom-call(bf16[1024,256]{1,0:T(8,128)(2,1)} %get-tuple-element.46.mixed_ref.o_ref, bf16[256,2048]{1,0:T(8,128)(2,1)} %get-tuple-element.47.w_ref, bf16[128,2048]{1,0:T(8,128)(2,1)} %get-tuple-element.48.x_ref, ...), custom_call_target="tpu_custom_call" | custom-call | flops 1073741824 | bytes 200000000 | tf_op jit(solution)/shard_map/out_project/pallas_call | solution.py:761
  234.2 1.8 dynamic-slice_bitcast_fusion.3
  235.9 1.6 pad_maximum_fusion.dz_ref.dz_all_ref
  237.5 34.4 %mlp.1 = (bf16[512,2048]{1,0:T(8,128)(2,1)}, bf16[512,2048]{1,0:T(8,128)(2,1)}, bf16[2048,512]{1,0:T(8,128)(2,1)}, bf16[2,512,1408]{2,1,0:T(8,128)(2,1)}, bf16[1408,512]{1,0:T(8,128)(2,1)}) custom-call(bf16[512,2048]{1,0:T(8,128)(2,1)} %bitcast.91, bf16[512,2048]{1,0:T(8,128)(2,1)} %pad_maximum_fusion.dz_ref.dz_all_ref, bf16[2,2048,1408]{2,1,0:T(8,128)(2,1)} %bitcast.90, ...), custom_call_target="tpu_custom_call" | custom-call | flops 17716740096 | bytes 50000000 | tf_op jit(solution)/shard_map/mlp/pallas_call | solution.py:866
  271.9 108.7 %turn.1 = (bf16[8,128,2048]{2,1,0:T(8,128)(2,1)}, f32[1,2048]{1,0:T(1,128)}, bf16[128,2048]{1,0:T(8,128)(2,1)}, bf16[8,64,1408]{2,1,0:T(8,128)(2,1)}, bf16[1376,256]{1,0:T(8,128)(2,1)}) custom-call(bf16[4,128,2048]{2,1,0:T(8,128)(2,1)} %bitcast.68, bf16[4,128,2048]{2,1,0:T(8,128)(2,1)} %bitcast.69, f32[128,2048]{1,0:T(8,128)} %get-tuple-element.55.hidden_ref, ...), custom_call_target="tpu_custom_call" | custom-call | bytes 200000000 | tf_op jit(solution)/shard_map/turn/pallas_call | solution.py:1063
  380.6 15.3 %attend_back.1 = (bf16[1024,768]{1,0:T(8,128)(2,1)}, bf16[1024,768]{1,0:T(8,128)(2,1)}, bf16[256,2048]{1,0:T(8,128)(2,1)}, bf16[128,2048]{1,0:T(8,128)(2,1)}) custom-call(s32[8]{0:T(128)} %select_reduce_fusion.order_ref.place_ref, s32[1]{0:T(128)} %bitcast.32.own_ref, bf16[1024,2048]{1,0:T(8,128)(2,1)} %bitcast.63, ...), custom_call_target="tpu_custom_call" | custom-call | flops 2147483648 | bytes 20000000 | tf_op jit(solution)/shard_map/attend_back/pallas_call | solution.py:665
  395.9 8.0 %multiply_reduce_fusion = (f32[2048]{0:T(1024)S(1)}, bf16[2048,768]{1,0:T(8,128)(2,1)}) fusion(bf16[4,512,768]{2,1,0:T(8,128)(2,1)S(1)} %copy-done.2, bf16[1024,2048]{1,0:T(8,128)(2,1)} %get-tuple-element.44.act_ref, bf16[1024,768]{1,0:T(8,128)(2,1)} %get-tuple-element.68), kind=kOutput, calls=%fused_computation.1 | convolution fusion | flops 3227514880 | bytes 12066816 | tf_op jit(solution)/shard_map/dot_general | solution.py:26
  403.9 0.6 pad_maximum_fusion.4.gains_ref
  404.6 178.5 %close.1 = (bf16[128,2048]{1,0:T(8,128)(2,1)}, bf16[8,64,11008]{2,1,0:T(8,128)(2,1)}, bf16[8,1376,256]{2,1,0:T(8,128)(2,1)}, bf16[8,512,768]{2,1,0:T(8,128)(2,1)...) custom-call(bf16[1024,768]{1,0:T(8,128)(2,1)} %get-tuple-element.65.grads_ref, bf16[2048,768]{1,0:T(8,128)(2,1)} %bitcast.66, ...), custom_call_target="tpu_custom_call" | custom-call | flops 3221225472 | bytes 400000000 | tf_op jit(solution)/shard_map/close/pallas_call | solution.py:1287
  583.0 12.7 %bitcast_convert_fusion = f32[512,11008]{1,0:T(8,128)} fusion(bf16[8,64,11008]{2,1,0:T(8,128)(2,1)} %get-tuple-element.76), kind=kLoop, calls=%fused_computation | loop fusion | flops 5636096 | bytes 33816576 | tf_op jit(solution)/shard_map/convert_element_type | solution.py:1475
  595.8 8.8 %widen.3 = f32[512,6144]{1,0:T(8,128)} custom-call(bf16[8,512,768]{2,1,0:T(8,128)(2,1)} %get-tuple-element.74.block_ref), custom_call_target="tpu_custom_call" | custom-call | tf_op jit(solution)/shard_map/widen/pallas_call | solution.py:1333
  604.6 6.5 %widen.5 = f32[1376,2048]{1,0:T(8,128)} custom-call(bf16[8,1376,256]{2,1,0:T(8,128)(2,1)} %get-tuple-element.77.block_ref), custom_call_target="tpu_custom_call" | custom-call | tf_op jit(solution)/shard_map/widen/pallas_call | solution.py:1333
  611.1 4.4 widen.4
  615.5 0.6 fusion.9
  616.1 0.8 copy.20
  616.9 0.8 copy.21
  (27 shorter events, 0.4 us)
Async XLA Ops:
  7.2 1.6 copy-start
  7.2 95.9 %all-gather.4.cloned.1.call-start = ((), (), s32[]{:S(2)}) async-start(), calls=%async_computation | async-start | bytes 1310720 | tf_op jit(solution)/shard_map/all_gather | solution.py:41
  9.5 224.6 %all-gather.6.cloned.1.call-start = ((), (), s32[]{:S(2)}) async-start(), calls=%async_computation.1 | async-start | bytes 2621440 | tf_op jit(solution)/shard_map/all_gather | solution.py:1422
  103.1 42.1 %copy-start.8 = (s32[1,8]{1,0:T(1,128)S(1)}, s32[1,8]{1,0:T(1,128)}, u32[]{:S(2)}) copy-start(s32[1,8]{1,0:T(1,128)} %param.12) | copy-start | bytes 100
  380.6 15.3 %copy-start.2 = (bf16[4,512,768]{2,1,0:T(8,128)(2,1)S(1)}, bf16[4,512,768]{2,1,0:T(8,128)(2,1)}, u32[]{:S(2)}) copy-start(bf16[4,512,768]{2,1,0:T(8,128)(2,1)} %get-tuple-element.45) | copy-start | bytes 9437188
  395.9 8.0 %copy-start.5 = (f32[2048]{0:T(1024)S(1)}, f32[2048]{0:T(1024)}, u32[]{:S(2)}) copy-start(f32[2048]{0:T(1024)} %param.13) | copy-start | bytes 24580
  395.9 8.0 %copy-start.7 = (f32[1,2048]{1,0:T(1,128)S(1)}, f32[1,2048]{1,0:T(1,128)}, u32[]{:S(2)}) copy-start(f32[1,2048]{1,0:T(1,128)} %get-tuple-element.71) | copy-start | bytes 24580
  611.1 6.6 %copy-start.1 = (bf16[512,2048]{1,0:T(8,128)(2,1)S(1)}, bf16[512,2048]{1,0:T(8,128)(2,1)}, u32[]{:S(2)}) copy-start(bf16[512,2048]{1,0:T(8,128)(2,1)} %param.15) | copy-start | bytes 6291460
  611.1 4.4 copy-start.6
  611.1 5.0 copy-start.3
  611.1 5.8 copy-start.4
Sparse Core Ops, SparseCore 0:
  10.2 45.0 all-gather.3
  145.3 51.7 all-gather.5

commit v5 on v4

--- a/solution.py
+++ b/solution.py
@@ -20,10 +20,6 @@
 VMEM_LIMIT = 60 * 1024 * 1024
 ATTEND_ROWS = 256
 CHUNK = 256
-
-
-def dot_left_t(left, right):
-    return lax.dot_general(left, right, (((0,), (0,)), ((), ())), preferred_element_type=F32)
 
 
 def rotary_tables(seq_pos):
@@ -35,14 +31,6 @@
         jnp.concatenate([cosine, cosine], axis=-1),
         jnp.concatenate([-sine, sine], axis=-1),
     )
-
-
-def gather_rows(values, axis):
-    return lax.all_gather(values, axis, axis=0, tiled=True)
-
-
-def take(values, index):
-    return lax.dynamic_index_in_dim(values, index, 0, keepdims=False)
 
 
 MESH = pl.DeviceIdType.MESH
@@ -322,9 +310,11 @@
     )
 
 
-def gather_kernel(ctx_size, wa_size, cuts, x_ref, w_ref, xs_ref, ws_ref, *sems):
+def gather_kernel(
+    ctx_size, wa_size, cuts, own_columns, x_ref, w_ref, gu_ref, xs_ref, ws_ref, cut_ref, *scratch
+):
     p = place_of(ctx_size, wa_size)
-    ring_send, ring_recv, local = sems[4:]
+    ring_send, ring_recv, local, piece_ref = scratch[4:]
     greet([p.beside] + p.ahead[1:], [p.up[1], p.down[1]])
     rows = w_ref.shape[0] // cuts
     half_rows = x_ref.shape[0] // 2
@@ -345,13 +335,29 @@
         x_ref,
         lambda d: xs_ref.at[d],
         lambda d, h: xs_ref.at[d, pl.ds(h * half_rows, half_rows)],
-        sems[:4],
+        scratch[:4],
     )
     spread.start()
-    own_x = pltpu.make_async_copy(x_ref, xs_ref.at[p.ctx], local.at[0])
-    own_w = pltpu.make_async_copy(w_ref, ws_ref.at[p.wa], local.at[1])
-    own_x.start()
-    own_w.start()
+    piece_rows = piece_ref.shape[0]
+    place = pl.ds(pl.multiple_of(p.ctx * piece_rows, piece_rows), piece_rows)
+    loads = [
+        pltpu.make_async_copy(x_ref, xs_ref.at[p.ctx], local.at[0]),
+        pltpu.make_async_copy(w_ref, ws_ref.at[p.wa], local.at[1]),
+        pltpu.make_async_copy(gu_ref.at[place], piece_ref, local.at[2]),
+    ]
+    for copy in loads:
+        copy.start()
+    loads[2].wait()
+    total = piece_ref.shape[1] // 2
+    hidden = cut_ref.shape[3]
+    for to in range(wa_size):
+        for part in range(2):
+            first = part * total + to * own_columns
+            cut_ref[to, part, :, :own_columns] = piece_ref[:, first : first + own_columns]
+            if hidden > own_columns:
+                cut_ref[to, part, :, own_columns:] = jnp.zeros(
+                    (piece_rows, hidden - own_columns), BF
+                )
     late = []
     for step in range(1, wa_size):
         for i in range(cuts):
@@ -368,27 +374,32 @@
     for copy in late:
         copy.wait_send()
     spread.finish()
-    own_x.wait()
-    own_w.wait()
-
-
-def gather_both(x, w, ctx_size, wa_size, cuts=4):
+    for copy in loads[:2]:
+        copy.wait()
+
+
+def gather_both(x, w, gu, own_columns, ctx_size, wa_size, cuts=4):
     anywhere = pl.BlockSpec(memory_space=pl.ANY)
+    piece_rows = w.shape[0] // ctx_size
+    hidden = -(-own_columns // 128) * 128
     return pl.pallas_call(
-        functools.partial(gather_kernel, ctx_size, wa_size, cuts),
+        functools.partial(gather_kernel, ctx_size, wa_size, cuts, own_columns),
         out_shape=(
             jax.ShapeDtypeStruct((ctx_size,) + x.shape, x.dtype),
             jax.ShapeDtypeStruct((wa_size,) + w.shape, w.dtype),
-        ),
-        in_specs=[anywhere] * 2,
-        out_specs=[anywhere] * 2,
+            jax.ShapeDtypeStruct((wa_size, 2, piece_rows, hidden), BF),
+        ),
+        in_specs=[anywhere] * 3,
+        out_specs=[anywhere] * 2 + [pl.BlockSpec(memory_space=pltpu.VMEM)],
         scratch_shapes=plane_sems(ctx_size)
         + [pltpu.SemaphoreType.DMA((wa_size - 1, cuts))] * 2
-        + [pltpu.SemaphoreType.DMA((2,))],
-        compiler_params=pltpu.CompilerParams(collective_id=0, has_side_effects=True),
+        + [pltpu.SemaphoreType.DMA((3,)), pltpu.VMEM((piece_rows, gu.shape[1]), BF)],
+        compiler_params=pltpu.CompilerParams(
+            collective_id=0, has_side_effects=True, vmem_limit_bytes=VMEM_LIMIT
+        ),
         cost_estimate=pl.CostEstimate(flops=0, bytes_accessed=200_000_000, transcendentals=0),
         name="gather_both",
-    )(x, w)
+    )(x, w, gu)
 
 
 def exchange_plane(peers, source, target, send_sem, recv_sem):
@@ -400,59 +411,21 @@
     ]
 
 
-def arrange_kernel(own_blocks, order_ref, first_ref, x_ref, gain_ref, act_ref, own_ref):
-    x = x_ref[...]
-    wide = x.astype(F32)
-    scale = lax.rsqrt(jnp.mean(wide * wide, axis=-1, keepdims=True) + EPSILON)
-    act_ref[...] = (wide * scale * gain_ref[...]).astype(BF)
-    at = pl.program_id(0) - first_ref[0]
-
-    @pl.when((at >= 0) & (at < own_blocks))
-    def _():
-        own_ref[...] = x
-
-
-def arrange(order, first, dealt, gain, own_blocks):
-    rows, width = dealt.shape
-    block = (BLOCK, width)
-
-    def own_place(i, order_ref, first_ref):
-        return (jnp.clip(i - first_ref[0], 0, own_blocks - 1), 0)
-
-    return pl.pallas_call(
-        functools.partial(arrange_kernel, own_blocks),
-        out_shape=(
-            jax.ShapeDtypeStruct((rows, width), BF),
-            jax.ShapeDtypeStruct((own_blocks * BLOCK, width), BF),
-        ),
-        grid_spec=pltpu.PrefetchScalarGridSpec(
-            num_scalar_prefetch=2,
-            grid=(rows // BLOCK,),
-            in_specs=[
-                pl.BlockSpec(block, lambda i, order_ref, first_ref: (order_ref[i], 0)),
-                pl.BlockSpec((1, width), lambda i, order_ref, first_ref: (0, 0)),
-            ],
-            out_specs=[
-                pl.BlockSpec(block, lambda i, order_ref, first_ref: (i, 0)),
-                pl.BlockSpec(block, own_place),
-            ],
-        ),
-        name="arrange",
-    )(order, first, dealt, gain)
-
-
 def attend_kernel(
     ctx_size,
     wa_size,
     heads,
     row_seg_ref,
     column_seg_ref,
-    act_ref,
+    x_ref,
     w_ref,
+    gain_ref,
+    pick_ref,
     cos_ref,
     sin_ref,
     gu_ref,
-    cols_ref,
+    act_t_ref,
+    own_ref,
     q_ref,
     k_ref,
     v_ref,
@@ -465,23 +438,23 @@
     local,
     out_send,
     out_recv,
+    dealt_ref,
 ):
     wa, ctx = lax.axis_index("wa"), lax.axis_index("ctx")
     up = [lax.rem(wa + s, wa_size) for s in range(wa_size)]
     peers = [lax.rem(ctx + i, ctx_size) for i in range(ctx_size)]
     greet(peers[1:], up[1:])
-    deal_out = exchange_plane(
-        peers,
-        lambda d: cols_ref.at[d],
-        lambda d: rows_ref.at[:, pl.ds(pl.multiple_of(d * cols_ref.shape[2], 128), cols_ref.shape[2])],
-        out_send,
-        out_recv,
-    )
-    own_out = pltpu.make_async_copy(
-        cols_ref.at[ctx],
-        rows_ref.at[:, pl.ds(pl.multiple_of(ctx * cols_ref.shape[2], 128), cols_ref.shape[2])],
-        local.at[1],
-    )
+    head_cols = heads * HEAD
+
+    def columns_of(d):
+        rows = pl.ds(pl.multiple_of(d * head_cols, head_cols), head_cols)
+        return w_ref.at[rows, pl.ds(3 * head_cols, head_cols)]
+
+    def rows_of(d):
+        return rows_ref.at[:, pl.ds(pl.multiple_of(d * head_cols, head_cols), head_cols)]
+
+    deal_out = exchange_plane(peers, columns_of, rows_of, out_send, out_recv)
+    own_out = pltpu.make_async_copy(columns_of(ctx), rows_of(ctx), local.at[1])
     own_out.start()
     deal = [
         send(gu_ref.at[up[s]], gw_ref.at[:, wa], gu_send.at[s], gu_recv.at[s], wa=up[s])
@@ -489,25 +462,42 @@
     ]
     own = pltpu.make_async_copy(gu_ref.at[wa], gw_ref.at[:, wa], local.at[0])
     own.start()
-    rows = act_ref.shape[0]
+    rows = x_ref.shape[0]
     step = ATTEND_ROWS
-    head_cols = heads * HEAD
 
     def project(i, carried):
         place = pl.ds(pl.multiple_of(i * step, step), step)
-        made = jnp.dot(act_ref[place, :], w_ref[...], preferred_element_type=F32)
+        x = x_ref[place, :].astype(F32)
+        scale = lax.rsqrt(jnp.mean(x * x, axis=-1, keepdims=True) + EPSILON)
+        act = (x * scale * gain_ref[...]).astype(BF)
+        act_t_ref[:, place] = act.T
+        made = jnp.dot(act, w_ref[:, : 3 * head_cols], preferred_element_type=F32)
         cosine, sine = cos_ref[place, :], sin_ref[place, :]
-        for head in range(heads):
+        for head in range(2 * heads):
             columns = slice(head * HEAD, (head + 1) * HEAD)
-            for part, target in ((0, q_ref), (1, k_ref)):
-                first = part * head_cols + head * HEAD
-                u = made[:, first : first + HEAD]
-                turned = u * cosine + pltpu.roll(u, HEAD // 2, 1) * sine
-                target[place, columns] = turned.astype(BF)
-        v_ref[place, :] = made[:, 2 * head_cols :].astype(BF)
+            u = made[:, columns]
+            dealt_ref[place, columns] = (
+                u * cosine + pltpu.roll(u, HEAD // 2, 1) * sine
+            ).astype(BF)
+        dealt_ref[place, 2 * head_cols :] = made[:, 2 * head_cols :].astype(BF)
         return carried
 
     lax.fori_loop(0, rows // step, project, 0)
+
+    def put_in_order(i, carried):
+        place = pl.ds(pl.multiple_of(i * step, step), step)
+        given = jnp.dot(pick_ref[place, :], dealt_ref[...], preferred_element_type=F32).astype(BF)
+        q_ref[place, :] = given[:, :head_cols]
+        k_ref[place, :] = given[:, head_cols : 2 * head_cols]
+        v_ref[place, :] = given[:, 2 * head_cols :]
+        return carried
+
+    lax.fori_loop(0, rows // step, put_in_order, 0)
+    own_rows = own_ref.shape[0]
+    own_place = pl.ds(pl.multiple_of(ctx * own_rows, own_rows), own_rows)
+    own_ref[...] = jnp.dot(
+        pick_ref[own_place, :], x_ref[...], preferred_element_type=F32
+    ).astype(BF)
     for i in range(rows // step):
         here = slice(i * step, (i + 1) * step)
         keys = (i + 1) * step
@@ -539,9 +529,9 @@
         copy.wait()
 
 
-def attend(segments, act, w, cosine, sine, gu, out_cols, ctx_size, wa_size):
-    rows, width = act.shape
-    head_cols = w.shape[1] // 3
+def attend(segments, x, w, gain, pick, cosine, sine, gu, ctx_size, wa_size):
+    rows, width = x.shape
+    head_cols = w.shape[1] // 4
     heads = head_cols // HEAD
     vmem = pl.BlockSpec(memory_space=pltpu.VMEM)
     anywhere = pl.BlockSpec(memory_space=pl.ANY)
@@ -549,18 +539,21 @@
     return pl.pallas_call(
         functools.partial(attend_kernel, ctx_size, wa_size, heads),
         out_shape=(
+            jax.ShapeDtypeStruct((width, rows), BF),
+            jax.ShapeDtypeStruct((rows // ctx_size, width), BF),
             heads_shape,
             heads_shape,
             heads_shape,
             heads_shape,
             jax.ShapeDtypeStruct((heads, rows, rows), BF),
             jax.ShapeDtypeStruct((2, wa_size) + gu.shape[2:], BF),
-            jax.ShapeDtypeStruct((out_cols.shape[1], width), BF),
-        ),
-        in_specs=[vmem] * 6 + [anywhere] * 2,
-        out_specs=[vmem] * 5 + [anywhere] * 2,
+            jax.ShapeDtypeStruct((head_cols, width), BF),
+        ),
+        in_specs=[vmem] * 8 + [anywhere],
+        out_specs=[vmem] * 7 + [anywhere] * 2,
         scratch_shapes=[pltpu.SemaphoreType.DMA((wa_size,))] * 3
-        + [pltpu.SemaphoreType.DMA((ctx_size,))] * 2,
+        + [pltpu.SemaphoreType.DMA((ctx_size,))] * 2
+        + [pltpu.VMEM((rows, 3 * head_cols), BF)],
         compiler_params=pltpu.CompilerParams(
             collective_id=4, has_side_effects=True, vmem_limit_bytes=VMEM_LIMIT
         ),
@@ -568,34 +561,95 @@
             flops=2 * rows * width * 3 * head_cols, bytes_accessed=100_000_000, transcendentals=0
         ),
         name="attend",
-    )(segments[:, None], segments[None, :], act, w, cosine, sine, gu, out_cols)
+    )(segments[:, None], segments[None, :], x, w, gain, pick, cosine, sine, gu)
 
 
 def attend_back_kernel(
+    ctx_size,
+    wa_size,
     heads,
-    place_ref,
-    own_ref,
     dy_ref,
     w_ref,
     o_ref,
     q_ref,
     k_ref,
     v_ref,
-    prob_ref,
     cos_ref,
     sin_ref,
+    prob_any,
+    act_t_any,
+    w_all_any,
+    unpick_any,
+    gu_ref,
+    down_ref,
     grads_ref,
-    dealt_ref,
-    d_out_ref,
     dh_ref,
+    dw_ref,
+    gain_ref,
+    parts_ref,
+    gu_in_ref,
+    downs_ref,
     do_ref,
     dk_ref,
     dv_ref,
+    d_out_ref,
+    given_ref,
+    prob_ref,
+    act_t_ref,
+    w_all_ref,
+    unpick_ref,
+    *sems,
 ):
+    p = place_of(ctx_size, wa_size)
+    gu_send, gu_recv, part_send, part_recv, local = sems[4:]
+    peers = [lax.rem(p.ctx + i, ctx_size) for i in range(ctx_size)]
+    greet(peers[1:], p.up[1:])
+    deal = [
+        send(gu_ref.at[:, p.up[s]], gu_in_ref.at[p.wa], gu_send.at[s], gu_recv.at[s], wa=p.up[s])
+        for s in range(1, wa_size)
+    ]
+    half_rows = down_ref.shape[0] // 2
+    spread = Spread(
+        p,
+        down_ref,
+        lambda d: downs_ref.at[d],
+        lambda d, h: downs_ref.at[d, pl.ds(h * half_rows, half_rows)],
+        sems[:4],
+    )
+    spread.start()
+    loads = [
+        pltpu.make_async_copy(source, target, local.at[3 + i])
+        for i, (source, target) in enumerate(
+            (
+                (prob_any, prob_ref),
+                (unpick_any, unpick_ref),
+                (act_t_any, act_t_ref),
+                (w_all_any, w_all_ref),
+            )
+        )
+    ]
+    for copy in loads:
+        copy.start()
     rows = dy_ref.shape[0]
     step = ATTEND_ROWS
     head_cols = heads * HEAD
     back_scale = 1.0 / math.sqrt(HEAD)
+    d_out_ref[...] = lax.dot_general(
+        o_ref[...], dy_ref[...], (((0,), (0,)), ((), ())), preferred_element_type=F32
+    ).astype(BF)
+
+    def part_of(device):
+        place = pl.ds(pl.multiple_of(device * head_cols, head_cols), head_cols)
+        return d_out_ref.at[:, place]
+
+    part_copies = exchange_plane(peers, part_of, lambda d: parts_ref.at[d], part_send, part_recv)
+    kept = [
+        pltpu.make_async_copy(gu_ref.at[:, p.wa], gu_in_ref.at[p.wa], local.at[0]),
+        pltpu.make_async_copy(down_ref, downs_ref.at[p.ctx], local.at[1]),
+        pltpu.make_async_copy(part_of(p.ctx), parts_ref.at[p.ctx], local.at[2]),
+    ]
+    for copy in kept:
+        copy.start()
 
     def project(i, carried):
         place = pl.ds(pl.multiple_of(i * step, step), step)
@@ -608,6 +662,7 @@
         return carried
 
     lax.fori_loop(0, rows // step, project, 0)
+    loads[0].wait()
     dk_ref[...] = jnp.zeros_like(dk_ref)
     dv_ref[...] = jnp.zeros_like(dv_ref)
 
@@ -632,57 +687,103 @@
             row_dot = jnp.sum(wide * d_probs, axis=-1, keepdims=True)
             d_scores = (wide * (d_probs - row_dot)).astype(BF)
             d_query = jnp.dot(d_scores, k_ref[:keys, columns], preferred_element_type=F32)
-            grads_ref[here, columns] = unrotate(d_query * back_scale, here).astype(BF)
+            given_ref[here, columns] = unrotate(d_query * back_scale, here).astype(BF)
             dk_ref[:keys, columns] += lax.dot_general(
                 d_scores, q, (((0,), (0,)), ((), ())), preferred_element_type=F32
             )
             dv_ref[:keys, columns] += lax.dot_general(
                 probs, d_o, (((0,), (0,)), ((), ())), preferred_element_type=F32
             )
-    for i in range(rows // BLOCK):
-        here = slice(i * BLOCK, (i + 1) * BLOCK)
-        for head in range(heads):
-            columns = slice(head * HEAD, (head + 1) * HEAD)
-            d_key = unrotate(dk_ref[here, columns] * back_scale, here)
-            grads_ref[here, head_cols + head * HEAD : head_cols + (head + 1) * HEAD] = d_key.astype(BF)
-        grads_ref[here, 2 * head_cols :] = dv_ref[here, :].astype(BF)
-        there = pl.ds(pl.multiple_of(place_ref[i] * BLOCK, BLOCK), BLOCK)
-        dealt_ref[there, :] = grads_ref[here, :]
-    for j in range(dh_ref.shape[0] // BLOCK):
-        at = pl.ds(pl.multiple_of(own_ref[j] * BLOCK, BLOCK), BLOCK)
-        dh_ref[j * BLOCK : (j + 1) * BLOCK, :] = dy_ref[at, :]
-    d_out_ref[...] = lax.dot_general(
-        o_ref[...], dy_ref[...], (((0,), (0,)), ((), ())), preferred_element_type=F32
+    for head in range(heads):
+        columns = slice(head * HEAD, (head + 1) * HEAD)
+        whole = slice(0, rows)
+        d_key = unrotate(dk_ref[:, columns] * back_scale, whole)
+        given_ref[:, head_cols + head * HEAD : head_cols + (head + 1) * HEAD] = d_key.astype(BF)
+    given_ref[:, 2 * head_cols :] = dv_ref[...].astype(BF)
+    arrivals = spread.arrivals()
+    next(arrivals)
+    next(arrivals)
+    for copy in loads[1:]:
+        copy.wait()
+
+    def put_back(i, carried):
+        place = pl.ds(pl.multiple_of(i * step, step), step)
+        grads_ref[place, :] = jnp.dot(
+            unpick_ref[place, :], given_ref[...], preferred_element_type=F32
+        ).astype(BF)
+        return carried
+
+    lax.fori_loop(0, rows // step, put_back, 0)
+    own_rows = dh_ref.shape[0]
+    own_place = pl.ds(pl.multiple_of(p.ctx * own_rows, own_rows), own_rows)
+    dh_ref[...] = jnp.dot(
+        unpick_ref[own_place, :], dy_ref[...], preferred_element_type=F32
     ).astype(BF)
-
-
-def attend_back(place, own, dy, w_rows, o, q, k, v, probs, cosine, sine):
+    wa_rows = dw_ref.shape[1]
+
+    def weights(i, carried):
+        place = pl.ds(pl.multiple_of(i * wa_rows, wa_rows), wa_rows)
+        made = jnp.dot(act_t_ref[place, :], grads_ref[...], preferred_element_type=F32)
+        dw_ref[i] = made.astype(BF)
+        gain_ref[place, :] = jnp.sum(
+            made * w_all_ref[place, : 3 * head_cols].astype(F32), axis=-1, keepdims=True
+        )
+        return carried
+
+    lax.fori_loop(0, wa_size, weights, 0)
+    for _ in arrivals:
+        pass
+    for copy in kept:
+        copy.wait()
+    spread.finish()
+    for copy in deal + part_copies:
+        copy.wait()
+
+
+def attend_back(
+    dy, w_rows, o, q, k, v, cosine, sine, probs, act_t, w_all, unpick, gu, down, ctx_size, wa_size
+):
     rows, width = dy.shape
     head_cols = o.shape[1]
     heads = head_cols // HEAD
     vmem = pl.BlockSpec(memory_space=pltpu.VMEM)
-    grads_shape = jax.ShapeDtypeStruct((rows, 3 * head_cols), BF)
+    anywhere = pl.BlockSpec(memory_space=pl.ANY)
     return pl.pallas_call(
-        functools.partial(attend_back_kernel, heads),
+        functools.partial(attend_back_kernel, ctx_size, wa_size, heads),
         out_shape=(
-            grads_shape,
-            grads_shape,
-            jax.ShapeDtypeStruct((head_cols, width), BF),
-            jax.ShapeDtypeStruct((own.shape[0] * BLOCK, width), BF),
-        ),
-        in_specs=[pl.BlockSpec(memory_space=pltpu.SMEM)] * 2 + [vmem] * 9,
-        out_specs=[vmem] * 4,
+            jax.ShapeDtypeStruct((rows, 3 * head_cols), BF),
+            jax.ShapeDtypeStruct((rows // ctx_size, width), BF),
+            jax.ShapeDtypeStruct((wa_size, width // wa_size, 3 * head_cols), BF),
+            jax.ShapeDtypeStruct((width, 1), F32),
+            jax.ShapeDtypeStruct((ctx_size, head_cols, head_cols), BF),
+            jax.ShapeDtypeStruct((wa_size, 2) + gu.shape[2:], BF),
+            jax.ShapeDtypeStruct((ctx_size,) + down.shape, BF),
+        ),
+        in_specs=[vmem] * 8 + [anywhere] * 6,
+        out_specs=[vmem] * 4 + [anywhere] * 3,
         scratch_shapes=[
             pltpu.VMEM((rows, head_cols), BF),
             pltpu.VMEM((rows, head_cols), F32),
             pltpu.VMEM((rows, head_cols), F32),
-        ],
-        compiler_params=pltpu.CompilerParams(vmem_limit_bytes=VMEM_LIMIT),
+            pltpu.VMEM((head_cols, width), BF),
+            pltpu.VMEM((rows, 3 * head_cols), BF),
+            pltpu.VMEM(probs.shape, BF),
+            pltpu.VMEM(act_t.shape, BF),
+            pltpu.VMEM(w_all.shape, BF),
+            pltpu.VMEM(unpick.shape, BF),
+        ]
+        + plane_sems(ctx_size)
+        + [pltpu.SemaphoreType.DMA((wa_size,))] * 2
+        + [pltpu.SemaphoreType.DMA((ctx_size,))] * 2
+        + [pltpu.SemaphoreType.DMA((7,))],
+        compiler_params=pltpu.CompilerParams(
+            collective_id=5, has_side_effects=True, vmem_limit_bytes=VMEM_LIMIT
+        ),
         cost_estimate=pl.CostEstimate(
-            flops=4 * rows * width * head_cols, bytes_accessed=20_000_000, transcendentals=0
+            flops=10 * rows * width * head_cols, bytes_accessed=100_000_000, transcendentals=0
         ),
         name="attend_back",
-    )(place, own, dy, w_rows, o, q, k, v, probs, cosine, sine)
+    )(dy, w_rows, o, q, k, v, cosine, sine, probs, act_t, w_all, unpick, gu, down)
 
 
 def out_kernel(
@@ -692,14 +793,16 @@
     w_ref,
     x_ref,
     gain_ref,
+    dz_ref,
     gu_ref,
     hidden_ref,
     acts_ref,
+    dzs_ref,
     gw_ref,
     *scratch,
 ):
     p = place_of(ctx_size, wa_size)
-    act_send, act_recv, local = scratch[12:]
+    act_send, act_recv, dz_send, dz_recv, local = scratch[12:]
     greet([p.beside] + p.ahead[1:], [p.up[1], p.down[1]])
     own = pltpu.make_async_copy(gu_ref, gw_ref.at[:, :, p.ctx], local.at[0])
     own.start()
@@ -716,32 +819,41 @@
         block = mixed_ref[pl.ds(pl.multiple_of(device * rows, rows), rows), :]
         return jnp.dot(block, w_ref[...], preferred_element_type=F32)
 
+    half_rows = rows // 2
+
+    def pass_on(slots, sems, s, i):
+        place = pl.ds(i * half_rows, half_rows)
+        return send(
+            slots.at[s, place],
+            slots.at[s + 1, place],
+            sems[0].at[s, i],
+            sems[1].at[s, i],
+            wa=p.up[1],
+        )
+
+    def ring_step(ring, slots, sems, s):
+        for i in range(2):
+            ring[2 * (s - 1) + i].wait_recv()
+            if s < wa_size - 1:
+                ring.append(pass_on(slots, sems, s, i))
+
+    dz_sems, act_sems = (dz_send, dz_recv), (act_send, act_recv)
+    dzs_ref[0] = dz_ref[...]
+    dz_ring = [pass_on(dzs_ref, dz_sems, 0, i) for i in range(2)]
     scatter = Scatter(p, part_of, scratch[:8])
     scatter.start()
+    ring_step(dz_ring, dzs_ref, dz_sems, 1)
     hidden = x_ref[...].astype(F32) + scatter.total()
+    spread.start()
     hidden_ref[...] = hidden
     scale = lax.rsqrt(jnp.mean(hidden * hidden, axis=-1, keepdims=True) + EPSILON)
     acts_ref[0] = (hidden * scale * gain_ref[...]).astype(BF)
-    half_rows = rows // 2
-
-    def pass_on(s, i):
-        place = pl.ds(i * half_rows, half_rows)
-        return send(
-            acts_ref.at[s, place],
-            acts_ref.at[s + 1, place],
-            act_send.at[s, i],
-            act_recv.at[s, i],
-            wa=p.up[1],
-        )
-
-    ring = [pass_on(0, 0), pass_on(0, 1)]
-    spread.start()
+    ring = [pass_on(acts_ref, act_sems, 0, i) for i in range(2)]
+    for s in range(2, wa_size):
+        ring_step(dz_ring, dzs_ref, dz_sems, s)
     arrivals = spread.arrivals()
     for s in range(1, wa_size):
-        for i in range(2):
-            ring[2 * (s - 1) + i].wait_recv()
-            if s < wa_size - 1:
-                ring.append(pass_on(s, i))
+        ring_step(ring, acts_ref, act_sems, s)
         if s == 2:
             next(arrivals)
             next(arrivals)
@@ -750,11 +862,11 @@
     scatter.finish()
     spread.finish()
     own.wait()
-    for copy in ring:
+    for copy in ring + dz_ring:
         copy.wait_send()
 
 
-def out_project(mixed, w_rows, x_own, gain, gu, ctx_size, wa_size):
+def out_project(mixed, w_rows, x_own, gain, dz, gu, ctx_size, wa_size):
     rows, width = x_own.shape
     vmem = pl.BlockSpec(memory_space=pltpu.VMEM)
     anywhere = pl.BlockSpec(memory_space=pl.ANY)
@@ -763,13 +875,14 @@
         out_shape=(
             jax.ShapeDtypeStruct((rows, width), F32),
             jax.ShapeDtypeStruct((wa_size, rows, width), BF),
+            jax.ShapeDtypeStruct((wa_size, rows, width), BF),
             jax.ShapeDtypeStruct((2, wa_size, ctx_size) + gu.shape[2:], BF),
         ),
-        in_specs=[vmem] * 4 + [anywhere],
-        out_specs=[vmem] * 2 + [anywhere],
+        in_specs=[vmem] * 5 + [anywhere],
+        out_specs=[vmem] * 3 + [anywhere],
         scratch_shapes=scatter_scratch(ctx_size, rows, width)
         + plane_sems(ctx_size)
-        + [pltpu.SemaphoreType.DMA((wa_size, 2))] * 2
+        + [pltpu.SemaphoreType.DMA((wa_size, 2))] * 4
         + [pltpu.SemaphoreType.DMA((1,))],
         compiler_params=pltpu.CompilerParams(
             collective_id=1, has_side_effects=True, vmem_limit_bytes=VMEM_LIMIT
@@ -778,7 +891,7 @@
             flops=2 * mixed.size * width, bytes_accessed=200_000_000, transcendentals=0
         ),
         name="out_project",
-    )(mixed, w_rows, x_own, gain, gu)
+    )(mixed, w_rows, x_own, gain, dz, gu)
 
 
 def mlp_kernel(
@@ -1103,26 +1216,23 @@
     x_ref,
     gain_ref,
     dh_ref,
-    gu_ref,
+    gu_in,
     dw_ref,
-    do_ref,
-    down_ref,
+    do_parts,
     gains_ref,
     out_ref,
     gus_ref,
-    downs_ref,
     qkvs_ref,
     outs_ref,
     sums_ref,
     *scratch,
 ):
     p = place_of(ctx_size, wa_size)
-    gu_in, rows_ref, dw_in, share_ref, do_in, out_share_ref = scratch[8:14]
-    do_parts, part_send, part_recv = scratch[43:46]
-    wa_gains, ctx_gains, local = scratch[14:17]
-    gu_sems, dw_sems, do_sems = scratch[17:19], scratch[19:21], scratch[21:23]
-    wa_sems, ctx_sems = scratch[23:25], scratch[25:27]
-    down_plane, gu_plane, qkv_plane, out_plane = (scratch[i : i + 4] for i in (27, 31, 35, 39))
+    rows_ref, dw_in, share_ref, do_in, out_share_ref = scratch[8:13]
+    wa_gains, ctx_gains, local = scratch[13:16]
+    dw_sems, do_sems = scratch[16:18], scratch[18:20]
+    wa_sems, ctx_sems = scratch[20:22], scratch[22:24]
+    gu_plane, qkv_plane, out_plane = (scratch[i : i + 4] for i in (24, 28, 32))
     peers = [lax.rem(p.ctx + i, ctx_size) for i in range(1, ctx_size)]
     greet(peers, p.up[1:])
     locals_ = []
@@ -1157,10 +1267,10 @@
             for s in range(1, wa_size)
         ]
 
-    def add_up(source, found, into, step):
+    def add_up(found, into, step):
         def one(i, carried):
             place = pl.ds(pl.multiple_of(i * step, step), step)
-            total = source(p.wa)[place, :].astype(F32)
+            total = found[0, place, :].astype(F32)
             for s in range(1, wa_size):
                 total = total + found[s, place, :].astype(F32)
             into[place, :] = total.astype(BF)
@@ -1168,45 +1278,37 @@
 
         lax.fori_loop(0, into.shape[0] // step, one, 0)
 
-    deal = [
-        send(
-            gu_ref.at[:, p.up[s]], gu_in.at[p.wa], gu_sems[0].at[s], gu_sems[1].at[s], wa=p.up[s]
-        )
-        for s in range(1, wa_size)
+    per_wa = ctx_size // wa_size
+
+    def do_block(device):
+        return do_parts.at[pl.ds(device * per_wa, per_wa)]
+
+    do_copies = over_wa(do_block, do_in, do_sems)
+    own_loads = [
+        pltpu.make_async_copy(do_block(p.wa), do_in.at[0], local.at[3]),
+        pltpu.make_async_copy(dw_ref.at[p.wa], dw_in.at[0], local.at[4]),
     ]
+    for copy in own_loads:
+        copy.start()
     rows = x_ref.shape[0]
+    qkv_columns = grads_ref.shape[1]
 
     def part_of(device):
         place = pl.ds(pl.multiple_of(device * rows, rows), rows)
         return lax.dot_general(
             grads_ref[place, :],
-            w_ref[...],
+            w_ref[:, :qkv_columns],
             (((1,), (1,)), ((), ())),
             preferred_element_type=F32,
         )
 
     scatter = Scatter(p, part_of, scratch[:8])
     scatter.start()
-    head_cols = do_ref.shape[0]
-
-    def do_part(device):
-        columns = pl.ds(pl.multiple_of(device * head_cols, head_cols), head_cols)
-        return do_ref.at[:, columns]
-
-    part_copies = exchange_plane(
-        [p.ctx] + peers, do_part, lambda d: do_parts.at[d], part_send, part_recv
-    )
-    keep(do_part(p.ctx), do_parts.at[p.ctx])
-    down_spread = spread_of(down_ref, downs_ref, down_plane)
     wa_gains[p.wa] = gains_ref[...]
     small = [
         send(gains_ref, wa_gains.at[p.wa], wa_sems[0].at[s], wa_sems[1].at[s], wa=p.up[s])
         for s in range(1, wa_size)
     ]
-    gu_in[p.wa] = gu_ref[:, p.wa]
-    for copy in deal:
-        copy.wait_recv()
-    dw_copies = over_wa(lambda d: dw_ref.at[d], dw_in, dw_sems)
     total_columns = rows_ref.shape[1] // 2
     own_columns = total_columns // wa_size
     for i in range(wa_size):
@@ -1225,13 +1327,24 @@
         send(own_gain, own_gain, ctx_sems[0].at[i], ctx_sems[1].at[i], ctx=peer)
         for i, peer in enumerate(peers)
     ]
+    for copy in do_copies:
+        copy.wait_recv()
+    dw_copies = over_wa(lambda d: dw_ref.at[d], dw_in, dw_sems)
+    own_loads[0].wait()
+    for i in range(per_wa):
+        place = pl.ds(i * do_parts.shape[1], do_parts.shape[1])
+        total = do_in[0, i].astype(F32)
+        for s in range(1, wa_size):
+            total = total + do_in[s, i].astype(F32)
+        out_share_ref[place, :] = total.astype(BF)
+    out_spread = spread_of(out_share_ref, outs_ref, out_plane)
     x = x_ref[...].astype(F32)
     scale = lax.rsqrt(jnp.mean(x * x, axis=-1, keepdims=True) + EPSILON)
     d_normed = scatter.total()
     out_ref[...] = norm_back(
         x, scale, gain_ref[...], d_normed, dh_ref[...].astype(F32)
     ).astype(BF)
-    for _ in down_spread.arrivals():
+    for _ in out_spread.arrivals():
         pass
     for _ in gu_spread.arrivals():
         pass
@@ -1243,71 +1356,49 @@
     sums_ref[...] = total_gain
     for copy in dw_copies:
         copy.wait_recv()
-    for copy in part_copies:
-        copy.wait_recv()
-    locals_[0].wait()
-    per_wa = ctx_size // wa_size
-
-    def do_block(device):
-        return do_parts.at[pl.ds(device * per_wa, per_wa)]
-
-    do_copies = over_wa(do_block, do_in, do_sems)
-    add_up(lambda d: dw_ref.at[d], dw_in, share_ref, 16)
+    own_loads[1].wait()
+    add_up(dw_in, share_ref, 16)
     qkv_spread = spread_of(share_ref, qkvs_ref, qkv_plane)
-    for copy in do_copies:
-        copy.wait_recv()
-    for i in range(per_wa):
-        place = pl.ds(i * head_cols, head_cols)
-        total = do_parts[p.wa * per_wa + i].astype(F32)
-        for s in range(1, wa_size):
-            total = total + do_in[s, i].astype(F32)
-        out_share_ref[place, :] = total.astype(BF)
-    out_spread = spread_of(out_share_ref, outs_ref, out_plane)
     for _ in qkv_spread.arrivals():
         pass
-    for _ in out_spread.arrivals():
-        pass
     scatter.finish()
-    for spread in (down_spread, gu_spread, qkv_spread, out_spread):
+    for spread in (gu_spread, qkv_spread, out_spread):
         spread.finish()
-    for copy in deal + dw_copies + do_copies + part_copies:
+    for copy in dw_copies + do_copies:
         copy.wait_send()
-    for copy in locals_[1:]:
+    for copy in locals_:
         copy.wait()
 
 
-def close(grads, w, x_own, gain, dh, gu, dw, do, down, gains_own, columns, ctx_size, wa_size):
+def close(grads, w, x_own, gain, dh, gu, dw, do, gains_own, columns, ctx_size, wa_size):
     rows, width = x_own.shape
     vmem = pl.BlockSpec(memory_space=pltpu.VMEM)
     anywhere = pl.BlockSpec(memory_space=pl.ANY)
     gu_shape = (gu.shape[2], columns)
-    out_shape = (width // wa_size, do.shape[0])
-    shapes = [gu_shape, down.shape, dw.shape[1:], out_shape]
+    out_shape = (width // wa_size, do.shape[1])
+    shapes = [gu_shape, dw.shape[1:], out_shape]
     gains = (2, width)
     return pl.pallas_call(
         functools.partial(close_kernel, ctx_size, wa_size),
         out_shape=(jax.ShapeDtypeStruct((rows, width), BF),)
         + tuple(jax.ShapeDtypeStruct((ctx_size,) + shape, BF) for shape in shapes)
         + (jax.ShapeDtypeStruct(gains, F32),),
-        in_specs=[vmem] * 10,
-        out_specs=[vmem] + [anywhere] * 4 + [vmem],
+        in_specs=[vmem] * 6 + [anywhere] * 2 + [vmem],
+        out_specs=[vmem] + [anywhere] * 3 + [vmem],
         scratch_shapes=scatter_scratch(ctx_size, rows, width)
         + [
-            pltpu.VMEM((wa_size, 2) + gu.shape[2:], BF),
             pltpu.VMEM(gu_shape, BF),
             pltpu.VMEM(dw.shape, BF),
             pltpu.VMEM(dw.shape[1:], BF),
-            pltpu.VMEM((wa_size, ctx_size // wa_size, do.shape[0], do.shape[0]), BF),
+            pltpu.VMEM((wa_size, ctx_size // wa_size) + do.shape[1:], BF),
             pltpu.VMEM(out_shape, BF),
             pltpu.VMEM((wa_size,) + gains, F32),
             pltpu.VMEM((ctx_size,) + gains, F32),
             pltpu.SemaphoreType.DMA((5,)),
         ]
-        + [pltpu.SemaphoreType.DMA((wa_size,))] * 8
+        + [pltpu.SemaphoreType.DMA((wa_size,))] * 6
         + [pltpu.SemaphoreType.DMA((ctx_size,))] * 2
-        + plane_sems(ctx_size) * 4
-        + [pltpu.VMEM((ctx_size, do.shape[0], do.shape[0]), BF)]
-        + [pltpu.SemaphoreType.DMA((ctx_size,))] * 2,
+        + plane_sems(ctx_size) * 3,
         compiler_params=pltpu.CompilerParams(
             collective_id=3, has_side_effects=True, vmem_limit_bytes=VMEM_LIMIT
         ),
@@ -1315,7 +1406,7 @@
             flops=2 * grads.size * width, bytes_accessed=400_000_000, transcendentals=0
         ),
         name="close",
-    )(grads, w, x_own, gain, dh, gu, dw, do, down, gains_own)
+    )(grads, w, x_own, gain, dh, gu, dw, do, gains_own)
 
 
 def widen(blocks, columns, order, step):
@@ -1361,68 +1452,48 @@
     ff_own = w_down.shape[0]
     piece_rows = wa_rows // ctx_size
 
-    block_ids = jnp.arange(block_total, dtype=jnp.int32)
-    inverse = jnp.sum(
-        jnp.where(block_order[None, :] == block_ids[:, None], block_ids[None, :], 0), axis=1
-    )
-
-    qkv_slice = jnp.concatenate(
+    own_cols = jnp.concatenate(
         [
             lax.dynamic_slice_in_dim(w_qkv, part * width + ctx_index * head_cols, head_cols, 1)
             for part in range(3)
-        ],
+        ]
+        + [lax.dynamic_slice_in_dim(w_out, ctx_index * head_cols, head_cols, 1)],
         axis=1,
     )
-    dealt, qkv_cols = gather_both(tokens[0], qkv_slice, ctx_size, wa_size)
+    dealt, all_cols, gu_send = gather_both(
+        tokens[0], own_cols, w_gate_up, ff_own, ctx_size, wa_size
+    )
     dealt = dealt.reshape(group_rows, width)
-    qkv_cols = qkv_cols.reshape(width, 3 * head_cols)
-    out_slice = lax.dynamic_slice_in_dim(w_out, ctx_index * head_cols, head_cols, 1)
-    out_cols = gather_rows(out_slice, "wa")
-    out_cols = out_cols.reshape(ctx_size, head_cols, head_cols)
-    gu_piece = lax.dynamic_slice_in_dim(w_gate_up, ctx_index * piece_rows, piece_rows, 0)
-    hidden_own = -(-ff_own // 128) * 128
-    gu_send = jnp.pad(
-        jnp.stack(
-            [
-                jnp.stack(
-                    [
-                        gu_piece[:, first + to * ff_own : first + (to + 1) * ff_own]
-                        for first in (0, ff_total)
-                    ]
-                )
-                for to in range(wa_size)
-            ]
-        ),
-        ((0, 0), (0, 0), (0, 0), (0, hidden_own - ff_own)),
-    )
-
-    positions = jnp.arange(group_rows, dtype=jnp.int32)
-    segments = (positions >= first_length).astype(jnp.int32)
-    cosine, sine = rotary_tables(positions - segments * first_length)
-    first_block = (ctx_index * own_blocks)[None].astype(jnp.int32)
-    act_one, own_given = arrange(inverse, first_block, dealt, norm1_gain[None, :], own_blocks)
-    query_b, key_b, value_b, mixed_b, probs_b, gu_mine, out_rows = attend(
+    all_cols = all_cols.reshape(width, 4 * head_cols)
+
+    rows_given = jnp.arange(group_rows, dtype=jnp.int32)
+    segments = (rows_given >= first_length).astype(jnp.int32)
+    in_block = jnp.arange(BLOCK, dtype=jnp.int32)
+    rows_dealt = (block_order[:, None] * BLOCK + in_block[None, :]).reshape(group_rows)
+    unpick = (rows_dealt[:, None] == rows_given[None, :]).astype(BF)
+    pick = (rows_given[:, None] == rows_dealt[None, :]).astype(BF)
+    given_tables = rotary_tables(rows_given - segments * first_length)
+    dealt_tables = rotary_tables(
+        rows_dealt - (rows_dealt >= first_length).astype(jnp.int32) * first_length
+    )
+    act_one_t, own_given, query_b, key_b, value_b, mixed_b, probs_b, gu_mine, out_rows = attend(
         segments,
-        act_one,
-        qkv_cols,
-        cosine,
-        sine,
+        dealt,
+        all_cols,
+        norm1_gain[None, :],
+        pick,
+        *dealt_tables,
         gu_send,
-        out_cols,
         ctx_size,
         wa_size,
     )
     gain_two = norm2_gain[None, :]
-    hidden, acts, gu_weight = out_project(
-        mixed_b, out_rows, own_given, gain_two, gu_mine, ctx_size, wa_size
-    )
-    gu_weight = gu_weight.reshape(2, width, hidden_own)
+    hidden, acts, grads_all, gu_weight = out_project(
+        mixed_b, out_rows, own_given, gain_two, grad_out[0], gu_mine, ctx_size, wa_size
+    )
+    gu_weight = gu_weight.reshape(2, width, gu_weight.shape[4])
     act_two = acts.reshape(wa_size * tok_rows, width)
-    early = lax.optimization_barrier((grad_out[0], mixed_b))[0]
-    grads_all = lax.all_gather(early, "wa", axis=0)
-    cotangent = jnp.concatenate(
-        [take(grads_all, (wa_index - s) % wa_size) for s in range(wa_size)], axis=0
-    )
+    cotangent = grads_all.reshape(wa_size * tok_rows, width)
 
     d_act, mlp_parts, act_t, d_gu, inner_t = mlp(act_two, cotangent, gu_weight, w_down)
     d_branches, gain_two_part, out_given, gu_piece_grad, down_piece_grad = turn(
@@ -1440,34 +1511,34 @@
         wa_size,
     )
     d_branch_b = d_branches.reshape(group_rows, width)
-    own_order = lax.dynamic_slice_in_dim(block_order, ctx_index * own_blocks, own_blocks)
-    d_qkv_b, dealt_qkv, d_out_part, d_hidden_dealt = attend_back(
-        inverse,
-        own_order,
+    dealt_qkv, d_hidden_dealt, qkv_parts, gain_column, out_parts, gu_pieces, downs = attend_back(
         d_branch_b,
         out_rows,
         mixed_b,
         query_b,
         key_b,
         value_b,
+        *given_tables,
         probs_b,
-        cosine,
-        sine,
-    )
-    qkv_grad = dot_left_t(act_one, d_qkv_b)
-    gain_one_part = jnp.sum(qkv_grad * qkv_cols.astype(F32), axis=1) / norm1_gain
-    qkv_parts = qkv_grad.astype(BF).reshape(wa_size, wa_rows, 3 * head_cols)
-    d_tokens, gus, downs, qkvs, outs, gain_sums = close(
+        act_one_t,
+        all_cols,
+        unpick,
+        gu_piece_grad.reshape((2, wa_size) + gu_piece_grad.shape[1:]),
+        down_piece_grad,
+        ctx_size,
+        wa_size,
+    )
+    gain_one_part = gain_column.reshape(1, width) / norm1_gain[None, :]
+    d_tokens, gus, qkvs, outs, gain_sums = close(
         dealt_qkv,
-        qkv_cols,
+        all_cols,
         tokens[0],
         norm1_gain[None, :],
         d_hidden_dealt,
-        gu_piece_grad.reshape(2, wa_size, piece_rows, hidden_own),
+        gu_pieces,
         qkv_parts,
-        d_out_part,
-        down_piece_grad,
-        jnp.concatenate([gain_one_part[None, :], gain_two_part], axis=0),
+        out_parts,
+        jnp.concatenate([gain_one_part, gain_two_part], axis=0),
         2 * ff_total,
         ctx_size,
         wa_size,

time: 630 us -> 592 us (0.940)
  Pallas kernels: 567 us -> 552 us
  between operations: 14.5 us -> 0.96 us
  matrix products: 7.98 us -> 0 us
  local copies, waits for them, and re-layouts: 10.1 us -> 3.51 us
    pallas_call x1, Pallas kernels: 178 us -> 134 us  [close(): pl.pallas_call(functools.partial(close_kernel, ctx_size, wa_size), out_sh...]
    pallas_call x3 -> x2, Pallas kernels: 95.2 us -> 119 us  [the longest x1 72.9 us: gather_both(): pl.pallas_call(functools.partial(gather_kernel, ctx_size, wa_size, cuts,...]
    dot_general x1 -> x0, matrix products: 7.98 us -> none  [dot_left_t(): lax.dot_general(left, right, (((0,), (0,)), ((), ())), preferred_element_...]
  transfers between devices with their start and end apart: 2 -> 0, of which waited for: 0 -> 0; matrix products, arithmetic and copies ran while one was open for 2% -> 0% of each run, Pallas kernels for 27% -> 0%
where the time goes in v5:
time: 592 us; the launch traced here: 585 us
  Pallas kernels  552 us (93%)
  other arithmetic  28.1 us (5%)
    pallas_call x1, Pallas kernels, close(): pl.pallas_call(functools.partial(close_kernel, ctx_size, wa_size), out_sh...  134 us
    pallas_call x1, Pallas kernels, turn(): pl.pallas_call(functools.partial(turn_kernel, ctx_size, wa_size), out_sha...  107 us
    pallas_call x1, Pallas kernels, out_project(): pl.pallas_call(functools.partial(out_kernel, ctx_size, wa_size), out_shap...  93.9 us
    pallas_call x1, Pallas kernels, gather_both(): pl.pallas_call(functools.partial(gather_kernel, ctx_size, wa_size, cuts,...  72.9 us
    pallas_call x1, Pallas kernels, attend_back(): pl.pallas_call(functools.partial(attend_back_kernel, ctx_size, wa_size, h...  46.4 us
    pallas_call x1, Pallas kernels, attend(): pl.pallas_call(functools.partial(attend_kernel, ctx_size, wa_size, heads)...  43.7 us
    pallas_call x1, Pallas kernels, mlp(): pl.pallas_call(mlp_kernel, out_shape=(jax.ShapeDtypeStruct((tokens, width...  34.7 us
    pallas_call x3, Pallas kernels, widen(): pl.pallas_call(body, out_shape=jax.ShapeDtypeStruct((rows, count * own),...  19.6 us

profile of v5, /device:TPU:9, one launch (start us, length us, event | category | flops | bytes accessed | tf_op | source)
XLA Modules:
  0.0 584.5 jit_solution(15511632071430006031)
XLA Ops:
  0.6 1.3 constant_dynamic-slice_fusion.3
  1.9 1.1 pad_maximum_fusion.w_ref
  3.0 72.9 %gather_both.1 = (bf16[8,128,2048]{2,1,0:T(8,128)(2,1)}, bf16[4,512,1024]{2,1,0:T(8,128)(2,1)}, bf16[4,2,64,1408]{3,2,1,0:T(8,128)(2,1)}) custom-call(bf16[128,2048]{1,0:T(8,128)(2,1)} %bitcast.40, bf16[512,1024]{1,0:T(8,128)(2,1)} %pad_maximum_fusion.w_ref, bf16[512,11008]{1,0:T(8,128)(2,1)} %gu_ref.1), custom_call_target="tpu_custom_call" | custom-call | bytes 200000000 | tf_op jit(solution)/shard_map/gather_both/pallas_call | solution.py:385
  76.0 0.0 copy-done.6
  76.0 0.0 copy-done.5
  76.0 0.1 subtract_convert_fusion
  76.1 3.7 fusion.4
  79.8 1.0 pad_maximum_fusion.2.sin_ref
  80.9 1.0 pad_maximum_fusion.1.cos_ref
  81.8 0.1 add_bitcast_fusion
  81.9 2.6 fusion.1
  84.5 0.9 fusion.2.row_seg_ref
  85.4 0.6 compare_convert_fusion.column_seg_ref
  86.0 43.7 %attend.1 = (bf16[2048,1024]{1,0:T(8,128)(2,1)}, bf16[128,2048]{1,0:T(8,128)(2,1)}, bf16[1024,256]{1,0:T(8,128)(2,1)}, bf16[1024,256]{1,0:T(8,128)(2,1)}, bf16[1...) custom-call(s32[1024,1]{1,0:T(8,128)} %fusion.2.row_seg_ref, ...), custom_call_target="tpu_custom_call" | custom-call | flops 3221225472 | bytes 100000000 | tf_op jit(solution)/shard_map/attend/pallas_call | solution.py:539
  129.8 93.9 %out_project.1 = (f32[128,2048]{1,0:T(8,128)}, bf16[4,128,2048]{2,1,0:T(8,128)(2,1)}, bf16[4,128,2048]{2,1,0:T(8,128)(2,1)}, bf16[2,4,8,64,1408]{4,3,2,1,0:T(8,128)(2,1)}) custom-call(bf16[1024,256]{1,0:T(8,128)(2,1)} %get-tuple-element.49.mixed_ref.o_ref, bf16[256,2048]{1,0:T(8,128)(2,1)} %get-tuple-element.50.w_ref, ...), custom_call_target="tpu_custom_call" | custom-call | flops 1073741824 | bytes 200000000 | tf_op jit(solution)/shard_map/out_project/pallas_call | solution.py:873
  223.7 34.7 %mlp.1 = (bf16[512,2048]{1,0:T(8,128)(2,1)}, bf16[512,2048]{1,0:T(8,128)(2,1)}, bf16[2048,512]{1,0:T(8,128)(2,1)}, bf16[2,512,1408]{2,1,0:T(8,128)(2,1)}, bf16[1408,512]{1,0:T(8,128)(2,1)}) custom-call(bf16[512,2048]{1,0:T(8,128)(2,1)} %bitcast.56, bf16[512,2048]{1,0:T(8,128)(2,1)} %bitcast.34, bf16[2,2048,1408]{2,1,0:T(8,128)(2,1)} %bitcast.55, ...), custom_call_target="tpu_custom_call" | custom-call | flops 17716740096 | bytes 50000000 | tf_op jit(solution)/shard_map/mlp/pallas_call | solution.py:979
  258.4 106.6 %turn.1 = (bf16[8,128,2048]{2,1,0:T(8,128)(2,1)}, f32[1,2048]{1,0:T(1,128)}, bf16[128,2048]{1,0:T(8,128)(2,1)}, bf16[8,64,1408]{2,1,0:T(8,128)(2,1)}, bf16[1376,256]{1,0:T(8,128)(2,1)}) custom-call(bf16[4,128,2048]{2,1,0:T(8,128)(2,1)} %bitcast.36, bf16[4,128,2048]{2,1,0:T(8,128)(2,1)} %bitcast.37, f32[128,2048]{1,0:T(8,128)} %get-tuple-element.58.hidden_ref, ...), custom_call_target="tpu_custom_call" | custom-call | bytes 200000000 | tf_op jit(solution)/shard_map/turn/pallas_call | solution.py:1176
  365.0 1.0 pad_maximum_fusion.4.sin_ref
  366.0 1.0 pad_maximum_fusion.3.cos_ref
  367.0 46.4 %attend_back.1 = (bf16[1024,768]{1,0:T(8,128)(2,1)}, bf16[128,2048]{1,0:T(8,128)(2,1)}, bf16[4,512,768]{2,1,0:T(8,128)(2,1)}, f32[2048,1]{1,0:T(8,128)}, bf16[8,...) custom-call(bf16[1024,2048]{1,0:T(8,128)(2,1)} %bitcast.33, ...), custom_call_target="tpu_custom_call" | custom-call | flops 5368709120 | bytes 100000000 | tf_op jit(solution)/shard_map/attend_back/pallas_call | solution.py:751
  413.5 1.6 reduce
  415.0 0.0 copy-done.2
  415.0 0.0 copy-done.4
  415.1 0.6 pad_maximum_fusion.5.gains_ref
  415.7 134.1 %close.1 = (bf16[128,2048]{1,0:T(8,128)(2,1)}, bf16[8,64,11008]{2,1,0:T(8,128)(2,1)}, bf16[8,512,768]{2,1,0:T(8,128)(2,1)}, bf16[8,512,256]{2,1,0:T(8,128)(2,1)}, f32[2,2048]{1,0:T(2,128)}) custom-call(bf16[1024,768]{1,0:T(8,128)(2,1)} %get-tuple-element.71.grads_ref, bf16[2048,1024]{1,0:T(8,128)(2,1)} %bitcast.31, bf16[128,2048]{1,0:T(8,128)(2,1)} %bitcast.41, ...), custom_call_target="tpu_custom_call" | custom-call | flops 3221225472 | bytes 400000000 | tf_op jit(solution)/shard_map/close/pallas_call | solution.py:1381
  549.8 12.7 %bitcast_convert_fusion = f32[512,11008]{1,0:T(8,128)} fusion(bf16[8,64,11008]{2,1,0:T(8,128)(2,1)} %get-tuple-element.82), kind=kLoop, calls=%fused_computation | loop fusion | flops 5636096 | bytes 33816576 | tf_op jit(solution)/shard_map/convert_element_type | solution.py:1546
  562.5 8.8 %widen.3 = f32[512,6144]{1,0:T(8,128)} custom-call(bf16[8,512,768]{2,1,0:T(8,128)(2,1)} %get-tuple-element.80.block_ref), custom_call_target="tpu_custom_call" | custom-call | tf_op jit(solution)/shard_map/widen/pallas_call | solution.py:1424
  571.3 4.2 widen.4
  575.5 0.6 fusion.5
  576.1 6.6 %widen.5 = f32[1376,2048]{1,0:T(8,128)} custom-call(bf16[8,1376,256]{2,1,0:T(8,128)(2,1)} %get-tuple-element.83.block_ref), custom_call_target="tpu_custom_call" | custom-call | tf_op jit(solution)/shard_map/widen/pallas_call | solution.py:1424
  582.8 0.8 copy.20
  583.6 0.8 copy.21
  (13 shorter events, 0.0 us)
Async XLA Ops:
  3.0 72.9 %copy-start.6 = (s32[1,8]{1,0:T(1,128)S(1)}, s32[1,8]{1,0:T(1,128)}, u32[]{:S(2)}) copy-start(s32[1,8]{1,0:T(1,128)} %param.12) | copy-start | bytes 100
  3.0 73.0 %copy-start.5 = (s32[1,2]{1,0:T(1,128)S(1)}, s32[1,2]{1,0:T(1,128)}, u32[]{:S(2)}) copy-start(s32[1,2]{1,0:T(1,128)} %param.11) | copy-start | bytes 28
  367.0 48.0 %copy-start.2 = (f32[2048]{0:T(1024)S(1)}, f32[2048]{0:T(1024)}, u32[]{:S(2)}) copy-start(f32[2048]{0:T(1024)} %param.13) | copy-start | bytes 24580
  367.0 48.0 %copy-start.4 = (f32[1,2048]{1,0:T(1,128)S(1)}, f32[1,2048]{1,0:T(1,128)}, u32[]{:S(2)}) copy-start(f32[1,2048]{1,0:T(1,128)} %get-tuple-element.77) | copy-start | bytes 24580
  571.3 4.2 copy-start.3
  576.1 6.6 %copy-start = (bf16[128,2048]{1,0:T(8,128)(2,1)S(1)}, bf16[128,2048]{1,0:T(8,128)(2,1)}, u32[]{:S(2)}) copy-start(bf16[128,2048]{1,0:T(8,128)(2,1)} %get-tuple-element.62) | copy-start | bytes 1572868
  576.1 7.4 %copy-start.1 = (bf16[128,2048]{1,0:T(8,128)(2,1)S(1)}, bf16[128,2048]{1,0:T(8,128)(2,1)}, u32[]{:S(2)}) copy-start(bf16[128,2048]{1,0:T(8,128)(2,1)} %get-tuple-element.78) | copy-start | bytes 1572868

commit v6 on v5

--- a/solution.py
+++ b/solution.py
@@ -4,6 +4,7 @@
 
 import jax
 import jax.numpy as jnp
+import numpy as np
 from jax import lax
 from jax.experimental import pallas as pl
 from jax.experimental.pallas import tpu as pltpu
@@ -20,17 +21,6 @@
 VMEM_LIMIT = 60 * 1024 * 1024
 ATTEND_ROWS = 256
 CHUNK = 256
-
-
-def rotary_tables(seq_pos):
-    half_width = HEAD // 2
-    inverse_freq = jnp.power(10000.0, -2.0 * jnp.arange(half_width, dtype=F32) / HEAD)
-    angles = seq_pos.astype(F32)[:, None] * inverse_freq[None, :]
-    cosine, sine = jnp.cos(angles), jnp.sin(angles)
-    return (
-        jnp.concatenate([cosine, cosine], axis=-1),
-        jnp.concatenate([-sine, sine], axis=-1),
-    )
 
 
 MESH = pl.DeviceIdType.MESH
@@ -311,7 +301,21 @@
 
 
 def gather_kernel(
-    ctx_size, wa_size, cuts, own_columns, x_ref, w_ref, gu_ref, xs_ref, ws_ref, cut_ref, *scratch
+    ctx_size,
+    wa_size,
+    cuts,
+    own_columns,
+    x_ref,
+    w_ref,
+    gu_ref,
+    dealt_column_ref,
+    length_ref,
+    freq_ref,
+    xs_ref,
+    ws_ref,
+    cut_ref,
+    tables_ref,
+    *scratch,
 ):
     p = place_of(ctx_size, wa_size)
     ring_send, ring_recv, local, piece_ref = scratch[4:]
@@ -358,6 +362,22 @@
                 cut_ref[to, part, :, own_columns:] = jnp.zeros(
                     (piece_rows, hidden - own_columns), BF
                 )
+    group_rows = tables_ref.shape[2]
+    table_rows = min(group_rows, 256)
+    first_length = length_ref[:, 0:1]
+    lane = lax.broadcasted_iota(jnp.int32, (table_rows, HEAD), 1)
+    sign = jnp.where(lane < HEAD // 2, -1.0, 1.0)
+
+    def tables(i, carried):
+        place = pl.ds(pl.multiple_of(i * table_rows, table_rows), table_rows)
+        given = lax.broadcasted_iota(jnp.int32, (table_rows, 1), 0) + i * table_rows
+        for kind, row in enumerate((dealt_column_ref[place, :], given)):
+            position = row - jnp.where(row >= first_length, first_length, 0)
+            angle = position.astype(F32) * freq_ref[...]
+            tables_ref[kind, 0, place, :] = jnp.cos(angle)
+            tables_ref[kind, 1, place, :] = jnp.sin(angle) * sign
+        return carried
+
     late = []
     for step in range(1, wa_size):
         for i in range(cuts):
@@ -371,6 +391,8 @@
         if step == 1:
             for _ in spread.arrivals():
                 pass
+        if step == 2 or wa_size == 2:
+            lax.fori_loop(0, group_rows // table_rows, tables, 0)
     for copy in late:
         copy.wait_send()
     spread.finish()
@@ -378,19 +400,23 @@
         copy.wait()
 
 
-def gather_both(x, w, gu, own_columns, ctx_size, wa_size, cuts=4):
+def gather_both(x, w, gu, dealt_column, length, own_columns, ctx_size, wa_size, cuts=4):
     anywhere = pl.BlockSpec(memory_space=pl.ANY)
     piece_rows = w.shape[0] // ctx_size
     hidden = -(-own_columns // 128) * 128
+    half = np.arange(HEAD) % (HEAD // 2)
+    freq = (10000.0 ** (-2.0 * half / HEAD)).astype(np.float32)[None, :]
+    vmem = pl.BlockSpec(memory_space=pltpu.VMEM)
     return pl.pallas_call(
         functools.partial(gather_kernel, ctx_size, wa_size, cuts, own_columns),
         out_shape=(
             jax.ShapeDtypeStruct((ctx_size,) + x.shape, x.dtype),
             jax.ShapeDtypeStruct((wa_size,) + w.shape, w.dtype),
             jax.ShapeDtypeStruct((wa_size, 2, piece_rows, hidden), BF),
+            jax.ShapeDtypeStruct((2, 2, dealt_column.shape[0], HEAD), F32),
         ),
-        in_specs=[anywhere] * 3,
-        out_specs=[anywhere] * 2 + [pl.BlockSpec(memory_space=pltpu.VMEM)],
+        in_specs=[anywhere] * 3 + [vmem] * 3,
+        out_specs=[anywhere] * 2 + [vmem] * 2,
         scratch_shapes=plane_sems(ctx_size)
         + [pltpu.SemaphoreType.DMA((wa_size - 1, cuts))] * 2
         + [pltpu.SemaphoreType.DMA((3,)), pltpu.VMEM((piece_rows, gu.shape[1]), BF)],
@@ -399,7 +425,7 @@
         ),
         cost_estimate=pl.CostEstimate(flops=0, bytes_accessed=200_000_000, transcendentals=0),
         name="gather_both",
-    )(x, w, gu)
+    )(x, w, gu, dealt_column, length, jnp.asarray(freq))
 
 
 def exchange_plane(peers, source, target, send_sem, recv_sem):
@@ -415,14 +441,12 @@
     ctx_size,
     wa_size,
     heads,
-    row_seg_ref,
-    column_seg_ref,
+    length_ref,
     x_ref,
     w_ref,
     gain_ref,
-    pick_ref,
-    cos_ref,
-    sin_ref,
+    dealt_row_ref,
+    tables_ref,
     gu_ref,
     act_t_ref,
     own_ref,
@@ -472,7 +496,7 @@
         act = (x * scale * gain_ref[...]).astype(BF)
         act_t_ref[:, place] = act.T
         made = jnp.dot(act, w_ref[:, : 3 * head_cols], preferred_element_type=F32)
-        cosine, sine = cos_ref[place, :], sin_ref[place, :]
+        cosine, sine = tables_ref[0, place, :], tables_ref[1, place, :]
         for head in range(2 * heads):
             columns = slice(head * HEAD, (head + 1) * HEAD)
             u = made[:, columns]
@@ -484,9 +508,13 @@
 
     lax.fori_loop(0, rows // step, project, 0)
 
+    def pick(first, count):
+        given_row = lax.broadcasted_iota(jnp.int32, (count, rows), 0) + first
+        return jnp.where(given_row == dealt_row_ref[...], 1.0, 0.0).astype(BF)
+
     def put_in_order(i, carried):
         place = pl.ds(pl.multiple_of(i * step, step), step)
-        given = jnp.dot(pick_ref[place, :], dealt_ref[...], preferred_element_type=F32).astype(BF)
+        given = jnp.dot(pick(i * step, step), dealt_ref[...], preferred_element_type=F32).astype(BF)
         q_ref[place, :] = given[:, :head_cols]
         k_ref[place, :] = given[:, head_cols : 2 * head_cols]
         v_ref[place, :] = given[:, 2 * head_cols :]
@@ -494,20 +522,23 @@
 
     lax.fori_loop(0, rows // step, put_in_order, 0)
     own_rows = own_ref.shape[0]
-    own_place = pl.ds(pl.multiple_of(ctx * own_rows, own_rows), own_rows)
     own_ref[...] = jnp.dot(
-        pick_ref[own_place, :], x_ref[...], preferred_element_type=F32
+        pick(ctx * own_rows, own_rows), x_ref[...], preferred_element_type=F32
     ).astype(BF)
+    first_length = length_ref[:, 0:1]
     for i in range(rows // step):
         here = slice(i * step, (i + 1) * step)
         keys = (i + 1) * step
         row = lax.broadcasted_iota(jnp.int32, (step, keys), 0) + i * step
         column = lax.broadcasted_iota(jnp.int32, (step, keys), 1)
-        allowed = (column <= row) & (row_seg_ref[here, :] == column_seg_ref[:, :keys])
+        late_row = jnp.where(row >= first_length, 1, 0)
+        late_column = jnp.where(column >= first_length, 1, 0)
+        allowed = (column <= row) & (late_row == late_column)
         if rows > WINDOW:
             allowed = allowed & (row - column < WINDOW)
-        for head in range(heads):
-            columns = slice(head * HEAD, (head + 1) * HEAD)
+
+        def one_head(head, carried):
+            columns = pl.ds(pl.multiple_of(head * HEAD, HEAD), HEAD)
             scores = lax.dot_general(
                 q_ref[here, columns],
                 k_ref[:keys, columns],
@@ -519,17 +550,21 @@
             weights = jnp.exp(scores - largest)
             total = jnp.sum(weights, axis=-1, keepdims=True)
             probs = (weights * (1.0 / total)).astype(BF)
-            prob_ref[head, here, :keys] = probs
+            prob_rows = pl.ds(pl.multiple_of(head * rows + i * step, step), step)
+            prob_ref[prob_rows, :keys] = probs
             o_ref[here, columns] = jnp.dot(
                 probs, v_ref[:keys, columns], preferred_element_type=F32
             ).astype(BF)
+            return carried
+
+        lax.fori_loop(0, heads, one_head, 0)
     own.wait()
     own_out.wait()
     for copy in deal + deal_out:
         copy.wait()
 
 
-def attend(segments, x, w, gain, pick, cosine, sine, gu, ctx_size, wa_size):
+def attend(length, x, w, gain, dealt_rows, tables, gu, ctx_size, wa_size):
     rows, width = x.shape
     head_cols = w.shape[1] // 4
     heads = head_cols // HEAD
@@ -545,11 +580,11 @@
             heads_shape,
             heads_shape,
             heads_shape,
-            jax.ShapeDtypeStruct((heads, rows, rows), BF),
+            jax.ShapeDtypeStruct((heads * rows, rows), BF),
             jax.ShapeDtypeStruct((2, wa_size) + gu.shape[2:], BF),
             jax.ShapeDtypeStruct((head_cols, width), BF),
         ),
-        in_specs=[vmem] * 8 + [anywhere],
+        in_specs=[vmem] * 6 + [anywhere],
         out_specs=[vmem] * 7 + [anywhere] * 2,
         scratch_shapes=[pltpu.SemaphoreType.DMA((wa_size,))] * 3
         + [pltpu.SemaphoreType.DMA((ctx_size,))] * 2
@@ -561,229 +596,7 @@
             flops=2 * rows * width * 3 * head_cols, bytes_accessed=100_000_000, transcendentals=0
         ),
         name="attend",
-    )(segments[:, None], segments[None, :], x, w, gain, pick, cosine, sine, gu)
-
-
-def attend_back_kernel(
-    ctx_size,
-    wa_size,
-    heads,
-    dy_ref,
-    w_ref,
-    o_ref,
-    q_ref,
-    k_ref,
-    v_ref,
-    cos_ref,
-    sin_ref,
-    prob_any,
-    act_t_any,
-    w_all_any,
-    unpick_any,
-    gu_ref,
-    down_ref,
-    grads_ref,
-    dh_ref,
-    dw_ref,
-    gain_ref,
-    parts_ref,
-    gu_in_ref,
-    downs_ref,
-    do_ref,
-    dk_ref,
-    dv_ref,
-    d_out_ref,
-    given_ref,
-    prob_ref,
-    act_t_ref,
-    w_all_ref,
-    unpick_ref,
-    *sems,
-):
-    p = place_of(ctx_size, wa_size)
-    gu_send, gu_recv, part_send, part_recv, local = sems[4:]
-    peers = [lax.rem(p.ctx + i, ctx_size) for i in range(ctx_size)]
-    greet(peers[1:], p.up[1:])
-    deal = [
-        send(gu_ref.at[:, p.up[s]], gu_in_ref.at[p.wa], gu_send.at[s], gu_recv.at[s], wa=p.up[s])
-        for s in range(1, wa_size)
-    ]
-    half_rows = down_ref.shape[0] // 2
-    spread = Spread(
-        p,
-        down_ref,
-        lambda d: downs_ref.at[d],
-        lambda d, h: downs_ref.at[d, pl.ds(h * half_rows, half_rows)],
-        sems[:4],
-    )
-    spread.start()
-    loads = [
-        pltpu.make_async_copy(source, target, local.at[3 + i])
-        for i, (source, target) in enumerate(
-            (
-                (prob_any, prob_ref),
-                (unpick_any, unpick_ref),
-                (act_t_any, act_t_ref),
-                (w_all_any, w_all_ref),
-            )
-        )
-    ]
-    for copy in loads:
-        copy.start()
-    rows = dy_ref.shape[0]
-    step = ATTEND_ROWS
-    head_cols = heads * HEAD
-    back_scale = 1.0 / math.sqrt(HEAD)
-    d_out_ref[...] = lax.dot_general(
-        o_ref[...], dy_ref[...], (((0,), (0,)), ((), ())), preferred_element_type=F32
-    ).astype(BF)
-
-    def part_of(device):
-        place = pl.ds(pl.multiple_of(device * head_cols, head_cols), head_cols)
-        return d_out_ref.at[:, place]
-
-    part_copies = exchange_plane(peers, part_of, lambda d: parts_ref.at[d], part_send, part_recv)
-    kept = [
-        pltpu.make_async_copy(gu_ref.at[:, p.wa], gu_in_ref.at[p.wa], local.at[0]),
-        pltpu.make_async_copy(down_ref, downs_ref.at[p.ctx], local.at[1]),
-        pltpu.make_async_copy(part_of(p.ctx), parts_ref.at[p.ctx], local.at[2]),
-    ]
-    for copy in kept:
-        copy.start()
-
-    def project(i, carried):
-        place = pl.ds(pl.multiple_of(i * step, step), step)
-        do_ref[place, :] = lax.dot_general(
-            dy_ref[place, :],
-            w_ref[...],
-            (((1,), (1,)), ((), ())),
-            preferred_element_type=F32,
-        ).astype(BF)
-        return carried
-
-    lax.fori_loop(0, rows // step, project, 0)
-    loads[0].wait()
-    dk_ref[...] = jnp.zeros_like(dk_ref)
-    dv_ref[...] = jnp.zeros_like(dv_ref)
-
-    def unrotate(u, place):
-        return u * cos_ref[place, :] - pltpu.roll(u, HEAD // 2, 1) * sin_ref[place, :]
-
-    for i in range(rows // step):
-        here = slice(i * step, (i + 1) * step)
-        keys = (i + 1) * step
-        for head in range(heads):
-            columns = slice(head * HEAD, (head + 1) * HEAD)
-            d_o = do_ref[here, columns]
-            q = q_ref[here, columns]
-            probs = prob_ref[head, here, :keys]
-            d_probs = lax.dot_general(
-                d_o,
-                v_ref[:keys, columns],
-                (((1,), (1,)), ((), ())),
-                preferred_element_type=F32,
-            )
-            wide = probs.astype(F32)
-            row_dot = jnp.sum(wide * d_probs, axis=-1, keepdims=True)
-            d_scores = (wide * (d_probs - row_dot)).astype(BF)
-            d_query = jnp.dot(d_scores, k_ref[:keys, columns], preferred_element_type=F32)
-            given_ref[here, columns] = unrotate(d_query * back_scale, here).astype(BF)
-            dk_ref[:keys, columns] += lax.dot_general(
-                d_scores, q, (((0,), (0,)), ((), ())), preferred_element_type=F32
-            )
-            dv_ref[:keys, columns] += lax.dot_general(
-                probs, d_o, (((0,), (0,)), ((), ())), preferred_element_type=F32
-            )
-    for head in range(heads):
-        columns = slice(head * HEAD, (head + 1) * HEAD)
-        whole = slice(0, rows)
-        d_key = unrotate(dk_ref[:, columns] * back_scale, whole)
-        given_ref[:, head_cols + head * HEAD : head_cols + (head + 1) * HEAD] = d_key.astype(BF)
-    given_ref[:, 2 * head_cols :] = dv_ref[...].astype(BF)
-    arrivals = spread.arrivals()
-    next(arrivals)
-    next(arrivals)
-    for copy in loads[1:]:
-        copy.wait()
-
-    def put_back(i, carried):
-        place = pl.ds(pl.multiple_of(i * step, step), step)
-        grads_ref[place, :] = jnp.dot(
-            unpick_ref[place, :], given_ref[...], preferred_element_type=F32
-        ).astype(BF)
-        return carried
-
-    lax.fori_loop(0, rows // step, put_back, 0)
-    own_rows = dh_ref.shape[0]
-    own_place = pl.ds(pl.multiple_of(p.ctx * own_rows, own_rows), own_rows)
-    dh_ref[...] = jnp.dot(
-        unpick_ref[own_place, :], dy_ref[...], preferred_element_type=F32
-    ).astype(BF)
-    wa_rows = dw_ref.shape[1]
-
-    def weights(i, carried):
-        place = pl.ds(pl.multiple_of(i * wa_rows, wa_rows), wa_rows)
-        made = jnp.dot(act_t_ref[place, :], grads_ref[...], preferred_element_type=F32)
-        dw_ref[i] = made.astype(BF)
-        gain_ref[place, :] = jnp.sum(
-            made * w_all_ref[place, : 3 * head_cols].astype(F32), axis=-1, keepdims=True
-        )
-        return carried
-
-    lax.fori_loop(0, wa_size, weights, 0)
-    for _ in arrivals:
-        pass
-    for copy in kept:
-        copy.wait()
-    spread.finish()
-    for copy in deal + part_copies:
-        copy.wait()
-
-
-def attend_back(
-    dy, w_rows, o, q, k, v, cosine, sine, probs, act_t, w_all, unpick, gu, down, ctx_size, wa_size
-):
-    rows, width = dy.shape
-    head_cols = o.shape[1]
-    heads = head_cols // HEAD
-    vmem = pl.BlockSpec(memory_space=pltpu.VMEM)
-    anywhere = pl.BlockSpec(memory_space=pl.ANY)
-    return pl.pallas_call(
-        functools.partial(attend_back_kernel, ctx_size, wa_size, heads),
-        out_shape=(
-            jax.ShapeDtypeStruct((rows, 3 * head_cols), BF),
-            jax.ShapeDtypeStruct((rows // ctx_size, width), BF),
-            jax.ShapeDtypeStruct((wa_size, width // wa_size, 3 * head_cols), BF),
-            jax.ShapeDtypeStruct((width, 1), F32),
-            jax.ShapeDtypeStruct((ctx_size, head_cols, head_cols), BF),
-            jax.ShapeDtypeStruct((wa_size, 2) + gu.shape[2:], BF),
-            jax.ShapeDtypeStruct((ctx_size,) + down.shape, BF),
-        ),
-        in_specs=[vmem] * 8 + [anywhere] * 6,
-        out_specs=[vmem] * 4 + [anywhere] * 3,
-        scratch_shapes=[
-            pltpu.VMEM((rows, head_cols), BF),
-            pltpu.VMEM((rows, head_cols), F32),
-            pltpu.VMEM((rows, head_cols), F32),
-            pltpu.VMEM((head_cols, width), BF),
-            pltpu.VMEM((rows, 3 * head_cols), BF),
-            pltpu.VMEM(probs.shape, BF),
-            pltpu.VMEM(act_t.shape, BF),
-            pltpu.VMEM(w_all.shape, BF),
-            pltpu.VMEM(unpick.shape, BF),
-        ]
-        + plane_sems(ctx_size)
-        + [pltpu.SemaphoreType.DMA((wa_size,))] * 2
-        + [pltpu.SemaphoreType.DMA((ctx_size,))] * 2
-        + [pltpu.SemaphoreType.DMA((7,))],
-        compiler_params=pltpu.CompilerParams(
-            collective_id=5, has_side_effects=True, vmem_limit_bytes=VMEM_LIMIT
-        ),
-        cost_estimate=pl.CostEstimate(
-            flops=10 * rows * width * head_cols, bytes_accessed=100_000_000, transcendentals=0
-        ),
-        name="attend_back",
-    )(dy, w_rows, o, q, k, v, cosine, sine, probs, act_t, w_all, unpick, gu, down)
+    )(length, x, w, gain, dealt_rows[None, :], tables, gu)
 
 
 def out_kernel(
@@ -901,29 +714,39 @@
     wd_any,
     d_act_ref,
     mlp_ref,
+    act_t_any,
+    d_gu_any,
+    inner_t_any,
+    gw_ref,
+    wd_ref,
+    inner_ref,
     act_t_ref,
     d_gu_ref,
     inner_t_ref,
-    gw_ref,
-    wd_ref,
-    inner_ref,
+    gw_sems,
     sems,
 ):
     hidden_rows = wd_any.shape[0]
     hidden = inner_ref.shape[1]
     width = act_ref.shape[1]
-    loads = [
-        pltpu.make_async_copy(gw_any.at[0], gw_ref.at[0], sems.at[0]),
-        pltpu.make_async_copy(gw_any.at[1], gw_ref.at[1], sems.at[1]),
-        pltpu.make_async_copy(wd_any, wd_ref.at[pl.ds(0, hidden_rows)], sems.at[2]),
-    ]
-    for copy in loads:
-        copy.start()
+    tiles = hidden // 128
+
+    def gw_load(i):
+        columns = pl.ds(pl.multiple_of(i * 128, 128), 128)
+        return pltpu.make_async_copy(
+            gw_any.at[:, :, columns], gw_ref.at[:, :, columns], gw_sems.at[i]
+        )
+
+    wd_load = pltpu.make_async_copy(wd_any, wd_ref.at[pl.ds(0, hidden_rows)], sems.at[0])
+    for i in range(tiles):
+        gw_load(i).start()
+        if i == 1:
+            wd_load.start()
     if hidden > hidden_rows:
         wd_ref[hidden_rows:, :] = jnp.zeros((hidden - hidden_rows, width), BF)
     act_t_ref[...] = act_ref[...].T
-    for copy in loads:
-        copy.wait()
+    act_t_store = pltpu.make_async_copy(act_t_ref, act_t_any, sems.at[1])
+    act_t_store.start()
     act = act_ref[...]
     dz = dz_ref[...]
 
@@ -931,6 +754,11 @@
         columns = pl.ds(first, size)
         gate = jnp.dot(act, gw_ref[0, :, columns], preferred_element_type=F32)
         up = jnp.dot(act, gw_ref[1, :, columns], preferred_element_type=F32)
+
+        @pl.when(first == 0)
+        def _():
+            wd_load.wait()
+
         d_inner = lax.dot_general(
             dz, wd_ref[columns, :], (((1,), (1,)), ((), ())), preferred_element_type=F32
         )
@@ -944,15 +772,26 @@
         d_gu_ref[1, :, columns] = d_up
         inner_t_ref[columns, :] = inner.T
 
-    whole = hidden // CHUNK
+    per_chunk = CHUNK // 128
 
     def one(i, carried):
-        part(pl.multiple_of(i * CHUNK, CHUNK), CHUNK)
+        for j in range(per_chunk):
+
+            @pl.when(i * per_chunk + j < tiles)
+            def _():
+                gw_load(i * per_chunk + j).wait()
+
+        first = jnp.minimum(i * per_chunk, tiles - per_chunk) * 128
+        part(pl.multiple_of(first, 128), CHUNK)
         return carried
 
-    lax.fori_loop(0, whole, one, 0)
-    if hidden > whole * CHUNK:
-        part(whole * CHUNK, hidden - whole * CHUNK)
+    lax.fori_loop(0, -(-tiles // per_chunk), one, 0)
+    stores = [
+        pltpu.make_async_copy(d_gu_ref, d_gu_any, sems.at[2]),
+        pltpu.make_async_copy(inner_t_ref, inner_t_any, sems.at[3]),
+    ]
+    for copy in stores:
+        copy.start()
 
     def two(i, carried):
         place = pl.ds(pl.multiple_of(i * CHUNK, CHUNK), CHUNK)
@@ -969,6 +808,8 @@
         return carried
 
     lax.fori_loop(0, width // CHUNK, two, 0)
+    for copy in stores + [act_t_store]:
+        copy.wait()
 
 
 def mlp(act, dz, gw, wd):
@@ -986,12 +827,16 @@
             jax.ShapeDtypeStruct((hidden, tokens), BF),
         ),
         in_specs=[vmem, vmem, anywhere, anywhere],
-        out_specs=[vmem] * 5,
+        out_specs=[vmem] * 2 + [anywhere] * 3,
         scratch_shapes=[
             pltpu.VMEM(gw.shape, BF),
             pltpu.VMEM((hidden, width), BF),
             pltpu.VMEM((tokens, hidden), BF),
-            pltpu.SemaphoreType.DMA((3,)),
+            pltpu.VMEM((width, tokens), BF),
+            pltpu.VMEM((2, tokens, hidden), BF),
+            pltpu.VMEM((hidden, tokens), BF),
+            pltpu.SemaphoreType.DMA((hidden // 128,)),
+            pltpu.SemaphoreType.DMA((4,)),
         ],
         compiler_params=pltpu.CompilerParams(vmem_limit_bytes=60 * 1024 * 1024),
         cost_estimate=pl.CostEstimate(
@@ -1208,39 +1053,52 @@
     )(parts, mlp, hidden, gain, dz, act_t, d_gu, inner_t, dz_all)
 
 
-def close_kernel(
+def finish_kernel(
     ctx_size,
     wa_size,
-    grads_ref,
+    heads,
+    dy_ref,
     w_ref,
+    o_ref,
+    q_ref,
+    k_ref,
+    v_ref,
+    tables_ref,
     x_ref,
     gain_ref,
-    dh_ref,
-    gu_in,
-    dw_ref,
-    do_parts,
-    gains_ref,
+    gain_two_ref,
+    dealt_column_ref,
+    prob_any,
+    act_t_any,
+    w_all_any,
+    gu_ref,
+    down_ref,
     out_ref,
     gus_ref,
+    downs_ref,
     qkvs_ref,
     outs_ref,
     sums_ref,
     *scratch,
 ):
     p = place_of(ctx_size, wa_size)
-    rows_ref, dw_in, share_ref, do_in, out_share_ref = scratch[8:13]
-    wa_gains, ctx_gains, local = scratch[13:16]
-    dw_sems, do_sems = scratch[16:18], scratch[18:20]
-    wa_sems, ctx_sems = scratch[20:22], scratch[22:24]
-    gu_plane, qkv_plane, out_plane = (scratch[i : i + 4] for i in (24, 28, 32))
-    peers = [lax.rem(p.ctx + i, ctx_size) for i in range(1, ctx_size)]
-    greet(peers, p.up[1:])
+    do_ref, dk_ref, dv_ref, d_out_ref, given_ref = scratch[8:13]
+    late_ref, w_all_ref = scratch[13:15]
+    grads_ref, dw_ref, parts_ref, gu_in_ref, gains_ref = scratch[15:20]
+    rows_ref, dw_in, share_ref, do_in, out_share_ref = scratch[20:25]
+    wa_gains, ctx_gains, local, load_sems = scratch[25:29]
+    gu_sems, dw_sems, do_sems, wa_sems = (scratch[i : i + 2] for i in (29, 31, 33, 35))
+    part_sems, ctx_sems = scratch[37:39], scratch[39:41]
+    down_plane, gu_plane, qkv_plane, out_plane = (scratch[i : i + 4] for i in (41, 45, 49, 53))
+    peers = [lax.rem(p.ctx + i, ctx_size) for i in range(ctx_size)]
+    greet(peers[1:], p.up[1:])
     locals_ = []
 
     def keep(source, target):
         copy = pltpu.make_async_copy(source, target, local.at[len(locals_)])
         copy.start()
         locals_.append(copy)
+        return copy
 
     def spread_of(own, slots, sems):
         half = slots.shape[1] // 2
@@ -1255,66 +1113,180 @@
         spread.start()
         return spread
 
-    def over_wa(source, target, sems):
-        return [
-            send(
-                source(p.up[s]),
-                target.at[s],
-                sems[0].at[s],
-                sems[1].at[s],
-                wa=p.up[s],
+    deal = [
+        send(
+            gu_ref.at[:, p.up[s]], gu_in_ref.at[p.wa], gu_sems[0].at[s], gu_sems[1].at[s], wa=p.up[s]
+        )
+        for s in range(1, wa_size)
+    ]
+    own_deal = keep(gu_ref.at[:, p.wa], gu_in_ref.at[p.wa])
+    down_spread = spread_of(down_ref, downs_ref, down_plane)
+    loads = [
+        pltpu.make_async_copy(source, target, load_sems.at[i])
+        for i, (source, target) in enumerate(
+            (
+                (prob_any, late_ref),
+                (w_all_any, w_all_ref),
+                (act_t_any, late_ref),
             )
-            for s in range(1, wa_size)
-        ]
-
-    def add_up(found, into, step):
-        def one(i, carried):
-            place = pl.ds(pl.multiple_of(i * step, step), step)
-            total = found[0, place, :].astype(F32)
-            for s in range(1, wa_size):
-                total = total + found[s, place, :].astype(F32)
-            into[place, :] = total.astype(BF)
+        )
+    ]
+    for copy in loads[:2]:
+        copy.start()
+    rows = dy_ref.shape[0]
+    width = dy_ref.shape[1]
+    step = ATTEND_ROWS
+    head_cols = heads * HEAD
+    qkv_cols = 3 * head_cols
+    back_scale = 1.0 / math.sqrt(HEAD)
+    d_out_ref[...] = lax.dot_general(
+        o_ref[...], dy_ref[...], (((0,), (0,)), ((), ())), preferred_element_type=F32
+    ).astype(BF)
+
+    def d_out_part(device):
+        place = pl.ds(pl.multiple_of(device * head_cols, head_cols), head_cols)
+        return d_out_ref.at[:, place]
+
+    part_copies = exchange_plane(
+        peers, d_out_part, lambda d: parts_ref.at[d], part_sems[0], part_sems[1]
+    )
+    own_part = keep(d_out_part(p.ctx), parts_ref.at[p.ctx])
+
+    def project(i, carried):
+        place = pl.ds(pl.multiple_of(i * step, step), step)
+        do_ref[place, :] = lax.dot_general(
+            dy_ref[place, :],
+            w_ref[...],
+            (((1,), (1,)), ((), ())),
+            preferred_element_type=F32,
+        ).astype(BF)
+        return carried
+
+    lax.fori_loop(0, rows // step, project, 0)
+    loads[0].wait()
+    dk_ref[...] = jnp.zeros_like(dk_ref)
+    dv_ref[...] = jnp.zeros_like(dv_ref)
+
+    def unrotate(u, place):
+        cosine, sine = tables_ref[0, place, :], tables_ref[1, place, :]
+        return u * cosine - pltpu.roll(u, HEAD // 2, 1) * sine
+
+    for i in range(rows // step):
+        here = slice(i * step, (i + 1) * step)
+        keys = (i + 1) * step
+
+        def back(head, carried):
+            columns = pl.ds(pl.multiple_of(head * HEAD, HEAD), HEAD)
+            d_o = do_ref[here, columns]
+            q = q_ref[here, columns]
+            prob_rows = pl.ds(pl.multiple_of(head * rows + i * step, step), step)
+            probs = late_ref[prob_rows, :keys]
+            d_probs = lax.dot_general(
+                d_o,
+                v_ref[:keys, columns],
+                (((1,), (1,)), ((), ())),
+                preferred_element_type=F32,
+            )
+            wide = probs.astype(F32)
+            row_dot = jnp.sum(wide * d_probs, axis=-1, keepdims=True)
+            d_scores = (wide * (d_probs - row_dot)).astype(BF)
+            d_query = jnp.dot(d_scores, k_ref[:keys, columns], preferred_element_type=F32)
+            given_ref[here, columns] = unrotate(d_query * back_scale, here).astype(BF)
+            dk_ref[:keys, columns] += lax.dot_general(
+                d_scores, q, (((0,), (0,)), ((), ())), preferred_element_type=F32
+            )
+            dv_ref[:keys, columns] += lax.dot_general(
+                probs, d_o, (((0,), (0,)), ((), ())), preferred_element_type=F32
+            )
             return carried
 
-        lax.fori_loop(0, into.shape[0] // step, one, 0)
-
-    per_wa = ctx_size // wa_size
-
-    def do_block(device):
-        return do_parts.at[pl.ds(device * per_wa, per_wa)]
-
-    do_copies = over_wa(do_block, do_in, do_sems)
-    own_loads = [
-        pltpu.make_async_copy(do_block(p.wa), do_in.at[0], local.at[3]),
-        pltpu.make_async_copy(dw_ref.at[p.wa], dw_in.at[0], local.at[4]),
-    ]
-    for copy in own_loads:
-        copy.start()
-    rows = x_ref.shape[0]
-    qkv_columns = grads_ref.shape[1]
+        lax.fori_loop(0, heads, back, 0)
+    loads[2].start()
+    for head in range(heads):
+        columns = slice(head * HEAD, (head + 1) * HEAD)
+        d_key = unrotate(dk_ref[:, columns] * back_scale, slice(0, rows))
+        given_ref[:, head_cols + head * HEAD : head_cols + (head + 1) * HEAD] = d_key.astype(BF)
+    given_ref[:, 2 * head_cols :] = dv_ref[...].astype(BF)
+    down_arrivals = down_spread.arrivals()
+    next(down_arrivals)
+    next(down_arrivals)
+    loads[1].wait()
+
+    def unpick(place, count):
+        given_row = lax.broadcasted_iota(jnp.int32, (count, rows), 1)
+        return jnp.where(given_row == dealt_column_ref[place, :], 1.0, 0.0).astype(BF)
+
+    def put_back(i, carried):
+        place = pl.ds(pl.multiple_of(i * step, step), step)
+        grads_ref[place, :] = jnp.dot(
+            unpick(place, step), given_ref[...], preferred_element_type=F32
+        ).astype(BF)
+        return carried
+
+    lax.fori_loop(0, rows // step, put_back, 0)
+    own_rows = x_ref.shape[0]
 
     def part_of(device):
-        place = pl.ds(pl.multiple_of(device * rows, rows), rows)
+        place = pl.ds(pl.multiple_of(device * own_rows, own_rows), own_rows)
         return lax.dot_general(
             grads_ref[place, :],
-            w_ref[:, :qkv_columns],
+            w_all_ref[:, :qkv_cols],
             (((1,), (1,)), ((), ())),
             preferred_element_type=F32,
         )
 
+    loads[2].wait()
+    wa_rows = dw_ref.shape[1]
+
+    def weights(i, carried):
+        place = pl.ds(pl.multiple_of(i * wa_rows, wa_rows), wa_rows)
+        made = jnp.dot(late_ref[place, :], grads_ref[...], preferred_element_type=F32)
+        dw_ref[i] = made.astype(BF)
+        return carried
+
+    lax.fori_loop(0, wa_size, weights, 0)
+    dw_copies = [
+        send(
+            dw_ref.at[p.up[s]], dw_in.at[s - 1], dw_sems[0].at[s], dw_sems[1].at[s], wa=p.up[s]
+        )
+        for s in range(1, wa_size)
+    ]
     scatter = Scatter(p, part_of, scratch[:8])
     scatter.start()
+    ones = jnp.ones((8, qkv_cols), BF)
+
+    def gains(i, carried):
+        place = pl.ds(pl.multiple_of(i * wa_rows, wa_rows), wa_rows)
+        products = dw_ref[i].astype(F32) * w_all_ref[place, :qkv_cols].astype(F32)
+        high = products.astype(BF)
+        low = (products - high.astype(F32)).astype(BF)
+        sums = [
+            lax.dot_general(
+                ones, part, (((1,), (1,)), ((), ())), preferred_element_type=F32
+            )
+            for part in (high, low)
+        ]
+        gains_ref[0:1, place] = (sums[0] + sums[1])[0:1] / gain_ref[:, place]
+        return carried
+
+    lax.fori_loop(0, wa_size, gains, 0)
+    gains_ref[1:2] = gain_two_ref[...]
     wa_gains[p.wa] = gains_ref[...]
     small = [
         send(gains_ref, wa_gains.at[p.wa], wa_sems[0].at[s], wa_sems[1].at[s], wa=p.up[s])
         for s in range(1, wa_size)
     ]
+    for _ in down_arrivals:
+        pass
+    own_deal.wait()
+    for copy in deal:
+        copy.wait_recv()
     total_columns = rows_ref.shape[1] // 2
     own_columns = total_columns // wa_size
     for i in range(wa_size):
         for part in range(2):
             first = part * total_columns + i * own_columns
-            rows_ref[:, first : first + own_columns] = gu_in[i, part, :, :own_columns]
+            rows_ref[:, first : first + own_columns] = gu_in_ref[i, part, :, :own_columns]
     gu_spread = spread_of(rows_ref, gus_ref, gu_plane)
     for copy in small:
         copy.wait()
@@ -1326,27 +1298,17 @@
     small = [
         send(own_gain, own_gain, ctx_sems[0].at[i], ctx_sems[1].at[i], ctx=peer)
         for i, peer in enumerate(peers)
+        if i > 0
     ]
-    for copy in do_copies:
-        copy.wait_recv()
-    dw_copies = over_wa(lambda d: dw_ref.at[d], dw_in, dw_sems)
-    own_loads[0].wait()
-    for i in range(per_wa):
-        place = pl.ds(i * do_parts.shape[1], do_parts.shape[1])
-        total = do_in[0, i].astype(F32)
-        for s in range(1, wa_size):
-            total = total + do_in[s, i].astype(F32)
-        out_share_ref[place, :] = total.astype(BF)
-    out_spread = spread_of(out_share_ref, outs_ref, out_plane)
+    dh_place = pl.ds(pl.multiple_of(p.ctx * own_rows, own_rows), own_rows)
+    d_hidden = jnp.dot(unpick(dh_place, own_rows), dy_ref[...], preferred_element_type=F32)
     x = x_ref[...].astype(F32)
     scale = lax.rsqrt(jnp.mean(x * x, axis=-1, keepdims=True) + EPSILON)
-    d_normed = scatter.total()
-    out_ref[...] = norm_back(
-        x, scale, gain_ref[...], d_normed, dh_ref[...].astype(F32)
-    ).astype(BF)
-    for _ in out_spread.arrivals():
-        pass
-    for _ in gu_spread.arrivals():
+    out_ref[...] = norm_back(x, scale, gain_ref[...], scatter.total(), d_hidden).astype(BF)
+    gu_arrivals = gu_spread.arrivals()
+    next(gu_arrivals)
+    next(gu_arrivals)
+    for _ in gu_arrivals:
         pass
     for copy in small:
         copy.wait()
@@ -1356,80 +1318,170 @@
     sums_ref[...] = total_gain
     for copy in dw_copies:
         copy.wait_recv()
-    own_loads[1].wait()
-    add_up(dw_in, share_ref, 16)
+    own_part.wait()
+    for copy in part_copies:
+        copy.wait_recv()
+    per_wa = ctx_size // wa_size
+
+    def d_out_block(device):
+        return parts_ref.at[pl.ds(device * per_wa, per_wa)]
+
+    do_copies = [
+        send(
+            d_out_block(p.up[s]), do_in.at[s], do_sems[0].at[s], do_sems[1].at[s], wa=p.up[s]
+        )
+        for s in range(1, wa_size)
+    ]
+
+    def add_up(i, carried):
+        place = pl.ds(pl.multiple_of(i * 16, 16), 16)
+        total = dw_ref[p.wa, place, :].astype(F32)
+        for s in range(1, wa_size):
+            total = total + dw_in[s - 1, place, :].astype(F32)
+        share_ref[place, :] = total.astype(BF)
+        return carried
+
+    lax.fori_loop(0, wa_rows // 16, add_up, 0)
     qkv_spread = spread_of(share_ref, qkvs_ref, qkv_plane)
+    for copy in do_copies:
+        copy.wait_recv()
+    for i in range(per_wa):
+        total = parts_ref[p.wa * per_wa + i].astype(F32)
+        for s in range(1, wa_size):
+            total = total + do_in[s, i].astype(F32)
+        out_share_ref[pl.ds(i * head_cols, head_cols), :] = total.astype(BF)
+    out_spread = spread_of(out_share_ref, outs_ref, out_plane)
     for _ in qkv_spread.arrivals():
         pass
+    for _ in out_spread.arrivals():
+        pass
     scatter.finish()
-    for spread in (gu_spread, qkv_spread, out_spread):
+    for spread in (down_spread, gu_spread, qkv_spread, out_spread):
         spread.finish()
-    for copy in dw_copies + do_copies:
+    for copy in deal + dw_copies + do_copies + part_copies:
         copy.wait_send()
     for copy in locals_:
-        copy.wait()
-
-
-def close(grads, w, x_own, gain, dh, gu, dw, do, gains_own, columns, ctx_size, wa_size):
-    rows, width = x_own.shape
+        if copy is not own_deal and copy is not own_part:
+            copy.wait()
+
+
+def finish(
+    dy,
+    w_rows,
+    o,
+    q,
+    k,
+    v,
+    tables,
+    x_own,
+    gain,
+    gain_two,
+    dealt_column,
+    probs,
+    act_t,
+    w_all,
+    gu,
+    down,
+    columns,
+    ctx_size,
+    wa_size,
+):
+    rows, width = dy.shape
+    head_cols = o.shape[1]
+    heads = head_cols // HEAD
+    own_rows = x_own.shape[0]
     vmem = pl.BlockSpec(memory_space=pltpu.VMEM)
     anywhere = pl.BlockSpec(memory_space=pl.ANY)
+    wa_rows = width // wa_size
     gu_shape = (gu.shape[2], columns)
-    out_shape = (width // wa_size, do.shape[1])
-    shapes = [gu_shape, dw.shape[1:], out_shape]
+    share_shape = (wa_rows, 3 * head_cols)
+    out_shape = (wa_rows, head_cols)
     gains = (2, width)
     return pl.pallas_call(
-        functools.partial(close_kernel, ctx_size, wa_size),
-        out_shape=(jax.ShapeDtypeStruct((rows, width), BF),)
-        + tuple(jax.ShapeDtypeStruct((ctx_size,) + shape, BF) for shape in shapes)
+        functools.partial(finish_kernel, ctx_size, wa_size, heads),
+        out_shape=(jax.ShapeDtypeStruct((own_rows, width), BF),)
+        + tuple(
+            jax.ShapeDtypeStruct((ctx_size,) + shape, BF)
+            for shape in (gu_shape, down.shape, share_shape, out_shape)
+        )
         + (jax.ShapeDtypeStruct(gains, F32),),
-        in_specs=[vmem] * 6 + [anywhere] * 2 + [vmem],
-        out_specs=[vmem] + [anywhere] * 3 + [vmem],
-        scratch_shapes=scatter_scratch(ctx_size, rows, width)
+        in_specs=[vmem] * 11 + [anywhere] * 5,
+        out_specs=[vmem] + [anywhere] * 4 + [vmem],
+        scratch_shapes=scatter_scratch(ctx_size, own_rows, width)
         + [
+            pltpu.VMEM((rows, head_cols), BF),
+            pltpu.VMEM((rows, head_cols), F32),
+            pltpu.VMEM((rows, head_cols), F32),
+            pltpu.VMEM((head_cols, width), BF),
+            pltpu.VMEM((rows, 3 * head_cols), BF),
+            pltpu.VMEM(act_t.shape, BF),
+            pltpu.VMEM(w_all.shape, BF),
+            pltpu.VMEM((rows, 3 * head_cols), BF),
+            pltpu.VMEM((wa_size,) + share_shape, BF),
+            pltpu.VMEM((ctx_size, head_cols, head_cols), BF),
+            pltpu.VMEM((wa_size, 2) + gu.shape[2:], BF),
+            pltpu.VMEM(gains, F32),
             pltpu.VMEM(gu_shape, BF),
-            pltpu.VMEM(dw.shape, BF),
-            pltpu.VMEM(dw.shape[1:], BF),
-            pltpu.VMEM((wa_size, ctx_size // wa_size) + do.shape[1:], BF),
+            pltpu.VMEM((wa_size - 1,) + share_shape, BF),
+            pltpu.VMEM(share_shape, BF),
+            pltpu.VMEM((wa_size, ctx_size // wa_size, head_cols, head_cols), BF),
             pltpu.VMEM(out_shape, BF),
             pltpu.VMEM((wa_size,) + gains, F32),
             pltpu.VMEM((ctx_size,) + gains, F32),
-            pltpu.SemaphoreType.DMA((5,)),
+            pltpu.SemaphoreType.DMA((6,)),
+            pltpu.SemaphoreType.DMA((4,)),
         ]
-        + [pltpu.SemaphoreType.DMA((wa_size,))] * 6
-        + [pltpu.SemaphoreType.DMA((ctx_size,))] * 2
-        + plane_sems(ctx_size) * 3,
+        + [pltpu.SemaphoreType.DMA((wa_size,))] * 8
+        + [pltpu.SemaphoreType.DMA((ctx_size,))] * 4
+        + plane_sems(ctx_size) * 4,
         compiler_params=pltpu.CompilerParams(
-            collective_id=3, has_side_effects=True, vmem_limit_bytes=VMEM_LIMIT
+            collective_id=3, has_side_effects=True, vmem_limit_bytes=VMEM_LIMIT + 2 * 1024 * 1024
         ),
         cost_estimate=pl.CostEstimate(
-            flops=2 * grads.size * width, bytes_accessed=400_000_000, transcendentals=0
+            flops=12 * rows * width * head_cols, bytes_accessed=400_000_000, transcendentals=0
         ),
-        name="close",
-    )(grads, w, x_own, gain, dh, gu, dw, do, gains_own)
-
-
-def widen(blocks, columns, order, step):
+        name="finish",
+    )(
+        dy,
+        w_rows,
+        o,
+        q,
+        k,
+        v,
+        tables,
+        x_own,
+        gain,
+        gain_two,
+        dealt_column,
+        probs,
+        act_t,
+        w_all,
+        gu,
+        down,
+    )
+
+
+def widen(blocks, columns, groups, step):
     count, rows, own = blocks.shape
-    parts = own // columns
+    parts, per_group = own // columns, count // groups
 
     def body(block_ref, out_ref):
         for i in range(parts):
-            for at, device in enumerate(order):
-                first = (i * count + at) * columns
+            for at in range(per_group):
+                first = (i * per_group + at) * columns
                 out_ref[:, first : first + columns] = block_ref[
-                    device, :, i * columns : (i + 1) * columns
+                    at, 0, :, i * columns : (i + 1) * columns
                 ].astype(F32)
 
     return pl.pallas_call(
         body,
         out_shape=jax.ShapeDtypeStruct((rows, count * own), F32),
-        grid=(rows // step,),
-        in_specs=[pl.BlockSpec((count, step, own), lambda r: (0, r, 0))],
-        out_specs=pl.BlockSpec((step, count * own), lambda r: (r, 0)),
+        grid=(rows // step, groups),
+        in_specs=[pl.BlockSpec((per_group, 1, step, own), lambda r, g: (0, g, r, 0))],
+        out_specs=pl.BlockSpec((step, per_group * own), lambda r, g: (r, g)),
         compiler_params=pltpu.CompilerParams(vmem_limit_bytes=VMEM_LIMIT),
         name="widen",
-    )(blocks)
+    )(blocks.reshape(per_group, groups, rows, own))
 
 
 def per_device(
@@ -1444,7 +1496,6 @@
     block_total = block_order.shape[0]
     group_rows = block_total * BLOCK
     own_blocks = tok_rows // BLOCK
-    first_length = lengths[0, 0]
     heads_own = HEADS // ctx_size
     head_cols = heads_own * HEAD
     wa_rows = width // wa_size
@@ -1460,29 +1511,21 @@
         + [lax.dynamic_slice_in_dim(w_out, ctx_index * head_cols, head_cols, 1)],
         axis=1,
     )
-    dealt, all_cols, gu_send = gather_both(
-        tokens[0], own_cols, w_gate_up, ff_own, ctx_size, wa_size
+    in_block = jnp.arange(BLOCK, dtype=jnp.int32)
+    rows_dealt = (block_order[:, None] * BLOCK + in_block[None, :]).reshape(group_rows)
+    dealt_column = rows_dealt[:, None]
+    dealt, all_cols, gu_send, tables = gather_both(
+        tokens[0], own_cols, w_gate_up, dealt_column, lengths, ff_own, ctx_size, wa_size
     )
     dealt = dealt.reshape(group_rows, width)
     all_cols = all_cols.reshape(width, 4 * head_cols)
-
-    rows_given = jnp.arange(group_rows, dtype=jnp.int32)
-    segments = (rows_given >= first_length).astype(jnp.int32)
-    in_block = jnp.arange(BLOCK, dtype=jnp.int32)
-    rows_dealt = (block_order[:, None] * BLOCK + in_block[None, :]).reshape(group_rows)
-    unpick = (rows_dealt[:, None] == rows_given[None, :]).astype(BF)
-    pick = (rows_given[:, None] == rows_dealt[None, :]).astype(BF)
-    given_tables = rotary_tables(rows_given - segments * first_length)
-    dealt_tables = rotary_tables(
-        rows_dealt - (rows_dealt >= first_length).astype(jnp.int32) * first_length
-    )
     act_one_t, own_given, query_b, key_b, value_b, mixed_b, probs_b, gu_mine, out_rows = attend(
-        segments,
+        lengths,
         dealt,
         all_cols,
         norm1_gain[None, :],
-        pick,
-        *dealt_tables,
+        rows_dealt,
+        tables[0],
         gu_send,
         ctx_size,
         wa_size,
@@ -1511,44 +1554,31 @@
         wa_size,
     )
     d_branch_b = d_branches.reshape(group_rows, width)
-    dealt_qkv, d_hidden_dealt, qkv_parts, gain_column, out_parts, gu_pieces, downs = attend_back(
+    d_tokens, gus, downs, qkvs, outs, gain_sums = finish(
         d_branch_b,
         out_rows,
         mixed_b,
         query_b,
         key_b,
         value_b,
-        *given_tables,
+        tables[1],
+        tokens[0],
+        norm1_gain[None, :],
+        gain_two_part,
+        dealt_column,
         probs_b,
         act_one_t,
         all_cols,
-        unpick,
         gu_piece_grad.reshape((2, wa_size) + gu_piece_grad.shape[1:]),
         down_piece_grad,
-        ctx_size,
-        wa_size,
-    )
-    gain_one_part = gain_column.reshape(1, width) / norm1_gain[None, :]
-    d_tokens, gus, qkvs, outs, gain_sums = close(
-        dealt_qkv,
-        all_cols,
-        tokens[0],
-        norm1_gain[None, :],
-        d_hidden_dealt,
-        gu_pieces,
-        qkv_parts,
-        out_parts,
-        jnp.concatenate([gain_one_part, gain_two_part], axis=0),
         2 * ff_total,
         ctx_size,
         wa_size,
     )
     d_gate_up = gus.reshape(wa_rows, 2 * ff_total).astype(F32)
-    in_order = list(range(ctx_size))
-    by_core = in_order[0::2] + in_order[1::2]
-    d_down = widen(downs, downs.shape[2], by_core, ff_own // 2 if ff_own % 32 == 0 else ff_own)
-    d_qkv = widen(qkvs, head_cols, in_order, 64)
-    d_out = widen(outs, head_cols, in_order, 128)
+    d_down = widen(downs, downs.shape[2], 2, ff_own // 2 if ff_own % 32 == 0 else ff_own)
+    d_qkv = widen(qkvs, head_cols, 1, 64)
+    d_out = widen(outs, head_cols, 1, 64)
     return (
         out_given[None],
         d_tokens[None],

time: 592 us -> 592 us (level)
  other arithmetic: 28.1 us -> 13.9 us
  Pallas kernels: 552 us -> 560 us
    pallas_call x2 -> x1, Pallas kernels: 181 us -> 180 us  [finish(): pl.pallas_call(functools.partial(finish_kernel, ctx_size, wa_size, heads)...]
where the time goes in v6:
time: 592 us; the launch traced here: 582 us
  Pallas kernels  560 us (95%)
  other arithmetic  13.9 us (2%)
  local copies, waits for them, and re-layouts  7.52 us (1%)
    pallas_call x1, Pallas kernels, finish(): pl.pallas_call(functools.partial(finish_kernel, ctx_size, wa_size, heads)...  180 us
    pallas_call x1, Pallas kernels, turn(): pl.pallas_call(functools.partial(turn_kernel, ctx_size, wa_size), out_sha...  107 us
    pallas_call x1, Pallas kernels, out_project(): pl.pallas_call(functools.partial(out_kernel, ctx_size, wa_size), out_shap...  94.1 us
    pallas_call x1, Pallas kernels, gather_both(): pl.pallas_call(functools.partial(gather_kernel, ctx_size, wa_size, cuts,...  74.6 us
    pallas_call x1, Pallas kernels, attend(): pl.pallas_call(functools.partial(attend_kernel, ctx_size, wa_size, heads)...  43.1 us
    pallas_call x1, Pallas kernels, mlp(): pl.pallas_call(mlp_kernel, out_shape=(jax.ShapeDtypeStruct((tokens, width...  39.5 us
    pallas_call x3, Pallas kernels, widen(): pl.pallas_call(body, out_shape=jax.ShapeDtypeStruct((rows, count * own),...  22.2 us
    convert_element_type x1, other arithmetic, per_device(): d_gate_up = gus.reshape(wa_rows, 2 * ff_total).astype(F32)  12.7 us

profile of v6, /device:TPU:9, one launch (start us, length us, event | category | flops | bytes accessed | tf_op | source)
XLA Modules:
  0.0 582.5 jit_solution(9447922907743683675)
XLA Ops:
  0.6 0.0 copy-start.4
  0.6 1.3 constant_dynamic-slice_fusion.3
  1.9 1.1 pad_maximum_fusion.w_ref
  3.0 0.0 copy-done.4
  3.0 0.1 iota_add_fusion
  3.1 0.0 copy-start.2
  3.1 1.0 copy.19.dealt_column_ref
  4.2 74.6 %gather_both.1 = (bf16[8,128,2048]{2,1,0:T(8,128)(2,1)}, bf16[4,512,1024]{2,1,0:T(8,128)(2,1)}, bf16[4,2,64,1408]{3,2,1,0:T(8,128)(2,1)}, f32[2,2,1024,128]{3,2,1,0:T(8,128)}) custom-call(bf16[128,2048]{1,0:T(8,128)(2,1)} %bitcast.43, bf16[512,1024]{1,0:T(8,128)(2,1)} %pad_maximum_fusion.w_ref, bf16[512,11008]{1,0:T(8,128)(2,1)} %gu_ref.1, ...), custom_call_target="tpu_custom_call" | custom-call | bytes 200000000 | tf_op jit(solution)/shard_map/gather_both/pallas_call | solution.py:410
  78.8 0.0 copy-done.2
  78.8 3.0 slice_bitcast_fusion
  81.8 43.1 %attend.1 = (bf16[2048,1024]{1,0:T(8,128)(2,1)}, bf16[128,2048]{1,0:T(8,128)(2,1)}, bf16[1024,256]{1,0:T(8,128)(2,1)}, bf16[1024,256]{1,0:T(8,128)(2,1)}, bf16[1...) custom-call(s32[1,2]{1,0:T(1,128)} %length_ref.3, ...), custom_call_target="tpu_custom_call" | custom-call | flops 3221225472 | bytes 100000000 | tf_op jit(solution)/shard_map/attend/pallas_call | solution.py:574
  124.9 94.1 %out_project.1 = (f32[128,2048]{1,0:T(8,128)}, bf16[4,128,2048]{2,1,0:T(8,128)(2,1)}, bf16[4,128,2048]{2,1,0:T(8,128)(2,1)}, bf16[2,4,8,64,1408]{4,3,2,1,0:T(8,128)(2,1)}) custom-call(bf16[1024,256]{1,0:T(8,128)(2,1)} %get-tuple-element.45.mixed_ref.o_ref, bf16[256,2048]{1,0:T(8,128)(2,1)} %get-tuple-element.46.w_ref, ...), custom_call_target="tpu_custom_call" | custom-call | flops 1073741824 | bytes 200000000 | tf_op jit(solution)/shard_map/out_project/pallas_call | solution.py:686
  219.0 39.5 %mlp.1 = (bf16[512,2048]{1,0:T(8,128)(2,1)}, bf16[512,2048]{1,0:T(8,128)(2,1)}, bf16[2048,512]{1,0:T(8,128)(2,1)}, bf16[2,512,1408]{2,1,0:T(8,128)(2,1)}, bf16[1408,512]{1,0:T(8,128)(2,1)}) custom-call(bf16[512,2048]{1,0:T(8,128)(2,1)} %bitcast.58, bf16[512,2048]{1,0:T(8,128)(2,1)} %bitcast.37, bf16[2,2048,1408]{2,1,0:T(8,128)(2,1)} %bitcast.56, ...), custom_call_target="tpu_custom_call" | custom-call | flops 17716740096 | bytes 50000000 | tf_op jit(solution)/shard_map/mlp/pallas_call | solution.py:820
  258.5 106.5 %turn.1 = (bf16[8,128,2048]{2,1,0:T(8,128)(2,1)}, f32[1,2048]{1,0:T(1,128)}, bf16[128,2048]{1,0:T(8,128)(2,1)}, bf16[8,64,1408]{2,1,0:T(8,128)(2,1)}, bf16[1376,256]{1,0:T(8,128)(2,1)}) custom-call(bf16[4,128,2048]{2,1,0:T(8,128)(2,1)} %bitcast.39, bf16[4,128,2048]{2,1,0:T(8,128)(2,1)} %bitcast.40, f32[128,2048]{1,0:T(8,128)} %get-tuple-element.54.hidden_ref, ...), custom_call_target="tpu_custom_call" | custom-call | bytes 200000000 | tf_op jit(solution)/shard_map/turn/pallas_call | solution.py:1021
  365.0 180.1 %finish.1 = (bf16[128,2048]{1,0:T(8,128)(2,1)}, bf16[8,64,11008]{2,1,0:T(8,128)(2,1)}, bf16[8,1376,256]{2,1,0:T(8,128)(2,1)}, bf16[8,512,768]{2,1,0:T(8,128)(2,1...) custom-call(bf16[1024,2048]{1,0:T(8,128)(2,1)} %bitcast.35, bf16[256,2048]{1,0:T(8,128)(2,1)} %get-tuple-element.46.w_ref, ...), custom_call_target="tpu_custom_call" | custom-call | flops 6442450944 | bytes 400000000 | tf_op jit(solution)/shard_map/finish/pallas_call | solution.py:1400
  545.1 12.7 %bitcast_convert_fusion = f32[512,11008]{1,0:T(8,128)} fusion(bf16[8,64,11008]{2,1,0:T(8,128)(2,1)} %get-tuple-element.72), kind=kLoop, calls=%fused_computation | loop fusion | flops 5636096 | bytes 33816576 | tf_op jit(solution)/shard_map/convert_element_type | solution.py:1578
  557.9 8.8 %widen.3 = f32[512,6144]{1,0:T(8,128)} custom-call(bf16[8,1,512,768]{3,2,1,0:T(8,128)(2,1)} %bitcast.31), custom_call_target="tpu_custom_call" | custom-call | tf_op jit(solution)/shard_map/widen/pallas_call | solution.py:1476
  566.7 7.3 %widen.5 = f32[1376,2048]{1,0:T(8,128)} custom-call(bf16[4,2,1376,256]{3,2,1,0:T(8,128)(2,1)} %bitcast.32), custom_call_target="tpu_custom_call" | custom-call | tf_op jit(solution)/shard_map/widen/pallas_call | solution.py:1476
  574.0 0.0 copy-start.3
  574.0 0.0 copy-start
  574.0 0.0 copy-start.1
  574.0 6.1 %widen.4 = f32[512,2048]{1,0:T(8,128)} custom-call(bf16[8,1,512,256]{3,2,1,0:T(8,128)(2,1)} %bitcast.36), custom_call_target="tpu_custom_call" | custom-call | tf_op jit(solution)/shard_map/widen/pallas_call | solution.py:1476
  580.1 0.0 copy-done.3
  580.1 0.6 fusion
  580.7 0.0 copy-done
  580.7 0.8 copy.23
  581.5 0.0 copy-done.1
  581.5 0.8 copy.24
  (1 shorter events, 0.0 us)
Async XLA Ops:
  0.6 2.4 copy-start.4
  3.1 75.6 %copy-start.2 = (s32[8,128]{1,0:T(8,128)}, s32[8,128]{1,0:T(8,128)S(1)}, u32[]{:S(2)}) copy-start(s32[8,128]{1,0:T(8,128)S(1)} %iota_add_fusion) | copy-start | bytes 12292
  574.0 6.1 %copy-start.3 = (f32[2,2048]{1,0:T(2,128)S(1)}, f32[2,2048]{1,0:T(2,128)}, u32[]{:S(2)}) copy-start(f32[2,2048]{1,0:T(2,128)} %get-tuple-element.69) | copy-start | bytes 49156
  574.0 6.7 %copy-start = (bf16[128,2048]{1,0:T(8,128)(2,1)S(1)}, bf16[128,2048]{1,0:T(8,128)(2,1)}, u32[]{:S(2)}) copy-start(bf16[128,2048]{1,0:T(8,128)(2,1)} %get-tuple-element.58) | copy-start | bytes 1572868
  574.0 7.5 %copy-start.1 = (bf16[128,2048]{1,0:T(8,128)(2,1)S(1)}, bf16[128,2048]{1,0:T(8,128)(2,1)}, u32[]{:S(2)}) copy-start(bf16[128,2048]{1,0:T(8,128)(2,1)} %get-tuple-element.68) | copy-start | bytes 1572868

commit v7 on v6

--- a/solution.py
+++ b/solution.py
@@ -314,7 +314,8 @@
     xs_ref,
     ws_ref,
     cut_ref,
-    tables_ref,
+    dealt_tables_ref,
+    given_tables_ref,
     *scratch,
 ):
     p = place_of(ctx_size, wa_size)
@@ -362,7 +363,7 @@
                 cut_ref[to, part, :, own_columns:] = jnp.zeros(
                     (piece_rows, hidden - own_columns), BF
                 )
-    group_rows = tables_ref.shape[2]
+    group_rows = given_tables_ref.shape[1]
     table_rows = min(group_rows, 256)
     first_length = length_ref[:, 0:1]
     lane = lax.broadcasted_iota(jnp.int32, (table_rows, HEAD), 1)
@@ -371,11 +372,14 @@
     def tables(i, carried):
         place = pl.ds(pl.multiple_of(i * table_rows, table_rows), table_rows)
         given = lax.broadcasted_iota(jnp.int32, (table_rows, 1), 0) + i * table_rows
-        for kind, row in enumerate((dealt_column_ref[place, :], given)):
+        for target, row in (
+            (dealt_tables_ref, dealt_column_ref[place, :]),
+            (given_tables_ref, given),
+        ):
             position = row - jnp.where(row >= first_length, first_length, 0)
             angle = position.astype(F32) * freq_ref[...]
-            tables_ref[kind, 0, place, :] = jnp.cos(angle)
-            tables_ref[kind, 1, place, :] = jnp.sin(angle) * sign
+            target[0, place, :] = jnp.cos(angle)
+            target[1, place, :] = jnp.sin(angle) * sign
         return carried
 
     late = []
@@ -413,10 +417,11 @@
             jax.ShapeDtypeStruct((ctx_size,) + x.shape, x.dtype),
             jax.ShapeDtypeStruct((wa_size,) + w.shape, w.dtype),
             jax.ShapeDtypeStruct((wa_size, 2, piece_rows, hidden), BF),
-            jax.ShapeDtypeStruct((2, 2, dealt_column.shape[0], HEAD), F32),
+            jax.ShapeDtypeStruct((2, dealt_column.shape[0], HEAD), F32),
+            jax.ShapeDtypeStruct((2, dealt_column.shape[0], HEAD), F32),
         ),
         in_specs=[anywhere] * 3 + [vmem] * 3,
-        out_specs=[anywhere] * 2 + [vmem] * 2,
+        out_specs=[anywhere] * 2 + [vmem] * 3,
         scratch_shapes=plane_sems(ctx_size)
         + [pltpu.SemaphoreType.DMA((wa_size - 1, cuts))] * 2
         + [pltpu.SemaphoreType.DMA((3,)), pltpu.VMEM((piece_rows, gu.shape[1]), BF)],
@@ -723,30 +728,30 @@
     act_t_ref,
     d_gu_ref,
     inner_t_ref,
-    gw_sems,
     sems,
 ):
     hidden_rows = wd_any.shape[0]
     hidden = inner_ref.shape[1]
     width = act_ref.shape[1]
-    tiles = hidden // 128
-
-    def gw_load(i):
-        columns = pl.ds(pl.multiple_of(i * 128, 128), 128)
-        return pltpu.make_async_copy(
-            gw_any.at[:, :, columns], gw_ref.at[:, :, columns], gw_sems.at[i]
-        )
-
-    wd_load = pltpu.make_async_copy(wd_any, wd_ref.at[pl.ds(0, hidden_rows)], sems.at[0])
-    for i in range(tiles):
-        gw_load(i).start()
-        if i == 1:
-            wd_load.start()
+    whole = hidden // CHUNK
+    ahead = min(2, whole) * CHUNK
+    loads = [
+        pltpu.make_async_copy(gw_any.at[:, :, :ahead], gw_ref.at[:, :, :ahead], sems.at[4]),
+        pltpu.make_async_copy(wd_any, wd_ref.at[pl.ds(0, hidden_rows)], sems.at[0]),
+    ]
+    if hidden > ahead:
+        loads.append(
+            pltpu.make_async_copy(gw_any.at[:, :, ahead:], gw_ref.at[:, :, ahead:], sems.at[5])
+        )
+    for copy in loads:
+        copy.start()
     if hidden > hidden_rows:
         wd_ref[hidden_rows:, :] = jnp.zeros((hidden - hidden_rows, width), BF)
     act_t_ref[...] = act_ref[...].T
     act_t_store = pltpu.make_async_copy(act_t_ref, act_t_any, sems.at[1])
     act_t_store.start()
+    for copy in loads[:2]:
+        copy.wait()
     act = act_ref[...]
     dz = dz_ref[...]
 
@@ -754,11 +759,6 @@
         columns = pl.ds(first, size)
         gate = jnp.dot(act, gw_ref[0, :, columns], preferred_element_type=F32)
         up = jnp.dot(act, gw_ref[1, :, columns], preferred_element_type=F32)
-
-        @pl.when(first == 0)
-        def _():
-            wd_load.wait()
-
         d_inner = lax.dot_general(
             dz, wd_ref[columns, :], (((1,), (1,)), ((), ())), preferred_element_type=F32
         )
@@ -772,20 +772,16 @@
         d_gu_ref[1, :, columns] = d_up
         inner_t_ref[columns, :] = inner.T
 
-    per_chunk = CHUNK // 128
-
     def one(i, carried):
-        for j in range(per_chunk):
-
-            @pl.when(i * per_chunk + j < tiles)
-            def _():
-                gw_load(i * per_chunk + j).wait()
-
-        first = jnp.minimum(i * per_chunk, tiles - per_chunk) * 128
-        part(pl.multiple_of(first, 128), CHUNK)
+        part(pl.multiple_of(i * CHUNK, CHUNK), CHUNK)
         return carried
 
-    lax.fori_loop(0, -(-tiles // per_chunk), one, 0)
+    lax.fori_loop(0, ahead // CHUNK, one, 0)
+    for copy in loads[2:]:
+        copy.wait()
+    lax.fori_loop(ahead // CHUNK, whole, one, 0)
+    if hidden > whole * CHUNK:
+        part(whole * CHUNK, hidden - whole * CHUNK)
     stores = [
         pltpu.make_async_copy(d_gu_ref, d_gu_any, sems.at[2]),
         pltpu.make_async_copy(inner_t_ref, inner_t_any, sems.at[3]),
@@ -835,8 +831,7 @@
             pltpu.VMEM((width, tokens), BF),
             pltpu.VMEM((2, tokens, hidden), BF),
             pltpu.VMEM((hidden, tokens), BF),
-            pltpu.SemaphoreType.DMA((hidden // 128,)),
-            pltpu.SemaphoreType.DMA((4,)),
+            pltpu.SemaphoreType.DMA((6,)),
         ],
         compiler_params=pltpu.CompilerParams(vmem_limit_bytes=60 * 1024 * 1024),
         cost_estimate=pl.CostEstimate(
@@ -1461,27 +1456,52 @@
     )
 
 
-def widen(blocks, columns, groups, step):
-    count, rows, own = blocks.shape
-    parts, per_group = own // columns, count // groups
-
-    def body(block_ref, out_ref):
-        for i in range(parts):
-            for at in range(per_group):
-                first = (i * per_group + at) * columns
-                out_ref[:, first : first + columns] = block_ref[
-                    at, 0, :, i * columns : (i + 1) * columns
-                ].astype(F32)
-
+def widen_kernel(count, head_cols, gu_ref, down_ref, qkv_ref, do_ref, *out_refs):
+    gu_out, down_out, qkv_out, do_out = out_refs
+    gu_out[...] = gu_ref[0].astype(F32)
+    down_out[...] = down_ref[0].astype(F32)
+    for device in range(count):
+        for part in range(3):
+            first = (part * count + device) * head_cols
+            qkv_out[:, first : first + head_cols] = qkv_ref[
+                device, :, part * head_cols : (part + 1) * head_cols
+            ].astype(F32)
+        first = device * head_cols
+        do_out[:, first : first + head_cols] = do_ref[device].astype(F32)
+
+
+def widen(gus, downs, qkvs, outs):
+    count, gu_rows, gu_columns = gus.shape
+    down_rows, down_columns = downs.shape[1:]
+    rows, qkv_columns = qkvs.shape[1:]
+    head_cols = outs.shape[2]
+    step = rows // count
     return pl.pallas_call(
-        body,
-        out_shape=jax.ShapeDtypeStruct((rows, count * own), F32),
-        grid=(rows // step, groups),
-        in_specs=[pl.BlockSpec((per_group, 1, step, own), lambda r, g: (0, g, r, 0))],
-        out_specs=pl.BlockSpec((step, per_group * own), lambda r, g: (r, g)),
+        functools.partial(widen_kernel, count, head_cols),
+        out_shape=(
+            jax.ShapeDtypeStruct((count * gu_rows, gu_columns), F32),
+            jax.ShapeDtypeStruct((down_rows, count * down_columns), F32),
+            jax.ShapeDtypeStruct((rows, count * qkv_columns), F32),
+            jax.ShapeDtypeStruct((rows, count * head_cols), F32),
+        ),
+        grid=(count,),
+        in_specs=[
+            pl.BlockSpec((1, gu_rows, gu_columns), lambda i: (i, 0, 0)),
+            pl.BlockSpec((1, down_rows, down_columns), lambda i: (i, 0, 0)),
+            pl.BlockSpec((count, step, qkv_columns), lambda i: (0, i, 0)),
+            pl.BlockSpec((count, step, head_cols), lambda i: (0, i, 0)),
+        ],
+        out_specs=[
+            pl.BlockSpec((gu_rows, gu_columns), lambda i: (i, 0)),
+            pl.BlockSpec(
+                (down_rows, down_columns), lambda i: (0, (i % 2) * (count // 2) + i // 2)
+            ),
+            pl.BlockSpec((step, count * qkv_columns), lambda i: (i, 0)),
+            pl.BlockSpec((step, count * head_cols), lambda i: (i, 0)),
+        ],
         compiler_params=pltpu.CompilerParams(vmem_limit_bytes=VMEM_LIMIT),
         name="widen",
-    )(blocks.reshape(per_group, groups, rows, own))
+    )(gus, downs, qkvs, outs)
 
 
 def per_device(
@@ -1514,7 +1534,7 @@
     in_block = jnp.arange(BLOCK, dtype=jnp.int32)
     rows_dealt = (block_order[:, None] * BLOCK + in_block[None, :]).reshape(group_rows)
     dealt_column = rows_dealt[:, None]
-    dealt, all_cols, gu_send, tables = gather_both(
+    dealt, all_cols, gu_send, dealt_tables, given_tables = gather_both(
         tokens[0], own_cols, w_gate_up, dealt_column, lengths, ff_own, ctx_size, wa_size
     )
     dealt = dealt.reshape(group_rows, width)
@@ -1525,7 +1545,7 @@
         all_cols,
         norm1_gain[None, :],
         rows_dealt,
-        tables[0],
+        dealt_tables,
         gu_send,
         ctx_size,
         wa_size,
@@ -1561,7 +1581,7 @@
         query_b,
         key_b,
         value_b,
-        tables[1],
+        given_tables,
         tokens[0],
         norm1_gain[None, :],
         gain_two_part,
@@ -1575,10 +1595,7 @@
         ctx_size,
         wa_size,
     )
-    d_gate_up = gus.reshape(wa_rows, 2 * ff_total).astype(F32)
-    d_down = widen(downs, downs.shape[2], 2, ff_own // 2 if ff_own % 32 == 0 else ff_own)
-    d_qkv = widen(qkvs, head_cols, 1, 64)
-    d_out = widen(outs, head_cols, 1, 64)
+    d_gate_up, d_down, d_qkv, d_out = widen(gus, downs, qkvs, outs)
     return (
         out_given[None],
         d_tokens[None],

time: 592 us -> 574 us (0.970)
  other arithmetic: 13.9 us -> 1.84 us
    convert_element_type x1 -> x0, other arithmetic: 12.7 us -> none  [per_device(): d_gate_up = gus.reshape(wa_rows, 2 * ff_total).astype(F32)]
    pallas_call x1, Pallas kernels: 39.5 us -> 32.1 us  [mlp(): pl.pallas_call(mlp_kernel, out_shape=(jax.ShapeDtypeStruct((tokens, width...]
    pallas_call x3 -> x1, Pallas kernels: 22.2 us -> 25.2 us  [widen(): pl.pallas_call(functools.partial(widen_kernel, count, head_cols), out_sha...]
where the time goes in v7:
time: 574 us; the launch traced here: 564 us
  Pallas kernels  556 us (97%)
    pallas_call x1, Pallas kernels, finish(): pl.pallas_call(functools.partial(finish_kernel, ctx_size, wa_size, heads)...  180 us
    pallas_call x1, Pallas kernels, turn(): pl.pallas_call(functools.partial(turn_kernel, ctx_size, wa_size), out_sha...  107 us
    pallas_call x1, Pallas kernels, out_project(): pl.pallas_call(functools.partial(out_kernel, ctx_size, wa_size), out_shap...  94.1 us
    pallas_call x1, Pallas kernels, gather_both(): pl.pallas_call(functools.partial(gather_kernel, ctx_size, wa_size, cuts,...  74.7 us
    pallas_call x1, Pallas kernels, attend(): pl.pallas_call(functools.partial(attend_kernel, ctx_size, wa_size, heads)...  43.2 us
    pallas_call x1, Pallas kernels, mlp(): pl.pallas_call(mlp_kernel, out_shape=(jax.ShapeDtypeStruct((tokens, width...  32.1 us
    pallas_call x1, Pallas kernels, widen(): pl.pallas_call(functools.partial(widen_kernel, count, head_cols), out_sha...  25.2 us

profile of v7, /device:TPU:9, one launch (start us, length us, event | category | flops | bytes accessed | tf_op | source)
XLA Modules:
  0.0 564.4 jit_solution(1201877620229383171)
XLA Ops:
  0.6 0.7 multiply_bitcast_fusion
  1.3 0.1 iota_add_fusion
  1.4 0.0 copy-start.2
  1.4 1.0 copy.19.dealt_column_ref
  2.4 1.3 constant_dynamic-slice_fusion.3
  3.7 1.1 pad_maximum_fusion.w_ref
  4.8 0.0 copy-done.2
  4.8 74.7 %gather_both.1 = (bf16[8,128,2048]{2,1,0:T(8,128)(2,1)}, bf16[4,512,1024]{2,1,0:T(8,128)(2,1)}, bf16[4,2,64,1408]{3,2,1,0:T(8,128)(2,1)}, f32[2,1024,128]{2,1,0:T(8,128)}, f32[2,1024,128]{2,1,0:T(8,128)}) custom-call(bf16[128,2048]{1,0:T(8,128)(2,1)} %bitcast.30, bf16[512,1024]{1,0:T(8,128)(2,1)} %pad_maximum_fusion.w_ref, bf16[512,11008]{1,0:T(8,128)(2,1)} %gu_ref.1, ...), custom_call_target="tpu_custom_call" | custom-call | bytes 200000000 | tf_op jit(solution)/shard_map/gather_both/pallas_call | solution.py:414
  79.5 43.2 %attend.1 = (bf16[2048,1024]{1,0:T(8,128)(2,1)}, bf16[128,2048]{1,0:T(8,128)(2,1)}, bf16[1024,256]{1,0:T(8,128)(2,1)}, bf16[1024,256]{1,0:T(8,128)(2,1)}, bf16[1...) custom-call(s32[1,2]{1,0:T(1,128)} %length_ref.3, ...), custom_call_target="tpu_custom_call" | custom-call | flops 3221225472 | bytes 100000000 | tf_op jit(solution)/shard_map/attend/pallas_call | solution.py:579
  122.6 94.1 %out_project.1 = (f32[128,2048]{1,0:T(8,128)}, bf16[4,128,2048]{2,1,0:T(8,128)(2,1)}, bf16[4,128,2048]{2,1,0:T(8,128)(2,1)}, bf16[2,4,8,64,1408]{4,3,2,1,0:T(8,128)(2,1)}) custom-call(bf16[1024,256]{1,0:T(8,128)(2,1)} %get-tuple-element.50.mixed_ref.o_ref, bf16[256,2048]{1,0:T(8,128)(2,1)} %get-tuple-element.51.w_ref, ...), custom_call_target="tpu_custom_call" | custom-call | flops 1073741824 | bytes 200000000 | tf_op jit(solution)/shard_map/out_project/pallas_call | solution.py:691
  216.8 32.1 %mlp.1 = (bf16[512,2048]{1,0:T(8,128)(2,1)}, bf16[512,2048]{1,0:T(8,128)(2,1)}, bf16[2048,512]{1,0:T(8,128)(2,1)}, bf16[2,512,1408]{2,1,0:T(8,128)(2,1)}, bf16[1408,512]{1,0:T(8,128)(2,1)}) custom-call(bf16[512,2048]{1,0:T(8,128)(2,1)} %bitcast.45, bf16[512,2048]{1,0:T(8,128)(2,1)} %bitcast.24, bf16[2,2048,1408]{2,1,0:T(8,128)(2,1)} %bitcast.43, ...), custom_call_target="tpu_custom_call" | custom-call | flops 17716740096 | bytes 50000000 | tf_op jit(solution)/shard_map/mlp/pallas_call | solution.py:816
  248.9 107.3 %turn.1 = (bf16[8,128,2048]{2,1,0:T(8,128)(2,1)}, f32[1,2048]{1,0:T(1,128)}, bf16[128,2048]{1,0:T(8,128)(2,1)}, bf16[8,64,1408]{2,1,0:T(8,128)(2,1)}, bf16[1376,256]{1,0:T(8,128)(2,1)}) custom-call(bf16[4,128,2048]{2,1,0:T(8,128)(2,1)} %bitcast.26, bf16[4,128,2048]{2,1,0:T(8,128)(2,1)} %bitcast.27, f32[128,2048]{1,0:T(8,128)} %get-tuple-element.59.hidden_ref, ...), custom_call_target="tpu_custom_call" | custom-call | bytes 200000000 | tf_op jit(solution)/shard_map/turn/pallas_call | solution.py:1016
  356.1 179.6 %finish.1 = (bf16[128,2048]{1,0:T(8,128)(2,1)}, bf16[8,64,11008]{2,1,0:T(8,128)(2,1)}, bf16[8,1376,256]{2,1,0:T(8,128)(2,1)}, bf16[8,512,768]{2,1,0:T(8,128)(2,1...) custom-call(bf16[1024,2048]{1,0:T(8,128)(2,1)} %bitcast.23, bf16[256,2048]{1,0:T(8,128)(2,1)} %get-tuple-element.51.w_ref, ...), custom_call_target="tpu_custom_call" | custom-call | flops 6442450944 | bytes 400000000 | tf_op jit(solution)/shard_map/finish/pallas_call | solution.py:1395
  535.7 1.4 fusion
  537.1 0.0 copy-start
  537.1 0.0 copy-start.1
  537.1 25.2 %widen.1 = (f32[512,11008]{1,0:T(8,128)}, f32[1376,2048]{1,0:T(8,128)}, f32[512,6144]{1,0:T(8,128)}, f32[512,2048]{1,0:T(8,128)}) custom-call(bf16[8,64,11008]{2,1,0:T(8,128)(2,1)} %get-tuple-element.76.gu_ref, bf16[8,1376,256]{2,1,0:T(8,128)(2,1)} %get-tuple-element.77.down_ref, bf16[8,512,768]{2,1,0:T(8,128)(2,1)} %get-tuple-element.78.qkv_ref, ...), custom_call_target="tpu_custom_call" | custom-call | tf_op jit(solution)/shard_map/widen/pallas_call | solution.py:1479
  562.4 0.0 copy-done
  562.4 0.8 copy.23
  563.2 0.0 copy-done.1
  563.2 0.8 copy.24
Async XLA Ops:
  1.4 3.4 copy-start.2
  537.1 25.3 %copy-start = (bf16[128,2048]{1,0:T(8,128)(2,1)S(1)}, bf16[128,2048]{1,0:T(8,128)(2,1)}, u32[]{:S(2)}) copy-start(bf16[128,2048]{1,0:T(8,128)(2,1)} %get-tuple-element.63) | copy-start | bytes 1572868
  537.1 26.1 %copy-start.1 = (bf16[128,2048]{1,0:T(8,128)(2,1)S(1)}, bf16[128,2048]{1,0:T(8,128)(2,1)}, u32[]{:S(2)}) copy-start(bf16[128,2048]{1,0:T(8,128)(2,1)} %get-tuple-element.74) | copy-start | bytes 1572868
